TPU v7x, 128 devices: a whole 4x4x4 slice. The times are simulated.
128 devices in a mesh: dp: 2 (over core), row: 4 (over x), col: 16 (over z, y).
Axes of the slice: x: 4, y: 4, z: 4, core: 2. Of those that a mesh axis runs over, the one named last changes fastest.
Arguments:
- forget_tokens: bfloat16 [256, 6144], P('dp', 'col'), may hold values from -6 to 6
- forget_cotangent: bfloat16 [256, 6144], P('dp', 'col'), may hold values from -6 to 6
- forget_labels: int32 [256], P('dp'), may hold values 0 or 1
- retain_tokens: bfloat16 [256, 6144], P('dp', 'col'), may hold values from -6 to 6
- ln_gain: float32 [6144], P('col'), may hold values from 0.25 to 1.75
- w_in: bfloat16 [6144, 24576], P('col', 'row'), may hold values from -0.078125 to 0.078125
- b_in: float32 [24576], P('row'), may hold values from -3 to 3
- w_out: bfloat16 [24576, 6144], P('row', 'col'), may hold values from -0.0390625 to 0.0390625
- b_out: float32 [6144], P('col'), may hold values from -3 to 3
- pruned: int32 [512], P('row'), may hold values from 0 to 24575, as said below
Outputs:
- saliency: float32 [24576], P('row')
- retain_out: bfloat16 [256, 6144], P(('dp', 'row'), 'col')
Inputs may be any that keep to these rules, and one draw needn't show every extreme that they name: `pruned`: entries r * 128 to (r + 1) * 128 - 1 are distinct neurons that all lie in the r-th of the equal neuron ranges of the row shards.
All inputs are finite; a program needn't handle non-finite values. No bound on the sum of `forget_labels` on one device may be relied on, other than what follows from the above.
Results may differ from a plain program's by a relative error of at most 0.0052.
Values may be sent and summed in bfloat16 or wider, within the bound.
No kernel may reach another device: no remote copies, remote signals or barrier semaphores. Data moves between devices by JAX's collectives and lax.ppermute only.
A program may use at most 128 MiB of HBM per device.

v0:
```python
import jax
import jax.numpy as jnp
from jax import lax
from jax.sharding import PartitionSpec as P

D = 6144


def gelu_exact(v):
    return v * 0.5 * (1.0 + lax.erf(v * 0.7071067811865476))


def gelu_slope(v):
    return (
        0.5 * (1.0 + lax.erf(v * 0.7071067811865476))
        + v * jnp.exp(-0.5 * v * v) * 0.3989422804014327
    )


def outer_rows(left, right):
    return lax.dot_general(
        left, right, (((0,), (0,)), ((), ())), preferred_element_type=jnp.float32
    )


def local(
    forget_tokens,
    forget_cotangent,
    forget_labels,
    retain_tokens,
    ln_gain,
    w_in,
    b_in,
    w_out,
    b_out,
    pruned,
):
    forget_rows = forget_tokens.shape[0]
    width_local = w_in.shape[0]
    neurons_local = w_in.shape[1]
    joined = jnp.concatenate([forget_tokens, retain_tokens], axis=0).astype(jnp.float32)
    mean_val = lax.psum(jnp.sum(joined, axis=1, keepdims=True), "col") / D
    centred = joined - mean_val
    var_val = lax.psum(jnp.sum(centred * centred, axis=1, keepdims=True), "col") / D
    normed = (centred * lax.rsqrt(var_val + 1e-06) * ln_gain).astype(jnp.bfloat16)
    partial_pre = jnp.dot(normed, w_in, preferred_element_type=jnp.float32)
    grad_y = forget_cotangent * forget_labels[:, None].astype(jnp.bfloat16)
    grad_part = lax.dot_general(
        grad_y, w_out, (((1,), (1,)), ((), ())), preferred_element_type=jnp.float32
    )
    share_width = neurons_local // lax.axis_size("col")
    share_start = lax.axis_index("col") * share_width
    bias_share = lax.dynamic_slice_in_dim(b_in, share_start, share_width, 0)
    pre_share = lax.psum_scatter(partial_pre, "col", scatter_dimension=1, tiled=True) + bias_share
    act_share = gelu_exact(pre_share).astype(jnp.bfloat16)
    act_all = lax.all_gather(act_share, "col", axis=1, tiled=True)
    grad_act_share = lax.psum_scatter(
        grad_part.astype(jnp.bfloat16), "col", scatter_dimension=1, tiled=True
    ).astype(jnp.float32)
    grad_pre_share = (grad_act_share * gelu_slope(pre_share[:forget_rows])).astype(jnp.bfloat16)
    grad_pre = lax.all_gather(grad_pre_share, "col", axis=1, tiled=True)
    act_f = act_all[:forget_rows]
    act_r = act_all[forget_rows:]
    normed_f = normed[:forget_rows]
    local_in = outer_rows(normed_f, grad_pre)
    local_out = outer_rows(act_f, grad_y)
    summed_in, summed_out = (
        lax.psum_scatter(
            local_in.astype(jnp.bfloat16), "dp", scatter_dimension=0, tiled=True
        ).astype(jnp.float32),
        lax.psum_scatter(
            local_out.astype(jnp.bfloat16), "dp", scatter_dimension=1, tiled=True
        ).astype(jnp.float32),
    )
    slice_rows = width_local // lax.axis_size("dp")
    slice_start = lax.axis_index("dp") * slice_rows
    weight_in_rows = lax.dynamic_slice_in_dim(w_in, slice_start, slice_rows, 0).astype(jnp.float32)
    weight_out_cols = lax.dynamic_slice_in_dim(w_out, slice_start, slice_rows, 1).astype(
        jnp.float32
    )
    terms = jnp.sum(jnp.abs(weight_in_rows * summed_in), axis=0) + jnp.sum(
        jnp.abs(weight_out_cols * summed_out), axis=1
    )
    saliency = lax.psum(terms, ("dp", "col")) / D
    neuron_ids = lax.axis_index("row") * neurons_local + jnp.arange(neurons_local, dtype=jnp.int32)
    is_pruned = jnp.any(pruned[:, None] == neuron_ids[None, :], axis=0)
    keep = jnp.where(is_pruned, 0.0, 1.0).astype(jnp.bfloat16)
    masked_r = act_r * keep[None, :]
    out_part = jnp.dot(masked_r, w_out, preferred_element_type=jnp.float32)
    retain_out = (
        lax.psum_scatter(out_part, "row", scatter_dimension=0, tiled=True) + b_out
    ).astype(jnp.bfloat16)
    return (saliency, retain_out)


def solution(mesh):
    in_specs = (
        P("dp", "col"),
        P("dp", "col"),
        P("dp"),
        P("dp", "col"),
        P("col"),
        P("col", "row"),
        P("row"),
        P("row", "col"),
        P("col"),
        P("row"),
    )
    out_specs = (P("row"), P(("dp", "row"), "col"))
    return jax.shard_map(local, mesh=mesh, in_specs=in_specs, out_specs=out_specs, check_vma=False)
```

profile of v0, /device:TPU:0, one launch (start us, length us, event | category | flops | bytes accessed | tf_op | source)
XLA Modules:
  0.0 548.9 jit_solution(13570674265357662978)
XLA Ops:
  7.2 0.0 reduce-scatter.8.cloned.1.call-start
  7.2 1.1 convert_reduce_fusion
  8.3 42.0 %psum.21 = f32[256,1]{0,1:T(1,128)S(1)} all-reduce(f32[256,1]{0,1:T(1,128)S(1)} %bitcast.16), channel_id=1, replica_groups=mesh['dp'=2,'row'=4,'col'=16] {'col'}, use_global_device_ids=true, to_apply=%region_1.0 | all-reduce | flops 256 | bytes 2048 | tf_op jit(solution)/shard_map/psum | solution.py:42
  50.3 1.1 fusion.5
  51.4 35.5 %psum.22 = f32[256,1]{0,1:T(1,128)S(1)} all-reduce(f32[256,1]{0,1:T(1,128)S(1)} %bitcast.17), channel_id=1, replica_groups=mesh['dp'=2,'row'=4,'col'=16] {'col'}, use_global_device_ids=true, to_apply=%region_3.0 | all-reduce | flops 256 | bytes 2048 | tf_op jit(solution)/shard_map/psum | solution.py:44
  86.9 1.1 fusion.7
  88.0 6.8 %fusion.19 = f32[256,6144]{1,0:T(8,128)} fusion(bf16[256,384]{1,0:T(8,128)(2,1)S(1)} %fusion.7, bf16[384,6144]{1,0:T(8,128)(2,1)} %param.15), kind=kOutput, calls=%fused_computation.39 | convolution fusion | flops 1207959552 | bytes 11206656 | tf_op jit(solution)/shard_map/dot_general | solution.py:46
  94.8 0.0 reduce-scatter.8.cloned.1.call-update
  94.8 0.0 reduce-scatter.16.cloned.1.call-start
  94.9 0.6 copy-done.5
  95.5 0.2 copy-done.2
  95.7 3.9 convolution_convert_fusion.2
  99.6 0.0 copy-start.4
  99.7 1.7 copy.16
  101.3 0.0 reduce-scatter.16.cloned.1.call-update
  101.3 0.0 all-gather.5.cloned.1.call-start
  101.4 0.8 dynamic_slice.10
  102.2 72.4 %reduce-scatter.8.cloned.1.call-done = f32[256,384]{1,0:T(8,128)} async-done(((f32[256,6144]{1,0:T(8,128)}), f32[256,384]{1,0:T(8,128)}) %reduce-scatter.8.cloned.1.call-update) | async-done | bytes 393232 | tf_op jit(solution)/shard_map/reduce_scatter | solution.py:54
  174.6 1.8 multiply_convert_fusion
  176.3 0.0 all-gather.5.cloned.1.call-update
  176.3 0.0 all-gather.3.cloned.1.call-start
  176.4 74.4 %reduce-scatter.16.cloned.1.call-done = bf16[384,128]{1,0:T(8,128)(2,1)} async-done(((bf16[6144,128]{1,0:T(8,128)(2,1)}), bf16[384,128]{1,0:T(8,128)(2,1)}) %reduce-scatter.16.cloned.1.call-update) | async-done | bytes 98320
  250.8 1.0 copy.17
  251.8 0.7 fusion.13
  252.5 0.0 all-gather.3.cloned.1.call-update
  252.6 0.0 reduce-scatter.14.cloned.1.call-start
  252.6 0.5 compare_reduce_fusion
  253.1 51.7 %all-gather.5.cloned.1.call-done = bf16[256,6144]{1,0:T(8,128)(2,1)} async-done(((bf16[256,384]{1,0:T(8,128)(2,1)}), bf16[256,6144]{1,0:T(8,128)(2,1)}) %all-gather.5.cloned.1.call-update) | async-done | bytes 3145744 | tf_op jit(solution)/shard_map/all_gather | solution.py:56
  304.8 4.5 fusion
  309.3 0.0 reduce-scatter.14.cloned.1.call-update
  309.3 0.0 reduce-scatter.10.cloned.1.call-start
  309.4 42.2 %all-gather.3.cloned.1.call-done = bf16[128,6144]{1,0:T(8,128)(2,1)} async-done(((bf16[128,384]{1,0:T(8,128)(2,1)}), bf16[128,6144]{1,0:T(8,128)(2,1)}) %all-gather.3.cloned.1.call-update) | async-done | bytes 1572880 | tf_op jit(solution)/shard_map/all_gather | solution.py:61
  351.6 4.9 convolution_convert_fusion.1
  356.5 0.0 reduce-scatter.10.cloned.1.call-update
  356.5 0.0 reduce-scatter.12.cloned.1.call-start
  356.6 1.8 copy-done.1
  358.4 3.7 convolution_convert_fusion
  362.1 0.0 reduce-scatter.12.cloned.1.call-update
  362.1 4.0 constant_dynamic-slice_fusion
  366.1 2.7 copy.18
  368.8 4.7 reduce-scatter.14.cloned.1.call-done
  373.5 1.4 add_convert_fusion
  374.9 16.0 %reduce-scatter.10.cloned.1.call-done = bf16[192,6144]{1,0:T(8,128)(2,1)} async-done(((bf16[384,6144]{1,0:T(8,128)(2,1)}), bf16[192,6144]{1,0:T(8,128)(2,1)}) %reduce-scatter.10.cloned.1.call-update) | async-done | bytes 2359312 | tf_op jit(solution)/shard_map/reduce_scatter | solution.py:68
  391.0 3.2 abs_reduce_fusion.1
  394.1 15.9 %reduce-scatter.12.cloned.1.call-done = bf16[6144,192]{0,1:T(8,128)(2,1)} async-done(((bf16[6144,384]{0,1:T(8,128)(2,1)}), bf16[6144,192]{0,1:T(8,128)(2,1)}) %reduce-scatter.12.cloned.1.call-update) | async-done | bytes 2359312 | tf_op jit(solution)/shard_map/reduce_scatter | solution.py:71
  410.0 2.5 abs_reduce_fusion
  412.5 128.9 %psum.23 = f32[6144]{0:T(1024)S(1)} all-reduce(f32[6144]{0:T(1024)S(1)} %add.84), channel_id=1, replica_groups=mesh['dp'=2,'row'=4,'col'=16] {'dp','col'}, use_global_device_ids=true, to_apply=%region_10.0 | all-reduce | flops 6144 | bytes 49152 | tf_op jit(solution)/shard_map/psum | solution.py:84
  541.5 0.6 broadcast_multiply_fusion
  (14 shorter events, 0.1 us)
Async XLA Ops:
  7.2 167.4 %reduce-scatter.8.cloned.1.call-start = ((), (), s32[]{:S(2)}) async-start(), calls=%async_computation.5 | async-start | bytes 6684672 | tf_op jit(solution)/shard_map/reduce_scatter | solution.py:54
  94.8 0.7 copy-start.5
  94.8 0.9 copy-start.2
  94.8 155.9 %reduce-scatter.16.cloned.1.call-start = ((), (), s32[]{:S(2)}) async-start(), calls=%async_computation.11 | async-start | bytes 1671168
  99.6 153.0 %copy-start.4 = (s32[128]{0:T(128)S(1)}, s32[128]{0:T(128)}, u32[]{:S(2)}) copy-start(s32[128]{0:T(128)} %param.19) | copy-start | bytes 1540
  101.3 203.5 %all-gather.5.cloned.1.call-start = ((), (), s32[]{:S(2)}) async-start(), calls=%async_computation.8 | async-start | bytes 3342336 | tf_op jit(solution)/shard_map/all_gather | solution.py:56
  176.3 175.2 %all-gather.3.cloned.1.call-start = ((), (), s32[]{:S(2)}) async-start(), calls=%async_computation.6 | async-start | bytes 1671168 | tf_op jit(solution)/shard_map/all_gather | solution.py:61
  252.6 121.0 %reduce-scatter.14.cloned.1.call-start = ((), (), s32[]{:S(2)}) async-start(), calls=%async_computation.10 | async-start | bytes 245760 | tf_op jit(solution)/shard_map/reduce_scatter | solution.py:91
  309.3 81.6 %reduce-scatter.10.cloned.1.call-start = ((), (), s32[]{:S(2)}) async-start(), calls=%async_computation.7 | async-start | bytes 7077888 | tf_op jit(solution)/shard_map/reduce_scatter | solution.py:68
  356.5 1.9 copy-start.1
  356.5 53.5 %reduce-scatter.12.cloned.1.call-start = ((), (), s32[]{:S(2)}) async-start(), calls=%async_computation.9 | async-start | bytes 7077888 | tf_op jit(solution)/shard_map/reduce_scatter | solution.py:71
  366.1 7.5 %copy-start.3 = (f32[384]{0:T(512)S(1)}, f32[384]{0:T(512)}, u32[]{:S(2)}) copy-start(f32[384]{0:T(512)} %param.18) | copy-start | bytes 4612
  368.8 41.3 %copy-start = (bf16[6144,192]{0,1:T(8,128)(2,1)S(1)}, bf16[6144,192]{0,1:T(8,128)(2,1)}, u32[]{:S(2)}) copy-start(bf16[6144,192]{0,1:T(8,128)(2,1)} %copy.18) | copy-start | bytes 7077892
Sparse Core Ops, SparseCore 0:
  95.0 79.5 reduce-scatter.7
  177.8 72.9 reduce-scatter.15
  252.9 51.8 all-gather.4
  306.8 44.7 all-gather.2
  353.8 19.6 reduce-scatter.13
  375.9 14.9 reduce-scatter.9
  393.4 16.6 reduce-scatter.11
where the time goes:
time: 551 us; the launch traced here: 549 us
  waiting for transfers between devices  277 us (50%)
  blocking collectives  206 us (37%)
  matrix products  23.8 us (4%)
  between operations  14.2 us (3%)
  other arithmetic  14 us (3%)
  local copies, waits for them, and re-layouts  12.8 us (2%)
    psum x1, blocking collectives, local(): saliency = lax.psum(terms, ('dp', 'col')) / D  129 us
    unnamed x8, waiting for transfers between devices  74.5 us
    reduce_scatter x1, waiting for transfers between devices, local(): lax.psum_scatter(partial_pre, 'col', scatter_dimension=1, tiled=True)  72.4 us
    all_gather x1, waiting for transfers between devices, local(): act_all = lax.all_gather(act_share, 'col', axis=1, tiled=True)  51.7 us
    all_gather x1, waiting for transfers between devices, local(): grad_pre = lax.all_gather(grad_pre_share, 'col', axis=1, tiled=True)  42.2 us
    psum x1, blocking collectives, local(): mean_val = lax.psum(jnp.sum(joined, axis=1, keepdims=True), 'col') / D  42 us
    psum x1, blocking collectives, local(): lax.psum(jnp.sum(centred * centred, axis=1, keepdims=True), 'col') / D  35.5 us
    reduce_scatter x1, waiting for transfers between devices, local(): lax.psum_scatter(local_in.astype(jnp.bfloat16), 'dp', scatter_dimension=0...  16 us
  transfers between devices with their start and end apart: 7, of which 7 were waited for; matrix products, arithmetic and copies ran while one was open for 6% of the time, Pallas kernels for 0%

commit v1 on v0

v1 whole, which is shorter than its diff:
```python
import jax
import jax.numpy as jnp
from jax import lax
from jax.sharding import PartitionSpec as P

D = 6144
SIDE = 4
BF16 = jnp.bfloat16
F32 = jnp.float32


def gelu_exact(v):
    return v * 0.5 * (1.0 + lax.erf(v * 0.7071067811865476))


def gelu_slope(v):
    return (
        0.5 * (1.0 + lax.erf(v * 0.7071067811865476))
        + v * jnp.exp(-0.5 * v * v) * 0.3989422804014327
    )


def shift_y(k):
    return [(z * 4 + y, z * 4 + (y + k) % 4) for z in range(4) for y in range(4)]


def shift_z(k):
    return [(z * 4 + y, ((z + k) % 4) * 4 + y) for z in range(4) for y in range(4)]


def shift_row(k):
    return [(r, (r + k) % 4) for r in range(4)]


SWAP = [(0, 1), (1, 0)]


def row_order(first, second):
    p = lax.broadcasted_iota(jnp.int32, (256, 256), 0)
    q = lax.broadcasted_iota(jnp.int32, (256, 256), 1)
    j, i, h, e = p // 64, (p // 16) % 4, (p // 8) % 2, p % 8
    src = h * 128 + (((first + j) % 4) * 4 + (second + i) % 4) * 8 + e
    return (src == q).astype(BF16)


def reorder(sel, x):
    return jnp.dot(sel, x, preferred_element_type=F32).astype(BF16)


def scatter_stage(parts, shift):
    got = [lax.ppermute(parts[j], "col", shift(j)) for j in (1, 2, 3)]
    return parts[0].astype(F32), [g.astype(F32) for g in got]


def scatter_sum(parts, first, second):
    rows = parts[0].shape[0] // 4
    got = [parts[0]] + [lax.ppermute(parts[j], "col", first(j)) for j in (1, 2, 3)]
    sums = []
    for i in range(4):
        own = got[0][i * rows : (i + 1) * rows].astype(F32)
        for j in (1, 2, 3):
            own = own + got[j][i * rows : (i + 1) * rows].astype(F32)
        sums.append(own)
    back = [lax.ppermute(sums[i].astype(BF16), "col", second(i)) for i in (1, 2, 3)]
    total = sums[0]
    for b in back:
        total = total + b.astype(F32)
    return total


def gather(block, first, second):
    group = jnp.concatenate(
        [block] + [lax.ppermute(block, "col", first(-i)) for i in (1, 2, 3)], axis=0
    )
    return [group] + [lax.ppermute(group, "col", second(-j)) for j in (1, 2, 3)]


def local(
    forget_tokens,
    forget_cotangent,
    forget_labels,
    retain_tokens,
    ln_gain,
    w_in,
    b_in,
    w_out,
    b_out,
    pruned,
):
    core = lax.axis_index("dp")
    row = lax.axis_index("row")
    col = lax.axis_index("col")
    y, z = col % 4, col // 4
    width = w_in.shape[0]
    half = w_in.shape[1] // 2

    grad_y_own = forget_cotangent * forget_labels[:, None].astype(BF16)
    own = jnp.concatenate([forget_tokens, retain_tokens, grad_y_own], axis=0)
    other = lax.ppermute(own, "dp", SWAP)

    x = own[:256].astype(F32)
    part_sum = jnp.sum(x, axis=1)
    centred = x - (part_sum / width)[:, None]
    part_m2 = jnp.sum(centred * centred, axis=1)
    stats = jnp.concatenate([part_sum, part_m2]).reshape(4, 128)
    stats = lax.all_to_all(
        jnp.broadcast_to(stats[None], (32, 4, 128)), ("dp", "col"), 0, 0, tiled=True
    )
    stats = stats.reshape(2, 16, 2, 256)
    sums, m2 = stats[:, :, 0], stats[:, :, 1]
    mean = jnp.sum(sums, axis=1) / D
    gap = sums / width - mean[:, None]
    var = (jnp.sum(m2, axis=1) + width * jnp.sum(gap * gap, axis=1)) / D
    scale = lax.rsqrt(var + 1e-06)

    def pick(v):
        mine = jnp.where(core == 0, v[0], v[1])
        theirs = jnp.where(core == 0, v[1], v[0])
        return mine[:, None], theirs[:, None]

    mean_own, mean_other = pick(mean)
    scale_own, scale_other = pick(scale)
    normed_own = ((x - mean_own) * scale_own * ln_gain).astype(BF16)
    normed_other = (
        (other[:256].astype(F32) - mean_other) * scale_other * ln_gain
    ).astype(BF16)

    sel_f = row_order(y, z)
    sel_r = row_order(z, y)
    grad_y = reorder(sel_f, jnp.concatenate([own[256:], other[256:]], axis=0))
    normed_f = reorder(sel_f, jnp.concatenate([normed_own[:128], normed_other[:128]], axis=0))
    normed_r = reorder(sel_r, jnp.concatenate([normed_own[128:], normed_other[128:]], axis=0))

    w_in_half = lax.dynamic_slice_in_dim(w_in, core * half, half, 1)
    w_out_half = lax.dynamic_slice_in_dim(w_out, core * half, half, 0)
    b_half = lax.dynamic_slice_in_dim(b_in, core * half, half, 0)

    grad_part = lax.dot_general(
        grad_y, w_out_half, (((1,), (1,)), ((), ())), preferred_element_type=F32
    ).astype(BF16)
    grad_act = scatter_sum([grad_part[j * 64 : (j + 1) * 64] for j in range(4)], shift_y, shift_z)
    part_f = jnp.dot(normed_f, w_in_half, preferred_element_type=F32).astype(BF16)
    pre_f = scatter_sum([part_f[j * 64 : (j + 1) * 64] for j in range(4)], shift_y, shift_z)
    part_r = jnp.dot(normed_r, w_in_half, preferred_element_type=F32).astype(BF16)
    pre_r = scatter_sum([part_r[j * 64 : (j + 1) * 64] for j in range(4)], shift_z, shift_y)

    pre_f = pre_f + b_half
    pre_r = pre_r + b_half
    act_f = gelu_exact(pre_f).astype(BF16)
    grad_pre = (grad_act * gelu_slope(pre_f)).astype(BF16)
    ids = row * w_in.shape[1] + core * half + jnp.arange(half, dtype=jnp.int32)
    is_pruned = jnp.any(pruned[:, None] == ids[None, :], axis=0)
    keep = jnp.where(is_pruned, 0.0, 1.0).astype(BF16)
    masked_r = gelu_exact(pre_r).astype(BF16) * keep[None, :]

    both = gather(jnp.concatenate([act_f, grad_pre], axis=0), shift_z, shift_y)
    both = jnp.concatenate(both, axis=0).reshape(4, 4, 2, 16, half)
    act_f = both[:, :, 0].reshape(256, half)
    grad_pre = both[:, :, 1].reshape(256, half)
    masked_r = jnp.concatenate(gather(masked_r, shift_y, shift_z), axis=0)

    def outer_rows(left, right):
        return lax.dot_general(
            left, right, (((0,), (0,)), ((), ())), preferred_element_type=F32
        )

    grad_w_in = outer_rows(normed_f, grad_pre)
    grad_w_out = outer_rows(act_f, grad_y)
    terms = jnp.sum(jnp.abs(w_in_half.astype(F32) * grad_w_in), axis=0) + jnp.sum(
        jnp.abs(w_out_half.astype(F32) * grad_w_out), axis=1
    )
    terms = jnp.broadcast_to(terms.reshape(1, half // 128, 128), (32, half // 128, 128))
    terms = lax.all_to_all(terms, ("dp", "col"), 0, 0, tiled=True)
    saliency = jnp.sum(terms.reshape(2, 16, half), axis=1).reshape(2 * half) / D

    out_part = jnp.dot(masked_r, w_out_half, preferred_element_type=F32)
    out_part = out_part.reshape(4, 4, 2, 8, width)
    mine = out_part[:, :, 0] + lax.ppermute(out_part[:, :, 1], "dp", SWAP)

    def for_row(r):
        return lax.dynamic_index_in_dim(mine, (r - z) % 4, 0, keepdims=False)

    total = for_row(row)
    for k in (1, 2, 3):
        total = total + lax.ppermute(for_row(row + k), "row", shift_row(k))
    retain_out = (total + b_out).astype(BF16)
    retain_out = lax.dynamic_slice_in_dim(
        jnp.concatenate([retain_out, retain_out], axis=0), (4 - y) % 4, 4, 0
    ).reshape(32, width)
    return (saliency, retain_out)


def solution(mesh):
    in_specs = (
        P("dp", "col"),
        P("dp", "col"),
        P("dp"),
        P("dp", "col"),
        P("col"),
        P("col", "row"),
        P("row"),
        P("row", "col"),
        P("col"),
        P("row"),
    )
    out_specs = (P("row"), P(("dp", "row"), "col"))
    return jax.shard_map(local, mesh=mesh, in_specs=in_specs, out_specs=out_specs, check_vma=False)
```

time: 551 us -> 178 us (0.32)
  waiting for transfers between devices: 277 us -> 61.4 us
  blocking collectives: 206 us -> 0 us
  starting transfers between devices: 0.29 us -> 65 us
  matrix products: 23.8 us -> 10.6 us
  between operations: 14.2 us -> 1.57 us
  local copies, waits for them, and re-layouts: 12.8 us -> 25.4 us
    psum x3 -> x0, blocking collectives: 206 us -> none  [the longest x1 129 us: local(): saliency = lax.psum(terms, ('dp', 'col')) / D]
    reduce_scatter x4 -> x0, waiting for transfers between devices: 109 us -> none  [the longest x1 72.4 us: local(): lax.psum_scatter(partial_pre, 'col', scatter_dimension=1, tiled=True)]
    all_gather x2 -> x0, waiting for transfers between devices: 93.9 us -> none  [the longest x1 51.7 us: local(): act_all = lax.all_gather(act_share, 'col', axis=1, tiled=True)]
    unnamed x8 -> x0, waiting for transfers between devices: 74.5 us -> none
    ppermute x0 -> x35, starting transfers between devices: none -> 51.6 us  [the longest x9 14.8 us: scatter_sum(): lax.ppermute(parts[j], 'col', first(j))]
    ppermute x0 -> x35, waiting for transfers between devices: none -> 50.4 us  [the longest x6 26.8 us: gather(): return [group] + [lax.ppermute(group, 'col', second(-j)) for j in (1, 2, 3)]]
    all_to_all x0 -> x2, starting transfers between devices: none -> 13.3 us  [the longest x1 8.42 us: local(): lax.all_to_all(jnp.broadcast_to(stats[None], (32, 4, 128)), ('dp', 'col')...]
    all_to_all x0 -> x2, waiting for transfers between devices: none -> 11 us  [the longest x1 9.76 us: local(): terms = lax.all_to_all(terms, ('dp', 'col'), 0, 0, tiled=True)]
  transfers between devices with their start and end apart: 7 -> 37, of which waited for: 7 -> 13; matrix products, arithmetic and copies ran while one was open for 6% -> 21% of each run, Pallas kernels for 0% -> 0%
where the time goes in v1:
time: 178 us; the launch traced here: 177 us
  starting transfers between devices  65 us (37%)
  waiting for transfers between devices  61.4 us (34%)
  local copies, waits for them, and re-layouts  25.4 us (14%)
  other arithmetic  13 us (7%)
  matrix products  10.6 us (6%)
    ppermute x6, waiting for transfers between devices, gather(): return [group] + [lax.ppermute(group, 'col', second(-j)) for j in (1, 2, 3)]  26.8 us
    unnamed x86, local copies, waits for them, and re-layouts  16 us
    ppermute x9, starting transfers between devices, scatter_sum(): lax.ppermute(parts[j], 'col', first(j))  14.8 us
    ppermute x9, waiting for transfers between devices, scatter_sum(): lax.ppermute(parts[j], 'col', first(j))  13.7 us
    ppermute x9, starting transfers between devices, scatter_sum(): lax.ppermute(sums[i].astype(BF16), 'col', second(i))  12.1 us
    ppermute x6, starting transfers between devices, gather(): return [group] + [lax.ppermute(group, 'col', second(-j)) for j in (1, 2, 3)]  10.9 us
    all_to_all x1, waiting for transfers between devices, local(): terms = lax.all_to_all(terms, ('dp', 'col'), 0, 0, tiled=True)  9.76 us
    ppermute x6, waiting for transfers between devices, gather(): lax.ppermute(block, 'col', first(-i))  8.94 us
  transfers between devices with their start and end apart: 37, of which 13 were waited for; matrix products, arithmetic and copies ran while one was open for 21% of the time, Pallas kernels for 0%

profile of v1, /device:TPU:0, one launch (start us, length us, event | category | flops | bytes accessed | tf_op | source)
XLA Modules:
  0.0 176.9 jit_solution(2448412048968460268)
XLA Ops:
  0.6 1.1 convert_reduce_fusion
  1.7 1.1 fusion.3
  3.5 8.4 %all-to-all-start = ((f32[32,4,128]{2,1,0:T(4,128)}), f32[32,4,128]{2,1,0:T(4,128)S(1)}, u32[]{:S(2)}, u32[]{:S(2)}) async-start(f32[32,4,128]{2,1,0:T(4,128)} %broadcast_in_dim.10), calls=%async_computation | async-start | bytes 131072 | tf_op jit(solution)/shard_map/all_to_all | solution.py:106
  16.1 2.0 %constant_dynamic-slice_fusion = bf16[3072,384]{1,0:T(8,128)(2,1)S(1)} fusion(bf16[6144,384]{1,0:T(8,128)(2,1)} %param.17, s32[]{:T(128)} %select_n.170), kind=kLoop, calls=%fused_computation.173 | loop fusion | bytes 4718596
  18.1 1.3 all-to-all-done
  21.9 1.7 copy-done.4
  24.6 1.1 copy-done
  27.3 2.5 %collective-permute-start.2 = (bf16[64,3072]{1,0:T(8,128)(2,1)}, bf16[64,3072]{1,0:T(8,128)(2,1)S(1)}, u32[]{:S(2)}, u32[]{:S(2)}) collective-permute-start(bf16[64,3072]{1,0:T(8,128)(2,1)} %get-tuple-element.30), channel_id=1, source_target_pairs={{0,2},{1,3},{2,0},{3,1},{4,6},{5,7},{6,4},{7,5},{8,10},{9,11},{10,... | collective-permute-start | bytes 1179656 | tf_op jit(solution)/shard_map/ppermute | solution.py:57
  29.8 1.5 collective-permute-start.3
  31.3 4.5 %convolution_convert_fusion = bf16[256,3072]{1,0:T(8,128)(2,1)} fusion(bf16[384,6144]{1,0:T(8,128)(2,1)} %param.15, s32[]{:T(128)} %select_n.170, bf16[128,384]{1,0:T(8,128)(2,1)} %get-tuple-element.36, bf16[128,384]{1,0:T(8,128)(2,1)} %get-tuple-element.34, s32[256]{0:T(256)S(1)} %get-tuple-element.61, s32[256]{0:T(256)} %copy-done.18, s32[256]{0:T(256)} %copy-done.14, ...), kind=kOutput, calls=%fused_computation.2 | convolution fusion | flops 659324928 | bytes 4139528 | tf_op jit(solution)/shard_map/dot_general | solution.py:144
  35.9 1.4 fusion.128
  37.2 1.5 collective-permute-start.19
  38.8 2.7 %collective-permute-start.20 = (bf16[64,3072]{1,0:T(8,128)(2,1)S(1)}, bf16[64,3072]{1,0:T(8,128)(2,1)S(1)}, u32[]{:S(2)}, u32[]{:S(2)}) collective-permute-start(bf16[64,3072]{1,0:T(8,128)(2,1)S(1)} %get-tuple-element.24), channel_id=1, source_target_pairs={{0,8},{1,9},{2,10},{3,11},{4,12},{5,13},{6,14},{7,15},{8,0},{9,1},... | collective-permute-start | bytes 1179656 | tf_op jit(solution)/shard_map/ppermute | solution.py:57
  43.4 1.5 collective-permute-start.21
  44.9 2.9 %collective-permute-done.2 = bf16[64,3072]{1,0:T(8,128)(2,1)S(1)} collective-permute-done((bf16[64,3072]{1,0:T(8,128)(2,1)}, bf16[64,3072]{1,0:T(8,128)(2,1)S(1)}, u32[]{:S(2)}, u32[]{:S(2)}) %collective-permute-start.2) | collective-permute-done | bytes 393248 | tf_op jit(solution)/shard_map/ppermute | solution.py:57
  48.1 2.4 %collective-permute-start.8 = (bf16[64,3072]{1,0:T(8,128)(2,1)S(1)}, bf16[64,3072]{1,0:T(8,128)(2,1)S(1)}, u32[]{:S(2)}, u32[]{:S(2)}) collective-permute-start(bf16[64,3072]{1,0:T(8,128)(2,1)S(1)} %get-tuple-element.27), channel_id=1, source_target_pairs={{0,2},{1,3},{2,0},{3,1},{4,6},{5,7},{6,4},{7,5},{8,10},{9,11},{10,... | collective-permute-start | bytes 1179656 | tf_op jit(solution)/shard_map/ppermute | solution.py:57
  50.5 1.1 add_convert_fusion.8
  51.7 2.1 %collective-permute-start.9 = (bf16[64,3072]{1,0:T(8,128)(2,1)S(1)}, bf16[64,3072]{1,0:T(8,128)(2,1)S(1)}, u32[]{:S(2)}, u32[]{:S(2)}) collective-permute-start(bf16[64,3072]{1,0:T(8,128)(2,1)S(1)} %get-tuple-element.26), channel_id=1, source_target_pairs={{0,3},{1,0},{2,1},{3,2},{4,7},{5,4},{6,5},{7,6},{8,11},{9,8},{10,9... | collective-permute-start | bytes 1179656 | tf_op jit(solution)/shard_map/ppermute | solution.py:57
  53.7 4.6 %collective-permute-done.20 = bf16[64,3072]{1,0:T(8,128)(2,1)S(1)} collective-permute-done((bf16[64,3072]{1,0:T(8,128)(2,1)S(1)}, bf16[64,3072]{1,0:T(8,128)(2,1)S(1)}, u32[]{:S(2)}, u32[]{:S(2)}) %collective-permute-start.20) | collective-permute-done | bytes 393248 | tf_op jit(solution)/shard_map/ppermute | solution.py:57
  58.4 2.7 %collective-permute-start.5 = (bf16[16,3072]{1,0:T(8,128)(2,1)S(1)}, bf16[16,3072]{1,0:T(8,128)(2,1)S(1)}, u32[]{:S(2)}, u32[]{:S(2)}) collective-permute-start(bf16[16,3072]{1,0:T(8,128)(2,1)S(1)} %get-tuple-element.21), channel_id=1, source_target_pairs={{0,8},{1,9},{2,10},{3,11},{4,12},{5,13},{6,14},{7,15},{8,0},{9,1},... | collective-permute-start | bytes 294920 | tf_op jit(solution)/shard_map/ppermute | solution.py:64
  61.1 1.1 add_convert_fusion.2
  62.2 5.8 %collective-permute-done.7 = bf16[64,3072]{1,0:T(8,128)(2,1)S(1)} collective-permute-done((bf16[64,3072]{1,0:T(8,128)(2,1)S(1)}, bf16[64,3072]{1,0:T(8,128)(2,1)S(1)}, u32[]{:S(2)}, u32[]{:S(2)}) %collective-permute-start.7) | collective-permute-done | bytes 393248 | tf_op jit(solution)/shard_map/ppermute | solution.py:57
  68.0 2.6 %collective-permute-start.6 = (bf16[16,3072]{1,0:T(8,128)(2,1)S(1)}, bf16[16,3072]{1,0:T(8,128)(2,1)S(1)}, u32[]{:S(2)}, u32[]{:S(2)}) collective-permute-start(bf16[16,3072]{1,0:T(8,128)(2,1)S(1)} %get-tuple-element.20), channel_id=1, source_target_pairs={{0,12},{1,13},{2,14},{3,15},{4,0},{5,1},{6,2},{7,3},{8,4},{9,5},{1... | collective-permute-start | bytes 294920 | tf_op jit(solution)/shard_map/ppermute | solution.py:64
  71.7 2.5 %collective-permute-start.24 = (bf16[16,3072]{1,0:T(8,128)(2,1)S(1)}, bf16[16,3072]{1,0:T(8,128)(2,1)S(1)}, u32[]{:S(2)}, u32[]{:S(2)}) collective-permute-start(bf16[16,3072]{1,0:T(8,128)(2,1)S(1)} %get-tuple-element.14), channel_id=1, source_target_pairs={{0,3},{1,0},{2,1},{3,2},{4,7},{5,4},{6,5},{7,6},{8,11},{9,8},{10,9... | collective-permute-start | bytes 294920 | tf_op jit(solution)/shard_map/ppermute | solution.py:64
  74.4 2.3 %collective-permute-start.11 = (bf16[16,3072]{1,0:T(8,128)(2,1)S(1)}, bf16[16,3072]{1,0:T(8,128)(2,1)S(1)}, u32[]{:S(2)}, u32[]{:S(2)}) collective-permute-start(bf16[16,3072]{1,0:T(8,128)(2,1)S(1)} %get-tuple-element.18), channel_id=1, source_target_pairs={{0,8},{1,9},{2,10},{3,11},{4,12},{5,13},{6,14},{7,15},{8,0},{9,1},... | collective-permute-start | bytes 294920 | tf_op jit(solution)/shard_map/ppermute | solution.py:64
  78.4 1.9 %constant_dynamic-update-slice_fusion.19 = (bf16[256,3072]{1,0:T(8,128)(2,1)S(1)}, bf16[16,3072]{1,0:T(8,128)(2,1)S(1)}, bf16[128,3072]{1,0:T(8,128)(2,1)}, bf16[16,3072]{1,0:T(8,128)(2,1)S(1)}, f32[16,3072]{1,0:T(8,128)S(1)}) fusion(bf16[3072]{0:T(1024)(128)(2,1)S(1)} %select_convert_fusion, f32[3072]{0:T(1024)S(1)} %dynamic-slice-done, ...), kind=kLoop, calls=%fused_computation.153 | loop fusion | flops 2064382 | bytes 1984512
  80.3 2.6 %collective-permute-start.25 = (bf16[16,3072]{1,0:T(8,128)(2,1)S(1)}, bf16[16,3072]{1,0:T(8,128)(2,1)S(1)}, u32[]{:S(2)}, u32[]{:S(2)}) collective-permute-start(bf16[16,3072]{1,0:T(8,128)(2,1)S(1)} %get-tuple-element.5), channel_id=1, source_target_pairs={{0,3},{1,0},{2,1},{3,2},{4,7},{5,4},{6,5},{7,6},{8,11},{9,8},{10,9... | collective-permute-start | bytes 294920 | tf_op jit(solution)/shard_map/ppermute | solution.py:73
  85.4 1.1 collective-permute-start.13
  86.5 1.9 %collective-permute-start.14 = (bf16[32,3072]{1,0:T(8,128)(2,1)S(1)}, bf16[32,3072]{1,0:T(8,128)(2,1)S(1)}, u32[]{:S(2)}, u32[]{:S(2)}) collective-permute-start(bf16[32,3072]{1,0:T(8,128)(2,1)S(1)} %pad_maximum_fusion.3), channel_id=1, source_target_pairs={{0,8},{1,9},{2,10},{3,11},{4,12},{5,13},{6,14},{7,15},{8,0},{9,1},... | collective-permute-start | bytes 589832 | tf_op jit(solution)/shard_map/ppermute | solution.py:73
  89.0 1.1 collective-permute-start.15
  90.2 2.2 %collective-permute-start.28 = (bf16[64,3072]{1,0:T(8,128)(2,1)S(1)}, bf16[64,3072]{1,0:T(8,128)(2,1)S(1)}, u32[]{:S(2)}, u32[]{:S(2)}) collective-permute-start(bf16[64,3072]{1,0:T(8,128)(2,1)S(1)} %pad_maximum_fusion), channel_id=1, source_target_pairs={{0,12},{1,13},{2,14},{3,15},{4,0},{5,1},{6,2},{7,3},{8,4},{9,5},{1... | collective-permute-start | bytes 1179656 | tf_op jit(solution)/shard_map/ppermute | solution.py:75
  93.3 3.1 %collective-permute-start.30 = (bf16[64,3072]{1,0:T(8,128)(2,1)S(1)}, bf16[64,3072]{1,0:T(8,128)(2,1)S(1)}, u32[]{:S(2)}, u32[]{:S(2)}) collective-permute-start(bf16[64,3072]{1,0:T(8,128)(2,1)S(1)} %pad_maximum_fusion), channel_id=1, source_target_pairs={{0,4},{1,5},{2,6},{3,7},{4,8},{5,9},{6,10},{7,11},{8,12},{9,13},{1... | collective-permute-start | bytes 1179656 | tf_op jit(solution)/shard_map/ppermute | solution.py:75
  98.0 8.5 %collective-permute-done.15 = bf16[32,3072]{1,0:T(8,128)(2,1)S(1)} collective-permute-done((bf16[32,3072]{1,0:T(8,128)(2,1)S(1)}, bf16[32,3072]{1,0:T(8,128)(2,1)S(1)}, u32[]{:S(2)}, u32[]{:S(2)}) %collective-permute-start.15) | collective-permute-done | bytes 196640 | tf_op jit(solution)/shard_map/ppermute | solution.py:73
  107.3 1.8 %collective-permute-start.16 = (bf16[128,3072]{1,0:T(8,128)(2,1)}, bf16[128,3072]{1,0:T(8,128)(2,1)}, u32[]{:S(2)}, u32[]{:S(2)}) collective-permute-start(bf16[128,3072]{1,0:T(8,128)(2,1)} %get-tuple-element.38), channel_id=1, source_target_pairs={{0,3},{1,0},{2,1},{3,2},{4,7},{5,4},{6,5},{7,6},{8,11},{9,8},{10,9... | collective-permute-start | bytes 2359304 | tf_op jit(solution)/shard_map/ppermute | solution.py:75
  109.2 1.5 collective-permute-done.28
  110.8 3.6 %collective-permute-done.30 = bf16[64,3072]{1,0:T(8,128)(2,1)S(1)} collective-permute-done((bf16[64,3072]{1,0:T(8,128)(2,1)S(1)}, bf16[64,3072]{1,0:T(8,128)(2,1)S(1)}, u32[]{:S(2)}, u32[]{:S(2)}) %collective-permute-start.30) | collective-permute-done | bytes 393248 | tf_op jit(solution)/shard_map/ppermute | solution.py:75
  115.5 2.8 %collective-permute-start.17 = (bf16[128,3072]{1,0:T(8,128)(2,1)}, bf16[128,3072]{1,0:T(8,128)(2,1)}, u32[]{:S(2)}, u32[]{:S(2)}) collective-permute-start(bf16[128,3072]{1,0:T(8,128)(2,1)} %get-tuple-element.38), channel_id=1, source_target_pairs={{0,2},{1,3},{2,0},{3,1},{4,6},{5,7},{6,4},{7,5},{8,10},{9,11},{10,... | collective-permute-start | bytes 2359304 | tf_op jit(solution)/shard_map/ppermute | solution.py:75
  118.3 2.6 %copy.25 = bf16[3072,384]{0,1:T(8,128)(2,1)} copy(bf16[3072,384]{1,0:T(8,128)(2,1)S(1)} %constant_dynamic-slice_fusion) | data formatting | bytes 4718592
  122.5 1.6 collective-permute-start.32
  124.0 2.7 %collective-permute-start.33 = (f32[4,8,384]{2,1,0:T(8,128)S(1)}, f32[4,8,384]{2,1,0:T(8,128)S(1)}, u32[]{:S(2)}, u32[]{:S(2)}) collective-permute-start(f32[4,8,384]{2,1,0:T(8,128)S(1)} %get-tuple-element.33), channel_id=1, source_target_pairs={{0,32},{16,48},{32,0},{48,16},{1,33},{17,49},{33,1},{49,17},{2,34}... | collective-permute-start | bytes 147464 | tf_op jit(solution)/shard_map/ppermute | solution.py:185
  126.8 1.4 collective-permute-start.34
  128.2 2.1 %constant_dynamic-update-slice_fusion.7 = bf16[512,3072]{1,0:T(8,128)(2,1)} fusion(bf16[512,3072]{1,0:T(8,128)(2,1)} %get-tuple-element.39, bf16[128,3072]{1,0:T(8,128)(2,1)} %collective-permute-done.16), kind=kLoop, calls=%fused_computation.141 | loop fusion | bytes 1572864
  130.3 7.5 %collective-permute-done.17 = bf16[128,3072]{1,0:T(8,128)(2,1)} collective-permute-done((bf16[128,3072]{1,0:T(8,128)(2,1)}, bf16[128,3072]{1,0:T(8,128)(2,1)}, u32[]{:S(2)}, u32[]{:S(2)}) %collective-permute-start.17) | collective-permute-done | bytes 786464 | tf_op jit(solution)/shard_map/ppermute | solution.py:75
  137.8 2.1 %constant_dynamic-update-slice_fusion.6 = bf16[512,3072]{1,0:T(8,128)(2,1)} fusion(bf16[512,3072]{1,0:T(8,128)(2,1)} %constant_dynamic-update-slice_fusion.7, bf16[128,3072]{1,0:T(8,128)(2,1)} %collective-permute-done.17), kind=kLoop, calls=%fused_computation.140 | loop fusion | bytes 1572864
  139.9 14.2 %collective-permute-done.18 = bf16[128,3072]{1,0:T(8,128)(2,1)S(1)} collective-permute-done((bf16[128,3072]{1,0:T(8,128)(2,1)}, bf16[128,3072]{1,0:T(8,128)(2,1)S(1)}, u32[]{:S(2)}, u32[]{:S(2)}) %collective-permute-start.18) | collective-permute-done | bytes 786464 | tf_op jit(solution)/shard_map/ppermute | solution.py:75
  155.0 2.3 %fusion.127 = (bf16[4,4,1,16,3072]{4,3,2,1,0:T(8,128)(2,1)S(1)}, bf16[4,4,1,16,3072]{4,3,2,1,0:T(8,128)(2,1)S(1)}) fusion(bf16[4,4,2,16,3072]{4,3,2,1,0:T(8,128)(2,1)} %bitcast.6), kind=kLoop, calls=%fused_computation.203 | loop fusion | bytes 6291456 | tf_op jit(solution)/shard_map/slice | solution.py:158
  160.7 4.9 %all-to-all-start.1 = ((f32[32,24,128]{2,1,0:T(8,128)}), f32[32,24,128]{2,1,0:T(8,128)S(1)}, u32[]{:S(2)}, u32[]{:S(2)}) async-start(f32[32,24,128]{2,1,0:T(8,128)} %broadcast_in_dim.11), calls=%async_computation.1 | async-start | bytes 786432 | tf_op jit(solution)/shard_map/all_to_all | solution.py:173
  166.4 9.8 %all-to-all-done.1 = f32[32,24,128]{2,1,0:T(8,128)S(1)} async-done(((f32[32,24,128]{2,1,0:T(8,128)}), f32[32,24,128]{2,1,0:T(8,128)S(1)}, u32[]{:S(2)}, u32[]{:S(2)}) %all-to-all-start.1) | async-done | bytes 393248 | tf_op jit(solution)/shard_map/all_to_all | solution.py:173
  (175 shorter events, 29.6 us)
Async XLA Ops:
  3.5 15.9 %all-to-all-start = ((f32[32,4,128]{2,1,0:T(4,128)}), f32[32,4,128]{2,1,0:T(4,128)S(1)}, u32[]{:S(2)}, u32[]{:S(2)}) async-start(f32[32,4,128]{2,1,0:T(4,128)} %broadcast_in_dim.10), calls=%async_computation | async-start | bytes 131072 | tf_op jit(solution)/shard_map/all_to_all | solution.py:106
  14.6 5.0 %collective-permute-start = (bf16[384,384]{1,0:T(8,128)(2,1)S(1)}, bf16[384,384]{1,0:T(8,128)(2,1)S(1)}, u32[]{:S(2)}, u32[]{:S(2)}) collective-permute-start(bf16[384,384]{1,0:T(8,128)(2,1)S(1)} %pad_maximum_fusion.1), channel_id=1, source_target_pairs={{0,64},{64,0},{1,65},{65,1},{2,66},{66,2},{3,67},{67,3},{4,68},{68... | collective-permute-start | bytes 884744 | tf_op jit(solution)/shard_map/ppermute | solution.py:99
  14.9 6.2 %copy-start.14 = (s32[256]{0:T(256)}, s32[256]{0:T(256)S(1)}, u32[]{:S(2)}) copy-start(s32[256]{0:T(256)S(1)} %get-tuple-element.62) | copy-start | bytes 3076
  14.9 6.2 %copy-start.16 = (s32[256]{0:T(256)}, s32[256]{0:T(256)S(1)}, u32[]{:S(2)}) copy-start(s32[256]{0:T(256)S(1)} %get-tuple-element.63) | copy-start | bytes 3076
  15.0 6.2 %copy-start.18 = (s32[256]{0:T(256)}, s32[256]{0:T(256)S(1)}, u32[]{:S(2)}) copy-start(s32[256]{0:T(256)S(1)} %get-tuple-element.64) | copy-start | bytes 3076
  15.0 6.2 %copy-start.20 = (s32[256]{0:T(256)}, s32[256]{0:T(256)S(1)}, u32[]{:S(2)}) copy-start(s32[256]{0:T(256)S(1)} %get-tuple-element.65) | copy-start | bytes 3076
  15.0 6.2 %copy-start.22 = (s32[256]{0:T(256)}, s32[256]{0:T(256)S(1)}, u32[]{:S(2)}) copy-start(s32[256]{0:T(256)S(1)} %get-tuple-element.66) | copy-start | bytes 3076
  15.0 6.2 %copy-start.24 = (s32[256]{0:T(256)}, s32[256]{0:T(256)S(1)}, u32[]{:S(2)}) copy-start(s32[256]{0:T(256)S(1)} %get-tuple-element.67) | copy-start | bytes 3076
  15.0 6.2 %copy-start.26 = (pred[256]{0:T(512)(128)(4,1)}, pred[256]{0:T(512)(128)(4,1)S(1)}, u32[]{:S(2)}) copy-start(pred[256]{0:T(512)(128)(4,1)S(1)} %get-tuple-element.54) | copy-start | bytes 772
  26.7 16.6 %collective-permute-start.1 = (bf16[64,3072]{1,0:T(8,128)(2,1)}, bf16[64,3072]{1,0:T(8,128)(2,1)S(1)}, u32[]{:S(2)}, u32[]{:S(2)}) collective-permute-start(bf16[64,3072]{1,0:T(8,128)(2,1)} %get-tuple-element.28), channel_id=1, source_target_pairs={{0,1},{1,2},{2,3},{3,0},{4,5},{5,6},{6,7},{7,4},{8,9},{9,10},{10,1... | collective-permute-start | bytes 1179656 | tf_op jit(solution)/shard_map/ppermute | solution.py:57
  27.3 20.5 %collective-permute-start.2 = (bf16[64,3072]{1,0:T(8,128)(2,1)}, bf16[64,3072]{1,0:T(8,128)(2,1)S(1)}, u32[]{:S(2)}, u32[]{:S(2)}) collective-permute-start(bf16[64,3072]{1,0:T(8,128)(2,1)} %get-tuple-element.30), channel_id=1, source_target_pairs={{0,2},{1,3},{2,0},{3,1},{4,6},{5,7},{6,4},{7,5},{8,10},{9,11},{10,... | collective-permute-start | bytes 1179656 | tf_op jit(solution)/shard_map/ppermute | solution.py:57
  29.8 18.3 %collective-permute-start.3 = (bf16[64,3072]{1,0:T(8,128)(2,1)}, bf16[64,3072]{1,0:T(8,128)(2,1)S(1)}, u32[]{:S(2)}, u32[]{:S(2)}) collective-permute-start(bf16[64,3072]{1,0:T(8,128)(2,1)} %get-tuple-element.29), channel_id=1, source_target_pairs={{0,3},{1,0},{2,1},{3,2},{4,7},{5,4},{6,5},{7,6},{8,11},{9,8},{10,9... | collective-permute-start | bytes 1179656 | tf_op jit(solution)/shard_map/ppermute | solution.py:57
  37.2 14.4 %collective-permute-start.19 = (bf16[64,3072]{1,0:T(8,128)(2,1)S(1)}, bf16[64,3072]{1,0:T(8,128)(2,1)S(1)}, u32[]{:S(2)}, u32[]{:S(2)}) collective-permute-start(bf16[64,3072]{1,0:T(8,128)(2,1)S(1)} %get-tuple-element.22), channel_id=1, source_target_pairs={{0,4},{1,5},{2,6},{3,7},{4,8},{5,9},{6,10},{7,11},{8,12},{9,13},{1... | collective-permute-start | bytes 1179656 | tf_op jit(solution)/shard_map/ppermute | solution.py:57
  38.8 19.6 %collective-permute-start.20 = (bf16[64,3072]{1,0:T(8,128)(2,1)S(1)}, bf16[64,3072]{1,0:T(8,128)(2,1)S(1)}, u32[]{:S(2)}, u32[]{:S(2)}) collective-permute-start(bf16[64,3072]{1,0:T(8,128)(2,1)S(1)} %get-tuple-element.24), channel_id=1, source_target_pairs={{0,8},{1,9},{2,10},{3,11},{4,12},{5,13},{6,14},{7,15},{8,0},{9,1},... | collective-permute-start | bytes 1179656 | tf_op jit(solution)/shard_map/ppermute | solution.py:57
  43.3 35.1 %dynamic-slice-start = ((f32[6144]{0:T(1024)}, s32[]{:T(128)}), f32[3072]{0:T(1024)S(1)}, s32[]{:S(2)}) async-start(f32[6144]{0:T(1024)} %param.16, s32[]{:T(128)} %select_n.170), calls=%async_computation.5 | async-start | bytes 25088 | tf_op jit(solution)/shard_map/dynamic_slice | solution.py:136
  43.4 15.0 %collective-permute-start.21 = (bf16[64,3072]{1,0:T(8,128)(2,1)S(1)}, bf16[64,3072]{1,0:T(8,128)(2,1)S(1)}, u32[]{:S(2)}, u32[]{:S(2)}) collective-permute-start(bf16[64,3072]{1,0:T(8,128)(2,1)S(1)} %get-tuple-element.23), channel_id=1, source_target_pairs={{0,12},{1,13},{2,14},{3,15},{4,0},{5,1},{6,2},{7,3},{8,4},{9,5},{1... | collective-permute-start | bytes 1179656 | tf_op jit(solution)/shard_map/ppermute | solution.py:57
  47.8 20.2 %collective-permute-start.7 = (bf16[64,3072]{1,0:T(8,128)(2,1)S(1)}, bf16[64,3072]{1,0:T(8,128)(2,1)S(1)}, u32[]{:S(2)}, u32[]{:S(2)}) collective-permute-start(bf16[64,3072]{1,0:T(8,128)(2,1)S(1)} %get-tuple-element.25), channel_id=1, source_target_pairs={{0,1},{1,2},{2,3},{3,0},{4,5},{5,6},{6,7},{7,4},{8,9},{9,10},{10,1... | collective-permute-start | bytes 1179656 | tf_op jit(solution)/shard_map/ppermute | solution.py:57
  48.1 22.5 %collective-permute-start.8 = (bf16[64,3072]{1,0:T(8,128)(2,1)S(1)}, bf16[64,3072]{1,0:T(8,128)(2,1)S(1)}, u32[]{:S(2)}, u32[]{:S(2)}) collective-permute-start(bf16[64,3072]{1,0:T(8,128)(2,1)S(1)} %get-tuple-element.27), channel_id=1, source_target_pairs={{0,2},{1,3},{2,0},{3,1},{4,6},{5,7},{6,4},{7,5},{8,10},{9,11},{10,... | collective-permute-start | bytes 1179656 | tf_op jit(solution)/shard_map/ppermute | solution.py:57
  51.7 19.0 %collective-permute-start.9 = (bf16[64,3072]{1,0:T(8,128)(2,1)S(1)}, bf16[64,3072]{1,0:T(8,128)(2,1)S(1)}, u32[]{:S(2)}, u32[]{:S(2)}) collective-permute-start(bf16[64,3072]{1,0:T(8,128)(2,1)S(1)} %get-tuple-element.26), channel_id=1, source_target_pairs={{0,3},{1,0},{2,1},{3,2},{4,7},{5,4},{6,5},{7,6},{8,11},{9,8},{10,9... | collective-permute-start | bytes 1179656 | tf_op jit(solution)/shard_map/ppermute | solution.py:57
  58.4 13.3 %collective-permute-start.4 = (bf16[16,3072]{1,0:T(8,128)(2,1)S(1)}, bf16[16,3072]{1,0:T(8,128)(2,1)S(1)}, u32[]{:S(2)}, u32[]{:S(2)}) collective-permute-start(bf16[16,3072]{1,0:T(8,128)(2,1)S(1)} %get-tuple-element.19), channel_id=1, source_target_pairs={{0,4},{1,5},{2,6},{3,7},{4,8},{5,9},{6,10},{7,11},{8,12},{9,13},{1... | collective-permute-start | bytes 294920 | tf_op jit(solution)/shard_map/ppermute | solution.py:64
  58.4 15.9 %collective-permute-start.5 = (bf16[16,3072]{1,0:T(8,128)(2,1)S(1)}, bf16[16,3072]{1,0:T(8,128)(2,1)S(1)}, u32[]{:S(2)}, u32[]{:S(2)}) collective-permute-start(bf16[16,3072]{1,0:T(8,128)(2,1)S(1)} %get-tuple-element.21), channel_id=1, source_target_pairs={{0,8},{1,9},{2,10},{3,11},{4,12},{5,13},{6,14},{7,15},{8,0},{9,1},... | collective-permute-start | bytes 294920 | tf_op jit(solution)/shard_map/ppermute | solution.py:64
  68.0 6.4 %collective-permute-start.6 = (bf16[16,3072]{1,0:T(8,128)(2,1)S(1)}, bf16[16,3072]{1,0:T(8,128)(2,1)S(1)}, u32[]{:S(2)}, u32[]{:S(2)}) collective-permute-start(bf16[16,3072]{1,0:T(8,128)(2,1)S(1)} %get-tuple-element.20), channel_id=1, source_target_pairs={{0,12},{1,13},{2,14},{3,15},{4,0},{5,1},{6,2},{7,3},{8,4},{9,5},{1... | collective-permute-start | bytes 294920 | tf_op jit(solution)/shard_map/ppermute | solution.py:64
  70.7 6.9 %collective-permute-start.22 = (bf16[16,3072]{1,0:T(8,128)(2,1)S(1)}, bf16[16,3072]{1,0:T(8,128)(2,1)S(1)}, u32[]{:S(2)}, u32[]{:S(2)}) collective-permute-start(bf16[16,3072]{1,0:T(8,128)(2,1)S(1)} %get-tuple-element.13), channel_id=1, source_target_pairs={{0,1},{1,2},{2,3},{3,0},{4,5},{5,6},{6,7},{7,4},{8,9},{9,10},{10,1... | collective-permute-start | bytes 294920 | tf_op jit(solution)/shard_map/ppermute | solution.py:64
  70.7 7.8 %collective-permute-start.23 = (bf16[16,3072]{1,0:T(8,128)(2,1)S(1)}, bf16[16,3072]{1,0:T(8,128)(2,1)S(1)}, u32[]{:S(2)}, u32[]{:S(2)}) collective-permute-start(bf16[16,3072]{1,0:T(8,128)(2,1)S(1)} %get-tuple-element.15), channel_id=1, source_target_pairs={{0,2},{1,3},{2,0},{3,1},{4,6},{5,7},{6,4},{7,5},{8,10},{9,11},{10,... | collective-permute-start | bytes 294920 | tf_op jit(solution)/shard_map/ppermute | solution.py:64
  71.7 6.8 %collective-permute-start.24 = (bf16[16,3072]{1,0:T(8,128)(2,1)S(1)}, bf16[16,3072]{1,0:T(8,128)(2,1)S(1)}, u32[]{:S(2)}, u32[]{:S(2)}) collective-permute-start(bf16[16,3072]{1,0:T(8,128)(2,1)S(1)} %get-tuple-element.14), channel_id=1, source_target_pairs={{0,3},{1,0},{2,1},{3,2},{4,7},{5,4},{6,5},{7,6},{8,11},{9,8},{10,9... | collective-permute-start | bytes 294920 | tf_op jit(solution)/shard_map/ppermute | solution.py:64
  74.3 9.6 %collective-permute-start.10 = (bf16[16,3072]{1,0:T(8,128)(2,1)S(1)}, bf16[16,3072]{1,0:T(8,128)(2,1)S(1)}, u32[]{:S(2)}, u32[]{:S(2)}) collective-permute-start(bf16[16,3072]{1,0:T(8,128)(2,1)S(1)} %get-tuple-element.16), channel_id=1, source_target_pairs={{0,4},{1,5},{2,6},{3,7},{4,8},{5,9},{6,10},{7,11},{8,12},{9,13},{1... | collective-permute-start | bytes 294920 | tf_op jit(solution)/shard_map/ppermute | solution.py:64
  74.4 10.1 %collective-permute-start.11 = (bf16[16,3072]{1,0:T(8,128)(2,1)S(1)}, bf16[16,3072]{1,0:T(8,128)(2,1)S(1)}, u32[]{:S(2)}, u32[]{:S(2)}) collective-permute-start(bf16[16,3072]{1,0:T(8,128)(2,1)S(1)} %get-tuple-element.18), channel_id=1, source_target_pairs={{0,8},{1,9},{2,10},{3,11},{4,12},{5,13},{6,14},{7,15},{8,0},{9,1},... | collective-permute-start | bytes 294920 | tf_op jit(solution)/shard_map/ppermute | solution.py:64
  77.5 7.0 %collective-permute-start.12 = (bf16[16,3072]{1,0:T(8,128)(2,1)S(1)}, bf16[16,3072]{1,0:T(8,128)(2,1)S(1)}, u32[]{:S(2)}, u32[]{:S(2)}) collective-permute-start(bf16[16,3072]{1,0:T(8,128)(2,1)S(1)} %get-tuple-element.17), channel_id=1, source_target_pairs={{0,12},{1,13},{2,14},{3,15},{4,0},{5,1},{6,2},{7,3},{8,4},{9,5},{1... | collective-permute-start | bytes 294920 | tf_op jit(solution)/shard_map/ppermute | solution.py:64
  80.3 8.7 %collective-permute-start.25 = (bf16[16,3072]{1,0:T(8,128)(2,1)S(1)}, bf16[16,3072]{1,0:T(8,128)(2,1)S(1)}, u32[]{:S(2)}, u32[]{:S(2)}) collective-permute-start(bf16[16,3072]{1,0:T(8,128)(2,1)S(1)} %get-tuple-element.5), channel_id=1, source_target_pairs={{0,3},{1,0},{2,1},{3,2},{4,7},{5,4},{6,5},{7,6},{8,11},{9,8},{10,9... | collective-permute-start | bytes 294920 | tf_op jit(solution)/shard_map/ppermute | solution.py:73
  82.9 7.3 %collective-permute-start.26 = (bf16[16,3072]{1,0:T(8,128)(2,1)S(1)}, bf16[16,3072]{1,0:T(8,128)(2,1)S(1)}, u32[]{:S(2)}, u32[]{:S(2)}) collective-permute-start(bf16[16,3072]{1,0:T(8,128)(2,1)S(1)} %get-tuple-element.5), channel_id=1, source_target_pairs={{0,2},{1,3},{2,0},{3,1},{4,6},{5,7},{6,4},{7,5},{8,10},{9,11},{10,... | collective-permute-start | bytes 294920 | tf_op jit(solution)/shard_map/ppermute | solution.py:73
  84.0 6.2 %collective-permute-start.27 = (bf16[16,3072]{1,0:T(8,128)(2,1)S(1)}, bf16[16,3072]{1,0:T(8,128)(2,1)S(1)}, u32[]{:S(2)}, u32[]{:S(2)}) collective-permute-start(bf16[16,3072]{1,0:T(8,128)(2,1)S(1)} %get-tuple-element.5), channel_id=1, source_target_pairs={{0,1},{1,2},{2,3},{3,0},{4,5},{5,6},{6,7},{7,4},{8,9},{9,10},{10,1... | collective-permute-start | bytes 294920 | tf_op jit(solution)/shard_map/ppermute | solution.py:73
  85.4 7.9 %collective-permute-start.13 = (bf16[32,3072]{1,0:T(8,128)(2,1)S(1)}, bf16[32,3072]{1,0:T(8,128)(2,1)S(1)}, u32[]{:S(2)}, u32[]{:S(2)}) collective-permute-start(bf16[32,3072]{1,0:T(8,128)(2,1)S(1)} %pad_maximum_fusion.3), channel_id=1, source_target_pairs={{0,12},{1,13},{2,14},{3,15},{4,0},{5,1},{6,2},{7,3},{8,4},{9,5},{1... | collective-permute-start | bytes 589832 | tf_op jit(solution)/shard_map/ppermute | solution.py:73
  86.5 10.7 %collective-permute-start.14 = (bf16[32,3072]{1,0:T(8,128)(2,1)S(1)}, bf16[32,3072]{1,0:T(8,128)(2,1)S(1)}, u32[]{:S(2)}, u32[]{:S(2)}) collective-permute-start(bf16[32,3072]{1,0:T(8,128)(2,1)S(1)} %pad_maximum_fusion.3), channel_id=1, source_target_pairs={{0,8},{1,9},{2,10},{3,11},{4,12},{5,13},{6,14},{7,15},{8,0},{9,1},... | collective-permute-start | bytes 589832 | tf_op jit(solution)/shard_map/ppermute | solution.py:73
  89.0 17.5 %collective-permute-start.15 = (bf16[32,3072]{1,0:T(8,128)(2,1)S(1)}, bf16[32,3072]{1,0:T(8,128)(2,1)S(1)}, u32[]{:S(2)}, u32[]{:S(2)}) collective-permute-start(bf16[32,3072]{1,0:T(8,128)(2,1)S(1)} %pad_maximum_fusion.3), channel_id=1, source_target_pairs={{0,4},{1,5},{2,6},{3,7},{4,8},{5,9},{6,10},{7,11},{8,12},{9,13},{1... | collective-permute-start | bytes 589832 | tf_op jit(solution)/shard_map/ppermute | solution.py:73
  90.2 20.5 %collective-permute-start.28 = (bf16[64,3072]{1,0:T(8,128)(2,1)S(1)}, bf16[64,3072]{1,0:T(8,128)(2,1)S(1)}, u32[]{:S(2)}, u32[]{:S(2)}) collective-permute-start(bf16[64,3072]{1,0:T(8,128)(2,1)S(1)} %pad_maximum_fusion), channel_id=1, source_target_pairs={{0,12},{1,13},{2,14},{3,15},{4,0},{5,1},{6,2},{7,3},{8,4},{9,5},{1... | collective-permute-start | bytes 1179656 | tf_op jit(solution)/shard_map/ppermute | solution.py:75
  92.4 18.4 %collective-permute-start.29 = (bf16[64,3072]{1,0:T(8,128)(2,1)S(1)}, bf16[64,3072]{1,0:T(8,128)(2,1)S(1)}, u32[]{:S(2)}, u32[]{:S(2)}) collective-permute-start(bf16[64,3072]{1,0:T(8,128)(2,1)S(1)} %pad_maximum_fusion), channel_id=1, source_target_pairs={{0,8},{1,9},{2,10},{3,11},{4,12},{5,13},{6,14},{7,15},{8,0},{9,1},... | collective-permute-start | bytes 1179656 | tf_op jit(solution)/shard_map/ppermute | solution.py:75
  93.3 21.1 %collective-permute-start.30 = (bf16[64,3072]{1,0:T(8,128)(2,1)S(1)}, bf16[64,3072]{1,0:T(8,128)(2,1)S(1)}, u32[]{:S(2)}, u32[]{:S(2)}) collective-permute-start(bf16[64,3072]{1,0:T(8,128)(2,1)S(1)} %pad_maximum_fusion), channel_id=1, source_target_pairs={{0,4},{1,5},{2,6},{3,7},{4,8},{5,9},{6,10},{7,11},{8,12},{9,13},{1... | collective-permute-start | bytes 1179656 | tf_op jit(solution)/shard_map/ppermute | solution.py:75
  107.3 19.4 %collective-permute-start.16 = (bf16[128,3072]{1,0:T(8,128)(2,1)}, bf16[128,3072]{1,0:T(8,128)(2,1)}, u32[]{:S(2)}, u32[]{:S(2)}) collective-permute-start(bf16[128,3072]{1,0:T(8,128)(2,1)} %get-tuple-element.38), channel_id=1, source_target_pairs={{0,3},{1,0},{2,1},{3,2},{4,7},{5,4},{6,5},{7,6},{8,11},{9,8},{10,9... | collective-permute-start | bytes 2359304 | tf_op jit(solution)/shard_map/ppermute | solution.py:75
  115.4 6.1 %collective-permute-start.31 = (f32[4,4,8,384]{3,2,1,0:T(8,128)S(1)}, f32[4,4,8,384]{3,2,1,0:T(8,128)}, u32[]{:S(2)}, u32[]{:S(2)}) collective-permute-start(f32[4,4,8,384]{3,2,1,0:T(8,128)S(1)} %slice_bitcast_fusion), channel_id=1, source_target_pairs={{0,64},{64,0},{1,65},{65,1},{2,66},{66,2},{3,67},{67,3},{4,68},{68... | collective-permute-start | bytes 589832 | tf_op jit(solution)/shard_map/ppermute | solution.py:178
  115.5 22.3 %collective-permute-start.17 = (bf16[128,3072]{1,0:T(8,128)(2,1)}, bf16[128,3072]{1,0:T(8,128)(2,1)}, u32[]{:S(2)}, u32[]{:S(2)}) collective-permute-start(bf16[128,3072]{1,0:T(8,128)(2,1)} %get-tuple-element.38), channel_id=1, source_target_pairs={{0,2},{1,3},{2,0},{3,1},{4,6},{5,7},{6,4},{7,5},{8,10},{9,11},{10,... | collective-permute-start | bytes 2359304 | tf_op jit(solution)/shard_map/ppermute | solution.py:75
  118.3 39.0 %slice-start = ((s8[4718592]{0:T(1024)(128)(4,1)}), s8[524288]{0:T(1024)(128)(4,1)S(1)}, s32[]{:S(2)}) async-start(s8[4718592]{0:T(1024)(128)(4,1)} %bitcast.58), calls=%async_computation.2 | async-start | bytes 1048576
  120.9 33.1 %collective-permute-start.18 = (bf16[128,3072]{1,0:T(8,128)(2,1)}, bf16[128,3072]{1,0:T(8,128)(2,1)S(1)}, u32[]{:S(2)}, u32[]{:S(2)}) collective-permute-start(bf16[128,3072]{1,0:T(8,128)(2,1)} %get-tuple-element.38), channel_id=1, source_target_pairs={{0,1},{1,2},{2,3},{3,0},{4,5},{5,6},{6,7},{7,4},{8,9},{9,10},{10,1... | collective-permute-start | bytes 2359304 | tf_op jit(solution)/shard_map/ppermute | solution.py:75
  122.5 43.2 %collective-permute-start.32 = (f32[4,8,384]{2,1,0:T(8,128)S(1)}, f32[4,8,384]{2,1,0:T(8,128)S(1)}, u32[]{:S(2)}, u32[]{:S(2)}) collective-permute-start(f32[4,8,384]{2,1,0:T(8,128)S(1)} %get-tuple-element.31), channel_id=1, source_target_pairs={{0,16},{16,32},{32,48},{48,0},{1,17},{17,33},{33,49},{49,1},{2,18}... | collective-permute-start | bytes 147464 | tf_op jit(solution)/shard_map/ppermute | solution.py:185
  124.0 41.7 %collective-permute-start.33 = (f32[4,8,384]{2,1,0:T(8,128)S(1)}, f32[4,8,384]{2,1,0:T(8,128)S(1)}, u32[]{:S(2)}, u32[]{:S(2)}) collective-permute-start(f32[4,8,384]{2,1,0:T(8,128)S(1)} %get-tuple-element.33), channel_id=1, source_target_pairs={{0,32},{16,48},{32,0},{48,16},{1,33},{17,49},{33,1},{49,17},{2,34}... | collective-permute-start | bytes 147464 | tf_op jit(solution)/shard_map/ppermute | solution.py:185
  126.8 38.9 %collective-permute-start.34 = (f32[4,8,384]{2,1,0:T(8,128)S(1)}, f32[4,8,384]{2,1,0:T(8,128)S(1)}, u32[]{:S(2)}, u32[]{:S(2)}) collective-permute-start(f32[4,8,384]{2,1,0:T(8,128)S(1)} %get-tuple-element.32), channel_id=1, source_target_pairs={{0,48},{16,0},{32,16},{48,32},{1,49},{17,1},{33,17},{49,33},{2,50}... | collective-permute-start | bytes 147464 | tf_op jit(solution)/shard_map/ppermute | solution.py:185
  130.3 27.0 %slice-start.1 = ((s8[4718592]{0:T(1024)(128)(4,1)}), s8[4194304]{0:T(1024)(128)(4,1)S(1)}, s32[]{:S(2)}) async-start(s8[4718592]{0:T(1024)(128)(4,1)} %bitcast.58), calls=%async_computation.3 | async-start | bytes 8388608
  159.0 6.7 %copy-start.13 = (f32[384]{0:T(512)S(1)}, f32[384]{0:T(512)}, u32[]{:S(2)}) copy-start(f32[384]{0:T(512)} %param.18) | copy-start | bytes 4612
  160.7 15.4 %all-to-all-start.1 = ((f32[32,24,128]{2,1,0:T(8,128)}), f32[32,24,128]{2,1,0:T(8,128)S(1)}, u32[]{:S(2)}, u32[]{:S(2)}) async-start(f32[32,24,128]{2,1,0:T(8,128)} %broadcast_in_dim.11), calls=%async_computation.1 | async-start | bytes 786432 | tf_op jit(solution)/shard_map/all_to_all | solution.py:173
  (27 other events, 111.1 us)

commit v2 on v0

v2 whole, which is shorter than its diff:
```python
import functools

import jax
import jax.numpy as jnp
from jax import lax
from jax.experimental import pallas as pl
from jax.experimental.pallas import tpu as pltpu
from jax.sharding import PartitionSpec as P

D = 6144
BF16 = jnp.bfloat16
F32 = jnp.float32
TILE = 512


def gelu_exact(v):
    return v * 0.5 * (1.0 + lax.erf(v * 0.7071067811865476))


def gelu_slope(v):
    return (
        0.5 * (1.0 + lax.erf(v * 0.7071067811865476))
        + v * jnp.exp(-0.5 * v * v) * 0.3989422804014327
    )


def shift_y(k):
    return [(z * 4 + y, z * 4 + (y + k) % 4) for z in range(4) for y in range(4)]


def shift_z(k):
    return [(z * 4 + y, ((z + k) % 4) * 4 + y) for z in range(4) for y in range(4)]


def shift_row(k):
    return [(r, (r + k) % 4) for r in range(4)]


SWAP = [(0, 1), (1, 0)]


def row_order(first, second):
    p = lax.broadcasted_iota(jnp.int32, (256, 256), 0)
    q = lax.broadcasted_iota(jnp.int32, (256, 256), 1)
    j, i = p >> 6, (p >> 4) & 3
    h, e = (p >> 3) & 1, p & 7
    src = h * 128 + (((first + j) & 3) * 4 + ((second + i) & 3)) * 8 + e
    return jnp.where(src == q, 1.0, 0.0).astype(BF16)


def reorder(sel, x):
    return jnp.dot(sel, x, preferred_element_type=F32).astype(BF16)


def centred_rows(own, other, gain):
    x = jnp.concatenate([own, other], axis=0).astype(F32)
    mean = jnp.sum(x, axis=1, keepdims=True) / x.shape[1]
    return ((x - mean) * gain).astype(BF16)


def forget_partials(where, own_x, other_x, own_g, other_g, gain, w_in, w_out, *rest):
    outs, (lhs_x, lhs_g) = rest[:4], rest[4:]

    @pl.when(pl.program_id(0) == 0)
    def _():
        sel = row_order(where[1], where[2])
        lhs_x[...] = reorder(sel, centred_rows(own_x[...], other_x[...], gain[...]))
        lhs_g[...] = reorder(sel, jnp.concatenate([own_g[...], other_g[...]], axis=0))

    pre = jnp.dot(lhs_x[...], w_in[...], preferred_element_type=F32).astype(BF16)
    grad = lax.dot_general(
        lhs_g[...], w_out[...], (((1,), (1,)), ((), ())), preferred_element_type=F32
    ).astype(BF16)
    for j in range(4):
        for i in range(4):
            at = (j * 4 + i) * 16
            outs[j][i * 32 : i * 32 + 16, :] = pre[at : at + 16]
            outs[j][i * 32 + 16 : i * 32 + 32, :] = grad[at : at + 16]


def retain_partials(where, own_x, other_x, gain, w_in, *rest):
    outs, g_out, lhs_x, lhs_gain = rest[:4], rest[4], rest[5], rest[6]

    @pl.when(pl.program_id(0) == 0)
    def _():
        sel = row_order(where[2], where[1])
        lhs_x[...] = reorder(sel, centred_rows(own_x[...], other_x[...], gain[...]))
        g0 = jnp.broadcast_to(gain[...], (16, gain.shape[1]))
        a = g0.astype(BF16)
        b = (g0 - a.astype(F32)).astype(BF16)
        c = (g0 - a.astype(F32) - b.astype(F32)).astype(BF16)
        lhs_gain[0:16, :] = a
        lhs_gain[16:32, :] = b
        lhs_gain[32:48, :] = c

    pre = jnp.dot(lhs_x[...], w_in[...], preferred_element_type=F32).astype(BF16)
    for j in range(4):
        outs[j][...] = pre[j * 64 : (j + 1) * 64]
    g = jnp.dot(lhs_gain[...], w_in[...], preferred_element_type=F32)
    g_out[...] = (g[32:40] + g[16:24]) + g[0:8]


def stage_sum(own, a, b, c, keep, *sends):
    rows = keep.shape[0]
    for i in range(4):
        at = slice(i * rows, (i + 1) * rows)
        total = (own[at, :].astype(F32) + a[at, :].astype(F32)) + (
            b[at, :].astype(F32) + c[at, :].astype(F32)
        )
        if i == 0:
            keep[...] = total
        else:
            sends[i - 1][...] = total.astype(BF16)


def preact(total, scale, gap, g_all, bias):
    corr = gap[:, 0:1] * g_all[0:1, :]
    for s in range(1, 16):
        corr = corr + gap[:, s : s + 1] * g_all[s : s + 1, :]
    return scale * (total + corr) + bias


def forget_act(keep, a, b, c, scale, gap, g_all, bias, out):
    total = (keep[...] + a[...].astype(F32)) + (b[...].astype(F32) + c[...].astype(F32))
    pre = preact(total[:16], scale[...], gap[...], g_all[...], bias[...])
    out[0:16, :] = gelu_exact(pre).astype(BF16)
    out[16:32, :] = (total[16:32] * gelu_slope(pre)).astype(BF16)


def retain_act(keep, a, b, c, scale, gap, g_all, bias, mask, out):
    total = (keep[...] + a[...].astype(F32)) + (b[...].astype(F32) + c[...].astype(F32))
    pre = preact(total, scale[...], gap[...], g_all[...], bias[...])
    out[...] = (gelu_exact(pre) * mask[...]).astype(BF16)


def saliency_terms(where, b0, b1, b2, b3, normed_t, grad_y, w_in, w_out, out):
    blocks = [b[i * 32 : i * 32 + 32, :] for b in (b0, b1, b2, b3) for i in range(4)]
    act = jnp.concatenate([b[:16] for b in blocks], axis=0)
    grad_pre = jnp.concatenate([b[16:] for b in blocks], axis=0)
    grad_in = jnp.dot(normed_t[...], grad_pre, preferred_element_type=F32)
    grad_out = lax.dot_general(
        act, grad_y[...], (((0,), (0,)), ((), ())), preferred_element_type=F32
    )
    term_in = jnp.sum(jnp.abs(w_in[...].astype(F32) * grad_in), axis=0, keepdims=True)
    prod = jnp.abs(w_out[...].astype(F32) * grad_out)
    lanes = (prod[:, 0:128] + prod[:, 128:256]) + prod[:, 256:384]
    term_out = jnp.sum(jnp.transpose(lanes), axis=0, keepdims=True)
    out[...] = term_in + term_out


def retain_product(where, b0, b1, b2, b3, w_out, out0, out1, acc):
    t = pl.program_id(0)
    act = jnp.concatenate([b0[...], b1[...], b2[...], b3[...]], axis=0)
    part = jnp.dot(act, w_out[...], preferred_element_type=F32)

    @pl.when(t == 0)
    def _():
        acc[...] = part

    @pl.when(t > 0)
    def _():
        acc[...] += part

    @pl.when(t == pl.num_programs(0) - 1)
    def _():
        for k in range(16):
            out0[k * 8 : k * 8 + 8, :] = acc[k * 16 : k * 16 + 8, :]
            out1[k * 8 : k * 8 + 8, :] = acc[k * 16 + 8 : k * 16 + 16, :]


def call(kernel, where, args, outs, scratch=(), steps=6, flops=0):
    def spec(shape, block, index):
        if block is None:
            return pl.BlockSpec(shape, lambda t, w: (0,) * len(shape))
        return pl.BlockSpec(block, index)

    size = sum(a.size * a.dtype.itemsize for a, _, _ in args)
    return pl.pallas_call(
        kernel,
        grid_spec=pltpu.PrefetchScalarGridSpec(
            num_scalar_prefetch=1,
            grid=(steps,),
            in_specs=[spec(a.shape, b, i) for a, b, i in args],
            out_specs=[spec(s, b, i) for s, _, b, i in outs],
            scratch_shapes=list(scratch),
        ),
        out_shape=[jax.ShapeDtypeStruct(s, d) for s, d, _, _ in outs],
        compiler_params=pltpu.CompilerParams(vmem_limit_bytes=40 * 2**20),
        cost_estimate=pl.CostEstimate(flops=flops, bytes_accessed=size, transcendentals=0),
    )(where, *[a for a, _, _ in args])


def whole(a):
    return (a, None, None)


def by_n(a, tile=TILE):
    return (a, (a.shape[0], tile), lambda t, w: (0, t))


def out_n(rows, n, dtype, tile=TILE):
    return ((rows, n), dtype, (rows, tile), lambda t, w: (0, t))


def drop_where(kernel):
    def inner(where, *refs):
        kernel(*refs)

    return inner


def permutes(parts, shift, sign=1):
    return [lax.ppermute(parts[k], "col", shift(sign * (k + 1))) for k in range(3)]


def after(value, *others):
    return lax.optimization_barrier((value, *others))[0]


def local(
    forget_tokens,
    forget_cotangent,
    forget_labels,
    retain_tokens,
    ln_gain,
    w_in,
    b_in,
    w_out,
    b_out,
    pruned,
):
    core = lax.axis_index("dp")
    row = lax.axis_index("row")
    col = lax.axis_index("col")
    y, z = col % 4, col // 4
    width = w_in.shape[0]
    half = w_in.shape[1] // 2
    steps = half // TILE
    where = jnp.stack([core, y, z]).astype(jnp.int32)
    gain = ln_gain[None, :]

    own_g = forget_cotangent * forget_labels[:, None].astype(BF16)
    own = jnp.concatenate([forget_tokens, own_g, retain_tokens], axis=0)
    other = lax.ppermute(own, "dp", SWAP)

    def rows_of(k):
        return lambda t, w: (k, 0)

    def third(a, k):
        return (a, (128, width), rows_of(k))

    w_in_tile = (w_in, (width, TILE), lambda t, w: (0, w[0] * steps + t))
    w_out_tile = (w_out, (TILE, width), lambda t, w: (w[0] * steps + t, 0))

    f_parts = call(
        forget_partials,
        where,
        [third(own, 0), third(other, 0), third(own, 1), third(other, 1), whole(gain),
         w_in_tile, w_out_tile],
        [out_n(128, half, BF16)] * 4,
        [pltpu.VMEM((256, width), BF16)] * 2,
        steps,
        4 * 256 * width * half,
    )
    f_got = permutes(f_parts[1:], shift_y)
    own_r, _ = lax.optimization_barrier((own, f_parts[0]))
    r_parts = call(
        retain_partials,
        where,
        [third(own_r, 2), third(other, 2), whole(gain), w_in_tile],
        [out_n(64, half, BF16)] * 4 + [out_n(8, half, F32)],
        [pltpu.VMEM((256, width), BF16), pltpu.VMEM((48, width), BF16)],
        steps,
        2 * 256 * width * half,
    )
    g_part = r_parts[4]
    r_got = permutes(r_parts[1:4], shift_z)

    own_s, other_s, _ = lax.optimization_barrier((own, other, r_parts[0]))
    tokens = jnp.stack([own_s, other_s]).reshape(2, 3, 128, width)[:, ::2].astype(F32)
    part_mean = jnp.sum(tokens, axis=3) / width
    centred = tokens - part_mean[..., None]
    part_m2 = jnp.sum(centred * centred, axis=3)
    share = jnp.concatenate(
        [part_mean.reshape(4, 128), part_m2.reshape(4, 128), g_part[0].reshape(half // 128, 128)]
    )
    share = lax.all_to_all(
        jnp.broadcast_to(share[None], (16,) + share.shape), "col", 0, 0, tiled=True
    )
    means = share[:, 0:4].reshape(16, 2, 2, 128)
    m2 = share[:, 4:8].reshape(16, 2, 2, 128)
    g_all = share[:, 8:].reshape(16, half)
    mean = jnp.mean(means, axis=0)
    gap = means - mean
    var = (jnp.sum(m2, axis=0) + width * jnp.sum(gap * gap, axis=0)) / D
    scale = lax.rsqrt(var + 1e-06)

    def owned(v, block):
        v = v.reshape(v.shape[:-1] + (16, 8))
        return lax.dynamic_index_in_dim(v, block, v.ndim - 2, False).reshape(
            v.shape[:-3] + (16,)
        )

    f_scale, f_gap = owned(scale[:, 0], y * 4 + z)[:, None], owned(gap[:, :, 0], y * 4 + z).T
    r_scale, r_gap = owned(scale[:, 1], z * 4 + y)[:, None], owned(gap[:, :, 1], z * 4 + y).T

    b_half = lax.dynamic_slice_in_dim(b_in, core * half, half, 0)[None, :]
    ids = row * w_in.shape[1] + core * half + jnp.arange(half, dtype=jnp.int32)
    is_pruned = jnp.any(pruned[:, None] == ids[None, :], axis=0)
    keep = jnp.where(is_pruned, 0.0, 1.0)[None, :]

    sel_f = row_order(y, z)
    tok = jnp.concatenate([own_s[:128], other_s[:128]], axis=0).astype(F32)
    normed_f = (tok - mean[:, 0].reshape(256, 1)) * scale[:, 0].reshape(256, 1) * gain
    normed_f = reorder(sel_f, normed_f.astype(BF16))
    grad_y = reorder(sel_f, jnp.concatenate([own_s[128:256], other_s[128:256]], axis=0))
    normed_t = normed_f.T

    f_sums = call(
        drop_where(stage_sum),
        where,
        [by_n(a, 1024) for a in [f_parts[0]] + f_got],
        [out_n(32, half, F32, 1024)] + [out_n(32, half, BF16, 1024)] * 3,
        steps=half // 1024,
    )
    f_back = permutes(f_sums[1:], shift_z)
    r_sums = call(
        drop_where(stage_sum),
        where,
        [by_n(a, 1024) for a in [r_parts[0]] + r_got],
        [out_n(16, half, F32, 1024)] + [out_n(16, half, BF16, 1024)] * 3,
        steps=half // 1024,
    )
    r_back = permutes(r_sums[1:], shift_y)

    f_block = call(
        drop_where(forget_act),
        where,
        [by_n(a, 1024) for a in [f_sums[0]] + f_back]
        + [whole(f_scale), whole(f_gap), by_n(g_all, 1024), by_n(b_half, 1024)],
        [out_n(32, half, BF16, 1024)],
        steps=half // 1024,
    )[0]
    f_group = jnp.concatenate([f_block] + permutes([f_block] * 3, shift_z, -1), axis=0)
    f_groups = [f_group] + permutes([f_group] * 3, shift_y, -1)
    r_block = call(
        drop_where(retain_act),
        where,
        [by_n(a, 1024) for a in [r_sums[0]] + r_back]
        + [whole(r_scale), whole(r_gap), by_n(g_all, 1024), by_n(b_half, 1024), by_n(keep, 1024)],
        [out_n(16, half, BF16, 1024)],
        steps=half // 1024,
    )[0]
    r_group = jnp.concatenate([r_block] + permutes([r_block] * 3, shift_y, -1), axis=0)
    r_groups = [r_group] + permutes([r_group] * 3, shift_z, -1)

    terms = call(
        saliency_terms,
        where,
        [by_n(a) for a in f_groups] + [whole(normed_t), whole(grad_y), w_in_tile, w_out_tile],
        [out_n(1, half, F32)],
        (),
        steps,
        4 * 256 * width * half,
    )[0]
    terms = jnp.broadcast_to(terms.reshape(1, half // 128, 128), (32, half // 128, 128))
    terms = lax.all_to_all(terms, ("dp", "col"), 0, 0, tiled=True)
    saliency = jnp.sum(terms.reshape(2, 16, half), axis=1).reshape(2 * half) / D

    mine, theirs = call(
        retain_product,
        where,
        [by_n(a) for a in r_groups] + [w_out_tile],
        [((128, width), F32, None, None)] * 2,
        [pltpu.VMEM((256, width), F32)],
        steps,
        2 * 256 * width * half,
    )
    mine = (mine + lax.ppermute(theirs, "dp", SWAP)).reshape(4, 4, 8, width)

    def for_row(r):
        return lax.dynamic_index_in_dim(mine, (r - z) % 4, 0, keepdims=False)

    total = for_row(row)
    for k in (1, 2, 3):
        total = total + lax.ppermute(for_row(row + k), "row", shift_row(k))
    retain_out = (total + b_out).astype(BF16)
    retain_out = lax.dynamic_slice_in_dim(
        jnp.concatenate([retain_out, retain_out], axis=0), (4 - y) % 4, 4, 0
    ).reshape(32, width)
    return (saliency, retain_out)


def solution(mesh):
    in_specs = (
        P("dp", "col"),
        P("dp", "col"),
        P("dp"),
        P("dp", "col"),
        P("col"),
        P("col", "row"),
        P("row"),
        P("row", "col"),
        P("col"),
        P("row"),
    )
    out_specs = (P("row"), P(("dp", "row"), "col"))
    return jax.shard_map(local, mesh=mesh, in_specs=in_specs, out_specs=out_specs, check_vma=False)
```

time: 551 us -> 165 us (0.30)
  waiting for transfers between devices: 277 us -> 53.7 us
  blocking collectives: 206 us -> 0 us
  starting transfers between devices: 0.29 us -> 61.5 us
  Pallas kernels: 0 us -> 25.7 us
  matrix products: 23.8 us -> 0.66 us
  between operations: 14.2 us -> 1.28 us
  other arithmetic: 14 us -> 5.95 us
    psum x3 -> x0, blocking collectives: 206 us -> none  [the longest x1 129 us: local(): saliency = lax.psum(terms, ('dp', 'col')) / D]
    reduce_scatter x4 -> x0, waiting for transfers between devices: 109 us -> none  [the longest x1 72.4 us: local(): lax.psum_scatter(partial_pre, 'col', scatter_dimension=1, tiled=True)]
    all_gather x2 -> x0, waiting for transfers between devices: 93.9 us -> none  [the longest x1 51.7 us: local(): act_all = lax.all_gather(act_share, 'col', axis=1, tiled=True)]
    unnamed x8 -> x0, waiting for transfers between devices: 74.5 us -> none
    ppermute x0 -> x29, starting transfers between devices: none -> 46.7 us  [the longest x24 40.2 us: permutes(): lax.ppermute(parts[k], 'col', shift(sign * (k + 1)))]
    ppermute x0 -> x29, waiting for transfers between devices: none -> 44 us  [the longest x24 42.2 us: permutes(): lax.ppermute(parts[k], 'col', shift(sign * (k + 1)))]
    pallas_call x0 -> x8, Pallas kernels: none -> 25.7 us  [call(): pl.pallas_call(kernel, grid_spec=pltpu.PrefetchScalarGridSpec(num_scalar_...]
    dot_general x5 -> x2, matrix products: 23.8 us -> 0.66 us  [reorder(): return jnp.dot(sel, x, preferred_element_type=F32).astype(BF16)]
  transfers between devices with their start and end apart: 7 -> 31, of which waited for: 7 -> 12; matrix products, arithmetic and copies ran while one was open for 6% -> 5% of each run, Pallas kernels for 0% -> 11%
where the time goes in v2:
time: 165 us; the launch traced here: 164 us
  starting transfers between devices  61.5 us (37%)
  waiting for transfers between devices  53.7 us (33%)
  Pallas kernels  25.7 us (16%)
  local copies, waits for them, and re-layouts  15.4 us (9%)
  other arithmetic  5.95 us (4%)
    ppermute x24, waiting for transfers between devices, permutes(): lax.ppermute(parts[k], 'col', shift(sign * (k + 1)))  42.2 us
    ppermute x24, starting transfers between devices, permutes(): lax.ppermute(parts[k], 'col', shift(sign * (k + 1)))  40.2 us
    pallas_call x8, Pallas kernels, call(): pl.pallas_call(kernel, grid_spec=pltpu.PrefetchScalarGridSpec(num_scalar_...  25.7 us
    all_to_all x1, waiting for transfers between devices, local(): terms = lax.all_to_all(terms, ('dp', 'col'), 0, 0, tiled=True)  9.76 us
    unnamed x44, local copies, waits for them, and re-layouts  9.4 us
    all_to_all x1, starting transfers between devices, local(): lax.all_to_all(jnp.broadcast_to(share[None], (16,) + share.shape), 'col',...  8.18 us
    all_to_all x1, starting transfers between devices, local(): terms = lax.all_to_all(terms, ('dp', 'col'), 0, 0, tiled=True)  6.6 us
    ppermute x3, starting transfers between devices, local(): total = total + lax.ppermute(for_row(row + k), 'row', shift_row(k))  6.32 us
  transfers between devices with their start and end apart: 31, of which 12 were waited for; matrix products, arithmetic and copies ran while one was open for 5% of the time, Pallas kernels for 11%

profile of v2, /device:TPU:0, one launch (start us, length us, event | category | flops | bytes accessed | tf_op | source)
XLA Modules:
  0.0 164.2 jit_solution(8715710818480689452)
XLA Ops:
  1.3 1.0 broadcast_multiply_fusion
  2.3 1.0 pad_maximum_fusion.3.own_x.own_g
  4.9 2.3 %copy-done = bf16[384,6144]{1,0:T(8,128)(2,1)S(1)} copy-done((bf16[384,6144]{1,0:T(8,128)(2,1)S(1)}, bf16[384,6144]{1,0:T(8,128)(2,1)}, u32[]{:S(2)}) %copy-start) | copy-done | bytes 4718616
  7.3 2.3 %copy-done.1 = bf16[6144,384]{1,0:T(8,128)(2,1)S(1)} copy-done((bf16[6144,384]{1,0:T(8,128)(2,1)S(1)}, bf16[6144,384]{1,0:T(8,128)(2,1)}, u32[]{:S(2)}) %copy-start.1) | copy-done | bytes 4718616
  9.6 5.0 %shard_map.113 = (bf16[128,3072]{1,0:T(8,128)(2,1)S(1)}, bf16[128,3072]{1,0:T(8,128)(2,1)}, bf16[128,3072]{1,0:T(8,128)(2,1)S(1)}, bf16[128,3072]{1,0:T(8,128)(2,1)S(1)}) custom-call(s32[3]{0:T(128)S(1)} %pad_add_fusion.where, bf16[384,384]{1,0:T(8,128)(2,1)S(1)} %pad_maximum_fusion.3.own_x.own_g, bf16[384,384]{1,0:T(8,128)(2,1)S(1)} %collective-permute-done.other_x.other_g, ...), custom_call_target="tpu_custom_call" | custom-call | flops 1207959552 | bytes 10618368 | tf_op jit(solution)/shard_map/pallas_call | solution.py:178
  14.6 3.3 %shard_map.115 = (bf16[64,3072]{1,0:T(8,128)(2,1)S(1)}, bf16[64,3072]{1,0:T(8,128)(2,1)S(1)}, bf16[64,3072]{1,0:T(8,128)(2,1)S(1)}, bf16[64,3072]{1,0:T(8,128)(2,1)S(1)}, f32[8,3072]{1,0:T(8,128)S(1)}) custom-call(s32[3]{0:T(128)S(1)} %pad_add_fusion.where, bf16[384,384]{1,0:T(8,128)(2,1)S(1)} %pad_maximum_fusion.3.own_x.own_g, ...), custom_call_target="tpu_custom_call" | custom-call | flops 603979776 | bytes 5309952 | tf_op jit(solution)/shard_map/pallas_call | solution.py:178
  20.1 8.2 %all-to-all-start = ((f32[16,32,128]{2,1,0:T(8,128)}), f32[16,32,128]{2,1,0:T(8,128)}, u32[]{:S(2)}, u32[]{:S(2)}) async-start(f32[16,32,128]{2,1,0:T(8,128)} %broadcast_in_dim.43), calls=%async_computation | async-start | bytes 524288 | tf_op jit(solution)/shard_map/all_to_all | solution.py:287
  29.2 1.9 %collective-permute-start.1 = (bf16[128,3072]{1,0:T(8,128)(2,1)}, bf16[128,3072]{1,0:T(8,128)(2,1)S(1)}, u32[]{:S(2)}, u32[]{:S(2)}) collective-permute-start(bf16[128,3072]{1,0:T(8,128)(2,1)} %get-tuple-element.25), channel_id=1, source_target_pairs={{0,1},{1,2},{2,3},{3,0},{4,5},{5,6},{6,7},{7,4},{8,9},{9,10},{10,1... | collective-permute-start | bytes 2359304 | tf_op jit(solution)/shard_map/ppermute | solution.py:213
  31.1 2.7 %collective-permute-start.2 = (bf16[128,3072]{1,0:T(8,128)(2,1)}, bf16[128,3072]{1,0:T(8,128)(2,1)S(1)}, u32[]{:S(2)}, u32[]{:S(2)}) collective-permute-start(bf16[128,3072]{1,0:T(8,128)(2,1)} %copy-done.5), channel_id=1, source_target_pairs={{0,2},{1,3},{2,0},{3,1},{4,6},{5,7},{6,4},{7,5},{8,10},{9,11},{10,... | collective-permute-start | bytes 2359304 | tf_op jit(solution)/shard_map/ppermute | solution.py:213
  33.7 1.5 collective-permute-start.3
  35.2 1.5 collective-permute-start.13
  36.7 2.7 %collective-permute-start.14 = (bf16[64,3072]{1,0:T(8,128)(2,1)}, bf16[64,3072]{1,0:T(8,128)(2,1)}, u32[]{:S(2)}, u32[]{:S(2)}) collective-permute-start(bf16[64,3072]{1,0:T(8,128)(2,1)} %copy-done.7), channel_id=1, source_target_pairs={{0,8},{1,9},{2,10},{3,11},{4,12},{5,13},{6,14},{7,15},{8,0},{9,1},... | collective-permute-start | bytes 1179656 | tf_op jit(solution)/shard_map/ppermute | solution.py:213
  39.3 0.9 slice_reduce_fusion.3
  40.3 7.8 %collective-permute-done.13.refs_1_ = bf16[64,3072]{1,0:T(8,128)(2,1)} collective-permute-done((bf16[64,3072]{1,0:T(8,128)(2,1)}, bf16[64,3072]{1,0:T(8,128)(2,1)}, u32[]{:S(2)}, u32[]{:S(2)}) %collective-permute-start.13) | collective-permute-done | bytes 393248 | tf_op jit(solution)/shard_map/ppermute | solution.py:213
  48.1 2.1 %collective-permute-start.15 = (bf16[64,3072]{1,0:T(8,128)(2,1)}, bf16[64,3072]{1,0:T(8,128)(2,1)S(1)}, u32[]{:S(2)}, u32[]{:S(2)}) collective-permute-start(bf16[64,3072]{1,0:T(8,128)(2,1)} %copy-done.6), channel_id=1, source_target_pairs={{0,12},{1,13},{2,14},{3,15},{4,0},{5,1},{6,2},{7,3},{8,4},{9,5},{1... | collective-permute-start | bytes 1179656 | tf_op jit(solution)/shard_map/ppermute | solution.py:213
  50.9 4.9 %collective-permute-done.14.refs_2_ = bf16[64,3072]{1,0:T(8,128)(2,1)} collective-permute-done((bf16[64,3072]{1,0:T(8,128)(2,1)}, bf16[64,3072]{1,0:T(8,128)(2,1)}, u32[]{:S(2)}, u32[]{:S(2)}) %collective-permute-start.14) | collective-permute-done | bytes 393248 | tf_op jit(solution)/shard_map/ppermute | solution.py:213
  56.1 3.3 %shard_map.118 = (f32[16,3072]{1,0:T(8,128)S(1)}, bf16[16,3072]{1,0:T(8,128)(2,1)}, bf16[16,3072]{1,0:T(8,128)(2,1)S(1)}, bf16[16,3072]{1,0:T(8,128)(2,1)S(1)}) custom-call(s32[3]{0:T(128)S(1)} %pad_add_fusion.where, bf16[64,3072]{1,0:T(8,128)(2,1)S(1)} %get-tuple-element.33.refs_0_, bf16[64,3072]{1,0:T(8,128)(2,1)} %collective-permute-done.13.refs_1_, ...), custom_call_target="tpu_custom_call" | custom-call | bytes 1572864 | tf_op jit(solution)/shard_map/pallas_call | solution.py:178
  59.7 10.1 %collective-permute-done.2.refs_2_ = bf16[128,3072]{1,0:T(8,128)(2,1)S(1)} collective-permute-done((bf16[128,3072]{1,0:T(8,128)(2,1)}, bf16[128,3072]{1,0:T(8,128)(2,1)S(1)}, u32[]{:S(2)}, u32[]{:S(2)}) %collective-permute-start.2) | collective-permute-done | bytes 786464 | tf_op jit(solution)/shard_map/ppermute | solution.py:213
  69.8 3.5 %shard_map.114 = (f32[32,3072]{1,0:T(8,128)S(1)}, bf16[32,3072]{1,0:T(8,128)(2,1)}, bf16[32,3072]{1,0:T(8,128)(2,1)S(1)}, bf16[32,3072]{1,0:T(8,128)(2,1)S(1)}) custom-call(s32[3]{0:T(128)S(1)} %pad_add_fusion.where, bf16[128,3072]{1,0:T(8,128)(2,1)S(1)} %get-tuple-element.24.refs_0_, bf16[128,3072]{1,0:T(8,128)(2,1)S(1)} %collective-permute-done.1.refs_1_, ...), custom_call_target="tpu_custom_call" | custom-call | bytes 3145728 | tf_op jit(solution)/shard_map/pallas_call | solution.py:178
  73.3 1.5 collective-permute-start.4
  74.9 0.9 slice.61
  78.8 1.5 collective-permute-start.18
  80.3 2.7 %collective-permute-start.5 = (bf16[32,3072]{1,0:T(8,128)(2,1)}, bf16[32,3072]{1,0:T(8,128)(2,1)S(1)}, u32[]{:S(2)}, u32[]{:S(2)}) collective-permute-start(bf16[32,3072]{1,0:T(8,128)(2,1)} %copy-done.10), channel_id=1, source_target_pairs={{0,8},{1,9},{2,10},{3,11},{4,12},{5,13},{6,14},{7,15},{8,0},{9,1},... | collective-permute-start | bytes 589832 | tf_op jit(solution)/shard_map/ppermute | solution.py:213
  83.0 1.5 collective-permute-start.6
  85.2 2.5 %shard_map.119 = bf16[16,3072]{1,0:T(8,128)(2,1)S(1)} custom-call(s32[3]{0:T(128)S(1)} %pad_add_fusion.where, f32[16,3072]{1,0:T(8,128)S(1)} %get-tuple-element.40.refs_0_, bf16[16,3072]{1,0:T(8,128)(2,1)} %collective-permute-done.16.refs_1_, bf16[16,3072]{1,0:T(8,128)(2,1)S(1)} %collective-permute-done.17.refs_2_, ...), custom_call_target="tpu_custom_call" | custom-call | bytes 713792 | tf_op jit(solution)/shard_map/pallas_call | solution.py:178
  87.6 0.9 collective-permute-start.21
  88.5 2.9 %collective-permute-start.20 = (bf16[16,3072]{1,0:T(8,128)(2,1)S(1)}, bf16[16,3072]{1,0:T(8,128)(2,1)S(1)}, u32[]{:S(2)}, u32[]{:S(2)}) collective-permute-start(bf16[16,3072]{1,0:T(8,128)(2,1)S(1)} %shard_map.119), channel_id=1, source_target_pairs={{0,2},{1,3},{2,0},{3,1},{4,6},{5,7},{6,4},{7,5},{8,10},{9,11},{10,... | collective-permute-start | bytes 294920 | tf_op jit(solution)/shard_map/ppermute | solution.py:213
  92.3 1.3 shard_map.116
  93.6 1.5 collective-permute-start.9
  95.1 1.8 %collective-permute-start.8 = (bf16[32,3072]{1,0:T(8,128)(2,1)S(1)}, bf16[32,3072]{1,0:T(8,128)(2,1)S(1)}, u32[]{:S(2)}, u32[]{:S(2)}) collective-permute-start(bf16[32,3072]{1,0:T(8,128)(2,1)S(1)} %shard_map.116), channel_id=1, source_target_pairs={{0,8},{1,9},{2,10},{3,11},{4,12},{5,13},{6,14},{7,15},{8,0},{9,1},... | collective-permute-start | bytes 589832 | tf_op jit(solution)/shard_map/ppermute | solution.py:213
  96.9 2.1 %collective-permute-start.7 = (bf16[32,3072]{1,0:T(8,128)(2,1)S(1)}, bf16[32,3072]{1,0:T(8,128)(2,1)S(1)}, u32[]{:S(2)}, u32[]{:S(2)}) collective-permute-start(bf16[32,3072]{1,0:T(8,128)(2,1)S(1)} %shard_map.116), channel_id=1, source_target_pairs={{0,12},{1,13},{2,14},{3,15},{4,0},{5,1},{6,2},{7,3},{8,4},{9,5},{1... | collective-permute-start | bytes 589832 | tf_op jit(solution)/shard_map/ppermute | solution.py:213
  99.2 1.6 collective-permute-start.23
  100.8 2.7 %collective-permute-done.9 = bf16[32,3072]{1,0:T(8,128)(2,1)S(1)} collective-permute-done((bf16[32,3072]{1,0:T(8,128)(2,1)S(1)}, bf16[32,3072]{1,0:T(8,128)(2,1)S(1)}, u32[]{:S(2)}, u32[]{:S(2)}) %collective-permute-start.9) | collective-permute-done | bytes 196640 | tf_op jit(solution)/shard_map/ppermute | solution.py:213
  103.6 3.4 %collective-permute-done.8 = bf16[32,3072]{1,0:T(8,128)(2,1)S(1)} collective-permute-done((bf16[32,3072]{1,0:T(8,128)(2,1)S(1)}, bf16[32,3072]{1,0:T(8,128)(2,1)S(1)}, u32[]{:S(2)}, u32[]{:S(2)}) %collective-permute-start.8) | collective-permute-done | bytes 196640 | tf_op jit(solution)/shard_map/ppermute | solution.py:213
  106.9 5.1 %collective-permute-done.7 = bf16[32,3072]{1,0:T(8,128)(2,1)S(1)} collective-permute-done((bf16[32,3072]{1,0:T(8,128)(2,1)S(1)}, bf16[32,3072]{1,0:T(8,128)(2,1)S(1)}, u32[]{:S(2)}, u32[]{:S(2)}) %collective-permute-start.7) | collective-permute-done | bytes 196640 | tf_op jit(solution)/shard_map/ppermute | solution.py:213
  112.1 1.5 collective-permute-start.12
  114.4 1.0 collective-permute-done.24.b3
  115.4 5.7 %collective-permute-start.10 = (bf16[128,3072]{1,0:T(8,128)(2,1)S(1)}, bf16[128,3072]{1,0:T(8,128)(2,1)S(1)}, u32[]{:S(2)}, u32[]{:S(2)}) collective-permute-start(bf16[128,3072]{1,0:T(8,128)(2,1)S(1)} %pad_maximum_fusion.b0), channel_id=1, source_target_pairs={{0,3},{1,0},{2,1},{3,2},{4,7},{5,4},{6,5},{7,6},{8,11},{9,8},{10,9... | collective-permute-start | bytes 2359304 | tf_op jit(solution)/shard_map/ppermute | solution.py:213
  121.5 2.5 %copy-done.2 = bf16[6144,384]{1,0:T(8,128)(2,1)S(1)} copy-done((bf16[6144,384]{1,0:T(8,128)(2,1)S(1)}, bf16[6144,384]{1,0:T(8,128)(2,1)}, u32[]{:S(2)}) %copy-start.2) | copy-done | bytes 4718616
  124.0 2.8 %shard_map.120 = (f32[128,384]{1,0:T(8,128)S(1)}, f32[128,384]{1,0:T(8,128)S(1)}) custom-call(s32[3]{0:T(128)S(1)} %pad_add_fusion.where, bf16[64,3072]{1,0:T(8,128)(2,1)S(1)} %pad_maximum_fusion.2.b0, bf16[64,3072]{1,0:T(8,128)(2,1)S(1)} %collective-permute-done.22.b1, bf16[64,3072]{1,0:T(8,128)(2,1)S(1)} %collective-permute-done.23.b2, ...), custom_call_target="tpu_custom_call" | custom-call | flops 603979776 | bytes 6291456 | tf_op jit(solution)/shard_map/pallas_call | solution.py:178
  127.3 1.0 collective-permute-done.25
  128.4 1.6 collective-permute-start.26
  129.9 1.7 %collective-permute-start.28 = (f32[4,8,384]{2,1,0:T(8,128)S(1)}, f32[4,8,384]{2,1,0:T(8,128)S(1)}, u32[]{:S(2)}, u32[]{:S(2)}) collective-permute-start(f32[4,8,384]{2,1,0:T(8,128)S(1)} %get-tuple-element.56), channel_id=1, source_target_pairs={{0,48},{16,0},{32,16},{48,32},{1,49},{17,1},{33,17},{49,33},{2,50}... | collective-permute-start | bytes 147464 | tf_op jit(solution)/shard_map/ppermute | solution.py:386
  131.7 6.8 %collective-permute-done.12.b3 = bf16[128,3072]{1,0:T(8,128)(2,1)S(1)} collective-permute-done((bf16[128,3072]{1,0:T(8,128)(2,1)S(1)}, bf16[128,3072]{1,0:T(8,128)(2,1)S(1)}, u32[]{:S(2)}, u32[]{:S(2)}) %collective-permute-start.12) | collective-permute-done | bytes 786464 | tf_op jit(solution)/shard_map/ppermute | solution.py:213
  138.4 3.0 %collective-permute-start.27 = (f32[4,8,384]{2,1,0:T(8,128)S(1)}, f32[4,8,384]{2,1,0:T(8,128)S(1)}, u32[]{:S(2)}, u32[]{:S(2)}) collective-permute-start(f32[4,8,384]{2,1,0:T(8,128)S(1)} %get-tuple-element.57), channel_id=1, source_target_pairs={{0,32},{16,48},{32,0},{48,16},{1,33},{17,49},{33,1},{49,17},{2,34}... | collective-permute-start | bytes 147464 | tf_op jit(solution)/shard_map/ppermute | solution.py:386
  141.5 4.1 %shard_map.117 = f32[1,3072]{1,0:T(1,128)S(1)} custom-call(s32[3]{0:T(128)S(1)} %pad_add_fusion.where, bf16[128,3072]{1,0:T(8,128)(2,1)S(1)} %pad_maximum_fusion.b0, bf16[128,3072]{1,0:T(8,128)(2,1)S(1)} %collective-permute-done.10.b1, bf16[128,3072]{1,0:T(8,128)(2,1)S(1)} %collective-permute-done.11.b2, bf16[128,3072]{1,0:T(8,128)(2,1)S(1)} %collective-permute-done.12.b3, ...), custom_call_target="tpu_custom_call" | custom-call | flops 1207959552 | bytes 12976128 | tf_op jit(solution)/shard_map/pallas_call | solution.py:178
  146.3 6.6 %all-to-all-start.1 = ((f32[32,24,128]{2,1,0:T(8,128)}), f32[32,24,128]{2,1,0:T(8,128)S(1)}, u32[]{:S(2)}, u32[]{:S(2)}) async-start(f32[32,24,128]{2,1,0:T(8,128)} %broadcast_in_dim.48), calls=%async_computation.1 | async-start | bytes 786432 | tf_op jit(solution)/shard_map/all_to_all | solution.py:367
  153.7 9.8 %all-to-all-done.1 = f32[32,24,128]{2,1,0:T(8,128)S(1)} async-done(((f32[32,24,128]{2,1,0:T(8,128)}), f32[32,24,128]{2,1,0:T(8,128)S(1)}, u32[]{:S(2)}, u32[]{:S(2)}) %all-to-all-start.1) | async-done | bytes 393248 | tf_op jit(solution)/shard_map/all_to_all | solution.py:367
  (116 shorter events, 15.0 us)
Async XLA Ops:
  3.2 1.7 %collective-permute-start = (bf16[384,384]{1,0:T(8,128)(2,1)S(1)}, bf16[384,384]{1,0:T(8,128)(2,1)S(1)}, u32[]{:S(2)}, u32[]{:S(2)}) collective-permute-start(bf16[384,384]{1,0:T(8,128)(2,1)S(1)} %pad_maximum_fusion.3.own_x.own_g), channel_id=1, source_target_pairs={{0,64},{64,0},{1,65},{65,1},{2,66},{66,2},{3,67},{67,3},{4,68},{68... | collective-permute-start | bytes 884744 | tf_op jit(solution)/shard_map/ppermute | solution.py:244
  4.9 2.3 %copy-start = (bf16[384,6144]{1,0:T(8,128)(2,1)S(1)}, bf16[384,6144]{1,0:T(8,128)(2,1)}, u32[]{:S(2)}) copy-start(bf16[384,6144]{1,0:T(8,128)(2,1)} %w_in.5) | copy-start | bytes 14155780
  14.5 3.4 %copy-start.4 = (bf16[128,3072]{1,0:T(8,128)(2,1)}, bf16[128,3072]{1,0:T(8,128)(2,1)S(1)}, u32[]{:S(2)}) copy-start(bf16[128,3072]{1,0:T(8,128)(2,1)S(1)} %get-tuple-element.27) | copy-start | bytes 2359300
  14.6 14.6 %copy-start.5 = (bf16[128,3072]{1,0:T(8,128)(2,1)}, bf16[128,3072]{1,0:T(8,128)(2,1)S(1)}, u32[]{:S(2)}) copy-start(bf16[128,3072]{1,0:T(8,128)(2,1)S(1)} %get-tuple-element.26) | copy-start | bytes 2359300
  17.9 13.2 %copy-start.8 = (bf16[64,3072]{1,0:T(8,128)(2,1)}, bf16[64,3072]{1,0:T(8,128)(2,1)S(1)}, u32[]{:S(2)}) copy-start(bf16[64,3072]{1,0:T(8,128)(2,1)S(1)} %get-tuple-element.37) | copy-start | bytes 1179652
  17.9 10.3 %copy-start.18 = (s32[128]{0:T(128)S(1)}, s32[128]{0:T(128)}, u32[]{:S(2)}) copy-start(s32[128]{0:T(128)} %param.19) | copy-start | bytes 1540
  17.9 10.6 %copy-start.15 = (f32[6144]{0:T(1024)S(1)}, f32[6144]{0:T(1024)}, u32[]{:S(2)}) copy-start(f32[6144]{0:T(1024)} %param.16) | copy-start | bytes 73732
  20.1 19.3 %all-to-all-start = ((f32[16,32,128]{2,1,0:T(8,128)}), f32[16,32,128]{2,1,0:T(8,128)}, u32[]{:S(2)}, u32[]{:S(2)}) async-start(f32[16,32,128]{2,1,0:T(8,128)} %broadcast_in_dim.43), calls=%async_computation | async-start | bytes 524288 | tf_op jit(solution)/shard_map/all_to_all | solution.py:287
  29.2 30.5 %collective-permute-start.1 = (bf16[128,3072]{1,0:T(8,128)(2,1)}, bf16[128,3072]{1,0:T(8,128)(2,1)S(1)}, u32[]{:S(2)}, u32[]{:S(2)}) collective-permute-start(bf16[128,3072]{1,0:T(8,128)(2,1)} %get-tuple-element.25), channel_id=1, source_target_pairs={{0,1},{1,2},{2,3},{3,0},{4,5},{5,6},{6,7},{7,4},{8,9},{9,10},{10,1... | collective-permute-start | bytes 2359304 | tf_op jit(solution)/shard_map/ppermute | solution.py:213
  31.1 38.8 %collective-permute-start.2 = (bf16[128,3072]{1,0:T(8,128)(2,1)}, bf16[128,3072]{1,0:T(8,128)(2,1)S(1)}, u32[]{:S(2)}, u32[]{:S(2)}) collective-permute-start(bf16[128,3072]{1,0:T(8,128)(2,1)} %copy-done.5), channel_id=1, source_target_pairs={{0,2},{1,3},{2,0},{3,1},{4,6},{5,7},{6,4},{7,5},{8,10},{9,11},{10,... | collective-permute-start | bytes 2359304 | tf_op jit(solution)/shard_map/ppermute | solution.py:213
  33.7 36.1 %collective-permute-start.3 = (bf16[128,3072]{1,0:T(8,128)(2,1)}, bf16[128,3072]{1,0:T(8,128)(2,1)}, u32[]{:S(2)}, u32[]{:S(2)}) collective-permute-start(bf16[128,3072]{1,0:T(8,128)(2,1)} %copy-done.4), channel_id=1, source_target_pairs={{0,3},{1,0},{2,1},{3,2},{4,7},{5,4},{6,5},{7,6},{8,11},{9,8},{10,9... | collective-permute-start | bytes 2359304 | tf_op jit(solution)/shard_map/ppermute | solution.py:213
  35.2 12.9 %collective-permute-start.13 = (bf16[64,3072]{1,0:T(8,128)(2,1)}, bf16[64,3072]{1,0:T(8,128)(2,1)}, u32[]{:S(2)}, u32[]{:S(2)}) collective-permute-start(bf16[64,3072]{1,0:T(8,128)(2,1)} %copy-done.8), channel_id=1, source_target_pairs={{0,4},{1,5},{2,6},{3,7},{4,8},{5,9},{6,10},{7,11},{8,12},{9,13},{1... | collective-permute-start | bytes 1179656 | tf_op jit(solution)/shard_map/ppermute | solution.py:213
  36.7 19.2 %collective-permute-start.14 = (bf16[64,3072]{1,0:T(8,128)(2,1)}, bf16[64,3072]{1,0:T(8,128)(2,1)}, u32[]{:S(2)}, u32[]{:S(2)}) collective-permute-start(bf16[64,3072]{1,0:T(8,128)(2,1)} %copy-done.7), channel_id=1, source_target_pairs={{0,8},{1,9},{2,10},{3,11},{4,12},{5,13},{6,14},{7,15},{8,0},{9,1},... | collective-permute-start | bytes 1179656 | tf_op jit(solution)/shard_map/ppermute | solution.py:213
  40.3 15.5 %copy-start.13 = (f32[4,128]{1,0:T(4,128)}, f32[4,128]{1,0:T(4,128)S(1)}, u32[]{:S(2)}) copy-start(f32[4,128]{1,0:T(4,128)S(1)} %broadcast_multiply_fusion.1) | copy-start | bytes 6148
  48.1 8.0 %collective-permute-start.15 = (bf16[64,3072]{1,0:T(8,128)(2,1)}, bf16[64,3072]{1,0:T(8,128)(2,1)S(1)}, u32[]{:S(2)}, u32[]{:S(2)}) collective-permute-start(bf16[64,3072]{1,0:T(8,128)(2,1)} %copy-done.6), channel_id=1, source_target_pairs={{0,12},{1,13},{2,14},{3,15},{4,0},{5,1},{6,2},{7,3},{8,4},{9,5},{1... | collective-permute-start | bytes 1179656 | tf_op jit(solution)/shard_map/ppermute | solution.py:213
  59.4 13.9 %copy-start.11 = (bf16[16,3072]{1,0:T(8,128)(2,1)}, bf16[16,3072]{1,0:T(8,128)(2,1)S(1)}, u32[]{:S(2)}) copy-start(bf16[16,3072]{1,0:T(8,128)(2,1)S(1)} %get-tuple-element.43) | copy-start | bytes 294916
  59.4 13.9 %copy-start.12 = (bf16[16,3072]{1,0:T(8,128)(2,1)}, bf16[16,3072]{1,0:T(8,128)(2,1)S(1)}, u32[]{:S(2)}) copy-start(bf16[16,3072]{1,0:T(8,128)(2,1)S(1)} %get-tuple-element.42) | copy-start | bytes 294916
  59.4 23.5 %collective-permute-start.16 = (bf16[16,3072]{1,0:T(8,128)(2,1)}, bf16[16,3072]{1,0:T(8,128)(2,1)}, u32[]{:S(2)}, u32[]{:S(2)}) collective-permute-start(bf16[16,3072]{1,0:T(8,128)(2,1)} %get-tuple-element.41), channel_id=1, source_target_pairs={{0,1},{1,2},{2,3},{3,0},{4,5},{5,6},{6,7},{7,4},{8,9},{9,10},{10,1... | collective-permute-start | bytes 294920 | tf_op jit(solution)/shard_map/ppermute | solution.py:213
  73.3 2.5 %copy-start.9 = (bf16[32,3072]{1,0:T(8,128)(2,1)}, bf16[32,3072]{1,0:T(8,128)(2,1)S(1)}, u32[]{:S(2)}) copy-start(bf16[32,3072]{1,0:T(8,128)(2,1)S(1)} %get-tuple-element.31) | copy-start | bytes 589828
  73.3 2.5 %copy-start.10 = (bf16[32,3072]{1,0:T(8,128)(2,1)}, bf16[32,3072]{1,0:T(8,128)(2,1)S(1)}, u32[]{:S(2)}) copy-start(bf16[32,3072]{1,0:T(8,128)(2,1)S(1)} %get-tuple-element.30) | copy-start | bytes 589828
  73.3 18.1 %collective-permute-start.4 = (bf16[32,3072]{1,0:T(8,128)(2,1)}, bf16[32,3072]{1,0:T(8,128)(2,1)S(1)}, u32[]{:S(2)}, u32[]{:S(2)}) collective-permute-start(bf16[32,3072]{1,0:T(8,128)(2,1)} %get-tuple-element.29), channel_id=1, source_target_pairs={{0,4},{1,5},{2,6},{3,7},{4,8},{5,9},{6,10},{7,11},{8,12},{9,13},{1... | collective-permute-start | bytes 589832 | tf_op jit(solution)/shard_map/ppermute | solution.py:213
  77.9 6.5 %collective-permute-start.17 = (bf16[16,3072]{1,0:T(8,128)(2,1)}, bf16[16,3072]{1,0:T(8,128)(2,1)S(1)}, u32[]{:S(2)}, u32[]{:S(2)}) collective-permute-start(bf16[16,3072]{1,0:T(8,128)(2,1)} %copy-done.12), channel_id=1, source_target_pairs={{0,2},{1,3},{2,0},{3,1},{4,6},{5,7},{6,4},{7,5},{8,10},{9,11},{10,... | collective-permute-start | bytes 294920 | tf_op jit(solution)/shard_map/ppermute | solution.py:213
  78.8 5.7 %collective-permute-start.18 = (bf16[16,3072]{1,0:T(8,128)(2,1)}, bf16[16,3072]{1,0:T(8,128)(2,1)S(1)}, u32[]{:S(2)}, u32[]{:S(2)}) collective-permute-start(bf16[16,3072]{1,0:T(8,128)(2,1)} %copy-done.11), channel_id=1, source_target_pairs={{0,3},{1,0},{2,1},{3,2},{4,7},{5,4},{6,5},{7,6},{8,11},{9,8},{10,9... | collective-permute-start | bytes 294920 | tf_op jit(solution)/shard_map/ppermute | solution.py:213
  80.3 12.0 %collective-permute-start.5 = (bf16[32,3072]{1,0:T(8,128)(2,1)}, bf16[32,3072]{1,0:T(8,128)(2,1)S(1)}, u32[]{:S(2)}, u32[]{:S(2)}) collective-permute-start(bf16[32,3072]{1,0:T(8,128)(2,1)} %copy-done.10), channel_id=1, source_target_pairs={{0,8},{1,9},{2,10},{3,11},{4,12},{5,13},{6,14},{7,15},{8,0},{9,1},... | collective-permute-start | bytes 589832 | tf_op jit(solution)/shard_map/ppermute | solution.py:213
  83.0 9.3 %collective-permute-start.6 = (bf16[32,3072]{1,0:T(8,128)(2,1)}, bf16[32,3072]{1,0:T(8,128)(2,1)S(1)}, u32[]{:S(2)}, u32[]{:S(2)}) collective-permute-start(bf16[32,3072]{1,0:T(8,128)(2,1)} %copy-done.9), channel_id=1, source_target_pairs={{0,12},{1,13},{2,14},{3,15},{4,0},{5,1},{6,2},{7,3},{8,4},{9,5},{1... | collective-permute-start | bytes 589832 | tf_op jit(solution)/shard_map/ppermute | solution.py:213
  87.6 9.3 %collective-permute-start.21 = (bf16[16,3072]{1,0:T(8,128)(2,1)S(1)}, bf16[16,3072]{1,0:T(8,128)(2,1)S(1)}, u32[]{:S(2)}, u32[]{:S(2)}) collective-permute-start(bf16[16,3072]{1,0:T(8,128)(2,1)S(1)} %shard_map.119), channel_id=1, source_target_pairs={{0,1},{1,2},{2,3},{3,0},{4,5},{5,6},{6,7},{7,4},{8,9},{9,10},{10,1... | collective-permute-start | bytes 294920 | tf_op jit(solution)/shard_map/ppermute | solution.py:213
  88.5 10.5 %collective-permute-start.20 = (bf16[16,3072]{1,0:T(8,128)(2,1)S(1)}, bf16[16,3072]{1,0:T(8,128)(2,1)S(1)}, u32[]{:S(2)}, u32[]{:S(2)}) collective-permute-start(bf16[16,3072]{1,0:T(8,128)(2,1)S(1)} %shard_map.119), channel_id=1, source_target_pairs={{0,2},{1,3},{2,0},{3,1},{4,6},{5,7},{6,4},{7,5},{8,10},{9,11},{10,... | collective-permute-start | bytes 294920 | tf_op jit(solution)/shard_map/ppermute | solution.py:213
  91.4 7.6 %collective-permute-start.19 = (bf16[16,3072]{1,0:T(8,128)(2,1)S(1)}, bf16[16,3072]{1,0:T(8,128)(2,1)S(1)}, u32[]{:S(2)}, u32[]{:S(2)}) collective-permute-start(bf16[16,3072]{1,0:T(8,128)(2,1)S(1)} %shard_map.119), channel_id=1, source_target_pairs={{0,3},{1,0},{2,1},{3,2},{4,7},{5,4},{6,5},{7,6},{8,11},{9,8},{10,9... | collective-permute-start | bytes 294920 | tf_op jit(solution)/shard_map/ppermute | solution.py:213
  93.6 10.0 %collective-permute-start.9 = (bf16[32,3072]{1,0:T(8,128)(2,1)S(1)}, bf16[32,3072]{1,0:T(8,128)(2,1)S(1)}, u32[]{:S(2)}, u32[]{:S(2)}) collective-permute-start(bf16[32,3072]{1,0:T(8,128)(2,1)S(1)} %shard_map.116), channel_id=1, source_target_pairs={{0,4},{1,5},{2,6},{3,7},{4,8},{5,9},{6,10},{7,11},{8,12},{9,13},{1... | collective-permute-start | bytes 589832 | tf_op jit(solution)/shard_map/ppermute | solution.py:213
  95.1 11.8 %collective-permute-start.8 = (bf16[32,3072]{1,0:T(8,128)(2,1)S(1)}, bf16[32,3072]{1,0:T(8,128)(2,1)S(1)}, u32[]{:S(2)}, u32[]{:S(2)}) collective-permute-start(bf16[32,3072]{1,0:T(8,128)(2,1)S(1)} %shard_map.116), channel_id=1, source_target_pairs={{0,8},{1,9},{2,10},{3,11},{4,12},{5,13},{6,14},{7,15},{8,0},{9,1},... | collective-permute-start | bytes 589832 | tf_op jit(solution)/shard_map/ppermute | solution.py:213
  96.9 15.2 %collective-permute-start.7 = (bf16[32,3072]{1,0:T(8,128)(2,1)S(1)}, bf16[32,3072]{1,0:T(8,128)(2,1)S(1)}, u32[]{:S(2)}, u32[]{:S(2)}) collective-permute-start(bf16[32,3072]{1,0:T(8,128)(2,1)S(1)} %shard_map.116), channel_id=1, source_target_pairs={{0,12},{1,13},{2,14},{3,15},{4,0},{5,1},{6,2},{7,3},{8,4},{9,5},{1... | collective-permute-start | bytes 589832 | tf_op jit(solution)/shard_map/ppermute | solution.py:213
  99.0 22.3 %copy-start.14 = (f32[4,128]{1,0:T(4,128)S(1)}, f32[4,128]{1,0:T(4,128)}, u32[]{:S(2)}) copy-start(f32[4,128]{1,0:T(4,128)} %copy-done.13) | copy-start | bytes 6148
  99.1 16.3 %collective-permute-start.24 = (bf16[64,3072]{1,0:T(8,128)(2,1)S(1)}, bf16[64,3072]{1,0:T(8,128)(2,1)S(1)}, u32[]{:S(2)}, u32[]{:S(2)}) collective-permute-start(bf16[64,3072]{1,0:T(8,128)(2,1)S(1)} %pad_maximum_fusion.2.b0), channel_id=1, source_target_pairs={{0,4},{1,5},{2,6},{3,7},{4,8},{5,9},{6,10},{7,11},{8,12},{9,13},{1... | collective-permute-start | bytes 1179656 | tf_op jit(solution)/shard_map/ppermute | solution.py:213
  99.2 22.2 %collective-permute-start.23 = (bf16[64,3072]{1,0:T(8,128)(2,1)S(1)}, bf16[64,3072]{1,0:T(8,128)(2,1)S(1)}, u32[]{:S(2)}, u32[]{:S(2)}) collective-permute-start(bf16[64,3072]{1,0:T(8,128)(2,1)S(1)} %pad_maximum_fusion.2.b0), channel_id=1, source_target_pairs={{0,8},{1,9},{2,10},{3,11},{4,12},{5,13},{6,14},{7,15},{8,0},{9,1},... | collective-permute-start | bytes 1179656 | tf_op jit(solution)/shard_map/ppermute | solution.py:213
  103.5 17.9 %collective-permute-start.22 = (bf16[64,3072]{1,0:T(8,128)(2,1)S(1)}, bf16[64,3072]{1,0:T(8,128)(2,1)S(1)}, u32[]{:S(2)}, u32[]{:S(2)}) collective-permute-start(bf16[64,3072]{1,0:T(8,128)(2,1)S(1)} %pad_maximum_fusion.2.b0), channel_id=1, source_target_pairs={{0,12},{1,13},{2,14},{3,15},{4,0},{5,1},{6,2},{7,3},{8,4},{9,5},{1... | collective-permute-start | bytes 1179656 | tf_op jit(solution)/shard_map/ppermute | solution.py:213
  112.1 26.3 %collective-permute-start.12 = (bf16[128,3072]{1,0:T(8,128)(2,1)S(1)}, bf16[128,3072]{1,0:T(8,128)(2,1)S(1)}, u32[]{:S(2)}, u32[]{:S(2)}) collective-permute-start(bf16[128,3072]{1,0:T(8,128)(2,1)S(1)} %pad_maximum_fusion.b0), channel_id=1, source_target_pairs={{0,1},{1,2},{2,3},{3,0},{4,5},{5,6},{6,7},{7,4},{8,9},{9,10},{10,1... | collective-permute-start | bytes 2359304 | tf_op jit(solution)/shard_map/ppermute | solution.py:213
  113.7 27.8 %collective-permute-start.11 = (bf16[128,3072]{1,0:T(8,128)(2,1)S(1)}, bf16[128,3072]{1,0:T(8,128)(2,1)S(1)}, u32[]{:S(2)}, u32[]{:S(2)}) collective-permute-start(bf16[128,3072]{1,0:T(8,128)(2,1)S(1)} %pad_maximum_fusion.b0), channel_id=1, source_target_pairs={{0,2},{1,3},{2,0},{3,1},{4,6},{5,7},{6,4},{7,5},{8,10},{9,11},{10,... | collective-permute-start | bytes 2359304 | tf_op jit(solution)/shard_map/ppermute | solution.py:213
  115.4 26.1 %collective-permute-start.10 = (bf16[128,3072]{1,0:T(8,128)(2,1)S(1)}, bf16[128,3072]{1,0:T(8,128)(2,1)S(1)}, u32[]{:S(2)}, u32[]{:S(2)}) collective-permute-start(bf16[128,3072]{1,0:T(8,128)(2,1)S(1)} %pad_maximum_fusion.b0), channel_id=1, source_target_pairs={{0,3},{1,0},{2,1},{3,2},{4,7},{5,4},{6,5},{7,6},{8,11},{9,8},{10,9... | collective-permute-start | bytes 2359304 | tf_op jit(solution)/shard_map/ppermute | solution.py:213
  121.1 20.4 %slice-start = ((s8[4718592]{0:T(1024)(128)(4,1)}), s8[4194304]{0:T(1024)(128)(4,1)S(1)}, s32[]{:S(2)}) async-start(s8[4718592]{0:T(1024)(128)(4,1)} %bitcast.52), calls=%async_computation.2 | async-start | bytes 8388608
  121.4 20.1 %slice-start.1 = ((s8[4718592]{0:T(1024)(128)(4,1)}), s8[524288]{0:T(1024)(128)(4,1)S(1)}, s32[]{:S(2)}) async-start(s8[4718592]{0:T(1024)(128)(4,1)} %bitcast.52), calls=%async_computation.3 | async-start | bytes 1048576
  121.4 2.5 %copy-start.2 = (bf16[6144,384]{1,0:T(8,128)(2,1)S(1)}, bf16[6144,384]{1,0:T(8,128)(2,1)}, u32[]{:S(2)}) copy-start(bf16[6144,384]{1,0:T(8,128)(2,1)} %w_out.5) | copy-start | bytes 14155780
  124.0 2.9 %copy-start.17 = (f32[384]{0:T(512)S(1)}, f32[384]{0:T(512)}, u32[]{:S(2)}) copy-start(f32[384]{0:T(512)} %param.14) | copy-start | bytes 4612
  126.8 1.5 collective-permute-start.25
  128.4 24.6 %collective-permute-start.26 = (f32[4,8,384]{2,1,0:T(8,128)S(1)}, f32[4,8,384]{2,1,0:T(8,128)S(1)}, u32[]{:S(2)}, u32[]{:S(2)}) collective-permute-start(f32[4,8,384]{2,1,0:T(8,128)S(1)} %get-tuple-element.55), channel_id=1, source_target_pairs={{0,16},{16,32},{32,48},{48,0},{1,17},{17,33},{33,49},{49,1},{2,18}... | collective-permute-start | bytes 147464 | tf_op jit(solution)/shard_map/ppermute | solution.py:386
  129.9 23.1 %collective-permute-start.28 = (f32[4,8,384]{2,1,0:T(8,128)S(1)}, f32[4,8,384]{2,1,0:T(8,128)S(1)}, u32[]{:S(2)}, u32[]{:S(2)}) collective-permute-start(f32[4,8,384]{2,1,0:T(8,128)S(1)} %get-tuple-element.56), channel_id=1, source_target_pairs={{0,48},{16,0},{32,16},{48,32},{1,49},{17,1},{33,17},{49,33},{2,50}... | collective-permute-start | bytes 147464 | tf_op jit(solution)/shard_map/ppermute | solution.py:386
  138.4 14.6 %copy-start.16 = (f32[384]{0:T(512)S(1)}, f32[384]{0:T(512)}, u32[]{:S(2)}) copy-start(f32[384]{0:T(512)} %param.18) | copy-start | bytes 4612
  138.4 14.6 %collective-permute-start.27 = (f32[4,8,384]{2,1,0:T(8,128)S(1)}, f32[4,8,384]{2,1,0:T(8,128)S(1)}, u32[]{:S(2)}, u32[]{:S(2)}) collective-permute-start(f32[4,8,384]{2,1,0:T(8,128)S(1)} %get-tuple-element.57), channel_id=1, source_target_pairs={{0,32},{16,48},{32,0},{48,16},{1,33},{17,49},{33,1},{49,17},{2,34}... | collective-permute-start | bytes 147464 | tf_op jit(solution)/shard_map/ppermute | solution.py:386
  146.3 17.1 %all-to-all-start.1 = ((f32[32,24,128]{2,1,0:T(8,128)}), f32[32,24,128]{2,1,0:T(8,128)S(1)}, u32[]{:S(2)}, u32[]{:S(2)}) async-start(f32[32,24,128]{2,1,0:T(8,128)} %broadcast_in_dim.48), calls=%async_computation.1 | async-start | bytes 786432 | tf_op jit(solution)/shard_map/all_to_all | solution.py:367
  (4 other events, 4.7 us)

commit v3 on v0

v3 whole, which is shorter than its diff:
```python
import functools

import jax
import jax.numpy as jnp
from jax import lax
from jax.experimental import pallas as pl
from jax.experimental.pallas import tpu as pltpu
from jax.sharding import PartitionSpec as P

D = 6144
BF16 = jnp.bfloat16
F32 = jnp.float32
TILE = 512
WIDE = 1024


def gelu_exact(v):
    return v * 0.5 * (1.0 + lax.erf(v * 0.7071067811865476))


def gelu_slope(v):
    return (
        0.5 * (1.0 + lax.erf(v * 0.7071067811865476))
        + v * jnp.exp(-0.5 * v * v) * 0.3989422804014327
    )


def shift_y(k):
    return [(z * 4 + y, z * 4 + (y + k) % 4) for z in range(4) for y in range(4)]


def shift_z(k):
    return [(z * 4 + y, ((z + k) % 4) * 4 + y) for z in range(4) for y in range(4)]


def shift_row(k):
    return [(r, (r + k) % 4) for r in range(4)]


SWAP = [(0, 1), (1, 0)]


def row_order(where, swap, kinds):
    size = 128 * kinds
    bit = kinds - 1
    p = lax.broadcasted_iota(jnp.int32, (size, size), 0)
    q = lax.broadcasted_iota(jnp.int32, (size, size), 1)
    e, h, b = p & 7, (p >> 3) & bit, p >> (3 + bit)
    j, i = b >> 2, b & 3
    by, bz = (i, j) if swap else (j, i)
    block = ((where[1] + by) & 3) * 4 + ((where[2] + bz) & 3)
    return jnp.where(h * 128 + block * 8 + e == q, 1.0, 0.0).astype(BF16)


def reorder(sel, x):
    return jnp.dot(sel, x, preferred_element_type=F32).astype(BF16)


def partials(swap, where, x_f, x_g, x_r, gain, w_in, w_out, *rest):
    outs, g_rows, rest = rest[:4], rest[4], rest[5:]
    lhs_x = rest[-1]
    if swap:
        g_out, lhs_gain = rest[0], rest[1]

    @pl.when(pl.program_id(0) == 0)
    def _():
        x = jnp.concatenate([x_f[...], x_r[...]], axis=0).astype(F32)
        mean = jnp.sum(x, axis=1, keepdims=True) / x.shape[1]
        x = ((x - mean) * gain[...]).astype(BF16)
        lhs_x[...] = reorder(row_order(where, swap, 2), x)
        g_rows[...] = reorder(row_order(where, swap, 1), x_g[...])
        if swap:
            g0 = jnp.broadcast_to(gain[...], (16, gain.shape[1]))
            a = g0.astype(BF16)
            b = (g0 - a.astype(F32)).astype(BF16)
            c = (g0 - a.astype(F32) - b.astype(F32)).astype(BF16)
            lhs_gain[0:16, :] = a
            lhs_gain[16:32, :] = b
            lhs_gain[32:48, :] = c

    pre = jnp.dot(lhs_x[...], w_in[...], preferred_element_type=F32)
    grad = lax.dot_general(
        g_rows[...], w_out[...], (((1,), (1,)), ((), ())), preferred_element_type=F32
    )
    for j in range(4):
        rows = []
        for i in range(4):
            at = j * 4 + i
            rows += [pre[at * 16 : at * 16 + 16], grad[at * 8 : at * 8 + 8]]
        outs[j][...] = jnp.concatenate(rows, axis=0).astype(BF16)
    if swap:
        g = jnp.dot(lhs_gain[...], w_in[...], preferred_element_type=F32)
        g_out[...] = (g[32:40] + g[16:24]) + g[0:8]


def stage_sum(own, a, b, c, keep, *sends):
    rows = keep.shape[0]
    total = (own[...].astype(F32) + a[...].astype(F32)) + (
        b[...].astype(F32) + c[...].astype(F32)
    )
    keep[...] = total[:rows]
    for i in (1, 2, 3):
        sends[i - 1][...] = total[i * rows : (i + 1) * rows].astype(BF16)


def activate(width, keep, a, b, c, means, m2, g_all, bias, mask, out):
    total = (keep[...] + a[...].astype(F32)) + (b[...].astype(F32) + c[...].astype(F32))
    m = means[...]
    gap = m - jnp.sum(m, axis=1, keepdims=True) / 16
    var = (
        jnp.sum(m2[...], axis=1, keepdims=True)
        + width * jnp.sum(gap * gap, axis=1, keepdims=True)
    ) / D
    pre = total[:16]
    for s in range(16):
        pre = pre + gap[:, s : s + 1] * g_all[s : s + 1, :]
    pre = lax.rsqrt(var + 1e-06) * pre + bias[...]
    act = gelu_exact(pre)
    act_r = act[8:16].astype(BF16).astype(F32) * mask[...]
    grad_pre = total[16:24] * gelu_slope(pre[:8])
    out[...] = jnp.concatenate([act[:8], act_r, grad_pre], axis=0).astype(BF16)


def regroup(b0, b1, b2, b3, forget, retain):
    blocks = [b[...].astype(F32) for b in (b0, b1, b2, b3)]
    forget[...] = jnp.concatenate(
        [b[0:8] for b in blocks] + [b[16:24] for b in blocks], axis=0
    ).astype(BF16)
    retain[...] = jnp.concatenate([b[8:16] for b in blocks], axis=0).astype(BF16)


def normalise(width, where, x_own, x_other, means, m2, gain, out):
    for k, x in enumerate((x_own, x_other)):
        m, q = means[k * 128 : k * 128 + 128, :], m2[k * 128 : k * 128 + 128, :]
        mean = jnp.sum(m, axis=1, keepdims=True) / 16
        gap = m - mean
        var = (
            jnp.sum(q, axis=1, keepdims=True) + width * jnp.sum(gap * gap, axis=1, keepdims=True)
        ) / D
        normed = ((x[...].astype(F32) - mean) * lax.rsqrt(var + 1e-06) * gain[...]).astype(BF16)
        rows = jnp.dot(row_order(where, k == 1, 1), normed, preferred_element_type=F32)
        out[:, k * 128 : k * 128 + 128] = jnp.transpose(rows).astype(BF16)


def saliency_terms(where, *refs):
    blocks, (normed_t, g_own, g_other, w_in, w_out, out) = refs[:8], refs[8:]
    act = jnp.concatenate([b[0:32, :] for b in blocks], axis=0)
    grad_pre = jnp.concatenate([b[32:64, :] for b in blocks], axis=0)
    grad_y = jnp.concatenate([g_own[...], g_other[...]], axis=0)
    grad_in = jnp.dot(normed_t[...], grad_pre, preferred_element_type=F32)
    grad_out = lax.dot_general(
        act, grad_y, (((0,), (0,)), ((), ())), preferred_element_type=F32
    )
    term_in = jnp.sum(jnp.abs(w_in[...].astype(F32) * grad_in), axis=0, keepdims=True)
    prod = jnp.abs(w_out[...].astype(F32) * grad_out)
    lanes = (prod[:, 0:128] + prod[:, 128:256]) + prod[:, 256:384]
    term_out = jnp.sum(jnp.transpose(lanes), axis=0, keepdims=True)
    out[...] = term_in + term_out


def retain_product(where, *refs):
    blocks, (w_out, mine, theirs, acc) = refs[:8], refs[8:]
    t = pl.program_id(0)
    act = jnp.concatenate([b[...] for b in blocks], axis=0)
    part = jnp.dot(act, w_out[...], preferred_element_type=F32)

    @pl.when(t == 0)
    def _():
        acc[...] = part

    @pl.when(t > 0)
    def _():
        acc[...] += part

    @pl.when(t == pl.num_programs(0) - 1)
    def _():
        mine[...] = acc[0:128, :]
        for j in range(4):
            for i in range(4):
                at = 128 + (j * 4 + i) * 8
                theirs[(i * 4 + j) * 8 : (i * 4 + j) * 8 + 8, :] = acc[at : at + 8, :]


def call(kernel, where, args, outs, scratch=(), steps=6):
    def spec(shape, block, index):
        if block is None:
            return pl.BlockSpec(shape, lambda t, w: (0,) * len(shape))
        return pl.BlockSpec(block, index)

    return pl.pallas_call(
        kernel,
        grid_spec=pltpu.PrefetchScalarGridSpec(
            num_scalar_prefetch=1,
            grid=(steps,),
            in_specs=[spec(a.shape, b, i) for a, b, i in args],
            out_specs=[spec(s, b, i) for s, _, b, i in outs],
            scratch_shapes=list(scratch),
        ),
        out_shape=[jax.ShapeDtypeStruct(s, d) for s, d, _, _ in outs],
        compiler_params=pltpu.CompilerParams(vmem_limit_bytes=40 * 2**20),
        cost_estimate=pl.CostEstimate(flops=1, bytes_accessed=1, transcendentals=0),
    )(where, *[a for a, _, _ in args])


def whole(a):
    return (a, None, None)


def by_n(a, tile=TILE):
    return (a, (a.shape[0], tile), lambda t, w: (0, t))


def out_n(rows, n, dtype, tile=TILE):
    return ((rows, n), dtype, (rows, tile), lambda t, w: (0, t))


def drop_where(kernel):
    def inner(where, *refs):
        kernel(*refs)

    return inner


def permutes(parts, shift, sign=1):
    return [lax.ppermute(parts[k], "col", shift(sign * (k + 1))) for k in range(3)]


def after(value, *others):
    return lax.optimization_barrier((value, *others))[0]


def local(
    forget_tokens,
    forget_cotangent,
    forget_labels,
    retain_tokens,
    ln_gain,
    w_in,
    b_in,
    w_out,
    b_out,
    pruned,
):
    core = lax.axis_index("dp")
    row = lax.axis_index("row")
    col = lax.axis_index("col")
    y, z = col % 4, col // 4
    width = w_in.shape[0]
    half = w_in.shape[1] // 2
    steps = half // TILE
    where = jnp.stack([core, y, z]).astype(jnp.int32)
    gain = ln_gain[None, :]

    own = (forget_tokens, forget_cotangent * forget_labels[:, None].astype(BF16), retain_tokens)
    other = lax.ppermute(jnp.concatenate(own, axis=0), "dp", SWAP)

    def third(k):
        return (other, (128, width), lambda t, w: (k, 0))

    w_in_tile = (w_in, (width, TILE), lambda t, w: (0, w[0] * steps + t))
    w_out_tile = (w_out, (TILE, width), lambda t, w: (w[0] * steps + t, 0))
    parts_out = [out_n(96, half, BF16)] * 4 + [((128, width), BF16, None, None)]
    lhs = pltpu.VMEM((256, width), BF16)
    weights = [whole(gain), w_in_tile, w_out_tile]
    a_parts = call(
        functools.partial(partials, False),
        where,
        [whole(v) for v in own] + weights,
        parts_out,
        [lhs],
        steps,
    )
    a_got = permutes(a_parts[1:4], shift_y)
    b_parts = call(
        functools.partial(partials, True),
        where,
        [third(0), third(1), third(2)] + weights,
        parts_out + [out_n(8, half, F32)],
        [pltpu.VMEM((48, width), BF16), lhs],
        steps,
    )
    b_got = permutes(b_parts[1:4], shift_z)
    g_own, g_other, g_part = a_parts[4], b_parts[4], b_parts[5]

    other_s, _ = lax.optimization_barrier((other, b_parts[0]))
    tokens = jnp.stack(
        [forget_tokens, retain_tokens, other_s[:128], other_s[256:]]
    ).astype(F32)
    part_mean = jnp.sum(tokens, axis=2) / width
    centred = tokens - part_mean[..., None]
    part_m2 = jnp.sum(centred * centred, axis=2)
    share = jnp.concatenate([part_mean, part_m2, g_part[0].reshape(half // 128, 128)])
    share, _ = lax.optimization_barrier((share, a_got[0]))
    share = lax.all_to_all(
        jnp.broadcast_to(share[None], (16,) + share.shape), "col", 0, 0, tiled=True
    )
    g_all = share[:, 8:].reshape(16, half)
    stats = share[:, 0:8].transpose(1, 2, 0)
    owned = lax.dynamic_slice_in_dim(stats, (y * 4 + z) * 8, 8, 1)

    def of_set(k):
        return (owned[2 * k : 2 * k + 2].reshape(16, 16), owned[4 + 2 * k : 6 + 2 * k].reshape(16, 16))

    normed_t = call(
        functools.partial(normalise, width),
        where,
        [whole(forget_tokens), third(0), whole(stats[0:4:2].reshape(256, 16)),
         whole(stats[4:8:2].reshape(256, 16)), whole(gain)],
        [((width, 256), BF16, None, None)],
        (),
        1,
    )[0]

    b_half = lax.dynamic_slice_in_dim(b_in, core * half, half, 0)[None, :]
    ids = row * w_in.shape[1] + core * half + jnp.arange(half, dtype=jnp.int32)
    is_pruned = jnp.any(pruned[:, None] == ids[None, :], axis=0)
    keep = jnp.where(is_pruned, 0.0, 1.0)[None, :]

    def join(*lists):
        flat = lax.optimization_barrier(tuple(v for group in lists for v in group))
        at, out = 0, []
        for group in lists:
            out.append(list(flat[at : at + len(group)]))
            at += len(group)
        return out

    def wide(kernel, args, extra, outs):
        return call(
            drop_where(kernel),
            where,
            [by_n(v, WIDE) for v in args] + extra,
            [out_n(rows, half, kind, WIDE) for rows, kind in outs],
            steps=half // WIDE,
        )

    def sums_of(parts, got):
        return wide(stage_sum, [parts[0]] + got, [], [(24, F32)] + [(24, BF16)] * 3)

    def block_of(k, sums, back):
        extra = [whole(v) for v in of_set(k)] + [by_n(v, WIDE) for v in (g_all, b_half, keep)]
        kernel = functools.partial(activate, width)
        return wide(kernel, [sums[0]] + back, extra, [(24, BF16)])[0]

    def regrouped(block, near):
        return wide(regroup, [block] + near, [], [(64, BF16), (32, BF16)])

    a_got, b_got = join(a_got, b_got)
    a_sums, b_sums = sums_of(a_parts, a_got), sums_of(b_parts, b_got)
    a_back, b_back = join(permutes(a_sums[1:], shift_z), permutes(b_sums[1:], shift_y))
    a_block, b_block = block_of(0, a_sums, a_back), block_of(1, b_sums, b_back)
    a_near, b_near = join(
        permutes([a_block] * 3, shift_z, -1), permutes([b_block] * 3, shift_y, -1)
    )
    a_forget, a_retain = regrouped(a_block, a_near)
    b_forget, b_retain = regrouped(b_block, b_near)
    a_far, b_far = permutes([a_forget] * 3, shift_y, -1), permutes([b_forget] * 3, shift_z, -1)
    a_forget, b_forget = [a_forget] + a_far, [b_forget] + b_far
    a_retain, b_retain, _ = lax.optimization_barrier((a_retain, b_retain, a_far[0]))
    a_retain = [a_retain] + permutes([a_retain] * 3, shift_y, -1)
    b_retain = [b_retain] + permutes([b_retain] * 3, shift_z, -1)

    terms = call(
        saliency_terms,
        where,
        [by_n(v) for v in a_forget + b_forget]
        + [whole(normed_t), whole(g_own), whole(g_other), w_in_tile, w_out_tile],
        [out_n(1, half, F32)],
        (),
        steps,
    )[0]
    terms = jnp.broadcast_to(terms.reshape(1, half // 128, 128), (32, half // 128, 128))
    terms = lax.all_to_all(terms, ("dp", "col"), 0, 0, tiled=True)
    saliency = jnp.sum(terms.reshape(2, 16, half), axis=1).reshape(2 * half) / D

    mine, theirs = call(
        retain_product,
        where,
        [by_n(v) for v in a_retain + b_retain] + [w_out_tile],
        [((128, width), F32, None, None)] * 2,
        [pltpu.VMEM((256, width), F32)],
        steps,
    )
    mine = (mine + lax.ppermute(theirs, "dp", SWAP)).reshape(4, 4, 8, width)

    def for_row(r):
        return lax.dynamic_index_in_dim(mine, (r - y) % 4, 0, keepdims=False)

    total = for_row(row)
    for k in (1, 2, 3):
        total = total + lax.ppermute(for_row(row + k), "row", shift_row(k))
    retain_out = (total + b_out).astype(BF16)
    retain_out = lax.dynamic_slice_in_dim(
        jnp.concatenate([retain_out, retain_out], axis=0), (4 - z) % 4, 4, 0
    ).reshape(32, width)
    return (saliency, retain_out)


def solution(mesh):
    in_specs = (
        P("dp", "col"),
        P("dp", "col"),
        P("dp"),
        P("dp", "col"),
        P("col"),
        P("col", "row"),
        P("row"),
        P("row", "col"),
        P("col"),
        P("row"),
    )
    out_specs = (P("row"), P(("dp", "row"), "col"))
    return jax.shard_map(local, mesh=mesh, in_specs=in_specs, out_specs=out_specs, check_vma=False)
```

time: 551 us -> 183 us (0.33)
  waiting for transfers between devices: 277 us -> 35.1 us
  blocking collectives: 206 us -> 0 us
  starting transfers between devices: 0.29 us -> 77.6 us
  Pallas kernels: 0 us -> 32.1 us
  matrix products: 23.8 us -> 0 us
  local copies, waits for them, and re-layouts: 12.8 us -> 31.5 us
  between operations: 14.2 us -> 1.05 us
  other arithmetic: 14 us -> 4.2 us
    psum x3 -> x0, blocking collectives: 206 us -> none  [the longest x1 129 us: local(): saliency = lax.psum(terms, ('dp', 'col')) / D]
    reduce_scatter x4 -> x0, waiting for transfers between devices: 109 us -> none  [the longest x1 72.4 us: local(): lax.psum_scatter(partial_pre, 'col', scatter_dimension=1, tiled=True)]
    all_gather x2 -> x0, waiting for transfers between devices: 93.9 us -> none  [the longest x1 51.7 us: local(): act_all = lax.all_gather(act_share, 'col', axis=1, tiled=True)]
    unnamed x8 -> x0, waiting for transfers between devices: 74.5 us -> none
    ppermute x0 -> x35, starting transfers between devices: none -> 53.8 us  [the longest x30 48.9 us: permutes(): lax.ppermute(parts[k], 'col', shift(sign * (k + 1)))]
    pallas_call x0 -> x11, Pallas kernels: none -> 32.1 us  [call(): pl.pallas_call(kernel, grid_spec=pltpu.PrefetchScalarGridSpec(num_scalar_...]
    ppermute x0 -> x35, waiting for transfers between devices: none -> 31.9 us  [the longest x30 28.1 us: permutes(): lax.ppermute(parts[k], 'col', shift(sign * (k + 1)))]
    dot_general x5 -> x0, matrix products: 23.8 us -> none  [the longest x2 8.6 us: outer_rows(): lax.dot_general(left, right, (((0,), (0,)), ((), ())), preferred_element_...]
  transfers between devices with their start and end apart: 7 -> 37, of which waited for: 7 -> 12; matrix products, arithmetic and copies ran while one was open for 6% -> 3% of each run, Pallas kernels for 0% -> 16%
where the time goes in v3:
time: 183 us; the launch traced here: 182 us
  starting transfers between devices  77.6 us (42%)
  waiting for transfers between devices  35.1 us (19%)
  Pallas kernels  32.1 us (18%)
  local copies, waits for them, and re-layouts  31.5 us (17%)
  other arithmetic  4.2 us (2%)
    ppermute x30, starting transfers between devices, permutes(): lax.ppermute(parts[k], 'col', shift(sign * (k + 1)))  48.9 us
    pallas_call x11, Pallas kernels, call(): pl.pallas_call(kernel, grid_spec=pltpu.PrefetchScalarGridSpec(num_scalar_...  32.1 us
    ppermute x30, waiting for transfers between devices, permutes(): lax.ppermute(parts[k], 'col', shift(sign * (k + 1)))  28.1 us
    unnamed x54, local copies, waits for them, and re-layouts  26.7 us
    all_to_all x1, starting transfers between devices, local(): lax.all_to_all(jnp.broadcast_to(share[None], (16,) + share.shape), 'col',...  15.3 us
    all_to_all x1, starting transfers between devices, local(): terms = lax.all_to_all(terms, ('dp', 'col'), 0, 0, tiled=True)  8.42 us
    ppermute x3, starting transfers between devices, local(): total = total + lax.ppermute(for_row(row + k), 'row', shift_row(k))  4.52 us
    ppermute x3, waiting for transfers between devices, local(): total = total + lax.ppermute(for_row(row + k), 'row', shift_row(k))  3.8 us
  transfers between devices with their start and end apart: 37, of which 12 were waited for; matrix products, arithmetic and copies ran while one was open for 3% of the time, Pallas kernels for 16%

profile of v3, /device:TPU:0, one launch (start us, length us, event | category | flops | bytes accessed | tf_op | source)
XLA Modules:
  0.0 181.5 jit_solution(7871481803329715412)
XLA Ops:
  4.1 2.3 %copy-done = bf16[6144,384]{1,0:T(8,128)(2,1)S(1)} copy-done((bf16[6144,384]{1,0:T(8,128)(2,1)S(1)}, bf16[6144,384]{1,0:T(8,128)(2,1)}, u32[]{:S(2)}) %copy-start) | copy-done | bytes 4718616
  6.5 2.3 %copy-done.4 = bf16[384,6144]{1,0:T(8,128)(2,1)S(1)} copy-done((bf16[384,6144]{1,0:T(8,128)(2,1)S(1)}, bf16[384,6144]{1,0:T(8,128)(2,1)}, u32[]{:S(2)}) %copy-start.4) | copy-done | bytes 4718616
  10.6 4.9 %shard_map.113 = (bf16[96,3072]{1,0:T(8,128)(2,1)S(1)}, bf16[96,3072]{1,0:T(8,128)(2,1)}, bf16[96,3072]{1,0:T(8,128)(2,1)}, bf16[96,3072]{1,0:T(8,128)(2,1)}, bf16[128,384]{1,0:T(8,128)(2,1)S(1)}) custom-call(s32[3]{0:T(128)S(1)} %pad_add_fusion.where, bf16[128,384]{1,0:T(8,128)(2,1)S(1)} %copy-done.7, bf16[128,384]{1,0:T(8,128)(2,1)S(1)} %broadcast_multiply_fusion.x_g, ...), custom_call_target="tpu_custom_call" | custom-call | flops 1 | bytes 1 | tf_op jit(solution)/shard_map/pallas_call | solution.py:190
  16.1 1.7 collective-permute-start
  17.7 2.9 %collective-permute-start.1 = (bf16[96,3072]{1,0:T(8,128)(2,1)}, bf16[96,3072]{1,0:T(8,128)(2,1)S(1)}, u32[]{:S(2)}, u32[]{:S(2)}) collective-permute-start(bf16[96,3072]{1,0:T(8,128)(2,1)} %get-tuple-element.51), channel_id=1, source_target_pairs={{0,2},{1,3},{2,0},{3,1},{4,6},{5,7},{6,4},{7,5},{8,10},{9,11},{10,... | collective-permute-start | bytes 1769480 | tf_op jit(solution)/shard_map/ppermute | solution.py:225
  20.6 1.3 collective-permute-start.2
  22.0 2.3 %copy-done.1 = bf16[6144,384]{1,0:T(8,128)(2,1)S(1)} copy-done((bf16[6144,384]{1,0:T(8,128)(2,1)S(1)}, bf16[6144,384]{1,0:T(8,128)(2,1)}, u32[]{:S(2)}) %copy-start.1) | copy-done | bytes 4718616
  24.3 2.3 %copy-done.5 = bf16[384,6144]{1,0:T(8,128)(2,1)S(1)} copy-done((bf16[384,6144]{1,0:T(8,128)(2,1)S(1)}, bf16[384,6144]{1,0:T(8,128)(2,1)}, u32[]{:S(2)}) %copy-start.5) | copy-done | bytes 4718616
  26.7 5.1 %shard_map.114 = (bf16[96,3072]{1,0:T(8,128)(2,1)S(1)}, bf16[96,3072]{1,0:T(8,128)(2,1)}, bf16[96,3072]{1,0:T(8,128)(2,1)}, bf16[96,3072]{1,0:T(8,128)(2,1)}, bf...) custom-call(s32[3]{0:T(128)S(1)} %pad_add_fusion.where, ...), custom_call_target="tpu_custom_call" | custom-call | flops 1 | bytes 1 | tf_op jit(solution)/shard_map/pallas_call | solution.py:190
  31.8 1.9 %collective-permute-start.4 = (bf16[96,3072]{1,0:T(8,128)(2,1)}, bf16[96,3072]{1,0:T(8,128)(2,1)}, u32[]{:S(2)}, u32[]{:S(2)}) collective-permute-start(bf16[96,3072]{1,0:T(8,128)(2,1)} %get-tuple-element.53), channel_id=1, source_target_pairs={{0,4},{1,5},{2,6},{3,7},{4,8},{5,9},{6,10},{7,11},{8,12},{9,13},{1... | collective-permute-start | bytes 1769480 | tf_op jit(solution)/shard_map/ppermute | solution.py:225
  33.7 3.6 %collective-permute-start.5 = (bf16[96,3072]{1,0:T(8,128)(2,1)}, bf16[96,3072]{1,0:T(8,128)(2,1)}, u32[]{:S(2)}, u32[]{:S(2)}) collective-permute-start(bf16[96,3072]{1,0:T(8,128)(2,1)} %get-tuple-element.54), channel_id=1, source_target_pairs={{0,8},{1,9},{2,10},{3,11},{4,12},{5,13},{6,14},{7,15},{8,0},{9,1},... | collective-permute-start | bytes 1769480 | tf_op jit(solution)/shard_map/ppermute | solution.py:225
  37.5 1.1 collective-permute-start.6
  39.6 15.3 %all-to-all-start = ((f32[16,32,128]{2,1,0:T(8,128)}), f32[16,32,128]{2,1,0:T(8,128)}, u32[]{:S(2)}, u32[]{:S(2)}) async-start(f32[16,32,128]{2,1,0:T(8,128)} %broadcast_in_dim.34), calls=%async_computation | async-start | bytes 524288 | tf_op jit(solution)/shard_map/all_to_all | solution.py:294
  55.4 10.2 %collective-permute-done.5.refs_2_ = bf16[96,3072]{1,0:T(8,128)(2,1)} collective-permute-done((bf16[96,3072]{1,0:T(8,128)(2,1)}, bf16[96,3072]{1,0:T(8,128)(2,1)}, u32[]{:S(2)}, u32[]{:S(2)}) %collective-permute-start.5) | collective-permute-done | bytes 589856 | tf_op jit(solution)/shard_map/ppermute | solution.py:225
  65.5 2.1 %shard_map.115 = (f32[24,3072]{1,0:T(8,128)S(1)}, bf16[24,3072]{1,0:T(8,128)(2,1)}, bf16[24,3072]{1,0:T(8,128)(2,1)S(1)}, bf16[24,3072]{1,0:T(8,128)(2,1)S(1)}) custom-call(s32[3]{0:T(128)S(1)} %pad_add_fusion.where, bf16[96,3072]{1,0:T(8,128)(2,1)S(1)} %get-tuple-element.49.refs_0_, bf16[96,3072]{1,0:T(8,128)(2,1)S(1)} %collective-permute-done.refs_1_, ...), custom_call_target="tpu_custom_call" | custom-call | flops 1 | bytes 1 | tf_op jit(solution)/shard_map/pallas_call | solution.py:190
  69.7 1.5 collective-permute-start.7
  72.1 2.1 %collective-permute-start.8 = (bf16[24,3072]{1,0:T(8,128)(2,1)}, bf16[24,3072]{1,0:T(8,128)(2,1)S(1)}, u32[]{:S(2)}, u32[]{:S(2)}) collective-permute-start(bf16[24,3072]{1,0:T(8,128)(2,1)} %copy-done.22), channel_id=1, source_target_pairs={{0,8},{1,9},{2,10},{3,11},{4,12},{5,13},{6,14},{7,15},{8,0},{9,1},... | collective-permute-start | bytes 442376 | tf_op jit(solution)/shard_map/ppermute | solution.py:225
  74.2 1.4 collective-permute-start.9
  75.6 3.1 %shard_map.116 = (f32[24,3072]{1,0:T(8,128)S(1)}, bf16[24,3072]{1,0:T(8,128)(2,1)S(1)}, bf16[24,3072]{1,0:T(8,128)(2,1)S(1)}, bf16[24,3072]{1,0:T(8,128)(2,1)S(1)}) custom-call(s32[3]{0:T(128)S(1)} %pad_add_fusion.where, bf16[96,3072]{1,0:T(8,128)(2,1)S(1)} %get-tuple-element.63.refs_0_, bf16[96,3072]{1,0:T(8,128)(2,1)} %collective-permute-done.4.refs_1_, ...), custom_call_target="tpu_custom_call" | custom-call | flops 1 | bytes 1 | tf_op jit(solution)/shard_map/pallas_call | solution.py:190
  79.4 1.1 collective-permute-start.11
  80.5 1.7 collective-permute-start.12
  83.3 4.0 %collective-permute-done.10.refs_1_ = bf16[24,3072]{1,0:T(8,128)(2,1)S(1)} collective-permute-done((bf16[24,3072]{1,0:T(8,128)(2,1)S(1)}, bf16[24,3072]{1,0:T(8,128)(2,1)S(1)}, u32[]{:S(2)}, u32[]{:S(2)}) %collective-permute-start.10) | collective-permute-done | bytes 147488 | tf_op jit(solution)/shard_map/ppermute | solution.py:225
  89.0 1.6 shard_map.117.refs_0_
  90.6 1.2 collective-permute-start.13
  91.9 2.2 %collective-permute-start.14 = (bf16[24,3072]{1,0:T(8,128)(2,1)S(1)}, bf16[24,3072]{1,0:T(8,128)(2,1)S(1)}, u32[]{:S(2)}, u32[]{:S(2)}) collective-permute-start(bf16[24,3072]{1,0:T(8,128)(2,1)S(1)} %shard_map.117.refs_0_), channel_id=1, source_target_pairs={{0,8},{1,9},{2,10},{3,11},{4,12},{5,13},{6,14},{7,15},{8,0},{9,1},... | collective-permute-start | bytes 442376 | tf_op jit(solution)/shard_map/ppermute | solution.py:225
  94.1 1.6 shard_map.118.refs_0_
  95.8 2.6 %collective-permute-start.16 = (bf16[24,3072]{1,0:T(8,128)(2,1)S(1)}, bf16[24,3072]{1,0:T(8,128)(2,1)S(1)}, u32[]{:S(2)}, u32[]{:S(2)}) collective-permute-start(bf16[24,3072]{1,0:T(8,128)(2,1)S(1)} %shard_map.118.refs_0_), channel_id=1, source_target_pairs={{0,3},{1,0},{2,1},{3,2},{4,7},{5,4},{6,5},{7,6},{8,11},{9,8},{10,9... | collective-permute-start | bytes 442376 | tf_op jit(solution)/shard_map/ppermute | solution.py:225
  99.3 1.1 collective-permute-done.15.refs_3_
  100.5 3.3 %collective-permute-done.16.refs_1_ = bf16[24,3072]{1,0:T(8,128)(2,1)S(1)} collective-permute-done((bf16[24,3072]{1,0:T(8,128)(2,1)S(1)}, bf16[24,3072]{1,0:T(8,128)(2,1)S(1)}, u32[]{:S(2)}, u32[]{:S(2)}) %collective-permute-start.16) | collective-permute-done | bytes 147488 | tf_op jit(solution)/shard_map/ppermute | solution.py:225
  103.8 2.2 %collective-permute-done.17.refs_2_ = bf16[24,3072]{1,0:T(8,128)(2,1)S(1)} collective-permute-done((bf16[24,3072]{1,0:T(8,128)(2,1)S(1)}, bf16[24,3072]{1,0:T(8,128)(2,1)S(1)}, u32[]{:S(2)}, u32[]{:S(2)}) %collective-permute-start.17) | collective-permute-done | bytes 147488 | tf_op jit(solution)/shard_map/ppermute | solution.py:225
  105.9 1.2 collective-permute-done.18.refs_3_
  107.1 1.9 %shard_map.119 = (bf16[64,3072]{1,0:T(8,128)(2,1)S(1)}, bf16[32,3072]{1,0:T(8,128)(2,1)}) custom-call(s32[3]{0:T(128)S(1)} %pad_add_fusion.where, bf16[24,3072]{1,0:T(8,128)(2,1)S(1)} %shard_map.117.refs_0_, bf16[24,3072]{1,0:T(8,128)(2,1)S(1)} %collective-permute-done.13.refs_1_, bf16[24,3072]{1,0:T(8,128)(2,1)S(1)} %collective-permute-done.14.refs_2_, ...), custom_call_target="tpu_custom_call" | custom-call | flops 1 | bytes 1 | tf_op jit(solution)/shard_map/pallas_call | solution.py:190
  111.1 1.9 %shard_map.120 = (bf16[64,3072]{1,0:T(8,128)(2,1)S(1)}, bf16[32,3072]{1,0:T(8,128)(2,1)}) custom-call(s32[3]{0:T(128)S(1)} %pad_add_fusion.where, bf16[24,3072]{1,0:T(8,128)(2,1)S(1)} %shard_map.118.refs_0_, bf16[24,3072]{1,0:T(8,128)(2,1)S(1)} %collective-permute-done.16.refs_1_, bf16[24,3072]{1,0:T(8,128)(2,1)S(1)} %collective-permute-done.17.refs_2_, ...), custom_call_target="tpu_custom_call" | custom-call | flops 1 | bytes 1 | tf_op jit(solution)/shard_map/pallas_call | solution.py:190
  113.0 3.0 %collective-permute-start.22 = (bf16[64,3072]{1,0:T(8,128)(2,1)S(1)}, bf16[64,3072]{1,0:T(8,128)(2,1)S(1)}, u32[]{:S(2)}, u32[]{:S(2)}) collective-permute-start(bf16[64,3072]{1,0:T(8,128)(2,1)S(1)} %get-tuple-element.87.refs_4_), channel_id=1, source_target_pairs={{0,12},{1,13},{2,14},{3,15},{4,0},{5,1},{6,2},{7,3},{8,4},{9,5},{1... | collective-permute-start | bytes 1179656 | tf_op jit(solution)/shard_map/ppermute | solution.py:225
  115.9 5.2 %collective-permute-done.19.refs_1_ = bf16[64,3072]{1,0:T(8,128)(2,1)S(1)} collective-permute-done((bf16[64,3072]{1,0:T(8,128)(2,1)S(1)}, bf16[64,3072]{1,0:T(8,128)(2,1)S(1)}, u32[]{:S(2)}, u32[]{:S(2)}) %collective-permute-start.19) | collective-permute-done | bytes 393248 | tf_op jit(solution)/shard_map/ppermute | solution.py:225
  121.1 4.8 %collective-permute-start.24 = (bf16[64,3072]{1,0:T(8,128)(2,1)S(1)}, bf16[64,3072]{1,0:T(8,128)(2,1)S(1)}, u32[]{:S(2)}, u32[]{:S(2)}) collective-permute-start(bf16[64,3072]{1,0:T(8,128)(2,1)S(1)} %get-tuple-element.87.refs_4_), channel_id=1, source_target_pairs={{0,4},{1,5},{2,6},{3,7},{4,8},{5,9},{6,10},{7,11},{8,12},{9,13},{1... | collective-permute-start | bytes 1179656 | tf_op jit(solution)/shard_map/ppermute | solution.py:225
  125.9 5.5 %collective-permute-start.25 = (bf16[32,3072]{1,0:T(8,128)(2,1)}, bf16[32,3072]{1,0:T(8,128)(2,1)S(1)}, u32[]{:S(2)}, u32[]{:S(2)}) collective-permute-start(bf16[32,3072]{1,0:T(8,128)(2,1)} %get-tuple-element.92.refs_0_), channel_id=1, source_target_pairs={{0,3},{1,0},{2,1},{3,2},{4,7},{5,4},{6,5},{7,6},{8,11},{9,8},{10,9... | collective-permute-start | bytes 589832 | tf_op jit(solution)/shard_map/ppermute | solution.py:225
  131.4 1.5 collective-permute-start.27
  132.9 3.7 %collective-permute-start.28 = (bf16[32,3072]{1,0:T(8,128)(2,1)}, bf16[32,3072]{1,0:T(8,128)(2,1)}, u32[]{:S(2)}, u32[]{:S(2)}) collective-permute-start(bf16[32,3072]{1,0:T(8,128)(2,1)} %get-tuple-element.93.refs_4_), channel_id=1, source_target_pairs={{0,12},{1,13},{2,14},{3,15},{4,0},{5,1},{6,2},{7,3},{8,4},{9,5},{1... | collective-permute-start | bytes 589832 | tf_op jit(solution)/shard_map/ppermute | solution.py:225
  140.2 2.3 %copy-done.2 = bf16[6144,384]{1,0:T(8,128)(2,1)S(1)} copy-done((bf16[6144,384]{1,0:T(8,128)(2,1)S(1)}, bf16[6144,384]{1,0:T(8,128)(2,1)}, u32[]{:S(2)}) %copy-start.2) | copy-done | bytes 4718616
  142.6 2.3 %copy-done.6 = bf16[384,6144]{1,0:T(8,128)(2,1)S(1)} copy-done((bf16[384,6144]{1,0:T(8,128)(2,1)S(1)}, bf16[384,6144]{1,0:T(8,128)(2,1)}, u32[]{:S(2)}) %copy-start.6) | copy-done | bytes 4718616
  147.7 4.2 %shard_map.122 = f32[1,3072]{1,0:T(1,128)S(1)} custom-call(s32[3]{0:T(128)S(1)} %pad_add_fusion.where, bf16[64,3072]{1,0:T(8,128)(2,1)S(1)} %get-tuple-element.83.refs_0_, bf16[64,3072]{1,0:T(8,128)(2,1)S(1)} %collective-permute-done.19.refs_1_, bf16[64,3072]{1,0:T(8,128)(2,1)S(1)} %collective-permute-done.20.refs_2_, ...), custom_call_target="tpu_custom_call" | custom-call | flops 1 | bytes 1 | tf_op jit(solution)/shard_map/pallas_call | solution.py:190
  152.7 8.4 %all-to-all-start.1 = ((f32[32,24,128]{2,1,0:T(8,128)}), f32[32,24,128]{2,1,0:T(8,128)S(1)}, u32[]{:S(2)}, u32[]{:S(2)}) async-start(f32[32,24,128]{2,1,0:T(8,128)} %broadcast_in_dim.39), calls=%async_computation.1 | async-start | bytes 786432 | tf_op jit(solution)/shard_map/all_to_all | solution.py:372
  161.2 2.3 %copy-done.3 = bf16[6144,384]{1,0:T(8,128)(2,1)S(1)} copy-done((bf16[6144,384]{1,0:T(8,128)(2,1)S(1)}, bf16[6144,384]{1,0:T(8,128)(2,1)}, u32[]{:S(2)}) %copy-start.3) | copy-done | bytes 4718616
  163.5 4.6 %shard_map.123 = (f32[128,384]{1,0:T(8,128)S(1)}, f32[128,384]{1,0:T(8,128)S(1)}) custom-call(s32[3]{0:T(128)S(1)} %pad_add_fusion.where, bf16[32,3072]{1,0:T(8,128)(2,1)} %get-tuple-element.92.refs_0_, bf16[32,3072]{1,0:T(8,128)(2,1)S(1)} %copy-done.16, bf16[32,3072]{1,0:T(8,128)(2,1)} %collective-permute-done.26.refs_2_, ...), custom_call_target="tpu_custom_call" | custom-call | flops 1 | bytes 1 | tf_op jit(solution)/shard_map/pallas_call | solution.py:190
  168.5 3.1 %all-to-all-done.1 = f32[32,24,128]{2,1,0:T(8,128)S(1)} async-done(((f32[32,24,128]{2,1,0:T(8,128)}), f32[32,24,128]{2,1,0:T(8,128)S(1)}, u32[]{:S(2)}, u32[]{:S(2)}) %all-to-all-start.1) | async-done | bytes 393248 | tf_op jit(solution)/shard_map/all_to_all | solution.py:372
  171.9 2.8 %collective-permute-start.34 = (f32[4,8,384]{2,1,0:T(8,128)S(1)}, f32[4,8,384]{2,1,0:T(8,128)S(1)}, u32[]{:S(2)}, u32[]{:S(2)}) collective-permute-start(f32[4,8,384]{2,1,0:T(8,128)S(1)} %get-tuple-element.101), channel_id=1, source_target_pairs={{0,48},{16,0},{32,16},{48,32},{1,49},{17,1},{33,17},{49,33},{2,50}... | collective-permute-start | bytes 147464 | tf_op jit(solution)/shard_map/ppermute | solution.py:390
  177.0 3.3 %collective-permute-done.33 = f32[4,8,384]{2,1,0:T(8,128)S(1)} collective-permute-done((f32[4,8,384]{2,1,0:T(8,128)S(1)}, f32[4,8,384]{2,1,0:T(8,128)S(1)}, u32[]{:S(2)}, u32[]{:S(2)}) %collective-permute-start.33) | collective-permute-done | bytes 49184 | tf_op jit(solution)/shard_map/ppermute | solution.py:390
  (127 shorter events, 28.4 us)
Async XLA Ops:
  3.2 18.8 %collective-permute-start.3 = (bf16[384,384]{1,0:T(8,128)(2,1)S(1)}, bf16[384,384]{1,0:T(8,128)(2,1)S(1)}, u32[]{:S(2)}, u32[]{:S(2)}) collective-permute-start(bf16[384,384]{1,0:T(8,128)(2,1)S(1)} %pad_maximum_fusion.1), channel_id=1, source_target_pairs={{0,64},{64,0},{1,65},{65,1},{2,66},{66,2},{3,67},{67,3},{4,68},{68... | collective-permute-start | bytes 884744 | tf_op jit(solution)/shard_map/ppermute | solution.py:255
  4.1 2.3 %copy-start = (bf16[6144,384]{1,0:T(8,128)(2,1)S(1)}, bf16[6144,384]{1,0:T(8,128)(2,1)}, u32[]{:S(2)}) copy-start(bf16[6144,384]{1,0:T(8,128)(2,1)} %refs_8_.1) | copy-start | bytes 14155780
  16.1 21.4 %collective-permute-start = (bf16[96,3072]{1,0:T(8,128)(2,1)}, bf16[96,3072]{1,0:T(8,128)(2,1)S(1)}, u32[]{:S(2)}, u32[]{:S(2)}) collective-permute-start(bf16[96,3072]{1,0:T(8,128)(2,1)} %get-tuple-element.50), channel_id=1, source_target_pairs={{0,1},{1,2},{2,3},{3,0},{4,5},{5,6},{6,7},{7,4},{8,9},{9,10},{10,1... | collective-permute-start | bytes 1769480 | tf_op jit(solution)/shard_map/ppermute | solution.py:225
  17.7 37.6 %collective-permute-start.1 = (bf16[96,3072]{1,0:T(8,128)(2,1)}, bf16[96,3072]{1,0:T(8,128)(2,1)S(1)}, u32[]{:S(2)}, u32[]{:S(2)}) collective-permute-start(bf16[96,3072]{1,0:T(8,128)(2,1)} %get-tuple-element.51), channel_id=1, source_target_pairs={{0,2},{1,3},{2,0},{3,1},{4,6},{5,7},{6,4},{7,5},{8,10},{9,11},{10,... | collective-permute-start | bytes 1769480 | tf_op jit(solution)/shard_map/ppermute | solution.py:225
  20.6 34.7 %collective-permute-start.2 = (bf16[96,3072]{1,0:T(8,128)(2,1)}, bf16[96,3072]{1,0:T(8,128)(2,1)S(1)}, u32[]{:S(2)}, u32[]{:S(2)}) collective-permute-start(bf16[96,3072]{1,0:T(8,128)(2,1)} %get-tuple-element.52), channel_id=1, source_target_pairs={{0,3},{1,0},{2,1},{3,2},{4,7},{5,4},{6,5},{7,6},{8,11},{9,8},{10,9... | collective-permute-start | bytes 1769480 | tf_op jit(solution)/shard_map/ppermute | solution.py:225
  22.0 2.3 %copy-start.1 = (bf16[6144,384]{1,0:T(8,128)(2,1)S(1)}, bf16[6144,384]{1,0:T(8,128)(2,1)}, u32[]{:S(2)}) copy-start(bf16[6144,384]{1,0:T(8,128)(2,1)} %refs_8_.1) | copy-start | bytes 14155780
  26.7 10.6 %copy-start.8 = (bf16[128,384]{1,0:T(8,128)(2,1)S(1)}, bf16[128,384]{1,0:T(8,128)(2,1)}, u32[]{:S(2)}) copy-start(bf16[128,384]{1,0:T(8,128)(2,1)} %x_own.1) | copy-start | bytes 294916
  26.7 10.6 %copy-start.10 = (bf16[128,384]{1,0:T(8,128)(2,1)S(1)}, bf16[128,384]{1,0:T(8,128)(2,1)}, u32[]{:S(2)}) copy-start(bf16[128,384]{1,0:T(8,128)(2,1)} %x_r.1) | copy-start | bytes 294916
  26.7 28.3 %copy-start.25 = (s32[128]{0:T(128)S(1)}, s32[128]{0:T(128)}, u32[]{:S(2)}) copy-start(s32[128]{0:T(128)} %param.19) | copy-start | bytes 1540
  26.7 28.6 %copy-start.23 = (f32[6144]{0:T(1024)S(1)}, f32[6144]{0:T(1024)}, u32[]{:S(2)}) copy-start(f32[6144]{0:T(1024)} %param.16) | copy-start | bytes 73732
  31.8 7.1 %copy-start.19 = (bf16[128,384]{1,0:T(8,128)(2,1)}, bf16[128,384]{1,0:T(8,128)(2,1)S(1)}, u32[]{:S(2)}) copy-start(bf16[128,384]{1,0:T(8,128)(2,1)S(1)} %get-tuple-element.89.refs_10_) | copy-start | bytes 294916
  31.8 23.6 %collective-permute-start.4 = (bf16[96,3072]{1,0:T(8,128)(2,1)}, bf16[96,3072]{1,0:T(8,128)(2,1)}, u32[]{:S(2)}, u32[]{:S(2)}) collective-permute-start(bf16[96,3072]{1,0:T(8,128)(2,1)} %get-tuple-element.53), channel_id=1, source_target_pairs={{0,4},{1,5},{2,6},{3,7},{4,8},{5,9},{6,10},{7,11},{8,12},{9,13},{1... | collective-permute-start | bytes 1769480 | tf_op jit(solution)/shard_map/ppermute | solution.py:225
  33.7 31.8 %collective-permute-start.5 = (bf16[96,3072]{1,0:T(8,128)(2,1)}, bf16[96,3072]{1,0:T(8,128)(2,1)}, u32[]{:S(2)}, u32[]{:S(2)}) collective-permute-start(bf16[96,3072]{1,0:T(8,128)(2,1)} %get-tuple-element.54), channel_id=1, source_target_pairs={{0,8},{1,9},{2,10},{3,11},{4,12},{5,13},{6,14},{7,15},{8,0},{9,1},... | collective-permute-start | bytes 1769480 | tf_op jit(solution)/shard_map/ppermute | solution.py:225
  37.5 28.0 %collective-permute-start.6 = (bf16[96,3072]{1,0:T(8,128)(2,1)}, bf16[96,3072]{1,0:T(8,128)(2,1)}, u32[]{:S(2)}, u32[]{:S(2)}) collective-permute-start(bf16[96,3072]{1,0:T(8,128)(2,1)} %get-tuple-element.55), channel_id=1, source_target_pairs={{0,12},{1,13},{2,14},{3,15},{4,0},{5,1},{6,2},{7,3},{8,4},{9,5},{1... | collective-permute-start | bytes 1769480 | tf_op jit(solution)/shard_map/ppermute | solution.py:225
  39.6 31.6 %all-to-all-start = ((f32[16,32,128]{2,1,0:T(8,128)}), f32[16,32,128]{2,1,0:T(8,128)}, u32[]{:S(2)}, u32[]{:S(2)}) async-start(f32[16,32,128]{2,1,0:T(8,128)} %broadcast_in_dim.34), calls=%async_computation | async-start | bytes 524288 | tf_op jit(solution)/shard_map/all_to_all | solution.py:294
  69.7 10.8 %collective-permute-start.7 = (bf16[24,3072]{1,0:T(8,128)(2,1)}, bf16[24,3072]{1,0:T(8,128)(2,1)S(1)}, u32[]{:S(2)}, u32[]{:S(2)}) collective-permute-start(bf16[24,3072]{1,0:T(8,128)(2,1)} %get-tuple-element.60), channel_id=1, source_target_pairs={{0,4},{1,5},{2,6},{3,7},{4,8},{5,9},{6,10},{7,11},{8,12},{9,13},{1... | collective-permute-start | bytes 442376 | tf_op jit(solution)/shard_map/ppermute | solution.py:225
  72.1 11.2 %collective-permute-start.8 = (bf16[24,3072]{1,0:T(8,128)(2,1)}, bf16[24,3072]{1,0:T(8,128)(2,1)S(1)}, u32[]{:S(2)}, u32[]{:S(2)}) collective-permute-start(bf16[24,3072]{1,0:T(8,128)(2,1)} %copy-done.22), channel_id=1, source_target_pairs={{0,8},{1,9},{2,10},{3,11},{4,12},{5,13},{6,14},{7,15},{8,0},{9,1},... | collective-permute-start | bytes 442376 | tf_op jit(solution)/shard_map/ppermute | solution.py:225
  74.2 9.1 %collective-permute-start.9 = (bf16[24,3072]{1,0:T(8,128)(2,1)}, bf16[24,3072]{1,0:T(8,128)(2,1)S(1)}, u32[]{:S(2)}, u32[]{:S(2)}) collective-permute-start(bf16[24,3072]{1,0:T(8,128)(2,1)} %copy-done.21), channel_id=1, source_target_pairs={{0,12},{1,13},{2,14},{3,15},{4,0},{5,1},{6,2},{7,3},{8,4},{9,5},{1... | collective-permute-start | bytes 442376 | tf_op jit(solution)/shard_map/ppermute | solution.py:225
  78.6 8.7 %collective-permute-start.10 = (bf16[24,3072]{1,0:T(8,128)(2,1)S(1)}, bf16[24,3072]{1,0:T(8,128)(2,1)S(1)}, u32[]{:S(2)}, u32[]{:S(2)}) collective-permute-start(bf16[24,3072]{1,0:T(8,128)(2,1)S(1)} %get-tuple-element.67), channel_id=1, source_target_pairs={{0,1},{1,2},{2,3},{3,0},{4,5},{5,6},{6,7},{7,4},{8,9},{9,10},{10,1... | collective-permute-start | bytes 442376 | tf_op jit(solution)/shard_map/ppermute | solution.py:225
  79.4 7.9 %collective-permute-start.11 = (bf16[24,3072]{1,0:T(8,128)(2,1)S(1)}, bf16[24,3072]{1,0:T(8,128)(2,1)S(1)}, u32[]{:S(2)}, u32[]{:S(2)}) collective-permute-start(bf16[24,3072]{1,0:T(8,128)(2,1)S(1)} %get-tuple-element.68), channel_id=1, source_target_pairs={{0,2},{1,3},{2,0},{3,1},{4,6},{5,7},{6,4},{7,5},{8,10},{9,11},{10,... | collective-permute-start | bytes 442376 | tf_op jit(solution)/shard_map/ppermute | solution.py:225
  80.5 7.5 %collective-permute-start.12 = (bf16[24,3072]{1,0:T(8,128)(2,1)S(1)}, bf16[24,3072]{1,0:T(8,128)(2,1)S(1)}, u32[]{:S(2)}, u32[]{:S(2)}) collective-permute-start(bf16[24,3072]{1,0:T(8,128)(2,1)S(1)} %get-tuple-element.69), channel_id=1, source_target_pairs={{0,3},{1,0},{2,1},{3,2},{4,7},{5,4},{6,5},{7,6},{8,11},{9,8},{10,9... | collective-permute-start | bytes 442376 | tf_op jit(solution)/shard_map/ppermute | solution.py:225
  90.6 7.8 %collective-permute-start.13 = (bf16[24,3072]{1,0:T(8,128)(2,1)S(1)}, bf16[24,3072]{1,0:T(8,128)(2,1)S(1)}, u32[]{:S(2)}, u32[]{:S(2)}) collective-permute-start(bf16[24,3072]{1,0:T(8,128)(2,1)S(1)} %shard_map.117.refs_0_), channel_id=1, source_target_pairs={{0,12},{1,13},{2,14},{3,15},{4,0},{5,1},{6,2},{7,3},{8,4},{9,5},{1... | collective-permute-start | bytes 442376 | tf_op jit(solution)/shard_map/ppermute | solution.py:225
  91.9 7.4 %collective-permute-start.14 = (bf16[24,3072]{1,0:T(8,128)(2,1)S(1)}, bf16[24,3072]{1,0:T(8,128)(2,1)S(1)}, u32[]{:S(2)}, u32[]{:S(2)}) collective-permute-start(bf16[24,3072]{1,0:T(8,128)(2,1)S(1)} %shard_map.117.refs_0_), channel_id=1, source_target_pairs={{0,8},{1,9},{2,10},{3,11},{4,12},{5,13},{6,14},{7,15},{8,0},{9,1},... | collective-permute-start | bytes 442376 | tf_op jit(solution)/shard_map/ppermute | solution.py:225
  94.1 6.4 %collective-permute-start.15 = (bf16[24,3072]{1,0:T(8,128)(2,1)S(1)}, bf16[24,3072]{1,0:T(8,128)(2,1)S(1)}, u32[]{:S(2)}, u32[]{:S(2)}) collective-permute-start(bf16[24,3072]{1,0:T(8,128)(2,1)S(1)} %shard_map.117.refs_0_), channel_id=1, source_target_pairs={{0,4},{1,5},{2,6},{3,7},{4,8},{5,9},{6,10},{7,11},{8,12},{9,13},{1... | collective-permute-start | bytes 442376 | tf_op jit(solution)/shard_map/ppermute | solution.py:225
  95.8 8.0 %collective-permute-start.16 = (bf16[24,3072]{1,0:T(8,128)(2,1)S(1)}, bf16[24,3072]{1,0:T(8,128)(2,1)S(1)}, u32[]{:S(2)}, u32[]{:S(2)}) collective-permute-start(bf16[24,3072]{1,0:T(8,128)(2,1)S(1)} %shard_map.118.refs_0_), channel_id=1, source_target_pairs={{0,3},{1,0},{2,1},{3,2},{4,7},{5,4},{6,5},{7,6},{8,11},{9,8},{10,9... | collective-permute-start | bytes 442376 | tf_op jit(solution)/shard_map/ppermute | solution.py:225
  98.4 7.6 %collective-permute-start.17 = (bf16[24,3072]{1,0:T(8,128)(2,1)S(1)}, bf16[24,3072]{1,0:T(8,128)(2,1)S(1)}, u32[]{:S(2)}, u32[]{:S(2)}) collective-permute-start(bf16[24,3072]{1,0:T(8,128)(2,1)S(1)} %shard_map.118.refs_0_), channel_id=1, source_target_pairs={{0,2},{1,3},{2,0},{3,1},{4,6},{5,7},{6,4},{7,5},{8,10},{9,11},{10,... | collective-permute-start | bytes 442376 | tf_op jit(solution)/shard_map/ppermute | solution.py:225
  98.4 8.7 %collective-permute-start.18 = (bf16[24,3072]{1,0:T(8,128)(2,1)S(1)}, bf16[24,3072]{1,0:T(8,128)(2,1)S(1)}, u32[]{:S(2)}, u32[]{:S(2)}) collective-permute-start(bf16[24,3072]{1,0:T(8,128)(2,1)S(1)} %shard_map.118.refs_0_), channel_id=1, source_target_pairs={{0,1},{1,2},{2,3},{3,0},{4,5},{5,6},{6,7},{7,4},{8,9},{9,10},{10,1... | collective-permute-start | bytes 442376 | tf_op jit(solution)/shard_map/ppermute | solution.py:225
  109.1 12.1 %collective-permute-start.19 = (bf16[64,3072]{1,0:T(8,128)(2,1)S(1)}, bf16[64,3072]{1,0:T(8,128)(2,1)S(1)}, u32[]{:S(2)}, u32[]{:S(2)}) collective-permute-start(bf16[64,3072]{1,0:T(8,128)(2,1)S(1)} %get-tuple-element.83.refs_0_), channel_id=1, source_target_pairs={{0,3},{1,0},{2,1},{3,2},{4,7},{5,4},{6,5},{7,6},{8,11},{9,8},{10,9... | collective-permute-start | bytes 1179656 | tf_op jit(solution)/shard_map/ppermute | solution.py:225
  110.0 16.0 %collective-permute-start.20 = (bf16[64,3072]{1,0:T(8,128)(2,1)S(1)}, bf16[64,3072]{1,0:T(8,128)(2,1)S(1)}, u32[]{:S(2)}, u32[]{:S(2)}) collective-permute-start(bf16[64,3072]{1,0:T(8,128)(2,1)S(1)} %get-tuple-element.83.refs_0_), channel_id=1, source_target_pairs={{0,2},{1,3},{2,0},{3,1},{4,6},{5,7},{6,4},{7,5},{8,10},{9,11},{10,... | collective-permute-start | bytes 1179656 | tf_op jit(solution)/shard_map/ppermute | solution.py:225
  110.2 21.2 %collective-permute-start.21 = (bf16[64,3072]{1,0:T(8,128)(2,1)S(1)}, bf16[64,3072]{1,0:T(8,128)(2,1)S(1)}, u32[]{:S(2)}, u32[]{:S(2)}) collective-permute-start(bf16[64,3072]{1,0:T(8,128)(2,1)S(1)} %get-tuple-element.83.refs_0_), channel_id=1, source_target_pairs={{0,1},{1,2},{2,3},{3,0},{4,5},{5,6},{6,7},{7,4},{8,9},{9,10},{10,1... | collective-permute-start | bytes 1179656 | tf_op jit(solution)/shard_map/ppermute | solution.py:225
  113.0 18.4 %collective-permute-start.22 = (bf16[64,3072]{1,0:T(8,128)(2,1)S(1)}, bf16[64,3072]{1,0:T(8,128)(2,1)S(1)}, u32[]{:S(2)}, u32[]{:S(2)}) collective-permute-start(bf16[64,3072]{1,0:T(8,128)(2,1)S(1)} %get-tuple-element.87.refs_4_), channel_id=1, source_target_pairs={{0,12},{1,13},{2,14},{3,15},{4,0},{5,1},{6,2},{7,3},{8,4},{9,5},{1... | collective-permute-start | bytes 1179656 | tf_op jit(solution)/shard_map/ppermute | solution.py:225
  115.9 17.0 %collective-permute-start.23 = (bf16[64,3072]{1,0:T(8,128)(2,1)S(1)}, bf16[64,3072]{1,0:T(8,128)(2,1)S(1)}, u32[]{:S(2)}, u32[]{:S(2)}) collective-permute-start(bf16[64,3072]{1,0:T(8,128)(2,1)S(1)} %get-tuple-element.87.refs_4_), channel_id=1, source_target_pairs={{0,8},{1,9},{2,10},{3,11},{4,12},{5,13},{6,14},{7,15},{8,0},{9,1},... | collective-permute-start | bytes 1179656 | tf_op jit(solution)/shard_map/ppermute | solution.py:225
  121.1 15.5 %collective-permute-start.24 = (bf16[64,3072]{1,0:T(8,128)(2,1)S(1)}, bf16[64,3072]{1,0:T(8,128)(2,1)S(1)}, u32[]{:S(2)}, u32[]{:S(2)}) collective-permute-start(bf16[64,3072]{1,0:T(8,128)(2,1)S(1)} %get-tuple-element.87.refs_4_), channel_id=1, source_target_pairs={{0,4},{1,5},{2,6},{3,7},{4,8},{5,9},{6,10},{7,11},{8,12},{9,13},{1... | collective-permute-start | bytes 1179656 | tf_op jit(solution)/shard_map/ppermute | solution.py:225
  125.9 11.8 %collective-permute-start.25 = (bf16[32,3072]{1,0:T(8,128)(2,1)}, bf16[32,3072]{1,0:T(8,128)(2,1)S(1)}, u32[]{:S(2)}, u32[]{:S(2)}) collective-permute-start(bf16[32,3072]{1,0:T(8,128)(2,1)} %get-tuple-element.92.refs_0_), channel_id=1, source_target_pairs={{0,3},{1,0},{2,1},{3,2},{4,7},{5,4},{6,5},{7,6},{8,11},{9,8},{10,9... | collective-permute-start | bytes 589832 | tf_op jit(solution)/shard_map/ppermute | solution.py:225
  131.4 29.7 %collective-permute-start.26 = (bf16[32,3072]{1,0:T(8,128)(2,1)}, bf16[32,3072]{1,0:T(8,128)(2,1)}, u32[]{:S(2)}, u32[]{:S(2)}) collective-permute-start(bf16[32,3072]{1,0:T(8,128)(2,1)} %get-tuple-element.92.refs_0_), channel_id=1, source_target_pairs={{0,2},{1,3},{2,0},{3,1},{4,6},{5,7},{6,4},{7,5},{8,10},{9,11},{10,... | collective-permute-start | bytes 589832 | tf_op jit(solution)/shard_map/ppermute | solution.py:225
  131.4 29.7 %collective-permute-start.27 = (bf16[32,3072]{1,0:T(8,128)(2,1)}, bf16[32,3072]{1,0:T(8,128)(2,1)}, u32[]{:S(2)}, u32[]{:S(2)}) collective-permute-start(bf16[32,3072]{1,0:T(8,128)(2,1)} %get-tuple-element.92.refs_0_), channel_id=1, source_target_pairs={{0,1},{1,2},{2,3},{3,0},{4,5},{5,6},{6,7},{7,4},{8,9},{9,10},{10,1... | collective-permute-start | bytes 589832 | tf_op jit(solution)/shard_map/ppermute | solution.py:225
  132.9 28.2 %collective-permute-start.28 = (bf16[32,3072]{1,0:T(8,128)(2,1)}, bf16[32,3072]{1,0:T(8,128)(2,1)}, u32[]{:S(2)}, u32[]{:S(2)}) collective-permute-start(bf16[32,3072]{1,0:T(8,128)(2,1)} %get-tuple-element.93.refs_4_), channel_id=1, source_target_pairs={{0,12},{1,13},{2,14},{3,15},{4,0},{5,1},{6,2},{7,3},{8,4},{9,5},{1... | collective-permute-start | bytes 589832 | tf_op jit(solution)/shard_map/ppermute | solution.py:225
  137.4 23.8 %collective-permute-start.29 = (bf16[32,3072]{1,0:T(8,128)(2,1)}, bf16[32,3072]{1,0:T(8,128)(2,1)}, u32[]{:S(2)}, u32[]{:S(2)}) collective-permute-start(bf16[32,3072]{1,0:T(8,128)(2,1)} %get-tuple-element.93.refs_4_), channel_id=1, source_target_pairs={{0,8},{1,9},{2,10},{3,11},{4,12},{5,13},{6,14},{7,15},{8,0},{9,1},... | collective-permute-start | bytes 589832 | tf_op jit(solution)/shard_map/ppermute | solution.py:225
  138.4 22.8 %collective-permute-start.30 = (bf16[32,3072]{1,0:T(8,128)(2,1)}, bf16[32,3072]{1,0:T(8,128)(2,1)}, u32[]{:S(2)}, u32[]{:S(2)}) collective-permute-start(bf16[32,3072]{1,0:T(8,128)(2,1)} %get-tuple-element.93.refs_4_), channel_id=1, source_target_pairs={{0,4},{1,5},{2,6},{3,7},{4,8},{5,9},{6,10},{7,11},{8,12},{9,13},{1... | collective-permute-start | bytes 589832 | tf_op jit(solution)/shard_map/ppermute | solution.py:225
  140.2 2.3 %copy-start.2 = (bf16[6144,384]{1,0:T(8,128)(2,1)S(1)}, bf16[6144,384]{1,0:T(8,128)(2,1)}, u32[]{:S(2)}) copy-start(bf16[6144,384]{1,0:T(8,128)(2,1)} %refs_8_.1) | copy-start | bytes 14155780
  147.7 13.5 %copy-start.16 = (bf16[32,3072]{1,0:T(8,128)(2,1)S(1)}, bf16[32,3072]{1,0:T(8,128)(2,1)}, u32[]{:S(2)}) copy-start(bf16[32,3072]{1,0:T(8,128)(2,1)} %copy-done.15) | copy-start | bytes 589828
  152.7 28.1 %copy-start.24 = (f32[384]{0:T(512)S(1)}, f32[384]{0:T(512)}, u32[]{:S(2)}) copy-start(f32[384]{0:T(512)} %param.18) | copy-start | bytes 4612
  152.7 19.0 %all-to-all-start.1 = ((f32[32,24,128]{2,1,0:T(8,128)}), f32[32,24,128]{2,1,0:T(8,128)S(1)}, u32[]{:S(2)}, u32[]{:S(2)}) async-start(f32[32,24,128]{2,1,0:T(8,128)} %broadcast_in_dim.39), calls=%async_computation.1 | async-start | bytes 786432 | tf_op jit(solution)/shard_map/all_to_all | solution.py:372
  161.2 2.3 %copy-start.3 = (bf16[6144,384]{1,0:T(8,128)(2,1)S(1)}, bf16[6144,384]{1,0:T(8,128)(2,1)}, u32[]{:S(2)}) copy-start(bf16[6144,384]{1,0:T(8,128)(2,1)} %refs_8_.1) | copy-start | bytes 14155780
  168.2 3.6 %collective-permute-start.31 = (f32[128,384]{1,0:T(8,128)S(1)}, f32[128,384]{1,0:T(8,128)S(1)}, u32[]{:S(2)}, u32[]{:S(2)}) collective-permute-start(f32[128,384]{1,0:T(8,128)S(1)} %get-tuple-element.95), channel_id=1, source_target_pairs={{0,64},{64,0},{1,65},{65,1},{2,66},{66,2},{3,67},{67,3},{4,68},{68... | collective-permute-start | bytes 589832 | tf_op jit(solution)/shard_map/ppermute | solution.py:383
  171.9 5.1 %collective-permute-start.34 = (f32[4,8,384]{2,1,0:T(8,128)S(1)}, f32[4,8,384]{2,1,0:T(8,128)S(1)}, u32[]{:S(2)}, u32[]{:S(2)}) collective-permute-start(f32[4,8,384]{2,1,0:T(8,128)S(1)} %get-tuple-element.101), channel_id=1, source_target_pairs={{0,48},{16,0},{32,16},{48,32},{1,49},{17,1},{33,17},{49,33},{2,50}... | collective-permute-start | bytes 147464 | tf_op jit(solution)/shard_map/ppermute | solution.py:390
  174.7 5.6 %collective-permute-start.33 = (f32[4,8,384]{2,1,0:T(8,128)S(1)}, f32[4,8,384]{2,1,0:T(8,128)S(1)}, u32[]{:S(2)}, u32[]{:S(2)}) collective-permute-start(f32[4,8,384]{2,1,0:T(8,128)S(1)} %get-tuple-element.102), channel_id=1, source_target_pairs={{0,32},{16,48},{32,0},{48,16},{1,33},{17,49},{33,1},{49,17},{2,34}... | collective-permute-start | bytes 147464 | tf_op jit(solution)/shard_map/ppermute | solution.py:390
  175.5 5.3 %collective-permute-start.32 = (f32[4,8,384]{2,1,0:T(8,128)S(1)}, f32[4,8,384]{2,1,0:T(8,128)S(1)}, u32[]{:S(2)}, u32[]{:S(2)}) collective-permute-start(f32[4,8,384]{2,1,0:T(8,128)S(1)} %get-tuple-element.100), channel_id=1, source_target_pairs={{0,16},{16,32},{32,48},{48,0},{1,17},{17,33},{33,49},{49,1},{2,18}... | collective-permute-start | bytes 147464 | tf_op jit(solution)/shard_map/ppermute | solution.py:390
  (15 other events, 16.7 us)

commit v4 on v0

v4 whole, which is shorter than its diff:
```python
import functools

import jax
import jax.numpy as jnp
from jax import lax
from jax.experimental import pallas as pl
from jax.experimental.pallas import tpu as pltpu
from jax.sharding import PartitionSpec as P

D = 6144
BF16 = jnp.bfloat16
F32 = jnp.float32
TILE = 512
WIDE = 1024
SMALL = 16 * 2**20


def gelu_exact(v):
    return v * 0.5 * (1.0 + lax.erf(v * 0.7071067811865476))


def gelu_slope(v):
    return (
        0.5 * (1.0 + lax.erf(v * 0.7071067811865476))
        + v * jnp.exp(-0.5 * v * v) * 0.3989422804014327
    )


def pairs(first, k):
    out = []
    for core in range(2):
        for z in range(4):
            for y in range(4):
                if (core == 0) == first:
                    to = z * 4 + (y + k) % 4
                else:
                    to = ((z + k) % 4) * 4 + y
                out.append((core * 16 + z * 4 + y, core * 16 + to))
    return out


def shift_row(k):
    return [(r, (r + k) % 4) for r in range(4)]


SWAP = [(0, 1), (1, 0)]


def row_order(where):
    p = lax.broadcasted_iota(jnp.int32, (256, 256), 0)
    q = lax.broadcasted_iota(jnp.int32, (256, 256), 1)
    e, h, i, j = p & 7, (p >> 3) & 1, (p >> 4) & 3, p >> 6
    second = where[0] == 1
    by = (where[1] + jnp.where(second, i, j)) & 3
    bz = (where[2] + jnp.where(second, j, i)) & 3
    return jnp.where(h * 128 + (by * 4 + bz) * 8 + e == q, 1.0, 0.0).astype(BF16)


def reorder(sel, x):
    return jnp.dot(sel, x, preferred_element_type=F32).astype(BF16)


def grad_partials(where, own, other, w_out, o0, o1, o2, o3, rows):
    @pl.when(pl.program_id(0) == 0)
    def _():
        rows[...] = reorder(row_order(where), jnp.concatenate([own[...], other[...]], axis=0))

    grad = lax.dot_general(
        rows[...], w_out[...], (((1,), (1,)), ((), ())), preferred_element_type=F32
    ).astype(BF16)
    for j, o in enumerate((o0, o1, o2, o3)):
        o[...] = grad[j * 64 : j * 64 + 64]


def merged_stats(width, stats, core):
    part = stats[pl.ds(core * 16, 16)]
    means, m2 = part[:, 0:2], part[:, 2:4]
    mean = jnp.sum(means, axis=0) / 16
    gap = means - mean[None]
    var = (jnp.sum(m2, axis=0) + width * jnp.sum(gap * gap, axis=0)) / D
    rows = jnp.concatenate([mean, lax.rsqrt(var + 1e-06), mean, mean], axis=0)
    return jnp.transpose(rows)


def normed_rows(x, merged, k, gain):
    x = (x[...].astype(F32) - merged[:, k : k + 1]) * merged[:, 2 + k : 3 + k] * gain[...]
    return x.astype(BF16)


def pre_partials(
    width, where, own_f, own_r, other_f, other_r, stats, gain, w_in, o0, o1, o2, o3, normed_t, lhs
):
    @pl.when(pl.program_id(0) == 0)
    def _():
        own = merged_stats(width, stats, where[0])
        other = merged_stats(width, stats, 1 - where[0])
        x_f = [normed_rows(own_f, own, 0, gain), normed_rows(other_f, other, 0, gain)]
        x_r = [normed_rows(own_r, own, 1, gain), normed_rows(other_r, other, 1, gain)]
        sel = row_order(where)
        rows = jnp.dot(sel, jnp.concatenate(x_f, axis=0), preferred_element_type=F32)
        lhs[0:256, :] = rows.astype(BF16)
        normed_t[...] = jnp.transpose(rows).astype(BF16)
        lhs[256:512, :] = reorder(sel, jnp.concatenate(x_r, axis=0))

    pre = jnp.dot(lhs[...], w_in[...], preferred_element_type=F32).astype(BF16)
    for j, o in enumerate((o0, o1, o2, o3)):
        for i in range(4):
            at = (j * 4 + i) * 16
            o[i * 32 : i * 32 + 16, :] = pre[at : at + 16]
            o[i * 32 + 16 : i * 32 + 32, :] = pre[256 + at : 256 + at + 16]


def stage_sum(p0, p1, p2, p3, g0, g1, g2, g3, keep, *sends):
    for i in range(4):
        parts = []
        for rows, (a, b, c, d) in ((32, (p0, p1, p2, p3)), (16, (g0, g1, g2, g3))):
            at = slice(i * rows, (i + 1) * rows)
            parts.append(
                (a[at, :].astype(F32) + b[at, :].astype(F32))
                + (c[at, :].astype(F32) + d[at, :].astype(F32))
            )
        total = jnp.concatenate(parts, axis=0)
        if i == 0:
            keep[...] = total
        else:
            sends[i - 1][...] = total.astype(BF16)


def activate(keep, a, b, c, bias, mask, out):
    total = (keep[...] + a[...].astype(F32)) + (b[...].astype(F32) + c[...].astype(F32))
    pre = total[:32] + bias[...]
    act = gelu_exact(pre)
    out[0:16, :] = act[:16].astype(BF16)
    out[16:32, :] = (total[32:48] * gelu_slope(pre[:16])).astype(BF16)
    out[32:48, :] = (act[16:32].astype(BF16).astype(F32) * mask[...]).astype(BF16)


def regroup(b0, b1, b2, b3, forget, retain):
    for i, b in enumerate((b0, b1, b2, b3)):
        at = i * 16
        forget[at : at + 16, :] = b[0:16, :]
        forget[64 + at : 64 + at + 16, :] = b[16:32, :]
        retain[at : at + 16, :] = b[32:48, :]


def saliency_terms(where, b0, b1, b2, b3, normed_t, grad_y, w_in, w_out, out):
    blocks = (b0, b1, b2, b3)
    act = jnp.concatenate([b[0:64, :] for b in blocks], axis=0)
    grad_pre = jnp.concatenate([b[64:128, :] for b in blocks], axis=0)
    grad_in = jnp.dot(normed_t[...], grad_pre, preferred_element_type=F32)
    grad_out = lax.dot_general(
        act, grad_y[...], (((0,), (0,)), ((), ())), preferred_element_type=F32
    )
    term_in = jnp.sum(jnp.abs(w_in[...].astype(F32) * grad_in), axis=0, keepdims=True)
    prod = jnp.abs(w_out[...].astype(F32) * grad_out)
    lanes = (prod[:, 0:128] + prod[:, 128:256]) + prod[:, 256:384]
    term_out = jnp.sum(jnp.transpose(lanes), axis=0, keepdims=True)
    out[...] = term_in + term_out


def retain_product(where, b0, b1, b2, b3, w_out, mine, theirs, acc):
    t = pl.program_id(0)
    act = jnp.concatenate([b0[...], b1[...], b2[...], b3[...]], axis=0)
    part = jnp.dot(act, w_out[...], preferred_element_type=F32)

    @pl.when(t == 0)
    def _():
        acc[...] = part

    @pl.when(t > 0)
    def _():
        acc[...] += part

    def store(swap):
        for j in range(4):
            for i in range(4):
                at = (j * 4 + i) * 16
                to = (i * 4 + j if swap else j * 4 + i) * 8
                mine[to : to + 8, :] = acc[at : at + 8, :]
                theirs[to : to + 8, :] = acc[at + 8 : at + 16, :]

    last = t == pl.num_programs(0) - 1

    @pl.when(last & (where[0] == 0))
    def _():
        store(False)

    @pl.when(last & (where[0] == 1))
    def _():
        store(True)


def call(kernel, where, args, outs, scratch=(), steps=6, vmem=None):
    def spec(shape, block, index):
        if block is None:
            return pl.BlockSpec(shape, lambda t, w: (0,) * len(shape))
        return pl.BlockSpec(block, index)

    return pl.pallas_call(
        kernel,
        grid_spec=pltpu.PrefetchScalarGridSpec(
            num_scalar_prefetch=1,
            grid=(steps,),
            in_specs=[spec(a.shape, b, i) for a, b, i in args],
            out_specs=[spec(s, b, i) for s, _, b, i in outs],
            scratch_shapes=list(scratch),
        ),
        out_shape=[jax.ShapeDtypeStruct(s, d) for s, d, _, _ in outs],
        compiler_params=pltpu.CompilerParams(vmem_limit_bytes=vmem),
        cost_estimate=pl.CostEstimate(flops=1, bytes_accessed=1, transcendentals=0),
    )(where, *[a for a, _, _ in args])


def whole(a):
    return (a, None, None)


def by_n(a, tile=TILE):
    return (a, (a.shape[0], tile), lambda t, w: (0, t))


def out_n(rows, n, dtype, tile=TILE):
    return ((rows, n), dtype, (rows, tile), lambda t, w: (0, t))


def drop_where(kernel):
    def inner(where, *refs):
        kernel(*refs)

    return inner


def permutes(parts, first, sign=1):
    return [
        lax.ppermute(parts[k], ("dp", "col"), pairs(first, sign * (k + 1))) for k in range(3)
    ]


def local(
    forget_tokens,
    forget_cotangent,
    forget_labels,
    retain_tokens,
    ln_gain,
    w_in,
    b_in,
    w_out,
    b_out,
    pruned,
):
    core = lax.axis_index("dp")
    row = lax.axis_index("row")
    col = lax.axis_index("col")
    y, z = col % 4, col // 4
    width = w_in.shape[0]
    half = w_in.shape[1] // 2
    steps = half // TILE
    where = jnp.stack([core, y, z]).astype(jnp.int32)
    gain = ln_gain[None, :]

    tokens = jnp.stack([forget_tokens, retain_tokens]).astype(F32)
    part_mean = jnp.sum(tokens, axis=2) / width
    centred = tokens - part_mean[..., None]
    part_m2 = jnp.sum(centred * centred, axis=2)
    stats = jnp.broadcast_to(jnp.concatenate([part_mean, part_m2])[None], (32, 4, 128))
    stats = lax.all_to_all(stats, ("dp", "col"), 0, 0, tiled=True)

    own_g = forget_cotangent * forget_labels[:, None].astype(BF16)
    other = lax.ppermute(
        jnp.concatenate([forget_tokens, own_g, retain_tokens], axis=0), "dp", SWAP
    )

    def third(k):
        return (other, (128, width), lambda t, w: (k, 0))

    w_in_tile = (w_in, (width, TILE), lambda t, w: (0, w[0] * steps + t))
    w_out_tile = (w_out, (TILE, width), lambda t, w: (w[0] * steps + t, 0))
    *g_parts, grad_y = call(
        grad_partials,
        where,
        [whole(own_g), third(1), w_out_tile],
        [out_n(64, half, BF16)] * 4 + [((256, width), BF16, None, None)],
        (),
        steps,
    )
    g_got = permutes(g_parts[1:], True)
    stats, _ = lax.optimization_barrier((stats, g_parts[0]))
    *p_parts, normed_t = call(
        functools.partial(pre_partials, width),
        where,
        [whole(forget_tokens), whole(retain_tokens), third(0), third(2), whole(stats),
         whole(gain), w_in_tile],
        [out_n(128, half, BF16)] * 4 + [((width, 256), BF16, None, None)],
        [pltpu.VMEM((512, width), BF16)],
        steps,
    )
    p_got = permutes(p_parts[1:], True)

    b_half = lax.dynamic_slice_in_dim(b_in, core * half, half, 0)[None, :]
    ids = row * w_in.shape[1] + core * half + jnp.arange(half, dtype=jnp.int32)
    is_pruned = jnp.any(pruned[:, None] == ids[None, :], axis=0)
    keep = jnp.where(is_pruned, 0.0, 1.0)[None, :]

    def wide(kernel, args, outs):
        return call(
            drop_where(kernel),
            where,
            [by_n(v, WIDE) for v in args],
            [out_n(rows, half, kind, WIDE) for rows, kind in outs],
            steps=half // WIDE,
            vmem=SMALL,
        )

    sums = wide(
        stage_sum,
        [p_parts[0]] + p_got + [g_parts[0]] + g_got,
        [(48, F32)] + [(48, BF16)] * 3,
    )
    back = permutes(sums[1:], False)
    block = wide(activate, [sums[0]] + back + [b_half, keep], [(48, BF16)])[0]
    near = permutes([block] * 3, False, -1)
    forget, retain = wide(regroup, [block] + near, [(128, BF16), (64, BF16)])
    far = permutes([forget] * 3, True, -1)
    retain, _ = lax.optimization_barrier((retain, far[0]))
    retain_far = permutes([retain] * 3, True, -1)

    terms = call(
        saliency_terms,
        where,
        [by_n(v) for v in [forget] + far] + [whole(normed_t), whole(grad_y), w_in_tile, w_out_tile],
        [out_n(1, half, F32)],
        (),
        steps,
    )[0]
    terms = jnp.broadcast_to(terms.reshape(1, half // 128, 128), (32, half // 128, 128))
    terms = lax.all_to_all(terms, ("dp", "col"), 0, 0, tiled=True)
    saliency = jnp.sum(terms.reshape(2, 16, half), axis=1).reshape(2 * half) / D

    mine, theirs = call(
        retain_product,
        where,
        [by_n(v) for v in [retain] + retain_far] + [w_out_tile],
        [((128, width), F32, None, None)] * 2,
        [pltpu.VMEM((256, width), F32)],
        steps,
    )
    mine = (mine + lax.ppermute(theirs, "dp", SWAP)).reshape(4, 4, 8, width)

    def for_row(r):
        return lax.dynamic_index_in_dim(mine, (r - y) % 4, 0, keepdims=False)

    total = for_row(row)
    for k in (1, 2, 3):
        total = total + lax.ppermute(for_row(row + k), "row", shift_row(k))
    retain_out = (total + b_out).astype(BF16)
    retain_out = lax.dynamic_slice_in_dim(
        jnp.concatenate([retain_out, retain_out], axis=0), (4 - z) % 4, 4, 0
    ).reshape(32, width)
    return (saliency, retain_out)


def solution(mesh):
    in_specs = (
        P("dp", "col"),
        P("dp", "col"),
        P("dp"),
        P("dp", "col"),
        P("col"),
        P("col", "row"),
        P("row"),
        P("row", "col"),
        P("col"),
        P("row"),
    )
    out_specs = (P("row"), P(("dp", "row"), "col"))
    return jax.shard_map(local, mesh=mesh, in_specs=in_specs, out_specs=out_specs, check_vma=False)
```

time: 551 us -> 160 us (0.29)
  waiting for transfers between devices: 277 us -> 60.8 us
  blocking collectives: 206 us -> 0 us
  starting transfers between devices: 0.29 us -> 48.5 us
  Pallas kernels: 0 us -> 33.2 us
  matrix products: 23.8 us -> 0 us
  between operations: 14.2 us -> 0.93 us
  other arithmetic: 14 us -> 7.42 us
    psum x3 -> x0, blocking collectives: 206 us -> none  [the longest x1 129 us: local(): saliency = lax.psum(terms, ('dp', 'col')) / D]
    reduce_scatter x4 -> x0, waiting for transfers between devices: 109 us -> none  [the longest x1 72.4 us: local(): lax.psum_scatter(partial_pre, 'col', scatter_dimension=1, tiled=True)]
    all_gather x2 -> x0, waiting for transfers between devices: 93.9 us -> none  [the longest x1 51.7 us: local(): act_all = lax.all_gather(act_share, 'col', axis=1, tiled=True)]
    unnamed x8 -> x0, waiting for transfers between devices: 74.5 us -> none
    ppermute x0 -> x23, waiting for transfers between devices: none -> 56.9 us  [the longest x18 54.9 us: permutes(): lax.ppermute(parts[k], ('dp', 'col'), pairs(first, sign * (k + 1)))]
    ppermute x0 -> x23, starting transfers between devices: none -> 34.7 us  [the longest x18 28.6 us: permutes(): lax.ppermute(parts[k], ('dp', 'col'), pairs(first, sign * (k + 1)))]
    pallas_call x0 -> x7, Pallas kernels: none -> 33.2 us  [call(): pl.pallas_call(kernel, grid_spec=pltpu.PrefetchScalarGridSpec(num_scalar_...]
    dot_general x5 -> x0, matrix products: 23.8 us -> none  [the longest x2 8.6 us: outer_rows(): lax.dot_general(left, right, (((0,), (0,)), ((), ())), preferred_element_...]
  transfers between devices with their start and end apart: 7 -> 25, of which waited for: 7 -> 11; matrix products, arithmetic and copies ran while one was open for 6% -> 5% of each run, Pallas kernels for 0% -> 18%
where the time goes in v4:
time: 160 us; the launch traced here: 159 us
  waiting for transfers between devices  60.8 us (38%)
  starting transfers between devices  48.5 us (30%)
  Pallas kernels  33.2 us (21%)
  local copies, waits for them, and re-layouts  7.74 us (5%)
  other arithmetic  7.42 us (5%)
    ppermute x18, waiting for transfers between devices, permutes(): lax.ppermute(parts[k], ('dp', 'col'), pairs(first, sign * (k + 1)))  54.9 us
    pallas_call x7, Pallas kernels, call(): pl.pallas_call(kernel, grid_spec=pltpu.PrefetchScalarGridSpec(num_scalar_...  33.2 us
    ppermute x18, starting transfers between devices, permutes(): lax.ppermute(parts[k], ('dp', 'col'), pairs(first, sign * (k + 1)))  28.6 us
    all_to_all x1, starting transfers between devices, local(): stats = lax.all_to_all(stats, ('dp', 'col'), 0, 0, tiled=True)  8.52 us
    ppermute x3, starting transfers between devices, local(): total = total + lax.ppermute(for_row(row + k), 'row', shift_row(k))  5.72 us
    all_to_all x1, starting transfers between devices, local(): terms = lax.all_to_all(terms, ('dp', 'col'), 0, 0, tiled=True)  5.33 us
    all_to_all x1, waiting for transfers between devices, local(): terms = lax.all_to_all(terms, ('dp', 'col'), 0, 0, tiled=True)  3.91 us
    unnamed x27, local copies, waits for them, and re-layouts  3.6 us
  transfers between devices with their start and end apart: 25, of which 11 were waited for; matrix products, arithmetic and copies ran while one was open for 5% of the time, Pallas kernels for 18%

profile of v4, /device:TPU:0, one launch (start us, length us, event | category | flops | bytes accessed | tf_op | source)
XLA Modules:
  0.0 158.6 jit_solution(10924454507377072463)
XLA Ops:
  1.3 1.0 broadcast_multiply_fusion.own
  2.3 1.0 pad_maximum_fusion
  3.4 1.1 convert_reduce_fusion
  4.5 1.1 fusion.1
  6.2 8.5 %all-to-all-start = ((f32[32,4,128]{2,1,0:T(4,128)}), f32[32,4,128]{2,1,0:T(4,128)S(1)}, u32[]{:S(2)}, u32[]{:S(2)}) async-start(f32[32,4,128]{2,1,0:T(4,128)} %broadcast_in_dim.18), calls=%async_computation | async-start | bytes 131072 | tf_op jit(solution)/shard_map/all_to_all | solution.py:266
  14.8 1.2 broadcast_in_dim.34.gain
  17.3 6.5 %shard_map.113 = (bf16[64,3072]{1,0:T(8,128)(2,1)}, bf16[64,3072]{1,0:T(8,128)(2,1)}, bf16[64,3072]{1,0:T(8,128)(2,1)}, bf16[64,3072]{1,0:T(8,128)(2,1)}, bf16[256,384]{1,0:T(8,128)(2,1)}) custom-call(s32[3]{0:T(128)} %pad_add_fusion.where, bf16[128,384]{1,0:T(8,128)(2,1)} %copy-done.6, bf16[384,384]{1,0:T(8,128)(2,1)} %copy-done.5, bf16[6144,384]{1,0:T(8,128)(2,1)} %w_out.5), custom_call_target="tpu_custom_call" | custom-call | flops 1 | bytes 1 | tf_op jit(solution)/shard_map/pallas_call | solution.py:199
  23.8 1.9 %collective-permute-start.4 = (bf16[64,3072]{1,0:T(8,128)(2,1)}, bf16[64,3072]{1,0:T(8,128)(2,1)S(1)}, u32[]{:S(2)}, u32[]{:S(2)}) collective-permute-start(bf16[64,3072]{1,0:T(8,128)(2,1)} %get-tuple-element.28), channel_id=1, source_target_pairs={{0,1},{1,2},{2,3},{3,0},{4,5},{5,6},{6,7},{7,4},{8,9},{9,10},{10,1... | collective-permute-start | bytes 1179656 | tf_op jit(solution)/shard_map/ppermute | solution.py:235
  25.7 7.7 %shard_map.114 = (bf16[128,3072]{1,0:T(8,128)(2,1)}, bf16[128,3072]{1,0:T(8,128)(2,1)}, bf16[128,3072]{1,0:T(8,128)(2,1)}, bf16[128,3072]{1,0:T(8,128)(2,1)}, bf16[384,256]{1,0:T(8,128)(2,1)}) custom-call(s32[3]{0:T(128)} %pad_add_fusion.where, bf16[128,384]{1,0:T(8,128)(2,1)} %own_f.1, bf16[128,384]{1,0:T(8,128)(2,1)} %own_r.1, bf16[384,384]{1,0:T(8,128)(2,1)} %copy-done.5, ...), custom_call_target="tpu_custom_call" | custom-call | flops 1 | bytes 1 | tf_op jit(solution)/shard_map/pallas_call | solution.py:199
  33.4 1.5 collective-permute-start.1
  34.9 1.7 %collective-permute-start.2 = (bf16[128,3072]{1,0:T(8,128)(2,1)}, bf16[128,3072]{1,0:T(8,128)(2,1)S(1)}, u32[]{:S(2)}, u32[]{:S(2)}) collective-permute-start(bf16[128,3072]{1,0:T(8,128)(2,1)} %get-tuple-element.26), channel_id=1, source_target_pairs={{0,2},{1,3},{2,0},{3,1},{4,6},{5,7},{6,4},{7,5},{8,10},{9,11},{10,... | collective-permute-start | bytes 2359304 | tf_op jit(solution)/shard_map/ppermute | solution.py:235
  36.6 2.1 %collective-permute-start.3 = (bf16[128,3072]{1,0:T(8,128)(2,1)}, bf16[128,3072]{1,0:T(8,128)(2,1)S(1)}, u32[]{:S(2)}, u32[]{:S(2)}) collective-permute-start(bf16[128,3072]{1,0:T(8,128)(2,1)} %get-tuple-element.27), channel_id=1, source_target_pairs={{0,3},{1,0},{2,1},{3,2},{4,7},{5,4},{6,5},{7,6},{8,11},{9,8},{10,9... | collective-permute-start | bytes 2359304 | tf_op jit(solution)/shard_map/ppermute | solution.py:235
  38.7 0.9 collective-permute-start.5
  39.6 1.7 %collective-permute-start.6 = (bf16[64,3072]{1,0:T(8,128)(2,1)}, bf16[64,3072]{1,0:T(8,128)(2,1)}, u32[]{:S(2)}, u32[]{:S(2)}) collective-permute-start(bf16[64,3072]{1,0:T(8,128)(2,1)} %get-tuple-element.30), channel_id=1, source_target_pairs={{0,3},{1,0},{2,1},{3,2},{4,7},{5,4},{6,5},{7,6},{8,11},{9,8},{10,9... | collective-permute-start | bytes 1179656 | tf_op jit(solution)/shard_map/ppermute | solution.py:235
  41.3 0.7 dynamic_slice.19
  42.0 17.4 %collective-permute-done.5.refs_6_ = bf16[64,3072]{1,0:T(8,128)(2,1)S(1)} collective-permute-done((bf16[64,3072]{1,0:T(8,128)(2,1)}, bf16[64,3072]{1,0:T(8,128)(2,1)S(1)}, u32[]{:S(2)}, u32[]{:S(2)}) %collective-permute-start.5) | collective-permute-done | bytes 393248 | tf_op jit(solution)/shard_map/ppermute | solution.py:235
  59.4 5.3 %collective-permute-done.6.refs_7_ = bf16[64,3072]{1,0:T(8,128)(2,1)} collective-permute-done((bf16[64,3072]{1,0:T(8,128)(2,1)}, bf16[64,3072]{1,0:T(8,128)(2,1)}, u32[]{:S(2)}, u32[]{:S(2)}) %collective-permute-start.6) | collective-permute-done | bytes 393248 | tf_op jit(solution)/shard_map/ppermute | solution.py:235
  64.8 1.1 copy-done
  65.9 3.0 %shard_map.115 = (f32[48,3072]{1,0:T(8,128)S(1)}, bf16[48,3072]{1,0:T(8,128)(2,1)S(1)}, bf16[48,3072]{1,0:T(8,128)(2,1)S(1)}, bf16[48,3072]{1,0:T(8,128)(2,1)S(1)}) custom-call(s32[3]{0:T(128)S(1)} %copy-done.4, bf16[128,3072]{1,0:T(8,128)(2,1)S(1)} %copy-done, bf16[128,3072]{1,0:T(8,128)(2,1)S(1)} %collective-permute-done.1.refs_1_, ...), custom_call_target="tpu_custom_call" | custom-call | flops 1 | bytes 1 | tf_op jit(solution)/shard_map/pallas_call | solution.py:199
  68.9 1.5 collective-permute-start.7
  70.5 2.7 %collective-permute-start.8 = (bf16[48,3072]{1,0:T(8,128)(2,1)S(1)}, bf16[48,3072]{1,0:T(8,128)(2,1)S(1)}, u32[]{:S(2)}, u32[]{:S(2)}) collective-permute-start(bf16[48,3072]{1,0:T(8,128)(2,1)S(1)} %get-tuple-element.33), channel_id=1, source_target_pairs={{0,8},{1,9},{2,10},{3,11},{4,12},{5,13},{6,14},{7,15},{8,0},{9,1},... | collective-permute-start | bytes 884744 | tf_op jit(solution)/shard_map/ppermute | solution.py:235
  73.1 1.5 collective-permute-start.9
  74.9 2.0 %collective-permute-done.7.refs_1_ = bf16[48,3072]{1,0:T(8,128)(2,1)S(1)} collective-permute-done((bf16[48,3072]{1,0:T(8,128)(2,1)S(1)}, bf16[48,3072]{1,0:T(8,128)(2,1)S(1)}, u32[]{:S(2)}, u32[]{:S(2)}) %collective-permute-start.7) | collective-permute-done | bytes 294944 | tf_op jit(solution)/shard_map/ppermute | solution.py:235
  76.9 4.1 %collective-permute-done.8.refs_2_ = bf16[48,3072]{1,0:T(8,128)(2,1)S(1)} collective-permute-done((bf16[48,3072]{1,0:T(8,128)(2,1)S(1)}, bf16[48,3072]{1,0:T(8,128)(2,1)S(1)}, u32[]{:S(2)}, u32[]{:S(2)}) %collective-permute-start.8) | collective-permute-done | bytes 294944 | tf_op jit(solution)/shard_map/ppermute | solution.py:235
  81.0 1.1 shard_map.116.refs_0_
  82.1 2.7 %collective-permute-start.10 = (bf16[48,3072]{1,0:T(8,128)(2,1)S(1)}, bf16[48,3072]{1,0:T(8,128)(2,1)S(1)}, u32[]{:S(2)}, u32[]{:S(2)}) collective-permute-start(bf16[48,3072]{1,0:T(8,128)(2,1)S(1)} %shard_map.116.refs_0_), channel_id=1, source_target_pairs={{0,12},{1,13},{2,14},{3,15},{4,0},{5,1},{6,2},{7,3},{8,4},{9,5},{1... | collective-permute-start | bytes 884744 | tf_op jit(solution)/shard_map/ppermute | solution.py:235
  84.8 1.4 collective-permute-start.11
  86.5 5.7 %collective-permute-done.10.refs_1_ = bf16[48,3072]{1,0:T(8,128)(2,1)S(1)} collective-permute-done((bf16[48,3072]{1,0:T(8,128)(2,1)S(1)}, bf16[48,3072]{1,0:T(8,128)(2,1)S(1)}, u32[]{:S(2)}, u32[]{:S(2)}) %collective-permute-start.10) | collective-permute-done | bytes 294944 | tf_op jit(solution)/shard_map/ppermute | solution.py:235
  92.2 0.9 collective-permute-done.11.refs_2_
  93.1 3.1 %collective-permute-done.12.refs_3_ = bf16[48,3072]{1,0:T(8,128)(2,1)S(1)} collective-permute-done((bf16[48,3072]{1,0:T(8,128)(2,1)S(1)}, bf16[48,3072]{1,0:T(8,128)(2,1)S(1)}, u32[]{:S(2)}, u32[]{:S(2)}) %collective-permute-start.12) | collective-permute-done | bytes 294944 | tf_op jit(solution)/shard_map/ppermute | solution.py:235
  96.1 0.9 shard_map.117
  97.1 2.7 %collective-permute-start.13 = (bf16[128,3072]{1,0:T(8,128)(2,1)S(1)}, bf16[128,3072]{1,0:T(8,128)(2,1)S(1)}, u32[]{:S(2)}, u32[]{:S(2)}) collective-permute-start(bf16[128,3072]{1,0:T(8,128)(2,1)S(1)} %get-tuple-element.35.b0), channel_id=1, source_target_pairs={{0,3},{1,0},{2,1},{3,2},{4,7},{5,4},{6,5},{7,6},{8,11},{9,8},{10,9... | collective-permute-start | bytes 2359304 | tf_op jit(solution)/shard_map/ppermute | solution.py:235
  99.7 1.4 collective-permute-start.14
  101.2 16.5 %collective-permute-done.13.b1 = bf16[128,3072]{1,0:T(8,128)(2,1)S(1)} collective-permute-done((bf16[128,3072]{1,0:T(8,128)(2,1)S(1)}, bf16[128,3072]{1,0:T(8,128)(2,1)S(1)}, u32[]{:S(2)}, u32[]{:S(2)}) %collective-permute-start.13) | collective-permute-done | bytes 786464 | tf_op jit(solution)/shard_map/ppermute | solution.py:235
  117.7 3.7 %collective-permute-start.16 = (bf16[64,3072]{1,0:T(8,128)(2,1)S(1)}, bf16[64,3072]{1,0:T(8,128)(2,1)}, u32[]{:S(2)}, u32[]{:S(2)}) collective-permute-start(bf16[64,3072]{1,0:T(8,128)(2,1)S(1)} %get-tuple-element.39.b0), channel_id=1, source_target_pairs={{0,3},{1,0},{2,1},{3,2},{4,7},{5,4},{6,5},{7,6},{8,11},{9,8},{10,9... | collective-permute-start | bytes 1179656 | tf_op jit(solution)/shard_map/ppermute | solution.py:235
  121.3 0.9 collective-permute-start.18
  122.2 0.9 copy-done.8
  123.4 7.7 %shard_map.118 = f32[1,3072]{1,0:T(1,128)} custom-call(s32[3]{0:T(128)} %pad_add_fusion.where, bf16[128,3072]{1,0:T(8,128)(2,1)} %copy-done.1, bf16[128,3072]{1,0:T(8,128)(2,1)} %copy-done.7, bf16[128,3072]{1,0:T(8,128)(2,1)} %copy-done.8, bf16[128,3072]{1,0:T(8,128)(2,1)} %copy-done.9, bf16[384,256]{1,0:T(8,128)(2,1)} %get-tuple-element.36.normed_t, ...), custom_call_target="tpu_custom_call" | custom-call | flops 1 | bytes 1 | tf_op jit(solution)/shard_map/pallas_call | solution.py:199
  131.1 1.5 broadcast_in_dim.39
  132.5 5.3 %all-to-all-start.1 = ((f32[32,24,128]{2,1,0:T(8,128)}), f32[32,24,128]{2,1,0:T(8,128)S(1)}, u32[]{:S(2)}, u32[]{:S(2)}) async-start(f32[32,24,128]{2,1,0:T(8,128)} %broadcast_in_dim.39), calls=%async_computation.1 | async-start | bytes 786432 | tf_op jit(solution)/shard_map/all_to_all | solution.py:336
  137.9 6.3 %shard_map.119 = (f32[128,384]{1,0:T(8,128)}, f32[128,384]{1,0:T(8,128)}) custom-call(s32[3]{0:T(128)} %pad_add_fusion.where, bf16[64,3072]{1,0:T(8,128)(2,1)} %copy-done.3, bf16[64,3072]{1,0:T(8,128)(2,1)} %collective-permute-done.16.b1, bf16[64,3072]{1,0:T(8,128)(2,1)} %collective-permute-done.17.b2, bf16[64,3072]{1,0:T(8,128)(2,1)} %collective-permute-done.18.b3, ...), custom_call_target="tpu_custom_call" | custom-call | flops 1 | bytes 1 | tf_op jit(solution)/shard_map/pallas_call | solution.py:199
  144.5 3.9 %all-to-all-done.1 = f32[32,24,128]{2,1,0:T(8,128)S(1)} async-done(((f32[32,24,128]{2,1,0:T(8,128)}), f32[32,24,128]{2,1,0:T(8,128)S(1)}, u32[]{:S(2)}, u32[]{:S(2)}) %all-to-all-start.1) | async-done | bytes 393248 | tf_op jit(solution)/shard_map/all_to_all | solution.py:336
  148.6 0.9 add.86
  149.5 1.6 collective-permute-start.20
  151.1 2.7 %collective-permute-start.21 = (f32[4,8,384]{2,1,0:T(8,128)S(1)}, f32[4,8,384]{2,1,0:T(8,128)S(1)}, u32[]{:S(2)}, u32[]{:S(2)}) collective-permute-start(f32[4,8,384]{2,1,0:T(8,128)S(1)} %get-tuple-element.44), channel_id=1, source_target_pairs={{0,32},{16,48},{32,0},{48,16},{1,33},{17,49},{33,1},{49,17},{2,34}... | collective-permute-start | bytes 147464 | tf_op jit(solution)/shard_map/ppermute | solution.py:354
  153.8 1.4 collective-permute-start.22
  155.9 0.8 collective-permute-done.21
  156.7 1.2 collective-permute-done.22
  (58 shorter events, 5.5 us)
Async XLA Ops:
  2.3 14.3 %copy-start.6 = (bf16[128,384]{1,0:T(8,128)(2,1)}, bf16[128,384]{1,0:T(8,128)(2,1)S(1)}, u32[]{:S(2)}) copy-start(bf16[128,384]{1,0:T(8,128)(2,1)S(1)} %broadcast_multiply_fusion.own) | copy-start | bytes 294916
  3.3 13.3 %collective-permute-start = (bf16[384,384]{1,0:T(8,128)(2,1)S(1)}, bf16[384,384]{1,0:T(8,128)(2,1)S(1)}, u32[]{:S(2)}, u32[]{:S(2)}) collective-permute-start(bf16[384,384]{1,0:T(8,128)(2,1)S(1)} %pad_maximum_fusion), channel_id=1, source_target_pairs={{0,64},{64,0},{1,65},{65,1},{2,66},{66,2},{3,67},{67,3},{4,68},{68... | collective-permute-start | bytes 884744 | tf_op jit(solution)/shard_map/ppermute | solution.py:269
  6.2 17.5 %all-to-all-start = ((f32[32,4,128]{2,1,0:T(4,128)}), f32[32,4,128]{2,1,0:T(4,128)S(1)}, u32[]{:S(2)}, u32[]{:S(2)}) async-start(f32[32,4,128]{2,1,0:T(4,128)} %broadcast_in_dim.18), calls=%async_computation | async-start | bytes 131072 | tf_op jit(solution)/shard_map/all_to_all | solution.py:266
  16.6 48.1 %copy-start.4 = (s32[3]{0:T(128)S(1)}, s32[3]{0:T(128)}, u32[]{:S(2)}) copy-start(s32[3]{0:T(128)} %pad_add_fusion.where) | copy-start | bytes 40
  16.6 0.7 copy-start.5
  23.8 41.0 %copy-start.2 = (bf16[64,3072]{1,0:T(8,128)(2,1)S(1)}, bf16[64,3072]{1,0:T(8,128)(2,1)}, u32[]{:S(2)}) copy-start(bf16[64,3072]{1,0:T(8,128)(2,1)} %get-tuple-element.22.refs_4_) | copy-start | bytes 1179652
  23.8 1.9 %copy-start.10 = (f32[32,4,128]{2,1,0:T(4,128)}, f32[32,4,128]{2,1,0:T(4,128)S(1)}, u32[]{:S(2)}) copy-start(f32[32,4,128]{2,1,0:T(4,128)S(1)} %all-to-all-done.stats) | copy-start | bytes 196612
  23.8 50.8 %copy-start.12 = (s32[128]{0:T(128)S(1)}, s32[128]{0:T(128)}, u32[]{:S(2)}) copy-start(s32[128]{0:T(128)} %param.19) | copy-start | bytes 1540
  23.8 15.8 %collective-permute-start.4 = (bf16[64,3072]{1,0:T(8,128)(2,1)}, bf16[64,3072]{1,0:T(8,128)(2,1)S(1)}, u32[]{:S(2)}, u32[]{:S(2)}) collective-permute-start(bf16[64,3072]{1,0:T(8,128)(2,1)} %get-tuple-element.28), channel_id=1, source_target_pairs={{0,1},{1,2},{2,3},{3,0},{4,5},{5,6},{6,7},{7,4},{8,9},{9,10},{10,1... | collective-permute-start | bytes 1179656 | tf_op jit(solution)/shard_map/ppermute | solution.py:235
  33.4 31.3 %collective-permute-start.1 = (bf16[128,3072]{1,0:T(8,128)(2,1)}, bf16[128,3072]{1,0:T(8,128)(2,1)S(1)}, u32[]{:S(2)}, u32[]{:S(2)}) collective-permute-start(bf16[128,3072]{1,0:T(8,128)(2,1)} %get-tuple-element.25), channel_id=1, source_target_pairs={{0,1},{1,2},{2,3},{3,0},{4,5},{5,6},{6,7},{7,4},{8,9},{9,10},{10,1... | collective-permute-start | bytes 2359304 | tf_op jit(solution)/shard_map/ppermute | solution.py:235
  34.9 29.9 %collective-permute-start.2 = (bf16[128,3072]{1,0:T(8,128)(2,1)}, bf16[128,3072]{1,0:T(8,128)(2,1)S(1)}, u32[]{:S(2)}, u32[]{:S(2)}) collective-permute-start(bf16[128,3072]{1,0:T(8,128)(2,1)} %get-tuple-element.26), channel_id=1, source_target_pairs={{0,2},{1,3},{2,0},{3,1},{4,6},{5,7},{6,4},{7,5},{8,10},{9,11},{10,... | collective-permute-start | bytes 2359304 | tf_op jit(solution)/shard_map/ppermute | solution.py:235
  36.6 28.1 %collective-permute-start.3 = (bf16[128,3072]{1,0:T(8,128)(2,1)}, bf16[128,3072]{1,0:T(8,128)(2,1)S(1)}, u32[]{:S(2)}, u32[]{:S(2)}) collective-permute-start(bf16[128,3072]{1,0:T(8,128)(2,1)} %get-tuple-element.27), channel_id=1, source_target_pairs={{0,3},{1,0},{2,1},{3,2},{4,7},{5,4},{6,5},{7,6},{8,11},{9,8},{10,9... | collective-permute-start | bytes 2359304 | tf_op jit(solution)/shard_map/ppermute | solution.py:235
  38.7 20.7 %collective-permute-start.5 = (bf16[64,3072]{1,0:T(8,128)(2,1)}, bf16[64,3072]{1,0:T(8,128)(2,1)S(1)}, u32[]{:S(2)}, u32[]{:S(2)}) collective-permute-start(bf16[64,3072]{1,0:T(8,128)(2,1)} %get-tuple-element.29), channel_id=1, source_target_pairs={{0,2},{1,3},{2,0},{3,1},{4,6},{5,7},{6,4},{7,5},{8,10},{9,11},{10,... | collective-permute-start | bytes 1179656 | tf_op jit(solution)/shard_map/ppermute | solution.py:235
  39.6 25.1 %collective-permute-start.6 = (bf16[64,3072]{1,0:T(8,128)(2,1)}, bf16[64,3072]{1,0:T(8,128)(2,1)}, u32[]{:S(2)}, u32[]{:S(2)}) collective-permute-start(bf16[64,3072]{1,0:T(8,128)(2,1)} %get-tuple-element.30), channel_id=1, source_target_pairs={{0,3},{1,0},{2,1},{3,2},{4,7},{5,4},{6,5},{7,6},{8,11},{9,8},{10,9... | collective-permute-start | bytes 1179656 | tf_op jit(solution)/shard_map/ppermute | solution.py:235
  64.7 1.1 copy-start
  68.9 8.0 %collective-permute-start.7 = (bf16[48,3072]{1,0:T(8,128)(2,1)S(1)}, bf16[48,3072]{1,0:T(8,128)(2,1)S(1)}, u32[]{:S(2)}, u32[]{:S(2)}) collective-permute-start(bf16[48,3072]{1,0:T(8,128)(2,1)S(1)} %get-tuple-element.32), channel_id=1, source_target_pairs={{0,4},{1,5},{2,6},{3,7},{4,8},{5,9},{6,10},{7,11},{8,12},{9,13},{1... | collective-permute-start | bytes 884744 | tf_op jit(solution)/shard_map/ppermute | solution.py:235
  70.5 10.5 %collective-permute-start.8 = (bf16[48,3072]{1,0:T(8,128)(2,1)S(1)}, bf16[48,3072]{1,0:T(8,128)(2,1)S(1)}, u32[]{:S(2)}, u32[]{:S(2)}) collective-permute-start(bf16[48,3072]{1,0:T(8,128)(2,1)S(1)} %get-tuple-element.33), channel_id=1, source_target_pairs={{0,8},{1,9},{2,10},{3,11},{4,12},{5,13},{6,14},{7,15},{8,0},{9,1},... | collective-permute-start | bytes 884744 | tf_op jit(solution)/shard_map/ppermute | solution.py:235
  73.1 7.9 %collective-permute-start.9 = (bf16[48,3072]{1,0:T(8,128)(2,1)S(1)}, bf16[48,3072]{1,0:T(8,128)(2,1)S(1)}, u32[]{:S(2)}, u32[]{:S(2)}) collective-permute-start(bf16[48,3072]{1,0:T(8,128)(2,1)S(1)} %get-tuple-element.34), channel_id=1, source_target_pairs={{0,12},{1,13},{2,14},{3,15},{4,0},{5,1},{6,2},{7,3},{8,4},{9,5},{1... | collective-permute-start | bytes 884744 | tf_op jit(solution)/shard_map/ppermute | solution.py:235
  82.1 10.1 %collective-permute-start.10 = (bf16[48,3072]{1,0:T(8,128)(2,1)S(1)}, bf16[48,3072]{1,0:T(8,128)(2,1)S(1)}, u32[]{:S(2)}, u32[]{:S(2)}) collective-permute-start(bf16[48,3072]{1,0:T(8,128)(2,1)S(1)} %shard_map.116.refs_0_), channel_id=1, source_target_pairs={{0,12},{1,13},{2,14},{3,15},{4,0},{5,1},{6,2},{7,3},{8,4},{9,5},{1... | collective-permute-start | bytes 884744 | tf_op jit(solution)/shard_map/ppermute | solution.py:235
  84.8 8.3 %collective-permute-start.11 = (bf16[48,3072]{1,0:T(8,128)(2,1)S(1)}, bf16[48,3072]{1,0:T(8,128)(2,1)S(1)}, u32[]{:S(2)}, u32[]{:S(2)}) collective-permute-start(bf16[48,3072]{1,0:T(8,128)(2,1)S(1)} %shard_map.116.refs_0_), channel_id=1, source_target_pairs={{0,8},{1,9},{2,10},{3,11},{4,12},{5,13},{6,14},{7,15},{8,0},{9,1},... | collective-permute-start | bytes 884744 | tf_op jit(solution)/shard_map/ppermute | solution.py:235
  86.2 10.0 %collective-permute-start.12 = (bf16[48,3072]{1,0:T(8,128)(2,1)S(1)}, bf16[48,3072]{1,0:T(8,128)(2,1)S(1)}, u32[]{:S(2)}, u32[]{:S(2)}) collective-permute-start(bf16[48,3072]{1,0:T(8,128)(2,1)S(1)} %shard_map.116.refs_0_), channel_id=1, source_target_pairs={{0,4},{1,5},{2,6},{3,7},{4,8},{5,9},{6,10},{7,11},{8,12},{9,13},{1... | collective-permute-start | bytes 884744 | tf_op jit(solution)/shard_map/ppermute | solution.py:235
  97.0 25.2 %copy-start.1 = (bf16[128,3072]{1,0:T(8,128)(2,1)}, bf16[128,3072]{1,0:T(8,128)(2,1)S(1)}, u32[]{:S(2)}) copy-start(bf16[128,3072]{1,0:T(8,128)(2,1)S(1)} %get-tuple-element.35.b0) | copy-start | bytes 2359300
  97.1 34.0 %copy-start.3 = (bf16[64,3072]{1,0:T(8,128)(2,1)}, bf16[64,3072]{1,0:T(8,128)(2,1)S(1)}, u32[]{:S(2)}) copy-start(bf16[64,3072]{1,0:T(8,128)(2,1)S(1)} %get-tuple-element.39.b0) | copy-start | bytes 1179652
  97.1 20.6 %collective-permute-start.13 = (bf16[128,3072]{1,0:T(8,128)(2,1)S(1)}, bf16[128,3072]{1,0:T(8,128)(2,1)S(1)}, u32[]{:S(2)}, u32[]{:S(2)}) collective-permute-start(bf16[128,3072]{1,0:T(8,128)(2,1)S(1)} %get-tuple-element.35.b0), channel_id=1, source_target_pairs={{0,3},{1,0},{2,1},{3,2},{4,7},{5,4},{6,5},{7,6},{8,11},{9,8},{10,9... | collective-permute-start | bytes 2359304 | tf_op jit(solution)/shard_map/ppermute | solution.py:235
  99.7 22.5 %collective-permute-start.14 = (bf16[128,3072]{1,0:T(8,128)(2,1)S(1)}, bf16[128,3072]{1,0:T(8,128)(2,1)S(1)}, u32[]{:S(2)}, u32[]{:S(2)}) collective-permute-start(bf16[128,3072]{1,0:T(8,128)(2,1)S(1)} %get-tuple-element.35.b0), channel_id=1, source_target_pairs={{0,2},{1,3},{2,0},{3,1},{4,6},{5,7},{6,4},{7,5},{8,10},{9,11},{10,... | collective-permute-start | bytes 2359304 | tf_op jit(solution)/shard_map/ppermute | solution.py:235
  101.1 21.1 %collective-permute-start.15 = (bf16[128,3072]{1,0:T(8,128)(2,1)S(1)}, bf16[128,3072]{1,0:T(8,128)(2,1)S(1)}, u32[]{:S(2)}, u32[]{:S(2)}) collective-permute-start(bf16[128,3072]{1,0:T(8,128)(2,1)S(1)} %get-tuple-element.35.b0), channel_id=1, source_target_pairs={{0,1},{1,2},{2,3},{3,0},{4,5},{5,6},{6,7},{7,4},{8,9},{9,10},{10,1... | collective-permute-start | bytes 2359304 | tf_op jit(solution)/shard_map/ppermute | solution.py:235
  117.7 4.6 %copy-start.7 = (bf16[128,3072]{1,0:T(8,128)(2,1)}, bf16[128,3072]{1,0:T(8,128)(2,1)S(1)}, u32[]{:S(2)}) copy-start(bf16[128,3072]{1,0:T(8,128)(2,1)S(1)} %collective-permute-done.13.b1) | copy-start | bytes 2359300
  117.7 20.2 %collective-permute-start.16 = (bf16[64,3072]{1,0:T(8,128)(2,1)S(1)}, bf16[64,3072]{1,0:T(8,128)(2,1)}, u32[]{:S(2)}, u32[]{:S(2)}) collective-permute-start(bf16[64,3072]{1,0:T(8,128)(2,1)S(1)} %get-tuple-element.39.b0), channel_id=1, source_target_pairs={{0,3},{1,0},{2,1},{3,2},{4,7},{5,4},{6,5},{7,6},{8,11},{9,8},{10,9... | collective-permute-start | bytes 1179656 | tf_op jit(solution)/shard_map/ppermute | solution.py:235
  121.3 16.5 %collective-permute-start.17 = (bf16[64,3072]{1,0:T(8,128)(2,1)S(1)}, bf16[64,3072]{1,0:T(8,128)(2,1)}, u32[]{:S(2)}, u32[]{:S(2)}) collective-permute-start(bf16[64,3072]{1,0:T(8,128)(2,1)S(1)} %get-tuple-element.39.b0), channel_id=1, source_target_pairs={{0,2},{1,3},{2,0},{3,1},{4,6},{5,7},{6,4},{7,5},{8,10},{9,11},{10,... | collective-permute-start | bytes 1179656 | tf_op jit(solution)/shard_map/ppermute | solution.py:235
  121.3 16.6 %collective-permute-start.18 = (bf16[64,3072]{1,0:T(8,128)(2,1)S(1)}, bf16[64,3072]{1,0:T(8,128)(2,1)}, u32[]{:S(2)}, u32[]{:S(2)}) collective-permute-start(bf16[64,3072]{1,0:T(8,128)(2,1)S(1)} %get-tuple-element.39.b0), channel_id=1, source_target_pairs={{0,1},{1,2},{2,3},{3,0},{4,5},{5,6},{6,7},{7,4},{8,9},{9,10},{10,1... | collective-permute-start | bytes 1179656 | tf_op jit(solution)/shard_map/ppermute | solution.py:235
  122.2 0.9 copy-start.8
  122.2 1.1 copy-start.9
  132.5 25.4 %copy-start.11 = (f32[384]{0:T(512)S(1)}, f32[384]{0:T(512)}, u32[]{:S(2)}) copy-start(f32[384]{0:T(512)} %param.18) | copy-start | bytes 4612
  132.5 15.9 %all-to-all-start.1 = ((f32[32,24,128]{2,1,0:T(8,128)}), f32[32,24,128]{2,1,0:T(8,128)S(1)}, u32[]{:S(2)}, u32[]{:S(2)}) async-start(f32[32,24,128]{2,1,0:T(8,128)} %broadcast_in_dim.39), calls=%async_computation.1 | async-start | bytes 786432 | tf_op jit(solution)/shard_map/all_to_all | solution.py:336
  144.2 4.3 %collective-permute-start.19 = (f32[128,384]{1,0:T(8,128)}, f32[128,384]{1,0:T(8,128)S(1)}, u32[]{:S(2)}, u32[]{:S(2)}) collective-permute-start(f32[128,384]{1,0:T(8,128)} %get-tuple-element.41), channel_id=1, source_target_pairs={{0,64},{64,0},{1,65},{65,1},{2,66},{66,2},{3,67},{67,3},{4,68},{68... | collective-permute-start | bytes 589832 | tf_op jit(solution)/shard_map/ppermute | solution.py:347
  149.5 6.4 %collective-permute-start.20 = (f32[4,8,384]{2,1,0:T(8,128)S(1)}, f32[4,8,384]{2,1,0:T(8,128)S(1)}, u32[]{:S(2)}, u32[]{:S(2)}) collective-permute-start(f32[4,8,384]{2,1,0:T(8,128)S(1)} %get-tuple-element.42), channel_id=1, source_target_pairs={{0,16},{16,32},{32,48},{48,0},{1,17},{17,33},{33,49},{49,1},{2,18}... | collective-permute-start | bytes 147464 | tf_op jit(solution)/shard_map/ppermute | solution.py:354
  151.1 5.6 %collective-permute-start.21 = (f32[4,8,384]{2,1,0:T(8,128)S(1)}, f32[4,8,384]{2,1,0:T(8,128)S(1)}, u32[]{:S(2)}, u32[]{:S(2)}) collective-permute-start(f32[4,8,384]{2,1,0:T(8,128)S(1)} %get-tuple-element.44), channel_id=1, source_target_pairs={{0,32},{16,48},{32,0},{48,16},{1,33},{17,49},{33,1},{49,17},{2,34}... | collective-permute-start | bytes 147464 | tf_op jit(solution)/shard_map/ppermute | solution.py:354
  153.8 4.1 %collective-permute-start.22 = (f32[4,8,384]{2,1,0:T(8,128)S(1)}, f32[4,8,384]{2,1,0:T(8,128)S(1)}, u32[]{:S(2)}, u32[]{:S(2)}) collective-permute-start(f32[4,8,384]{2,1,0:T(8,128)S(1)} %get-tuple-element.43), channel_id=1, source_target_pairs={{0,48},{16,0},{32,16},{48,32},{1,49},{17,1},{33,17},{49,33},{2,50}... | collective-permute-start | bytes 147464 | tf_op jit(solution)/shard_map/ppermute | solution.py:354

commit v5 on v4

--- a/solution.py
+++ b/solution.py
@@ -10,8 +10,8 @@
 D = 6144
 BF16 = jnp.bfloat16
 F32 = jnp.float32
-TILE = 512
-WIDE = 1024
+TILE = 1536
+WIDE = 1536
 SMALL = 16 * 2**20
 
 
@@ -60,79 +60,82 @@
     return jnp.dot(sel, x, preferred_element_type=F32).astype(BF16)
 
 
-def grad_partials(where, own, other, w_out, o0, o1, o2, o3, rows):
+def partials(where, f0, f1, g0, g1, r0, r1, gain, w_in, w_out, *rest):
+    outs, (rows_g, g_out, lhs, lhs_gain) = rest[:4], rest[4:]
+
     @pl.when(pl.program_id(0) == 0)
     def _():
-        rows[...] = reorder(row_order(where), jnp.concatenate([own[...], other[...]], axis=0))
-
+        sel = row_order(where)
+
+        def centred(own, other):
+            x = jnp.concatenate([own[...], other[...]], axis=0).astype(F32)
+            mean = jnp.sum(x, axis=1, keepdims=True) / x.shape[1]
+            return ((x - mean) * gain[...]).astype(BF16)
+
+        lhs[0:256, :] = reorder(sel, centred(f0, f1))
+        lhs[256:512, :] = reorder(sel, centred(r0, r1))
+        rows_g[...] = reorder(sel, jnp.concatenate([g0[...], g1[...]], axis=0))
+        a = jnp.broadcast_to(gain[...], (16, gain.shape[1]))
+        for k in range(3):
+            part = a.astype(BF16)
+            lhs_gain[k * 16 : k * 16 + 16, :] = part
+            a = a - part.astype(F32)
+
+    pre = jnp.dot(lhs[...], w_in[...], preferred_element_type=F32).astype(BF16)
     grad = lax.dot_general(
-        rows[...], w_out[...], (((1,), (1,)), ((), ())), preferred_element_type=F32
+        rows_g[...], w_out[...], (((1,), (1,)), ((), ())), preferred_element_type=F32
     ).astype(BF16)
-    for j, o in enumerate((o0, o1, o2, o3)):
-        o[...] = grad[j * 64 : j * 64 + 64]
-
-
-def merged_stats(width, stats, core):
-    part = stats[pl.ds(core * 16, 16)]
-    means, m2 = part[:, 0:2], part[:, 2:4]
-    mean = jnp.sum(means, axis=0) / 16
-    gap = means - mean[None]
-    var = (jnp.sum(m2, axis=0) + width * jnp.sum(gap * gap, axis=0)) / D
-    rows = jnp.concatenate([mean, lax.rsqrt(var + 1e-06), mean, mean], axis=0)
-    return jnp.transpose(rows)
-
-
-def normed_rows(x, merged, k, gain):
-    x = (x[...].astype(F32) - merged[:, k : k + 1]) * merged[:, 2 + k : 3 + k] * gain[...]
-    return x.astype(BF16)
-
-
-def pre_partials(
-    width, where, own_f, own_r, other_f, other_r, stats, gain, w_in, o0, o1, o2, o3, normed_t, lhs
-):
-    @pl.when(pl.program_id(0) == 0)
-    def _():
-        own = merged_stats(width, stats, where[0])
-        other = merged_stats(width, stats, 1 - where[0])
-        x_f = [normed_rows(own_f, own, 0, gain), normed_rows(other_f, other, 0, gain)]
-        x_r = [normed_rows(own_r, own, 1, gain), normed_rows(other_r, other, 1, gain)]
-        sel = row_order(where)
-        rows = jnp.dot(sel, jnp.concatenate(x_f, axis=0), preferred_element_type=F32)
-        lhs[0:256, :] = rows.astype(BF16)
-        normed_t[...] = jnp.transpose(rows).astype(BF16)
-        lhs[256:512, :] = reorder(sel, jnp.concatenate(x_r, axis=0))
-
-    pre = jnp.dot(lhs[...], w_in[...], preferred_element_type=F32).astype(BF16)
-    for j, o in enumerate((o0, o1, o2, o3)):
+    for j, o in enumerate(outs):
         for i in range(4):
-            at = (j * 4 + i) * 16
-            o[i * 32 : i * 32 + 16, :] = pre[at : at + 16]
-            o[i * 32 + 16 : i * 32 + 32, :] = pre[256 + at : 256 + at + 16]
-
-
-def stage_sum(p0, p1, p2, p3, g0, g1, g2, g3, keep, *sends):
+            at, to = (j * 4 + i) * 16, i * 48
+            o[to : to + 16, :] = pre[at : at + 16]
+            o[to + 16 : to + 32, :] = pre[256 + at : 256 + at + 16]
+            o[to + 32 : to + 48, :] = grad[at : at + 16]
+    g = jnp.dot(lhs_gain[...], w_in[...], preferred_element_type=F32)
+    g_out[...] = (g[32:40] + g[16:24]) + g[0:8]
+
+
+def stage_sum(own, a, b, c, keep, *sends):
     for i in range(4):
-        parts = []
-        for rows, (a, b, c, d) in ((32, (p0, p1, p2, p3)), (16, (g0, g1, g2, g3))):
-            at = slice(i * rows, (i + 1) * rows)
-            parts.append(
-                (a[at, :].astype(F32) + b[at, :].astype(F32))
-                + (c[at, :].astype(F32) + d[at, :].astype(F32))
-            )
-        total = jnp.concatenate(parts, axis=0)
+        at = slice(i * 48, i * 48 + 48)
+        total = (own[at, :].astype(F32) + a[at, :].astype(F32)) + (
+            b[at, :].astype(F32) + c[at, :].astype(F32)
+        )
         if i == 0:
             keep[...] = total
         else:
             sends[i - 1][...] = total.astype(BF16)
 
 
-def activate(keep, a, b, c, bias, mask, out):
+def merged(width, means, m2):
+    gap = means - jnp.sum(means, axis=1, keepdims=True) / 16
+    var = (
+        jnp.sum(m2, axis=1, keepdims=True) + width * jnp.sum(gap * gap, axis=1, keepdims=True)
+    ) / D
+    return gap, lax.rsqrt(var + 1e-06)
+
+
+def activate(width, keep, a, b, c, means, m2, g_all, bias, mask, out):
     total = (keep[...] + a[...].astype(F32)) + (b[...].astype(F32) + c[...].astype(F32))
-    pre = total[:32] + bias[...]
+    gap, scale = merged(width, means[...], m2[...])
+    pre = total[:32]
+    for s in range(16):
+        pre = pre + gap[:, s : s + 1] * g_all[s : s + 1, :]
+    pre = scale * pre + bias[...]
     act = gelu_exact(pre)
     out[0:16, :] = act[:16].astype(BF16)
     out[16:32, :] = (total[32:48] * gelu_slope(pre[:16])).astype(BF16)
     out[32:48, :] = (act[16:32].astype(BF16).astype(F32) * mask[...]).astype(BF16)
+
+
+def normalise(width, where, own, other, means, m2, gain, out):
+    x = jnp.concatenate([own[...], other[...]], axis=0).astype(F32)
+    m = means[...]
+    _, scale = merged(width, m, m2[...])
+    mean = jnp.sum(m, axis=1, keepdims=True) / 16
+    x = ((x - mean) * scale * gain[...]).astype(BF16)
+    rows = jnp.dot(row_order(where), x, preferred_element_type=F32)
+    out[...] = jnp.transpose(rows).astype(BF16)
 
 
 def regroup(b0, b1, b2, b3, forget, retain):
@@ -155,7 +158,7 @@
     prod = jnp.abs(w_out[...].astype(F32) * grad_out)
     lanes = (prod[:, 0:128] + prod[:, 128:256]) + prod[:, 256:384]
     term_out = jnp.sum(jnp.transpose(lanes), axis=0, keepdims=True)
-    out[...] = term_in + term_out
+    out[...] = jnp.broadcast_to((term_in + term_out)[None], out.shape)
 
 
 def retain_product(where, b0, b1, b2, b3, w_out, mine, theirs, acc):
@@ -258,66 +261,72 @@
     where = jnp.stack([core, y, z]).astype(jnp.int32)
     gain = ln_gain[None, :]
 
-    tokens = jnp.stack([forget_tokens, retain_tokens]).astype(F32)
+    own_g = forget_cotangent * forget_labels[:, None].astype(BF16)
+    other = lax.ppermute(
+        jnp.concatenate([forget_tokens, own_g, retain_tokens], axis=0), "dp", SWAP
+    )
+
+    def third(k):
+        return (other, (128, width), lambda t, w: (k, 0))
+
+    w_in_tile = (w_in, (width, TILE), lambda t, w: (0, w[0] * steps + t))
+    w_out_tile = (w_out, (TILE, width), lambda t, w: (w[0] * steps + t, 0))
+    *parts, grad_y, g_part = call(
+        partials,
+        where,
+        [whole(forget_tokens), third(0), whole(own_g), third(1), whole(retain_tokens), third(2),
+         whole(gain), w_in_tile, w_out_tile],
+        [out_n(192, half, BF16)] * 4 + [((256, width), BF16, None, None), out_n(8, half, F32)],
+        [pltpu.VMEM((512, width), BF16), pltpu.VMEM((48, width), BF16)],
+        steps,
+    )
+    got = permutes(parts[1:], True)
+
+    tokens = jnp.stack([forget_tokens, retain_tokens, other[:128], other[256:]])
+    tokens, _ = lax.optimization_barrier((tokens, parts[0]))
+    tokens = tokens.astype(F32)
     part_mean = jnp.sum(tokens, axis=2) / width
     centred = tokens - part_mean[..., None]
     part_m2 = jnp.sum(centred * centred, axis=2)
-    stats = jnp.broadcast_to(jnp.concatenate([part_mean, part_m2])[None], (32, 4, 128))
-    stats = lax.all_to_all(stats, ("dp", "col"), 0, 0, tiled=True)
-
-    own_g = forget_cotangent * forget_labels[:, None].astype(BF16)
-    other = lax.ppermute(
-        jnp.concatenate([forget_tokens, own_g, retain_tokens], axis=0), "dp", SWAP
-    )
-
-    def third(k):
-        return (other, (128, width), lambda t, w: (k, 0))
-
-    w_in_tile = (w_in, (width, TILE), lambda t, w: (0, w[0] * steps + t))
-    w_out_tile = (w_out, (TILE, width), lambda t, w: (w[0] * steps + t, 0))
-    *g_parts, grad_y = call(
-        grad_partials,
+    share = jnp.concatenate([part_mean, part_m2, g_part[0].reshape(half // 128, 128)])
+    share = jnp.broadcast_to(share[None], (16,) + share.shape)
+    share = lax.all_to_all(share, "col", 0, 0, tiled=True)
+    g_all = share[:, 8:].reshape(16, half)
+    stats = share[:, 0:8].transpose(1, 2, 0)
+    owned = lax.dynamic_slice_in_dim(stats, (y * 4 + z) * 8, 8, 1)
+    owned = owned.reshape(2, 2, 2, 8, 16).transpose(0, 2, 1, 3, 4).reshape(2, 32, 16)
+    normed_t = call(
+        functools.partial(normalise, width),
         where,
-        [whole(own_g), third(1), w_out_tile],
-        [out_n(64, half, BF16)] * 4 + [((256, width), BF16, None, None)],
+        [whole(forget_tokens), third(0), whole(stats[0:4:2].reshape(256, 16)),
+         whole(stats[4:8:2].reshape(256, 16)), whole(gain)],
+        [((width, 256), BF16, None, None)],
         (),
-        steps,
-    )
-    g_got = permutes(g_parts[1:], True)
-    stats, _ = lax.optimization_barrier((stats, g_parts[0]))
-    *p_parts, normed_t = call(
-        functools.partial(pre_partials, width),
-        where,
-        [whole(forget_tokens), whole(retain_tokens), third(0), third(2), whole(stats),
-         whole(gain), w_in_tile],
-        [out_n(128, half, BF16)] * 4 + [((width, 256), BF16, None, None)],
-        [pltpu.VMEM((512, width), BF16)],
-        steps,
-    )
-    p_got = permutes(p_parts[1:], True)
+        1,
+    )[0]
 
     b_half = lax.dynamic_slice_in_dim(b_in, core * half, half, 0)[None, :]
     ids = row * w_in.shape[1] + core * half + jnp.arange(half, dtype=jnp.int32)
     is_pruned = jnp.any(pruned[:, None] == ids[None, :], axis=0)
     keep = jnp.where(is_pruned, 0.0, 1.0)[None, :]
 
-    def wide(kernel, args, outs):
+    def wide(kernel, args, outs, extra=()):
         return call(
             drop_where(kernel),
             where,
-            [by_n(v, WIDE) for v in args],
+            [by_n(v, WIDE) for v in args] + [whole(v) for v in extra],
             [out_n(rows, half, kind, WIDE) for rows, kind in outs],
             steps=half // WIDE,
             vmem=SMALL,
         )
 
-    sums = wide(
-        stage_sum,
-        [p_parts[0]] + p_got + [g_parts[0]] + g_got,
-        [(48, F32)] + [(48, BF16)] * 3,
-    )
+    sums = wide(stage_sum, [parts[0]] + got, [(48, F32)] + [(48, BF16)] * 3)
     back = permutes(sums[1:], False)
-    block = wide(activate, [sums[0]] + back + [b_half, keep], [(48, BF16)])[0]
+
+    def act(keep, a, b, c, g_all, bias, mask, means, m2, out):
+        activate(width, keep, a, b, c, means, m2, g_all, bias, mask, out)
+
+    block = wide(act, [sums[0]] + back + [g_all, b_half, keep], [(48, BF16)], (owned[0], owned[1]))[0]
     near = permutes([block] * 3, False, -1)
     forget, retain = wide(regroup, [block] + near, [(128, BF16), (64, BF16)])
     far = permutes([forget] * 3, True, -1)
@@ -328,11 +337,10 @@
         saliency_terms,
         where,
         [by_n(v) for v in [forget] + far] + [whole(normed_t), whole(grad_y), w_in_tile, w_out_tile],
-        [out_n(1, half, F32)],
+        [((32, 1, half), F32, (32, 1, TILE), lambda t, w: (0, 0, t))],
         (),
         steps,
     )[0]
-    terms = jnp.broadcast_to(terms.reshape(1, half // 128, 128), (32, half // 128, 128))
     terms = lax.all_to_all(terms, ("dp", "col"), 0, 0, tiled=True)
     saliency = jnp.sum(terms.reshape(2, 16, half), axis=1).reshape(2 * half) / D
 

time: 160 us -> 154 us (0.963)
  local copies, waits for them, and re-layouts: 7.74 us -> 16 us
  Pallas kernels: 33.2 us -> 26.5 us
  waiting for transfers between devices: 60.8 us -> 55.3 us
  starting transfers between devices: 48.5 us -> 45.9 us
    ppermute x18 -> x15, waiting for transfers between devices: 54.9 us -> 26.7 us  [permutes(): lax.ppermute(parts[k], ('dp', 'col'), pairs(first, sign * (k + 1)))]
    all_to_all x1, waiting for transfers between devices: 0.01 us -> 19.8 us  [local(): share = lax.all_to_all(share, 'col', 0, 0, tiled=True)]
    pallas_call x7, Pallas kernels: 33.2 us -> 26.5 us  [call(): pl.pallas_call(kernel, grid_spec=pltpu.PrefetchScalarGridSpec(num_scalar_...]
    unnamed x27 -> x41, local copies, waits for them, and re-layouts: 3.6 us -> 7.26 us
    slice x0 -> x7, local copies, waits for them, and re-layouts: none -> 3.4 us  [the longest x1 0.94 us: local(): g_all = share[:, 8:].reshape(16, half)]
    all_to_all x1, starting transfers between devices: 8.52 us -> 5.59 us  [local(): share = lax.all_to_all(share, 'col', 0, 0, tiled=True)]
    ppermute x18 -> x15, starting transfers between devices: 28.6 us -> 30.4 us  [permutes(): lax.ppermute(parts[k], ('dp', 'col'), pairs(first, sign * (k + 1)))]
    ppermute x3, waiting for transfers between devices: 2.02 us -> 3.83 us  [local(): total = total + lax.ppermute(for_row(row + k), 'row', shift_row(k))]
  transfers between devices with their start and end apart: 25 -> 22, of which waited for: 11 -> 10; matrix products, arithmetic and copies ran while one was open for 5% -> 10% of each run, Pallas kernels for 18% -> 9%
where the time goes in v5:
time: 154 us; the launch traced here: 153 us
  waiting for transfers between devices  55.3 us (36%)
  starting transfers between devices  45.9 us (30%)
  Pallas kernels  26.5 us (17%)
  local copies, waits for them, and re-layouts  16 us (10%)
  other arithmetic  7.97 us (5%)
    ppermute x15, starting transfers between devices, permutes(): lax.ppermute(parts[k], ('dp', 'col'), pairs(first, sign * (k + 1)))  30.4 us
    ppermute x15, waiting for transfers between devices, permutes(): lax.ppermute(parts[k], ('dp', 'col'), pairs(first, sign * (k + 1)))  26.7 us
    pallas_call x7, Pallas kernels, call(): pl.pallas_call(kernel, grid_spec=pltpu.PrefetchScalarGridSpec(num_scalar_...  26.5 us
    all_to_all x1, waiting for transfers between devices, local(): share = lax.all_to_all(share, 'col', 0, 0, tiled=True)  19.8 us
    unnamed x41, local copies, waits for them, and re-layouts  7.26 us
    all_to_all x1, starting transfers between devices, local(): share = lax.all_to_all(share, 'col', 0, 0, tiled=True)  5.59 us
    all_to_all x1, starting transfers between devices, local(): terms = lax.all_to_all(terms, ('dp', 'col'), 0, 0, tiled=True)  5.16 us
    all_to_all x1, waiting for transfers between devices, local(): terms = lax.all_to_all(terms, ('dp', 'col'), 0, 0, tiled=True)  5.05 us
  transfers between devices with their start and end apart: 22, of which 10 were waited for; matrix products, arithmetic and copies ran while one was open for 10% of the time, Pallas kernels for 9%

profile of v5, /device:TPU:0, one launch (start us, length us, event | category | flops | bytes accessed | tf_op | source)
XLA Modules:
  0.0 152.8 jit_solution(17015895794019122328)
XLA Ops:
  1.3 1.0 broadcast_multiply_fusion.g0
  2.3 1.0 pad_maximum_fusion.1
  3.4 1.3 broadcast_in_dim.14.gain
  6.7 7.6 %shard_map.113 = (bf16[192,3072]{1,0:T(8,128)(2,1)}, bf16[192,3072]{1,0:T(8,128)(2,1)}, bf16[192,3072]{1,0:T(8,128)(2,1)}, bf16[192,3072]{1,0:T(8,128)(2,1)}, bf...) custom-call(s32[3]{0:T(128)} %pad_add_fusion.where, bf16[128,384]{1,0:T(8,128)(2,1)} %own.1, bf16[384,384]{1,0:T(8,128)(2,1)} %copy-done.8, ...), custom_call_target="tpu_custom_call" | custom-call | flops 1 | bytes 1 | tf_op jit(solution)/shard_map/pallas_call | solution.py:202
  14.2 1.7 %collective-permute-start.1 = (bf16[192,3072]{1,0:T(8,128)(2,1)}, bf16[192,3072]{1,0:T(8,128)(2,1)S(1)}, u32[]{:S(2)}, u32[]{:S(2)}) collective-permute-start(bf16[192,3072]{1,0:T(8,128)(2,1)} %get-tuple-element.19), channel_id=1, source_target_pairs={{0,1},{1,2},{2,3},{3,0},{4,5},{5,6},{6,7},{7,4},{8,9},{9,10},{10,1... | collective-permute-start | bytes 3538952 | tf_op jit(solution)/shard_map/ppermute | solution.py:238
  15.9 2.9 %collective-permute-start.2 = (bf16[192,3072]{1,0:T(8,128)(2,1)}, bf16[192,3072]{1,0:T(8,128)(2,1)S(1)}, u32[]{:S(2)}, u32[]{:S(2)}) collective-permute-start(bf16[192,3072]{1,0:T(8,128)(2,1)} %get-tuple-element.20), channel_id=1, source_target_pairs={{0,2},{1,3},{2,0},{3,1},{4,6},{5,7},{6,4},{7,5},{8,10},{9,11},{10,... | collective-permute-start | bytes 3538952 | tf_op jit(solution)/shard_map/ppermute | solution.py:238
  18.8 1.3 collective-permute-start.3
  20.2 0.9 slice.31
  21.1 1.0 slice_bitcast_fusion.1
  22.6 0.8 broadcast_in_dim.15
  23.4 5.6 %all-to-all-start = ((f32[16,32,128]{2,1,0:T(8,128)}), f32[16,32,128]{2,1,0:T(8,128)}, u32[]{:S(2)}, u32[]{:S(2)}) async-start(f32[16,32,128]{2,1,0:T(8,128)} %broadcast_in_dim.15), calls=%async_computation | async-start | bytes 524288 | tf_op jit(solution)/shard_map/all_to_all | solution.py:293
  29.0 1.5 compare_reduce_fusion
  31.2 1.3 broadcast_select_fusion
  32.5 19.8 %all-to-all-done = f32[16,32,128]{2,1,0:T(8,128)} async-done(((f32[16,32,128]{2,1,0:T(8,128)}), f32[16,32,128]{2,1,0:T(8,128)}, u32[]{:S(2)}, u32[]{:S(2)}) %all-to-all-start) | async-done | bytes 262176 | tf_op jit(solution)/shard_map/all_to_all | solution.py:293
  52.2 0.9 slice.40
  53.9 1.5 slice_bitcast_fusion.2
  55.4 3.2 %shard_map.114 = (f32[48,3072]{1,0:T(8,128)S(1)}, bf16[48,3072]{1,0:T(8,128)(2,1)}, bf16[48,3072]{1,0:T(8,128)(2,1)}, bf16[48,3072]{1,0:T(8,128)(2,1)}) custom-call(s32[3]{0:T(128)S(1)} %copy-done.7, bf16[192,3072]{1,0:T(8,128)(2,1)S(1)} %copy-done, bf16[192,3072]{1,0:T(8,128)(2,1)S(1)} %collective-permute-done.1.refs_1_, ...), custom_call_target="tpu_custom_call" | custom-call | flops 1 | bytes 1 | tf_op jit(solution)/shard_map/pallas_call | solution.py:202
  58.6 0.8 copy-done.3
  59.4 1.9 %collective-permute-start.5 = (bf16[48,3072]{1,0:T(8,128)(2,1)}, bf16[48,3072]{1,0:T(8,128)(2,1)S(1)}, u32[]{:S(2)}, u32[]{:S(2)}) collective-permute-start(bf16[48,3072]{1,0:T(8,128)(2,1)} %get-tuple-element.24), channel_id=1, source_target_pairs={{0,8},{1,9},{2,10},{3,11},{4,12},{5,13},{6,14},{7,15},{8,0},{9,1},... | collective-permute-start | bytes 884744 | tf_op jit(solution)/shard_map/ppermute | solution.py:238
  61.3 1.5 %collective-permute-start.6 = (bf16[48,3072]{1,0:T(8,128)(2,1)}, bf16[48,3072]{1,0:T(8,128)(2,1)S(1)}, u32[]{:S(2)}, u32[]{:S(2)}) collective-permute-start(bf16[48,3072]{1,0:T(8,128)(2,1)} %get-tuple-element.25), channel_id=1, source_target_pairs={{0,12},{1,13},{2,14},{3,15},{4,0},{5,1},{6,2},{7,3},{8,4},{9,5},{1... | collective-permute-start | bytes 884744 | tf_op jit(solution)/shard_map/ppermute | solution.py:238
  63.0 7.7 %collective-permute-done.4.refs_1_ = bf16[48,3072]{1,0:T(8,128)(2,1)S(1)} collective-permute-done((bf16[48,3072]{1,0:T(8,128)(2,1)}, bf16[48,3072]{1,0:T(8,128)(2,1)S(1)}, u32[]{:S(2)}, u32[]{:S(2)}) %collective-permute-start.4) | collective-permute-done | bytes 294944 | tf_op jit(solution)/shard_map/ppermute | solution.py:238
  70.7 0.9 collective-permute-done.6.refs_3_
  71.6 0.9 copy-done.1
  72.5 1.1 copy-done.4
  74.3 1.9 %shard_map.115.refs_0_ = bf16[48,3072]{1,0:T(8,128)(2,1)S(1)} custom-call(s32[3]{0:T(128)S(1)} %copy-done.7, f32[48,3072]{1,0:T(8,128)S(1)} %copy-done.4, bf16[48,3072]{1,0:T(8,128)(2,1)S(1)} %collective-permute-done.4.refs_1_, bf16[48,3072]{1,0:T(8,128)(2,1)S(1)} %collective-permute-done.5.refs_2_, bf16[48,3072]{1,0:T(8,128)(2,1)S(1)} %collective-permute-done.6.refs_3_, ...), custom_call_target="tpu_custom_call" | custom-call | flops 1 | bytes 1 | tf_op jit(solution)/shard_map/pallas_call | solution.py:202
  76.2 2.6 %collective-permute-start.7 = (bf16[48,3072]{1,0:T(8,128)(2,1)S(1)}, bf16[48,3072]{1,0:T(8,128)(2,1)S(1)}, u32[]{:S(2)}, u32[]{:S(2)}) collective-permute-start(bf16[48,3072]{1,0:T(8,128)(2,1)S(1)} %shard_map.115.refs_0_), channel_id=1, source_target_pairs={{0,12},{1,13},{2,14},{3,15},{4,0},{5,1},{6,2},{7,3},{8,4},{9,5},{1... | collective-permute-start | bytes 884744 | tf_op jit(solution)/shard_map/ppermute | solution.py:238
  78.8 0.9 collective-permute-start.9
  79.7 6.5 %collective-permute-done.7.refs_1_ = bf16[48,3072]{1,0:T(8,128)(2,1)S(1)} collective-permute-done((bf16[48,3072]{1,0:T(8,128)(2,1)S(1)}, bf16[48,3072]{1,0:T(8,128)(2,1)S(1)}, u32[]{:S(2)}, u32[]{:S(2)}) %collective-permute-start.7) | collective-permute-done | bytes 294944 | tf_op jit(solution)/shard_map/ppermute | solution.py:238
  86.2 0.9 collective-permute-done.8.refs_2_
  87.1 2.8 %collective-permute-done.9.refs_3_ = bf16[48,3072]{1,0:T(8,128)(2,1)S(1)} collective-permute-done((bf16[48,3072]{1,0:T(8,128)(2,1)S(1)}, bf16[48,3072]{1,0:T(8,128)(2,1)S(1)}, u32[]{:S(2)}, u32[]{:S(2)}) %collective-permute-start.9) | collective-permute-done | bytes 294944 | tf_op jit(solution)/shard_map/ppermute | solution.py:238
  89.9 0.9 shard_map.116
  90.8 2.4 %collective-permute-start.10 = (bf16[128,3072]{1,0:T(8,128)(2,1)S(1)}, bf16[128,3072]{1,0:T(8,128)(2,1)S(1)}, u32[]{:S(2)}, u32[]{:S(2)}) collective-permute-start(bf16[128,3072]{1,0:T(8,128)(2,1)S(1)} %get-tuple-element.28.b0), channel_id=1, source_target_pairs={{0,3},{1,0},{2,1},{3,2},{4,7},{5,4},{6,5},{7,6},{8,11},{9,8},{10,9... | collective-permute-start | bytes 2359304 | tf_op jit(solution)/shard_map/ppermute | solution.py:238
  93.2 2.6 %collective-permute-start.11 = (bf16[128,3072]{1,0:T(8,128)(2,1)S(1)}, bf16[128,3072]{1,0:T(8,128)(2,1)S(1)}, u32[]{:S(2)}, u32[]{:S(2)}) collective-permute-start(bf16[128,3072]{1,0:T(8,128)(2,1)S(1)} %get-tuple-element.28.b0), channel_id=1, source_target_pairs={{0,2},{1,3},{2,0},{3,1},{4,6},{5,7},{6,4},{7,5},{8,10},{9,11},{10,... | collective-permute-start | bytes 2359304 | tf_op jit(solution)/shard_map/ppermute | solution.py:238
  95.8 7.9 %collective-permute-done.10.b1 = bf16[128,3072]{1,0:T(8,128)(2,1)S(1)} collective-permute-done((bf16[128,3072]{1,0:T(8,128)(2,1)S(1)}, bf16[128,3072]{1,0:T(8,128)(2,1)S(1)}, u32[]{:S(2)}, u32[]{:S(2)}) %collective-permute-start.10) | collective-permute-done | bytes 786464 | tf_op jit(solution)/shard_map/ppermute | solution.py:238
  103.7 2.7 %collective-permute-start.13 = (bf16[64,3072]{1,0:T(8,128)(2,1)S(1)}, bf16[64,3072]{1,0:T(8,128)(2,1)S(1)}, u32[]{:S(2)}, u32[]{:S(2)}) collective-permute-start(bf16[64,3072]{1,0:T(8,128)(2,1)S(1)} %get-tuple-element.31.b0), channel_id=1, source_target_pairs={{0,3},{1,0},{2,1},{3,2},{4,7},{5,4},{6,5},{7,6},{8,11},{9,8},{10,9... | collective-permute-start | bytes 1179656 | tf_op jit(solution)/shard_map/ppermute | solution.py:238
  106.4 9.8 %collective-permute-start.14 = (bf16[64,3072]{1,0:T(8,128)(2,1)S(1)}, bf16[64,3072]{1,0:T(8,128)(2,1)}, u32[]{:S(2)}, u32[]{:S(2)}) collective-permute-start(bf16[64,3072]{1,0:T(8,128)(2,1)S(1)} %get-tuple-element.31.b0), channel_id=1, source_target_pairs={{0,2},{1,3},{2,0},{3,1},{4,6},{5,7},{6,4},{7,5},{8,10},{9,11},{10,... | collective-permute-start | bytes 1179656 | tf_op jit(solution)/shard_map/ppermute | solution.py:238
  116.3 0.7 copy.18
  117.0 0.8 copy.19
  117.8 2.9 %shard_map.117.normed_t = bf16[384,256]{1,0:T(8,128)(2,1)} custom-call(s32[3]{0:T(128)} %pad_add_fusion.where, bf16[128,384]{1,0:T(8,128)(2,1)} %own.1, bf16[384,384]{1,0:T(8,128)(2,1)} %copy-done.8, f32[256,16]{1,0:T(8,128)} %bitcast.60, f32[256,16]{1,0:T(8,128)} %bitcast.61, f32[1,384]{1,0:T(1,128)} %broadcast_in_dim.14.gain), custom_call_target="tpu_custom_call" | custom-call | flops 1 | bytes 1 | tf_op jit(solution)/shard_map/pallas_call | solution.py:202
  120.7 0.9 copy-done.13
  121.6 5.8 %shard_map.118 = f32[32,1,3072]{2,1,0:T(1,128)} custom-call(s32[3]{0:T(128)} %pad_add_fusion.where, bf16[128,3072]{1,0:T(8,128)(2,1)} %copy-done.2, bf16[128,3072]{1,0:T(8,128)(2,1)} %copy-done.12, bf16[128,3072]{1,0:T(8,128)(2,1)} %copy-done.13, bf16[128,3072]{1,0:T(8,128)(2,1)} %collective-permute-done.12.b3, bf16[384,256]{1,0:T(8,128)(2,1)} %shard_map.117.normed_t, ...), custom_call_target="tpu_custom_call" | custom-call | flops 1 | bytes 1 | tf_op jit(solution)/shard_map/pallas_call | solution.py:202
  127.4 5.2 %all-to-all-start.1 = ((f32[32,1,3072]{2,1,0:T(1,128)}), f32[32,1,3072]{2,1,0:T(1,128)S(1)}, u32[]{:S(2)}, u32[]{:S(2)}) async-start(f32[32,1,3072]{2,1,0:T(1,128)} %shard_map.118), calls=%async_computation.1 | async-start | bytes 786432 | tf_op jit(solution)/shard_map/all_to_all | solution.py:344
  133.3 4.3 %shard_map.119 = (f32[128,384]{1,0:T(8,128)}, f32[128,384]{1,0:T(8,128)}) custom-call(s32[3]{0:T(128)} %pad_add_fusion.where, bf16[64,3072]{1,0:T(8,128)(2,1)} %copy-done.5, bf16[64,3072]{1,0:T(8,128)(2,1)} %copy-done.14, bf16[64,3072]{1,0:T(8,128)(2,1)} %collective-permute-done.14.b2, bf16[64,3072]{1,0:T(8,128)(2,1)} %collective-permute-done.15.b3, ...), custom_call_target="tpu_custom_call" | custom-call | flops 1 | bytes 1 | tf_op jit(solution)/shard_map/pallas_call | solution.py:202
  137.9 5.0 %all-to-all-done.1 = f32[32,1,3072]{2,1,0:T(1,128)S(1)} async-done(((f32[32,1,3072]{2,1,0:T(1,128)}), f32[32,1,3072]{2,1,0:T(1,128)S(1)}, u32[]{:S(2)}, u32[]{:S(2)}) %all-to-all-start.1) | async-done | bytes 393248 | tf_op jit(solution)/shard_map/all_to_all | solution.py:344
  143.1 2.8 %collective-permute-start.19 = (f32[4,8,384]{2,1,0:T(8,128)S(1)}, f32[4,8,384]{2,1,0:T(8,128)S(1)}, u32[]{:S(2)}, u32[]{:S(2)}) collective-permute-start(f32[4,8,384]{2,1,0:T(8,128)S(1)} %get-tuple-element.39), channel_id=1, source_target_pairs={{0,48},{16,0},{32,16},{48,32},{1,49},{17,1},{33,17},{49,33},{2,50}... | collective-permute-start | bytes 147464 | tf_op jit(solution)/shard_map/ppermute | solution.py:362
  146.0 0.8 collective-permute-start.18
  146.8 0.9 collective-permute-start.17
  148.3 3.3 %collective-permute-done.18 = f32[4,8,384]{2,1,0:T(8,128)S(1)} collective-permute-done((f32[4,8,384]{2,1,0:T(8,128)S(1)}, f32[4,8,384]{2,1,0:T(8,128)S(1)}, u32[]{:S(2)}, u32[]{:S(2)}) %collective-permute-start.18) | collective-permute-done | bytes 49184 | tf_op jit(solution)/shard_map/ppermute | solution.py:362
  (76 shorter events, 8.6 us)
Async XLA Ops:
  2.3 3.7 %copy-start.11 = (bf16[128,384]{1,0:T(8,128)(2,1)}, bf16[128,384]{1,0:T(8,128)(2,1)S(1)}, u32[]{:S(2)}) copy-start(bf16[128,384]{1,0:T(8,128)(2,1)S(1)} %broadcast_multiply_fusion.g0) | copy-start | bytes 294916
  3.3 2.6 %collective-permute-start = (bf16[384,384]{1,0:T(8,128)(2,1)S(1)}, bf16[384,384]{1,0:T(8,128)(2,1)S(1)}, u32[]{:S(2)}, u32[]{:S(2)}) collective-permute-start(bf16[384,384]{1,0:T(8,128)(2,1)S(1)} %pad_maximum_fusion.1), channel_id=1, source_target_pairs={{0,64},{64,0},{1,65},{65,1},{2,66},{66,2},{3,67},{67,3},{4,68},{68... | collective-permute-start | bytes 884744 | tf_op jit(solution)/shard_map/ppermute | solution.py:265
  5.9 16.1 %copy-start.9 = (bf16[128,384]{1,0:T(8,128)(2,1)S(1)}, bf16[128,384]{1,0:T(8,128)(2,1)}, u32[]{:S(2)}) copy-start(bf16[128,384]{1,0:T(8,128)(2,1)} %own.1) | copy-start | bytes 294916
  5.9 16.1 %copy-start.10 = (bf16[128,384]{1,0:T(8,128)(2,1)S(1)}, bf16[128,384]{1,0:T(8,128)(2,1)}, u32[]{:S(2)}) copy-start(bf16[128,384]{1,0:T(8,128)(2,1)} %r0.1) | copy-start | bytes 294916
  5.9 0.7 copy-start.8
  14.2 41.2 %collective-permute-start.1 = (bf16[192,3072]{1,0:T(8,128)(2,1)}, bf16[192,3072]{1,0:T(8,128)(2,1)S(1)}, u32[]{:S(2)}, u32[]{:S(2)}) collective-permute-start(bf16[192,3072]{1,0:T(8,128)(2,1)} %get-tuple-element.19), channel_id=1, source_target_pairs={{0,1},{1,2},{2,3},{3,0},{4,5},{5,6},{6,7},{7,4},{8,9},{9,10},{10,1... | collective-permute-start | bytes 3538952 | tf_op jit(solution)/shard_map/ppermute | solution.py:238
  15.9 39.5 %collective-permute-start.2 = (bf16[192,3072]{1,0:T(8,128)(2,1)}, bf16[192,3072]{1,0:T(8,128)(2,1)S(1)}, u32[]{:S(2)}, u32[]{:S(2)}) collective-permute-start(bf16[192,3072]{1,0:T(8,128)(2,1)} %get-tuple-element.20), channel_id=1, source_target_pairs={{0,2},{1,3},{2,0},{3,1},{4,6},{5,7},{6,4},{7,5},{8,10},{9,11},{10,... | collective-permute-start | bytes 3538952 | tf_op jit(solution)/shard_map/ppermute | solution.py:238
  18.8 36.6 %collective-permute-start.3 = (bf16[192,3072]{1,0:T(8,128)(2,1)}, bf16[192,3072]{1,0:T(8,128)(2,1)}, u32[]{:S(2)}, u32[]{:S(2)}) collective-permute-start(bf16[192,3072]{1,0:T(8,128)(2,1)} %get-tuple-element.21), channel_id=1, source_target_pairs={{0,3},{1,0},{2,1},{3,2},{4,7},{5,4},{6,5},{7,6},{8,11},{9,8},{10,9... | collective-permute-start | bytes 3538952 | tf_op jit(solution)/shard_map/ppermute | solution.py:238
  22.1 6.8 %copy-start.17 = (s32[3072]{0:T(1024)S(1)}, s32[3072]{0:T(1024)}, u32[]{:S(2)}) copy-start(s32[3072]{0:T(1024)} %iota_add_fusion) | copy-start | bytes 36868
  22.3 33.1 %copy-start = (bf16[192,3072]{1,0:T(8,128)(2,1)S(1)}, bf16[192,3072]{1,0:T(8,128)(2,1)}, u32[]{:S(2)}) copy-start(bf16[192,3072]{1,0:T(8,128)(2,1)} %get-tuple-element.18.refs_0_) | copy-start | bytes 3538948
  22.3 33.1 %copy-start.7 = (s32[3]{0:T(128)S(1)}, s32[3]{0:T(128)}, u32[]{:S(2)}) copy-start(s32[3]{0:T(128)} %pad_add_fusion.where) | copy-start | bytes 40
  23.4 28.9 %all-to-all-start = ((f32[16,32,128]{2,1,0:T(8,128)}), f32[16,32,128]{2,1,0:T(8,128)}, u32[]{:S(2)}, u32[]{:S(2)}) async-start(f32[16,32,128]{2,1,0:T(8,128)} %broadcast_in_dim.15), calls=%async_computation | async-start | bytes 524288 | tf_op jit(solution)/shard_map/all_to_all | solution.py:293
  58.6 0.8 copy-start.3
  59.4 11.3 %collective-permute-start.4 = (bf16[48,3072]{1,0:T(8,128)(2,1)}, bf16[48,3072]{1,0:T(8,128)(2,1)S(1)}, u32[]{:S(2)}, u32[]{:S(2)}) collective-permute-start(bf16[48,3072]{1,0:T(8,128)(2,1)} %get-tuple-element.23), channel_id=1, source_target_pairs={{0,4},{1,5},{2,6},{3,7},{4,8},{5,9},{6,10},{7,11},{8,12},{9,13},{1... | collective-permute-start | bytes 884744 | tf_op jit(solution)/shard_map/ppermute | solution.py:238
  59.4 11.3 %collective-permute-start.5 = (bf16[48,3072]{1,0:T(8,128)(2,1)}, bf16[48,3072]{1,0:T(8,128)(2,1)S(1)}, u32[]{:S(2)}, u32[]{:S(2)}) collective-permute-start(bf16[48,3072]{1,0:T(8,128)(2,1)} %get-tuple-element.24), channel_id=1, source_target_pairs={{0,8},{1,9},{2,10},{3,11},{4,12},{5,13},{6,14},{7,15},{8,0},{9,1},... | collective-permute-start | bytes 884744 | tf_op jit(solution)/shard_map/ppermute | solution.py:238
  61.3 10.3 %collective-permute-start.6 = (bf16[48,3072]{1,0:T(8,128)(2,1)}, bf16[48,3072]{1,0:T(8,128)(2,1)S(1)}, u32[]{:S(2)}, u32[]{:S(2)}) collective-permute-start(bf16[48,3072]{1,0:T(8,128)(2,1)} %get-tuple-element.25), channel_id=1, source_target_pairs={{0,12},{1,13},{2,14},{3,15},{4,0},{5,1},{6,2},{7,3},{8,4},{9,5},{1... | collective-permute-start | bytes 884744 | tf_op jit(solution)/shard_map/ppermute | solution.py:238
  71.6 0.9 copy-start.1
  72.5 1.1 copy-start.4
  73.6 0.7 copy-start.6
  76.2 40.0 %copy-start.16 = (f32[8,128,16]{1,0,2:T(8,128)S(1)}, f32[8,128,16]{1,0,2:T(8,128)}, u32[]{:S(2)}) copy-start(f32[8,128,16]{1,0,2:T(8,128)} %get-tuple-element.36) | copy-start | bytes 196612
  76.2 10.0 %collective-permute-start.7 = (bf16[48,3072]{1,0:T(8,128)(2,1)S(1)}, bf16[48,3072]{1,0:T(8,128)(2,1)S(1)}, u32[]{:S(2)}, u32[]{:S(2)}) collective-permute-start(bf16[48,3072]{1,0:T(8,128)(2,1)S(1)} %shard_map.115.refs_0_), channel_id=1, source_target_pairs={{0,12},{1,13},{2,14},{3,15},{4,0},{5,1},{6,2},{7,3},{8,4},{9,5},{1... | collective-permute-start | bytes 884744 | tf_op jit(solution)/shard_map/ppermute | solution.py:238
  78.8 8.3 %collective-permute-start.8 = (bf16[48,3072]{1,0:T(8,128)(2,1)S(1)}, bf16[48,3072]{1,0:T(8,128)(2,1)S(1)}, u32[]{:S(2)}, u32[]{:S(2)}) collective-permute-start(bf16[48,3072]{1,0:T(8,128)(2,1)S(1)} %shard_map.115.refs_0_), channel_id=1, source_target_pairs={{0,8},{1,9},{2,10},{3,11},{4,12},{5,13},{6,14},{7,15},{8,0},{9,1},... | collective-permute-start | bytes 884744 | tf_op jit(solution)/shard_map/ppermute | solution.py:238
  78.8 11.1 %collective-permute-start.9 = (bf16[48,3072]{1,0:T(8,128)(2,1)S(1)}, bf16[48,3072]{1,0:T(8,128)(2,1)S(1)}, u32[]{:S(2)}, u32[]{:S(2)}) collective-permute-start(bf16[48,3072]{1,0:T(8,128)(2,1)S(1)} %shard_map.115.refs_0_), channel_id=1, source_target_pairs={{0,4},{1,5},{2,6},{3,7},{4,8},{5,9},{6,10},{7,11},{8,12},{9,13},{1... | collective-permute-start | bytes 884744 | tf_op jit(solution)/shard_map/ppermute | solution.py:238
  90.7 30.0 %copy-start.2 = (bf16[128,3072]{1,0:T(8,128)(2,1)}, bf16[128,3072]{1,0:T(8,128)(2,1)S(1)}, u32[]{:S(2)}) copy-start(bf16[128,3072]{1,0:T(8,128)(2,1)S(1)} %get-tuple-element.28.b0) | copy-start | bytes 2359300
  90.7 36.7 %copy-start.5 = (bf16[64,3072]{1,0:T(8,128)(2,1)}, bf16[64,3072]{1,0:T(8,128)(2,1)S(1)}, u32[]{:S(2)}) copy-start(bf16[64,3072]{1,0:T(8,128)(2,1)S(1)} %get-tuple-element.31.b0) | copy-start | bytes 1179652
  90.8 12.9 %collective-permute-start.10 = (bf16[128,3072]{1,0:T(8,128)(2,1)S(1)}, bf16[128,3072]{1,0:T(8,128)(2,1)S(1)}, u32[]{:S(2)}, u32[]{:S(2)}) collective-permute-start(bf16[128,3072]{1,0:T(8,128)(2,1)S(1)} %get-tuple-element.28.b0), channel_id=1, source_target_pairs={{0,3},{1,0},{2,1},{3,2},{4,7},{5,4},{6,5},{7,6},{8,11},{9,8},{10,9... | collective-permute-start | bytes 2359304 | tf_op jit(solution)/shard_map/ppermute | solution.py:238
  93.2 27.5 %collective-permute-start.11 = (bf16[128,3072]{1,0:T(8,128)(2,1)S(1)}, bf16[128,3072]{1,0:T(8,128)(2,1)S(1)}, u32[]{:S(2)}, u32[]{:S(2)}) collective-permute-start(bf16[128,3072]{1,0:T(8,128)(2,1)S(1)} %get-tuple-element.28.b0), channel_id=1, source_target_pairs={{0,2},{1,3},{2,0},{3,1},{4,6},{5,7},{6,4},{7,5},{8,10},{9,11},{10,... | collective-permute-start | bytes 2359304 | tf_op jit(solution)/shard_map/ppermute | solution.py:238
  95.8 24.9 %collective-permute-start.12 = (bf16[128,3072]{1,0:T(8,128)(2,1)S(1)}, bf16[128,3072]{1,0:T(8,128)(2,1)}, u32[]{:S(2)}, u32[]{:S(2)}) collective-permute-start(bf16[128,3072]{1,0:T(8,128)(2,1)S(1)} %get-tuple-element.28.b0), channel_id=1, source_target_pairs={{0,1},{1,2},{2,3},{3,0},{4,5},{5,6},{6,7},{7,4},{8,9},{9,10},{10,1... | collective-permute-start | bytes 2359304 | tf_op jit(solution)/shard_map/ppermute | solution.py:238
  103.7 17.0 %copy-start.12 = (bf16[128,3072]{1,0:T(8,128)(2,1)}, bf16[128,3072]{1,0:T(8,128)(2,1)S(1)}, u32[]{:S(2)}) copy-start(bf16[128,3072]{1,0:T(8,128)(2,1)S(1)} %collective-permute-done.10.b1) | copy-start | bytes 2359300
  103.7 28.9 %collective-permute-start.13 = (bf16[64,3072]{1,0:T(8,128)(2,1)S(1)}, bf16[64,3072]{1,0:T(8,128)(2,1)S(1)}, u32[]{:S(2)}, u32[]{:S(2)}) collective-permute-start(bf16[64,3072]{1,0:T(8,128)(2,1)S(1)} %get-tuple-element.31.b0), channel_id=1, source_target_pairs={{0,3},{1,0},{2,1},{3,2},{4,7},{5,4},{6,5},{7,6},{8,11},{9,8},{10,9... | collective-permute-start | bytes 1179656 | tf_op jit(solution)/shard_map/ppermute | solution.py:238
  106.4 26.2 %collective-permute-start.14 = (bf16[64,3072]{1,0:T(8,128)(2,1)S(1)}, bf16[64,3072]{1,0:T(8,128)(2,1)}, u32[]{:S(2)}, u32[]{:S(2)}) collective-permute-start(bf16[64,3072]{1,0:T(8,128)(2,1)S(1)} %get-tuple-element.31.b0), channel_id=1, source_target_pairs={{0,2},{1,3},{2,0},{3,1},{4,6},{5,7},{6,4},{7,5},{8,10},{9,11},{10,... | collective-permute-start | bytes 1179656 | tf_op jit(solution)/shard_map/ppermute | solution.py:238
  116.2 16.4 %collective-permute-start.15 = (bf16[64,3072]{1,0:T(8,128)(2,1)S(1)}, bf16[64,3072]{1,0:T(8,128)(2,1)}, u32[]{:S(2)}, u32[]{:S(2)}) collective-permute-start(bf16[64,3072]{1,0:T(8,128)(2,1)S(1)} %get-tuple-element.31.b0), channel_id=1, source_target_pairs={{0,1},{1,2},{2,3},{3,0},{4,5},{5,6},{6,7},{7,4},{8,9},{9,10},{10,1... | collective-permute-start | bytes 1179656 | tf_op jit(solution)/shard_map/ppermute | solution.py:238
  120.7 0.9 copy-start.13
  127.4 15.5 %all-to-all-start.1 = ((f32[32,1,3072]{2,1,0:T(1,128)}), f32[32,1,3072]{2,1,0:T(1,128)S(1)}, u32[]{:S(2)}, u32[]{:S(2)}) async-start(f32[32,1,3072]{2,1,0:T(1,128)} %shard_map.118), calls=%async_computation.1 | async-start | bytes 786432 | tf_op jit(solution)/shard_map/all_to_all | solution.py:344
  132.6 0.8 copy-start.14
  137.7 5.4 %copy-start.15 = (f32[128,384]{1,0:T(8,128)S(1)}, f32[128,384]{1,0:T(8,128)}, u32[]{:S(2)}) copy-start(f32[128,384]{1,0:T(8,128)} %get-tuple-element.32) | copy-start | bytes 589828
  137.7 14.4 %copy-start.18 = (f32[384]{0:T(512)S(1)}, f32[384]{0:T(512)}, u32[]{:S(2)}) copy-start(f32[384]{0:T(512)} %param.18) | copy-start | bytes 4612
  137.7 5.4 %collective-permute-start.16 = (f32[128,384]{1,0:T(8,128)}, f32[128,384]{1,0:T(8,128)S(1)}, u32[]{:S(2)}, u32[]{:S(2)}) collective-permute-start(f32[128,384]{1,0:T(8,128)} %get-tuple-element.33), channel_id=1, source_target_pairs={{0,64},{64,0},{1,65},{65,1},{2,66},{66,2},{3,67},{67,3},{4,68},{68... | collective-permute-start | bytes 589832 | tf_op jit(solution)/shard_map/ppermute | solution.py:355
  143.1 5.1 %collective-permute-start.19 = (f32[4,8,384]{2,1,0:T(8,128)S(1)}, f32[4,8,384]{2,1,0:T(8,128)S(1)}, u32[]{:S(2)}, u32[]{:S(2)}) collective-permute-start(f32[4,8,384]{2,1,0:T(8,128)S(1)} %get-tuple-element.39), channel_id=1, source_target_pairs={{0,48},{16,0},{32,16},{48,32},{1,49},{17,1},{33,17},{49,33},{2,50}... | collective-permute-start | bytes 147464 | tf_op jit(solution)/shard_map/ppermute | solution.py:362
  146.0 5.6 %collective-permute-start.18 = (f32[4,8,384]{2,1,0:T(8,128)S(1)}, f32[4,8,384]{2,1,0:T(8,128)S(1)}, u32[]{:S(2)}, u32[]{:S(2)}) collective-permute-start(f32[4,8,384]{2,1,0:T(8,128)S(1)} %get-tuple-element.40), channel_id=1, source_target_pairs={{0,32},{16,48},{32,0},{48,16},{1,33},{17,49},{33,1},{49,17},{2,34}... | collective-permute-start | bytes 147464 | tf_op jit(solution)/shard_map/ppermute | solution.py:362
  146.8 5.3 %collective-permute-start.17 = (f32[4,8,384]{2,1,0:T(8,128)S(1)}, f32[4,8,384]{2,1,0:T(8,128)S(1)}, u32[]{:S(2)}, u32[]{:S(2)}) collective-permute-start(f32[4,8,384]{2,1,0:T(8,128)S(1)} %get-tuple-element.38), channel_id=1, source_target_pairs={{0,16},{16,32},{32,48},{48,0},{1,17},{17,33},{33,49},{49,1},{2,18}... | collective-permute-start | bytes 147464 | tf_op jit(solution)/shard_map/ppermute | solution.py:362

commit v6 on v5

--- a/solution.py
+++ b/solution.py
@@ -61,7 +61,7 @@
 
 
 def partials(where, f0, f1, g0, g1, r0, r1, gain, w_in, w_out, *rest):
-    outs, (rows_g, g_out, lhs, lhs_gain) = rest[:4], rest[4:]
+    outs, (rows_g, g_out, lhs) = rest[:4], rest[4:]
 
     @pl.when(pl.program_id(0) == 0)
     def _():
@@ -78,10 +78,11 @@
         a = jnp.broadcast_to(gain[...], (16, gain.shape[1]))
         for k in range(3):
             part = a.astype(BF16)
-            lhs_gain[k * 16 : k * 16 + 16, :] = part
+            lhs[512 + k * 16 : 528 + k * 16, :] = part
             a = a - part.astype(F32)
 
-    pre = jnp.dot(lhs[...], w_in[...], preferred_element_type=F32).astype(BF16)
+    product = jnp.dot(lhs[...], w_in[...], preferred_element_type=F32)
+    pre, g = product[:512].astype(BF16), product[512:]
     grad = lax.dot_general(
         rows_g[...], w_out[...], (((1,), (1,)), ((), ())), preferred_element_type=F32
     ).astype(BF16)
@@ -91,7 +92,6 @@
             o[to : to + 16, :] = pre[at : at + 16]
             o[to + 16 : to + 32, :] = pre[256 + at : 256 + at + 16]
             o[to + 32 : to + 48, :] = grad[at : at + 16]
-    g = jnp.dot(lhs_gain[...], w_in[...], preferred_element_type=F32)
     g_out[...] = (g[32:40] + g[16:24]) + g[0:8]
 
 
@@ -107,33 +107,58 @@
             sends[i - 1][...] = total.astype(BF16)
 
 
-def merged(width, means, m2):
-    gap = means - jnp.sum(means, axis=1, keepdims=True) / 16
+def merged(width, means, m2, axis):
+    mean = jnp.sum(means, axis=axis, keepdims=True) / 16
+    gap = means - mean
     var = (
-        jnp.sum(m2, axis=1, keepdims=True) + width * jnp.sum(gap * gap, axis=1, keepdims=True)
+        jnp.sum(m2, axis=axis, keepdims=True)
+        + width * jnp.sum(gap * gap, axis=axis, keepdims=True)
     ) / D
-    return gap, lax.rsqrt(var + 1e-06)
-
-
-def activate(width, keep, a, b, c, means, m2, g_all, bias, mask, out):
+    return gap, mean, lax.rsqrt(var + 1e-06)
+
+
+def activate(width, where, keep, a, b, c, bias, mask, share, out):
+    t = pl.program_id(0)
     total = (keep[...] + a[...].astype(F32)) + (b[...].astype(F32) + c[...].astype(F32))
-    gap, scale = merged(width, means[...], m2[...])
-    pre = total[:32]
-    for s in range(16):
-        pre = pre + gap[:, s : s + 1] * g_all[s : s + 1, :]
-    pre = scale * pre + bias[...]
+    token = lax.broadcasted_iota(jnp.int32, (8, 128), 0) + (where[1] * 4 + where[2]) * 8
+    hot = jnp.where(lax.broadcasted_iota(jnp.int32, (8, 128), 1) == token, 1.0, 0.0)
+
+    def pick(first):
+        cols = [
+            lax.dot_general(
+                hot,
+                share[:, first + k, :],
+                (((1,), (1,)), ((), ())),
+                precision=lax.Precision.HIGHEST,
+                preferred_element_type=F32,
+            )
+            for k in (0, 2, 1, 3)
+        ]
+        return jnp.concatenate(cols, axis=0)
+
+    gap, _, scale = merged(width, pick(0), pick(4), 1)
+    blocks = total.shape[1] // 128
+    pre = []
+    for r in range(blocks):
+        part = total[:32, r * 128 : r * 128 + 128]
+        for s in range(16):
+            part = part + gap[:, s : s + 1] * share[s, pl.ds(8 + t * blocks + r, 1), :]
+        pre.append(part)
+    pre = scale * jnp.concatenate(pre, axis=1) + bias[...]
     act = gelu_exact(pre)
     out[0:16, :] = act[:16].astype(BF16)
     out[16:32, :] = (total[32:48] * gelu_slope(pre[:16])).astype(BF16)
     out[32:48, :] = (act[16:32].astype(BF16).astype(F32) * mask[...]).astype(BF16)
 
 
-def normalise(width, where, own, other, means, m2, gain, out):
-    x = jnp.concatenate([own[...], other[...]], axis=0).astype(F32)
-    m = means[...]
-    _, scale = merged(width, m, m2[...])
-    mean = jnp.sum(m, axis=1, keepdims=True) / 16
-    x = ((x - mean) * scale * gain[...]).astype(BF16)
+def normalise(width, where, own, other, share, gain, out):
+    normed = []
+    for x, k in ((own, 0), (other, 2)):
+        _, mean, scale = merged(width, share[:, k, :], share[:, k + 4, :], 0)
+        rows = jnp.concatenate([mean, scale, mean, mean, mean, mean, mean, mean], axis=0)
+        cols = jnp.transpose(rows)
+        normed.append((x[...].astype(F32) - cols[:, 0:1]) * cols[:, 1:2] * gain[...])
+    x = jnp.concatenate(normed, axis=0).astype(BF16)
     rows = jnp.dot(row_order(where), x, preferred_element_type=F32)
     out[...] = jnp.transpose(rows).astype(BF16)
 
@@ -262,27 +287,24 @@
     gain = ln_gain[None, :]
 
     own_g = forget_cotangent * forget_labels[:, None].astype(BF16)
-    other = lax.ppermute(
-        jnp.concatenate([forget_tokens, own_g, retain_tokens], axis=0), "dp", SWAP
-    )
-
-    def third(k):
-        return (other, (128, width), lambda t, w: (k, 0))
+    other_f = lax.ppermute(forget_tokens, "dp", SWAP)
+    other_r = lax.ppermute(retain_tokens, "dp", SWAP)
+    other_g = lax.ppermute(own_g, "dp", SWAP)
 
     w_in_tile = (w_in, (width, TILE), lambda t, w: (0, w[0] * steps + t))
     w_out_tile = (w_out, (TILE, width), lambda t, w: (w[0] * steps + t, 0))
     *parts, grad_y, g_part = call(
         partials,
         where,
-        [whole(forget_tokens), third(0), whole(own_g), third(1), whole(retain_tokens), third(2),
-         whole(gain), w_in_tile, w_out_tile],
+        [whole(v) for v in (forget_tokens, other_f, own_g, other_g, retain_tokens, other_r, gain)]
+        + [w_in_tile, w_out_tile],
         [out_n(192, half, BF16)] * 4 + [((256, width), BF16, None, None), out_n(8, half, F32)],
-        [pltpu.VMEM((512, width), BF16), pltpu.VMEM((48, width), BF16)],
+        [pltpu.VMEM((560, width), BF16)],
         steps,
     )
     got = permutes(parts[1:], True)
 
-    tokens = jnp.stack([forget_tokens, retain_tokens, other[:128], other[256:]])
+    tokens = jnp.stack([forget_tokens, retain_tokens, other_f, other_r])
     tokens, _ = lax.optimization_barrier((tokens, parts[0]))
     tokens = tokens.astype(F32)
     part_mean = jnp.sum(tokens, axis=2) / width
@@ -291,43 +313,41 @@
     share = jnp.concatenate([part_mean, part_m2, g_part[0].reshape(half // 128, 128)])
     share = jnp.broadcast_to(share[None], (16,) + share.shape)
     share = lax.all_to_all(share, "col", 0, 0, tiled=True)
-    g_all = share[:, 8:].reshape(16, half)
-    stats = share[:, 0:8].transpose(1, 2, 0)
-    owned = lax.dynamic_slice_in_dim(stats, (y * 4 + z) * 8, 8, 1)
-    owned = owned.reshape(2, 2, 2, 8, 16).transpose(0, 2, 1, 3, 4).reshape(2, 32, 16)
-    normed_t = call(
-        functools.partial(normalise, width),
-        where,
-        [whole(forget_tokens), third(0), whole(stats[0:4:2].reshape(256, 16)),
-         whole(stats[4:8:2].reshape(256, 16)), whole(gain)],
-        [((width, 256), BF16, None, None)],
-        (),
-        1,
-    )[0]
-
     b_half = lax.dynamic_slice_in_dim(b_in, core * half, half, 0)[None, :]
     ids = row * w_in.shape[1] + core * half + jnp.arange(half, dtype=jnp.int32)
     is_pruned = jnp.any(pruned[:, None] == ids[None, :], axis=0)
     keep = jnp.where(is_pruned, 0.0, 1.0)[None, :]
 
-    def wide(kernel, args, outs, extra=()):
+    def wide(kernel, args, outs, extra=(), vmem=SMALL):
         return call(
             drop_where(kernel),
             where,
             [by_n(v, WIDE) for v in args] + [whole(v) for v in extra],
             [out_n(rows, half, kind, WIDE) for rows, kind in outs],
             steps=half // WIDE,
-            vmem=SMALL,
+            vmem=vmem,
         )
 
     sums = wide(stage_sum, [parts[0]] + got, [(48, F32)] + [(48, BF16)] * 3)
     back = permutes(sums[1:], False)
-
-    def act(keep, a, b, c, g_all, bias, mask, means, m2, out):
-        activate(width, keep, a, b, c, means, m2, g_all, bias, mask, out)
-
-    block = wide(act, [sums[0]] + back + [g_all, b_half, keep], [(48, BF16)], (owned[0], owned[1]))[0]
+    block = call(
+        functools.partial(activate, width),
+        where,
+        [by_n(v, WIDE) for v in [sums[0]] + back + [b_half, keep]] + [whole(share)],
+        [out_n(48, half, BF16, WIDE)],
+        steps=half // WIDE,
+    )[0]
     near = permutes([block] * 3, False, -1)
+    share, _ = lax.optimization_barrier((share, block))
+    normed_t = call(
+        functools.partial(normalise, width),
+        where,
+        [whole(forget_tokens), whole(other_f), whole(share), whole(gain)],
+        [((width, 256), BF16, None, None)],
+        (),
+        1,
+    )[0]
+    near[0], normed_t = lax.optimization_barrier((near[0], normed_t))
     forget, retain = wide(regroup, [block] + near, [(128, BF16), (64, BF16)])
     far = permutes([forget] * 3, True, -1)
     retain, _ = lax.optimization_barrier((retain, far[0]))
@@ -342,7 +362,6 @@
         steps,
     )[0]
     terms = lax.all_to_all(terms, ("dp", "col"), 0, 0, tiled=True)
-    saliency = jnp.sum(terms.reshape(2, 16, half), axis=1).reshape(2 * half) / D
 
     mine, theirs = call(
         retain_product,
@@ -357,9 +376,12 @@
     def for_row(r):
         return lax.dynamic_index_in_dim(mine, (r - y) % 4, 0, keepdims=False)
 
+    from_rows = [lax.ppermute(for_row(row + k), "row", shift_row(k)) for k in (1, 2, 3)]
+    terms, _ = lax.optimization_barrier((terms, from_rows[0]))
+    saliency = jnp.sum(terms.reshape(2, 16, half), axis=1).reshape(2 * half) / D
     total = for_row(row)
-    for k in (1, 2, 3):
-        total = total + lax.ppermute(for_row(row + k), "row", shift_row(k))
+    for part in from_rows:
+        total = total + part
     retain_out = (total + b_out).astype(BF16)
     retain_out = lax.dynamic_slice_in_dim(
         jnp.concatenate([retain_out, retain_out], axis=0), (4 - z) % 4, 4, 0

time: 154 us -> 140 us (0.909)
  local copies, waits for them, and re-layouts: 16 us -> 10.4 us
  waiting for transfers between devices: 55.3 us -> 50.5 us
  starting transfers between devices: 45.9 us -> 42.2 us
  Pallas kernels: 26.5 us -> 29.1 us
    all_to_all x1, waiting for transfers between devices: 19.8 us -> 0.01 us  [local(): share = lax.all_to_all(share, 'col', 0, 0, tiled=True)]
    ppermute x15, waiting for transfers between devices: 26.7 us -> 46.1 us  [permutes(): lax.ppermute(parts[k], ('dp', 'col'), pairs(first, sign * (k + 1)))]
    ppermute x15, starting transfers between devices: 30.4 us -> 25.2 us  [permutes(): lax.ppermute(parts[k], ('dp', 'col'), pairs(first, sign * (k + 1)))]
    all_to_all x1, waiting for transfers between devices: 5.05 us -> 0.01 us  [local(): terms = lax.all_to_all(terms, ('dp', 'col'), 0, 0, tiled=True)]
    pallas_call x7, Pallas kernels: 26.5 us -> 29.1 us  [call(): pl.pallas_call(kernel, grid_spec=pltpu.PrefetchScalarGridSpec(num_scalar_...]
    slice x6 -> x0, local copies, waits for them, and re-layouts: 2.5 us -> none  [the longest x1 0.94 us: local(): g_all = share[:, 8:].reshape(16, half)]
    ppermute x4 -> x6, starting transfers between devices: 4.58 us -> 5.86 us  [the longest x3 5.11 us: local(): lax.ppermute(for_row(row + k), 'row', shift_row(k))]
    unnamed x41 -> x42, local copies, waits for them, and re-layouts: 7.26 us -> 6.21 us
  transfers between devices with their start and end apart: 22 -> 24, of which waited for: 10 -> 12; matrix products, arithmetic and copies ran while one was open for 10% -> 8% of each run, Pallas kernels for 9% -> 12%
where the time goes in v6:
time: 140 us; the launch traced here: 139 us
  waiting for transfers between devices  50.5 us (36%)
  starting transfers between devices  42.2 us (30%)
  Pallas kernels  29.1 us (21%)
  local copies, waits for them, and re-layouts  10.4 us (7%)
  other arithmetic  6.47 us (5%)
    ppermute x15, waiting for transfers between devices, permutes(): lax.ppermute(parts[k], ('dp', 'col'), pairs(first, sign * (k + 1)))  46.1 us
    pallas_call x7, Pallas kernels, call(): pl.pallas_call(kernel, grid_spec=pltpu.PrefetchScalarGridSpec(num_scalar_...  29.1 us
    ppermute x15, starting transfers between devices, permutes(): lax.ppermute(parts[k], ('dp', 'col'), pairs(first, sign * (k + 1)))  25.2 us
    unnamed x42, local copies, waits for them, and re-layouts  6.21 us
    all_to_all x1, starting transfers between devices, local(): share = lax.all_to_all(share, 'col', 0, 0, tiled=True)  5.59 us
    all_to_all x1, starting transfers between devices, local(): terms = lax.all_to_all(terms, ('dp', 'col'), 0, 0, tiled=True)  5.21 us
    ppermute x3, starting transfers between devices, local(): lax.ppermute(for_row(row + k), 'row', shift_row(k))  5.11 us
    ppermute x3, waiting for transfers between devices, local(): lax.ppermute(for_row(row + k), 'row', shift_row(k))  3.01 us
  transfers between devices with their start and end apart: 24, of which 12 were waited for; matrix products, arithmetic and copies ran while one was open for 8% of the time, Pallas kernels for 12%

profile of v6, /device:TPU:0, one launch (start us, length us, event | category | flops | bytes accessed | tf_op | source)
XLA Modules:
  0.0 139.5 jit_solution(17118699990847521505)
XLA Ops:
  0.7 0.7 convert_element_type.10
  1.4 1.0 broadcast_multiply_fusion.g0
  3.0 1.3 broadcast_in_dim.14.gain
  4.3 0.6 pad_add_fusion.where
  5.6 0.6 copy-done.11
  6.2 7.5 %shard_map.113 = (bf16[192,3072]{1,0:T(8,128)(2,1)}, bf16[192,3072]{1,0:T(8,128)(2,1)}, bf16[192,3072]{1,0:T(8,128)(2,1)}, bf16[192,3072]{1,0:T(8,128)(2,1)}, bf...) custom-call(s32[3]{0:T(128)} %pad_add_fusion.where, bf16[128,384]{1,0:T(8,128)(2,1)} %own.1, bf16[128,384]{1,0:T(8,128)(2,1)} %copy-done.7, ...), custom_call_target="tpu_custom_call" | custom-call | flops 1 | bytes 1 | tf_op jit(solution)/shard_map/pallas_call | solution.py:227
  13.8 1.7 %collective-permute-start.3 = (bf16[192,3072]{1,0:T(8,128)(2,1)}, bf16[192,3072]{1,0:T(8,128)(2,1)S(1)}, u32[]{:S(2)}, u32[]{:S(2)}) collective-permute-start(bf16[192,3072]{1,0:T(8,128)(2,1)} %get-tuple-element.23), channel_id=1, source_target_pairs={{0,1},{1,2},{2,3},{3,0},{4,5},{5,6},{6,7},{7,4},{8,9},{9,10},{10,1... | collective-permute-start | bytes 3538952 | tf_op jit(solution)/shard_map/ppermute | solution.py:263
  15.5 2.9 %collective-permute-start.4 = (bf16[192,3072]{1,0:T(8,128)(2,1)}, bf16[192,3072]{1,0:T(8,128)(2,1)S(1)}, u32[]{:S(2)}, u32[]{:S(2)}) collective-permute-start(bf16[192,3072]{1,0:T(8,128)(2,1)} %get-tuple-element.24), channel_id=1, source_target_pairs={{0,2},{1,3},{2,0},{3,1},{4,6},{5,7},{6,4},{7,5},{8,10},{9,11},{10,... | collective-permute-start | bytes 3538952 | tf_op jit(solution)/shard_map/ppermute | solution.py:263
  18.4 1.3 collective-permute-start.5
  19.8 0.9 slice.3
  20.7 1.2 pad_maximum_fusion
  22.3 0.7 broadcast_in_dim.30
  23.1 5.6 %all-to-all-start = ((f32[16,32,128]{2,1,0:T(8,128)}), f32[16,32,128]{2,1,0:T(8,128)}, u32[]{:S(2)}, u32[]{:S(2)}) async-start(f32[16,32,128]{2,1,0:T(8,128)} %broadcast_in_dim.30), calls=%async_computation | async-start | bytes 524288 | tf_op jit(solution)/shard_map/all_to_all | solution.py:315
  28.7 2.8 %collective-permute-done.3.refs_1_ = bf16[192,3072]{1,0:T(8,128)(2,1)S(1)} collective-permute-done((bf16[192,3072]{1,0:T(8,128)(2,1)}, bf16[192,3072]{1,0:T(8,128)(2,1)S(1)}, u32[]{:S(2)}, u32[]{:S(2)}) %collective-permute-start.3) | collective-permute-done | bytes 1179680 | tf_op jit(solution)/shard_map/ppermute | solution.py:263
  31.5 15.4 %collective-permute-done.4.refs_2_ = bf16[192,3072]{1,0:T(8,128)(2,1)S(1)} collective-permute-done((bf16[192,3072]{1,0:T(8,128)(2,1)}, bf16[192,3072]{1,0:T(8,128)(2,1)S(1)}, u32[]{:S(2)}, u32[]{:S(2)}) %collective-permute-start.4) | collective-permute-done | bytes 1179680 | tf_op jit(solution)/shard_map/ppermute | solution.py:263
  46.9 3.2 %shard_map.114 = (f32[48,3072]{1,0:T(8,128)S(1)}, bf16[48,3072]{1,0:T(8,128)(2,1)}, bf16[48,3072]{1,0:T(8,128)(2,1)}, bf16[48,3072]{1,0:T(8,128)(2,1)}) custom-call(s32[3]{0:T(128)S(1)} %copy-done.5, bf16[192,3072]{1,0:T(8,128)(2,1)S(1)} %copy-done, bf16[192,3072]{1,0:T(8,128)(2,1)S(1)} %collective-permute-done.3.refs_1_, ...), custom_call_target="tpu_custom_call" | custom-call | flops 1 | bytes 1 | tf_op jit(solution)/shard_map/pallas_call | solution.py:227
  50.1 0.8 copy-done.3
  50.9 1.9 %collective-permute-start.6 = (bf16[48,3072]{1,0:T(8,128)(2,1)}, bf16[48,3072]{1,0:T(8,128)(2,1)S(1)}, u32[]{:S(2)}, u32[]{:S(2)}) collective-permute-start(bf16[48,3072]{1,0:T(8,128)(2,1)} %get-tuple-element.27), channel_id=1, source_target_pairs={{0,4},{1,5},{2,6},{3,7},{4,8},{5,9},{6,10},{7,11},{8,12},{9,13},{1... | collective-permute-start | bytes 884744 | tf_op jit(solution)/shard_map/ppermute | solution.py:263
  52.8 3.6 %collective-permute-start.7 = (bf16[48,3072]{1,0:T(8,128)(2,1)}, bf16[48,3072]{1,0:T(8,128)(2,1)S(1)}, u32[]{:S(2)}, u32[]{:S(2)}) collective-permute-start(bf16[48,3072]{1,0:T(8,128)(2,1)} %get-tuple-element.28), channel_id=1, source_target_pairs={{0,8},{1,9},{2,10},{3,11},{4,12},{5,13},{6,14},{7,15},{8,0},{9,1},... | collective-permute-start | bytes 884744 | tf_op jit(solution)/shard_map/ppermute | solution.py:263
  56.3 1.0 collective-permute-start.8
  57.6 1.3 dynamic_slice.19
  59.8 4.6 %collective-permute-done.7.b = bf16[48,3072]{1,0:T(8,128)(2,1)S(1)} collective-permute-done((bf16[48,3072]{1,0:T(8,128)(2,1)}, bf16[48,3072]{1,0:T(8,128)(2,1)S(1)}, u32[]{:S(2)}, u32[]{:S(2)}) %collective-permute-start.7) | collective-permute-done | bytes 294944 | tf_op jit(solution)/shard_map/ppermute | solution.py:263
  64.4 0.7 copy-done.15
  65.3 4.4 %shard_map.115.refs_0_ = bf16[48,3072]{1,0:T(8,128)(2,1)} custom-call(s32[3]{0:T(128)} %pad_add_fusion.where, f32[48,3072]{1,0:T(8,128)} %copy-done.3, bf16[48,3072]{1,0:T(8,128)(2,1)} %copy-done.14, bf16[48,3072]{1,0:T(8,128)(2,1)} %copy-done.15, bf16[48,3072]{1,0:T(8,128)(2,1)} %copy-done.16, f32[1,3072]{1,0:T(1,128)} %bitcast.40, f32[1,3072]{1,0:T(1,128)} %bitcast.41, ...), custom_call_target="tpu_custom_call" | custom-call | flops 1 | bytes 1 | tf_op jit(solution)/shard_map/pallas_call | solution.py:227
  69.6 2.0 %collective-permute-start.9 = (bf16[48,3072]{1,0:T(8,128)(2,1)}, bf16[48,3072]{1,0:T(8,128)(2,1)S(1)}, u32[]{:S(2)}, u32[]{:S(2)}) collective-permute-start(bf16[48,3072]{1,0:T(8,128)(2,1)} %shard_map.115.refs_0_), channel_id=1, source_target_pairs={{0,12},{1,13},{2,14},{3,15},{4,0},{5,1},{6,2},{7,3},{8,4},{9,5},{1... | collective-permute-start | bytes 884744 | tf_op jit(solution)/shard_map/ppermute | solution.py:263
  71.6 1.4 %collective-permute-start.10 = (bf16[48,3072]{1,0:T(8,128)(2,1)}, bf16[48,3072]{1,0:T(8,128)(2,1)S(1)}, u32[]{:S(2)}, u32[]{:S(2)}) collective-permute-start(bf16[48,3072]{1,0:T(8,128)(2,1)} %shard_map.115.refs_0_), channel_id=1, source_target_pairs={{0,8},{1,9},{2,10},{3,11},{4,12},{5,13},{6,14},{7,15},{8,0},{9,1},... | collective-permute-start | bytes 884744 | tf_op jit(solution)/shard_map/ppermute | solution.py:263
  73.5 3.0 %shard_map.116.normed_t = bf16[384,256]{1,0:T(8,128)(2,1)} custom-call(s32[3]{0:T(128)} %pad_add_fusion.where, bf16[128,384]{1,0:T(8,128)(2,1)} %own.1, bf16[128,384]{1,0:T(8,128)(2,1)} %copy-done.7, f32[16,32,128]{2,1,0:T(8,128)} %all-to-all-done.share, f32[1,384]{1,0:T(1,128)} %broadcast_in_dim.14.gain), custom_call_target="tpu_custom_call" | custom-call | flops 1 | bytes 1 | tf_op jit(solution)/shard_map/pallas_call | solution.py:227
  76.5 2.9 %collective-permute-done.9.refs_1_ = bf16[48,3072]{1,0:T(8,128)(2,1)S(1)} collective-permute-done((bf16[48,3072]{1,0:T(8,128)(2,1)}, bf16[48,3072]{1,0:T(8,128)(2,1)S(1)}, u32[]{:S(2)}, u32[]{:S(2)}) %collective-permute-start.9) | collective-permute-done | bytes 294944 | tf_op jit(solution)/shard_map/ppermute | solution.py:263
  79.3 0.8 collective-permute-done.10.refs_2_
  80.1 3.1 %collective-permute-done.11.refs_3_ = bf16[48,3072]{1,0:T(8,128)(2,1)S(1)} collective-permute-done((bf16[48,3072]{1,0:T(8,128)(2,1)}, bf16[48,3072]{1,0:T(8,128)(2,1)S(1)}, u32[]{:S(2)}, u32[]{:S(2)}) %collective-permute-start.11) | collective-permute-done | bytes 294944 | tf_op jit(solution)/shard_map/ppermute | solution.py:263
  83.2 1.0 copy-done.1
  84.2 0.9 shard_map.117
  85.1 2.5 %collective-permute-start.12 = (bf16[128,3072]{1,0:T(8,128)(2,1)S(1)}, bf16[128,3072]{1,0:T(8,128)(2,1)S(1)}, u32[]{:S(2)}, u32[]{:S(2)}) collective-permute-start(bf16[128,3072]{1,0:T(8,128)(2,1)S(1)} %get-tuple-element.34.b0), channel_id=1, source_target_pairs={{0,3},{1,0},{2,1},{3,2},{4,7},{5,4},{6,5},{7,6},{8,11},{9,8},{10,9... | collective-permute-start | bytes 2359304 | tf_op jit(solution)/shard_map/ppermute | solution.py:263
  87.5 1.4 %collective-permute-start.13 = (bf16[128,3072]{1,0:T(8,128)(2,1)S(1)}, bf16[128,3072]{1,0:T(8,128)(2,1)S(1)}, u32[]{:S(2)}, u32[]{:S(2)}) collective-permute-start(bf16[128,3072]{1,0:T(8,128)(2,1)S(1)} %get-tuple-element.34.b0), channel_id=1, source_target_pairs={{0,2},{1,3},{2,0},{3,1},{4,6},{5,7},{6,4},{7,5},{8,10},{9,11},{10,... | collective-permute-start | bytes 2359304 | tf_op jit(solution)/shard_map/ppermute | solution.py:263
  89.5 16.0 %collective-permute-done.12.b1 = bf16[128,3072]{1,0:T(8,128)(2,1)S(1)} collective-permute-done((bf16[128,3072]{1,0:T(8,128)(2,1)S(1)}, bf16[128,3072]{1,0:T(8,128)(2,1)S(1)}, u32[]{:S(2)}, u32[]{:S(2)}) %collective-permute-start.12) | collective-permute-done | bytes 786464 | tf_op jit(solution)/shard_map/ppermute | solution.py:263
  105.5 3.7 %collective-permute-start.15 = (bf16[64,3072]{1,0:T(8,128)(2,1)S(1)}, bf16[64,3072]{1,0:T(8,128)(2,1)S(1)}, u32[]{:S(2)}, u32[]{:S(2)}) collective-permute-start(bf16[64,3072]{1,0:T(8,128)(2,1)S(1)} %get-tuple-element.38.b0), channel_id=1, source_target_pairs={{0,3},{1,0},{2,1},{3,2},{4,7},{5,4},{6,5},{7,6},{8,11},{9,8},{10,9... | collective-permute-start | bytes 1179656 | tf_op jit(solution)/shard_map/ppermute | solution.py:263
  109.1 0.9 collective-permute-start.17
  110.0 0.9 copy-done.10
  111.1 5.8 %shard_map.118 = f32[32,1,3072]{2,1,0:T(1,128)} custom-call(s32[3]{0:T(128)} %pad_add_fusion.where, bf16[128,3072]{1,0:T(8,128)(2,1)} %copy-done.2, bf16[128,3072]{1,0:T(8,128)(2,1)} %copy-done.8, bf16[128,3072]{1,0:T(8,128)(2,1)} %copy-done.9, bf16[128,3072]{1,0:T(8,128)(2,1)} %copy-done.10, bf16[384,256]{1,0:T(8,128)(2,1)} %shard_map.116.normed_t, ...), custom_call_target="tpu_custom_call" | custom-call | flops 1 | bytes 1 | tf_op jit(solution)/shard_map/pallas_call | solution.py:227
  116.9 5.2 %all-to-all-start.1 = ((f32[32,1,3072]{2,1,0:T(1,128)}), f32[32,1,3072]{2,1,0:T(1,128)S(1)}, u32[]{:S(2)}, u32[]{:S(2)}) async-start(f32[32,1,3072]{2,1,0:T(1,128)} %shard_map.118), calls=%async_computation.1 | async-start | bytes 786432 | tf_op jit(solution)/shard_map/all_to_all | solution.py:364
  122.9 4.3 %shard_map.119 = (f32[128,384]{1,0:T(8,128)}, f32[128,384]{1,0:T(8,128)}) custom-call(s32[3]{0:T(128)} %pad_add_fusion.where, bf16[64,3072]{1,0:T(8,128)(2,1)} %copy-done.4, bf16[64,3072]{1,0:T(8,128)(2,1)} %copy-done.13, bf16[64,3072]{1,0:T(8,128)(2,1)} %collective-permute-done.16.b2, bf16[64,3072]{1,0:T(8,128)(2,1)} %collective-permute-done.17.b3, ...), custom_call_target="tpu_custom_call" | custom-call | flops 1 | bytes 1 | tf_op jit(solution)/shard_map/pallas_call | solution.py:227
  127.5 1.4 collective-permute-done.18
  128.9 0.9 add.86
  129.9 1.6 %collective-permute-start.19 = (f32[4,8,384]{2,1,0:T(8,128)S(1)}, f32[4,8,384]{2,1,0:T(8,128)S(1)}, u32[]{:S(2)}, u32[]{:S(2)}) collective-permute-start(f32[4,8,384]{2,1,0:T(8,128)S(1)} %get-tuple-element.44), channel_id=1, source_target_pairs={{0,16},{16,32},{32,48},{48,0},{1,17},{17,33},{33,49},{49,1},{2,18}... | collective-permute-start | bytes 147464 | tf_op jit(solution)/shard_map/ppermute | solution.py:379
  131.4 1.8 %collective-permute-start.21 = (f32[4,8,384]{2,1,0:T(8,128)S(1)}, f32[4,8,384]{2,1,0:T(8,128)S(1)}, u32[]{:S(2)}, u32[]{:S(2)}) collective-permute-start(f32[4,8,384]{2,1,0:T(8,128)S(1)} %get-tuple-element.43), channel_id=1, source_target_pairs={{0,48},{16,0},{32,16},{48,32},{1,49},{17,1},{33,17},{49,33},{2,50}... | collective-permute-start | bytes 147464 | tf_op jit(solution)/shard_map/ppermute | solution.py:379
  133.2 1.8 %collective-permute-start.20 = (f32[4,8,384]{2,1,0:T(8,128)S(1)}, f32[4,8,384]{2,1,0:T(8,128)S(1)}, u32[]{:S(2)}, u32[]{:S(2)}) collective-permute-start(f32[4,8,384]{2,1,0:T(8,128)S(1)} %get-tuple-element.42), channel_id=1, source_target_pairs={{0,32},{16,48},{32,0},{48,16},{1,33},{17,49},{33,1},{49,17},{2,34}... | collective-permute-start | bytes 147464 | tf_op jit(solution)/shard_map/ppermute | solution.py:379
  136.0 2.7 %collective-permute-done.20 = f32[4,8,384]{2,1,0:T(8,128)S(1)} collective-permute-done((f32[4,8,384]{2,1,0:T(8,128)S(1)}, f32[4,8,384]{2,1,0:T(8,128)S(1)}, u32[]{:S(2)}, u32[]{:S(2)}) %collective-permute-start.20) | collective-permute-done | bytes 49184 | tf_op jit(solution)/shard_map/ppermute | solution.py:379
  138.8 0.7 fusion.7
  (70 shorter events, 6.5 us)
Async XLA Ops:
  0.6 4.3 %collective-permute-start = (bf16[128,384]{1,0:T(8,128)(2,1)}, bf16[128,384]{1,0:T(8,128)(2,1)S(1)}, u32[]{:S(2)}, u32[]{:S(2)}) collective-permute-start(bf16[128,384]{1,0:T(8,128)(2,1)} %own.1), channel_id=1, source_target_pairs={{0,64},{64,0},{1,65},{65,1},{2,66},{66,2},{3,67},{67,3},{4,68},{68... | collective-permute-start | bytes 294920 | tf_op jit(solution)/shard_map/ppermute | solution.py:290
  2.4 2.6 %copy-start.12 = (bf16[128,384]{1,0:T(8,128)(2,1)}, bf16[128,384]{1,0:T(8,128)(2,1)S(1)}, u32[]{:S(2)}) copy-start(bf16[128,384]{1,0:T(8,128)(2,1)S(1)} %broadcast_multiply_fusion.g0) | copy-start | bytes 294916
  2.4 2.5 %collective-permute-start.1 = (bf16[128,384]{1,0:T(8,128)(2,1)S(1)}, bf16[128,384]{1,0:T(8,128)(2,1)S(1)}, u32[]{:S(2)}, u32[]{:S(2)}) collective-permute-start(bf16[128,384]{1,0:T(8,128)(2,1)S(1)} %broadcast_multiply_fusion.g0), channel_id=1, source_target_pairs={{0,64},{64,0},{1,65},{65,1},{2,66},{66,2},{3,67},{67,3},{4,68},{68... | collective-permute-start | bytes 294920 | tf_op jit(solution)/shard_map/ppermute | solution.py:292
  3.0 2.0 %collective-permute-start.2 = (bf16[128,384]{1,0:T(8,128)(2,1)}, bf16[128,384]{1,0:T(8,128)(2,1)S(1)}, u32[]{:S(2)}, u32[]{:S(2)}) collective-permute-start(bf16[128,384]{1,0:T(8,128)(2,1)} %r0.1), channel_id=1, source_target_pairs={{0,64},{64,0},{1,65},{65,1},{2,66},{66,2},{3,67},{67,3},{4,68},{68... | collective-permute-start | bytes 294920 | tf_op jit(solution)/shard_map/ppermute | solution.py:291
  4.9 0.6 copy-start.7
  4.9 0.7 copy-start.17
  5.6 0.6 copy-start.11
  13.8 17.7 %collective-permute-start.3 = (bf16[192,3072]{1,0:T(8,128)(2,1)}, bf16[192,3072]{1,0:T(8,128)(2,1)S(1)}, u32[]{:S(2)}, u32[]{:S(2)}) collective-permute-start(bf16[192,3072]{1,0:T(8,128)(2,1)} %get-tuple-element.23), channel_id=1, source_target_pairs={{0,1},{1,2},{2,3},{3,0},{4,5},{5,6},{6,7},{7,4},{8,9},{9,10},{10,1... | collective-permute-start | bytes 3538952 | tf_op jit(solution)/shard_map/ppermute | solution.py:263
  15.5 31.4 %collective-permute-start.4 = (bf16[192,3072]{1,0:T(8,128)(2,1)}, bf16[192,3072]{1,0:T(8,128)(2,1)S(1)}, u32[]{:S(2)}, u32[]{:S(2)}) collective-permute-start(bf16[192,3072]{1,0:T(8,128)(2,1)} %get-tuple-element.24), channel_id=1, source_target_pairs={{0,2},{1,3},{2,0},{3,1},{4,6},{5,7},{6,4},{7,5},{8,10},{9,11},{10,... | collective-permute-start | bytes 3538952 | tf_op jit(solution)/shard_map/ppermute | solution.py:263
  18.4 28.5 %collective-permute-start.5 = (bf16[192,3072]{1,0:T(8,128)(2,1)}, bf16[192,3072]{1,0:T(8,128)(2,1)}, u32[]{:S(2)}, u32[]{:S(2)}) collective-permute-start(bf16[192,3072]{1,0:T(8,128)(2,1)} %get-tuple-element.25), channel_id=1, source_target_pairs={{0,3},{1,0},{2,1},{3,2},{4,7},{5,4},{6,5},{7,6},{8,11},{9,8},{10,9... | collective-permute-start | bytes 3538952 | tf_op jit(solution)/shard_map/ppermute | solution.py:263
  20.7 26.2 %copy-start = (bf16[192,3072]{1,0:T(8,128)(2,1)S(1)}, bf16[192,3072]{1,0:T(8,128)(2,1)}, u32[]{:S(2)}) copy-start(bf16[192,3072]{1,0:T(8,128)(2,1)} %get-tuple-element.22.refs_0_) | copy-start | bytes 3538948
  20.7 26.2 %copy-start.5 = (s32[3]{0:T(128)S(1)}, s32[3]{0:T(128)}, u32[]{:S(2)}) copy-start(s32[3]{0:T(128)} %pad_add_fusion.where) | copy-start | bytes 40
  23.1 36.5 %all-to-all-start = ((f32[16,32,128]{2,1,0:T(8,128)}), f32[16,32,128]{2,1,0:T(8,128)}, u32[]{:S(2)}, u32[]{:S(2)}) async-start(f32[16,32,128]{2,1,0:T(8,128)} %broadcast_in_dim.30), calls=%async_computation | async-start | bytes 524288 | tf_op jit(solution)/shard_map/all_to_all | solution.py:315
  28.7 28.7 %copy-start.19 = (s32[128]{0:T(128)S(1)}, s32[128]{0:T(128)}, u32[]{:S(2)}) copy-start(s32[128]{0:T(128)} %param.19) | copy-start | bytes 1540
  50.1 0.8 copy-start.3
  50.9 8.9 %collective-permute-start.6 = (bf16[48,3072]{1,0:T(8,128)(2,1)}, bf16[48,3072]{1,0:T(8,128)(2,1)S(1)}, u32[]{:S(2)}, u32[]{:S(2)}) collective-permute-start(bf16[48,3072]{1,0:T(8,128)(2,1)} %get-tuple-element.27), channel_id=1, source_target_pairs={{0,4},{1,5},{2,6},{3,7},{4,8},{5,9},{6,10},{7,11},{8,12},{9,13},{1... | collective-permute-start | bytes 884744 | tf_op jit(solution)/shard_map/ppermute | solution.py:263
  52.8 11.7 %collective-permute-start.7 = (bf16[48,3072]{1,0:T(8,128)(2,1)}, bf16[48,3072]{1,0:T(8,128)(2,1)S(1)}, u32[]{:S(2)}, u32[]{:S(2)}) collective-permute-start(bf16[48,3072]{1,0:T(8,128)(2,1)} %get-tuple-element.28), channel_id=1, source_target_pairs={{0,8},{1,9},{2,10},{3,11},{4,12},{5,13},{6,14},{7,15},{8,0},{9,1},... | collective-permute-start | bytes 884744 | tf_op jit(solution)/shard_map/ppermute | solution.py:263
  56.3 8.1 %collective-permute-start.8 = (bf16[48,3072]{1,0:T(8,128)(2,1)}, bf16[48,3072]{1,0:T(8,128)(2,1)S(1)}, u32[]{:S(2)}, u32[]{:S(2)}) collective-permute-start(bf16[48,3072]{1,0:T(8,128)(2,1)} %get-tuple-element.29), channel_id=1, source_target_pairs={{0,12},{1,13},{2,14},{3,15},{4,0},{5,1},{6,2},{7,3},{8,4},{9,5},{1... | collective-permute-start | bytes 884744 | tf_op jit(solution)/shard_map/ppermute | solution.py:263
  59.8 4.6 %copy-start.14 = (bf16[48,3072]{1,0:T(8,128)(2,1)}, bf16[48,3072]{1,0:T(8,128)(2,1)S(1)}, u32[]{:S(2)}) copy-start(bf16[48,3072]{1,0:T(8,128)(2,1)S(1)} %collective-permute-done.6.a) | copy-start | bytes 884740
  64.4 0.7 copy-start.15
  64.4 0.9 copy-start.16
  65.3 17.9 %copy-start.6 = (s32[3]{0:T(128)S(1)}, s32[3]{0:T(128)}, u32[]{:S(2)}) copy-start(s32[3]{0:T(128)} %pad_add_fusion.where) | copy-start | bytes 40
  69.6 9.7 %collective-permute-start.9 = (bf16[48,3072]{1,0:T(8,128)(2,1)}, bf16[48,3072]{1,0:T(8,128)(2,1)S(1)}, u32[]{:S(2)}, u32[]{:S(2)}) collective-permute-start(bf16[48,3072]{1,0:T(8,128)(2,1)} %shard_map.115.refs_0_), channel_id=1, source_target_pairs={{0,12},{1,13},{2,14},{3,15},{4,0},{5,1},{6,2},{7,3},{8,4},{9,5},{1... | collective-permute-start | bytes 884744 | tf_op jit(solution)/shard_map/ppermute | solution.py:263
  71.6 8.5 %collective-permute-start.10 = (bf16[48,3072]{1,0:T(8,128)(2,1)}, bf16[48,3072]{1,0:T(8,128)(2,1)S(1)}, u32[]{:S(2)}, u32[]{:S(2)}) collective-permute-start(bf16[48,3072]{1,0:T(8,128)(2,1)} %shard_map.115.refs_0_), channel_id=1, source_target_pairs={{0,8},{1,9},{2,10},{3,11},{4,12},{5,13},{6,14},{7,15},{8,0},{9,1},... | collective-permute-start | bytes 884744 | tf_op jit(solution)/shard_map/ppermute | solution.py:263
  73.0 10.2 %collective-permute-start.11 = (bf16[48,3072]{1,0:T(8,128)(2,1)}, bf16[48,3072]{1,0:T(8,128)(2,1)S(1)}, u32[]{:S(2)}, u32[]{:S(2)}) collective-permute-start(bf16[48,3072]{1,0:T(8,128)(2,1)} %shard_map.115.refs_0_), channel_id=1, source_target_pairs={{0,4},{1,5},{2,6},{3,7},{4,8},{5,9},{6,10},{7,11},{8,12},{9,13},{1... | collective-permute-start | bytes 884744 | tf_op jit(solution)/shard_map/ppermute | solution.py:263
  83.2 1.0 copy-start.1
  85.0 25.9 %copy-start.2 = (bf16[128,3072]{1,0:T(8,128)(2,1)}, bf16[128,3072]{1,0:T(8,128)(2,1)S(1)}, u32[]{:S(2)}) copy-start(bf16[128,3072]{1,0:T(8,128)(2,1)S(1)} %get-tuple-element.34.b0) | copy-start | bytes 2359300
  85.0 31.9 %copy-start.4 = (bf16[64,3072]{1,0:T(8,128)(2,1)}, bf16[64,3072]{1,0:T(8,128)(2,1)S(1)}, u32[]{:S(2)}) copy-start(bf16[64,3072]{1,0:T(8,128)(2,1)S(1)} %get-tuple-element.38.b0) | copy-start | bytes 1179652
  85.1 20.4 %collective-permute-start.12 = (bf16[128,3072]{1,0:T(8,128)(2,1)S(1)}, bf16[128,3072]{1,0:T(8,128)(2,1)S(1)}, u32[]{:S(2)}, u32[]{:S(2)}) collective-permute-start(bf16[128,3072]{1,0:T(8,128)(2,1)S(1)} %get-tuple-element.34.b0), channel_id=1, source_target_pairs={{0,3},{1,0},{2,1},{3,2},{4,7},{5,4},{6,5},{7,6},{8,11},{9,8},{10,9... | collective-permute-start | bytes 2359304 | tf_op jit(solution)/shard_map/ppermute | solution.py:263
  87.5 22.5 %collective-permute-start.13 = (bf16[128,3072]{1,0:T(8,128)(2,1)S(1)}, bf16[128,3072]{1,0:T(8,128)(2,1)S(1)}, u32[]{:S(2)}, u32[]{:S(2)}) collective-permute-start(bf16[128,3072]{1,0:T(8,128)(2,1)S(1)} %get-tuple-element.34.b0), channel_id=1, source_target_pairs={{0,2},{1,3},{2,0},{3,1},{4,6},{5,7},{6,4},{7,5},{8,10},{9,11},{10,... | collective-permute-start | bytes 2359304 | tf_op jit(solution)/shard_map/ppermute | solution.py:263
  88.9 21.1 %collective-permute-start.14 = (bf16[128,3072]{1,0:T(8,128)(2,1)S(1)}, bf16[128,3072]{1,0:T(8,128)(2,1)S(1)}, u32[]{:S(2)}, u32[]{:S(2)}) collective-permute-start(bf16[128,3072]{1,0:T(8,128)(2,1)S(1)} %get-tuple-element.34.b0), channel_id=1, source_target_pairs={{0,1},{1,2},{2,3},{3,0},{4,5},{5,6},{6,7},{7,4},{8,9},{9,10},{10,1... | collective-permute-start | bytes 2359304 | tf_op jit(solution)/shard_map/ppermute | solution.py:263
  105.5 5.4 %copy-start.8 = (bf16[128,3072]{1,0:T(8,128)(2,1)}, bf16[128,3072]{1,0:T(8,128)(2,1)S(1)}, u32[]{:S(2)}) copy-start(bf16[128,3072]{1,0:T(8,128)(2,1)S(1)} %collective-permute-done.12.b1) | copy-start | bytes 2359300
  105.5 16.7 %collective-permute-start.15 = (bf16[64,3072]{1,0:T(8,128)(2,1)S(1)}, bf16[64,3072]{1,0:T(8,128)(2,1)S(1)}, u32[]{:S(2)}, u32[]{:S(2)}) collective-permute-start(bf16[64,3072]{1,0:T(8,128)(2,1)S(1)} %get-tuple-element.38.b0), channel_id=1, source_target_pairs={{0,3},{1,0},{2,1},{3,2},{4,7},{5,4},{6,5},{7,6},{8,11},{9,8},{10,9... | collective-permute-start | bytes 1179656 | tf_op jit(solution)/shard_map/ppermute | solution.py:263
  109.1 13.0 %collective-permute-start.16 = (bf16[64,3072]{1,0:T(8,128)(2,1)S(1)}, bf16[64,3072]{1,0:T(8,128)(2,1)}, u32[]{:S(2)}, u32[]{:S(2)}) collective-permute-start(bf16[64,3072]{1,0:T(8,128)(2,1)S(1)} %get-tuple-element.38.b0), channel_id=1, source_target_pairs={{0,2},{1,3},{2,0},{3,1},{4,6},{5,7},{6,4},{7,5},{8,10},{9,11},{10,... | collective-permute-start | bytes 1179656 | tf_op jit(solution)/shard_map/ppermute | solution.py:263
  109.1 13.3 %collective-permute-start.17 = (bf16[64,3072]{1,0:T(8,128)(2,1)S(1)}, bf16[64,3072]{1,0:T(8,128)(2,1)}, u32[]{:S(2)}, u32[]{:S(2)}) collective-permute-start(bf16[64,3072]{1,0:T(8,128)(2,1)S(1)} %get-tuple-element.38.b0), channel_id=1, source_target_pairs={{0,1},{1,2},{2,3},{3,0},{4,5},{5,6},{6,7},{7,4},{8,9},{9,10},{10,1... | collective-permute-start | bytes 1179656 | tf_op jit(solution)/shard_map/ppermute | solution.py:263
  110.0 1.1 copy-start.9
  110.0 0.9 copy-start.10
  116.9 18.1 %all-to-all-start.1 = ((f32[32,1,3072]{2,1,0:T(1,128)}), f32[32,1,3072]{2,1,0:T(1,128)S(1)}, u32[]{:S(2)}, u32[]{:S(2)}) async-start(f32[32,1,3072]{2,1,0:T(1,128)} %shard_map.118), calls=%async_computation.1 | async-start | bytes 786432 | tf_op jit(solution)/shard_map/all_to_all | solution.py:364
  122.2 0.8 copy-start.13
  127.2 11.5 %copy-start.18 = (f32[384]{0:T(512)S(1)}, f32[384]{0:T(512)}, u32[]{:S(2)}) copy-start(f32[384]{0:T(512)} %param.18) | copy-start | bytes 4612
  127.2 1.7 %collective-permute-start.18 = (f32[128,384]{1,0:T(8,128)}, f32[128,384]{1,0:T(8,128)S(1)}, u32[]{:S(2)}, u32[]{:S(2)}) collective-permute-start(f32[128,384]{1,0:T(8,128)} %get-tuple-element.40), channel_id=1, source_target_pairs={{0,64},{64,0},{1,65},{65,1},{2,66},{66,2},{3,67},{67,3},{4,68},{68... | collective-permute-start | bytes 589832 | tf_op jit(solution)/shard_map/ppermute | solution.py:374
  129.9 5.4 %collective-permute-start.19 = (f32[4,8,384]{2,1,0:T(8,128)S(1)}, f32[4,8,384]{2,1,0:T(8,128)S(1)}, u32[]{:S(2)}, u32[]{:S(2)}) collective-permute-start(f32[4,8,384]{2,1,0:T(8,128)S(1)} %get-tuple-element.44), channel_id=1, source_target_pairs={{0,16},{16,32},{32,48},{48,0},{1,17},{17,33},{33,49},{49,1},{2,18}... | collective-permute-start | bytes 147464 | tf_op jit(solution)/shard_map/ppermute | solution.py:379
  131.4 4.6 %collective-permute-start.21 = (f32[4,8,384]{2,1,0:T(8,128)S(1)}, f32[4,8,384]{2,1,0:T(8,128)S(1)}, u32[]{:S(2)}, u32[]{:S(2)}) collective-permute-start(f32[4,8,384]{2,1,0:T(8,128)S(1)} %get-tuple-element.43), channel_id=1, source_target_pairs={{0,48},{16,0},{32,16},{48,32},{1,49},{17,1},{33,17},{49,33},{2,50}... | collective-permute-start | bytes 147464 | tf_op jit(solution)/shard_map/ppermute | solution.py:379
  133.2 5.6 %collective-permute-start.20 = (f32[4,8,384]{2,1,0:T(8,128)S(1)}, f32[4,8,384]{2,1,0:T(8,128)S(1)}, u32[]{:S(2)}, u32[]{:S(2)}) collective-permute-start(f32[4,8,384]{2,1,0:T(8,128)S(1)} %get-tuple-element.42), channel_id=1, source_target_pairs={{0,32},{16,48},{32,0},{48,16},{1,33},{17,49},{33,1},{49,17},{2,34}... | collective-permute-start | bytes 147464 | tf_op jit(solution)/shard_map/ppermute | solution.py:379

commit v7 on v6

--- a/solution.py
+++ b/solution.py
@@ -11,7 +11,7 @@
 BF16 = jnp.bfloat16
 F32 = jnp.float32
 TILE = 1536
-WIDE = 1536
+WIDE = 3072
 SMALL = 16 * 2**20
 
 
@@ -60,7 +60,7 @@
     return jnp.dot(sel, x, preferred_element_type=F32).astype(BF16)
 
 
-def partials(where, f0, f1, g0, g1, r0, r1, gain, w_in, w_out, *rest):
+def partials(where, f0, f1, g0, g1, r0, r1, l0, l1, gain, w_in, w_out, *rest):
     outs, (rows_g, g_out, lhs) = rest[:4], rest[4:]
 
     @pl.when(pl.program_id(0) == 0)
@@ -74,6 +74,8 @@
 
         lhs[0:256, :] = reorder(sel, centred(f0, f1))
         lhs[256:512, :] = reorder(sel, centred(r0, r1))
+        kept = jnp.concatenate([l0[...], l1[...]], axis=1) == 1
+        sel = jnp.where(kept, sel.astype(F32), 0.0).astype(BF16)
         rows_g[...] = reorder(sel, jnp.concatenate([g0[...], g1[...]], axis=0))
         a = jnp.broadcast_to(gain[...], (16, gain.shape[1]))
         for k in range(3):
@@ -218,7 +220,7 @@
         store(True)
 
 
-def call(kernel, where, args, outs, scratch=(), steps=6, vmem=None):
+def call(kernel, where, args, outs, scratch=(), steps=6, vmem=28 * 2**20):
     def spec(shape, block, index):
         if block is None:
             return pl.BlockSpec(shape, lambda t, w: (0,) * len(shape))
@@ -286,21 +288,24 @@
     where = jnp.stack([core, y, z]).astype(jnp.int32)
     gain = ln_gain[None, :]
 
-    own_g = forget_cotangent * forget_labels[:, None].astype(BF16)
+    labels = forget_labels[None, :]
     other_f = lax.ppermute(forget_tokens, "dp", SWAP)
     other_r = lax.ppermute(retain_tokens, "dp", SWAP)
-    other_g = lax.ppermute(own_g, "dp", SWAP)
+    other_g = lax.ppermute(forget_cotangent, "dp", SWAP)
+    other_labels = lax.ppermute(labels, "dp", SWAP)
 
     w_in_tile = (w_in, (width, TILE), lambda t, w: (0, w[0] * steps + t))
     w_out_tile = (w_out, (TILE, width), lambda t, w: (w[0] * steps + t, 0))
     *parts, grad_y, g_part = call(
         partials,
         where,
-        [whole(v) for v in (forget_tokens, other_f, own_g, other_g, retain_tokens, other_r, gain)]
+        [whole(v) for v in (forget_tokens, other_f, forget_cotangent, other_g)]
+        + [whole(v) for v in (retain_tokens, other_r, labels, other_labels, gain)]
         + [w_in_tile, w_out_tile],
         [out_n(192, half, BF16)] * 4 + [((256, width), BF16, None, None), out_n(8, half, F32)],
         [pltpu.VMEM((560, width), BF16)],
         steps,
+        None,
     )
     got = permutes(parts[1:], True)
 
@@ -350,7 +355,12 @@
     near[0], normed_t = lax.optimization_barrier((near[0], normed_t))
     forget, retain = wide(regroup, [block] + near, [(128, BF16), (64, BF16)])
     far = permutes([forget] * 3, True, -1)
-    retain, _ = lax.optimization_barrier((retain, far[0]))
+    first, last, _ = lax.optimization_barrier((w_in, w_out, forget))
+    first = lax.dynamic_slice_in_dim(first, core * half, half, 1)
+    last = lax.dynamic_slice_in_dim(last, core * half, half, 0)
+    retain, far[0], first, last = lax.optimization_barrier((retain, far[0], first, last))
+    w_in_tile = (first, (width, TILE), lambda t, w: (0, t))
+    w_out_tile = (last, (TILE, width), lambda t, w: (t, 0))
     retain_far = permutes([retain] * 3, True, -1)
 
     terms = call(

time: 140 us -> 132 us (0.943)
  Pallas kernels: 29.1 us -> 21.3 us
  other arithmetic: 6.47 us -> 3.99 us
    pallas_call x7, Pallas kernels: 29.1 us -> 21.3 us  [call(): pl.pallas_call(kernel, grid_spec=pltpu.PrefetchScalarGridSpec(num_scalar_...]
    dynamic_slice x0 -> x2, local copies, waits for them, and re-layouts: none -> 3.76 us  [the longest x1 1.9 us: local(): last = lax.dynamic_slice_in_dim(last, core * half, half, 0)]
    ppermute x15, waiting for transfers between devices: 46.1 us -> 49.4 us  [permutes(): lax.ppermute(parts[k], ('dp', 'col'), pairs(first, sign * (k + 1)))]
    unnamed x42 -> x32, local copies, waits for them, and re-layouts: 6.21 us -> 3.69 us
    ppermute x3, waiting for transfers between devices: 3.01 us -> 0.88 us  [local(): lax.ppermute(for_row(row + k), 'row', shift_row(k))]
  transfers between devices with their start and end apart: 24 -> 25, of which waited for: 12 -> 11; matrix products, arithmetic and copies ran while one was open for 8% -> 9% of each run, Pallas kernels for 12% -> 9%
where the time goes in v7:
time: 132 us
  waiting for transfers between devices  51.9 us (39%)
  starting transfers between devices  43 us (33%)
  Pallas kernels  21.3 us (16%)
  local copies, waits for them, and re-layouts  10.4 us (8%)
  other arithmetic  3.99 us (3%)
    ppermute x15, waiting for transfers between devices, permutes(): lax.ppermute(parts[k], ('dp', 'col'), pairs(first, sign * (k + 1)))  49.4 us
    ppermute x15, starting transfers between devices, permutes(): lax.ppermute(parts[k], ('dp', 'col'), pairs(first, sign * (k + 1)))  25.3 us
    pallas_call x7, Pallas kernels, call(): pl.pallas_call(kernel, grid_spec=pltpu.PrefetchScalarGridSpec(num_scalar_...  21.3 us
    ppermute x3, starting transfers between devices, local(): lax.ppermute(for_row(row + k), 'row', shift_row(k))  5.72 us
    all_to_all x1, starting transfers between devices, local(): share = lax.all_to_all(share, 'col', 0, 0, tiled=True)  5.53 us
    all_to_all x1, starting transfers between devices, local(): terms = lax.all_to_all(terms, ('dp', 'col'), 0, 0, tiled=True)  5.32 us
    unnamed x32, local copies, waits for them, and re-layouts  3.69 us
  transfers between devices with their start and end apart: 25, of which 11 were waited for; matrix products, arithmetic and copies ran while one was open for 9% of the time, Pallas kernels for 9%

profile of v7, /device:TPU:0, one launch (start us, length us, event | category | flops | bytes accessed | tf_op | source)
XLA Modules:
  0.0 131.5 jit_solution(7100089725550041029)
XLA Ops:
  2.3 1.2 broadcast_in_dim.29.gain
  4.2 0.6 copy-done.10
  4.9 7.5 %shard_map.113 = (bf16[192,3072]{1,0:T(8,128)(2,1)}, bf16[192,3072]{1,0:T(8,128)(2,1)}, bf16[192,3072]{1,0:T(8,128)(2,1)}, bf16[192,3072]{1,0:T(8,128)(2,1)}, bf...) custom-call(s32[3]{0:T(128)} %pad_add_fusion.where, bf16[128,384]{1,0:T(8,128)(2,1)} %own.1, bf16[128,384]{1,0:T(8,128)(2,1)} %copy-done.2, ...), custom_call_target="tpu_custom_call" | custom-call | flops 1 | bytes 1 | tf_op jit(solution)/shard_map/pallas_call | solution.py:229
  12.3 1.7 %collective-permute-start.4 = (bf16[192,3072]{1,0:T(8,128)(2,1)}, bf16[192,3072]{1,0:T(8,128)(2,1)S(1)}, u32[]{:S(2)}, u32[]{:S(2)}) collective-permute-start(bf16[192,3072]{1,0:T(8,128)(2,1)} %get-tuple-element.28), channel_id=1, source_target_pairs={{0,1},{1,2},{2,3},{3,0},{4,5},{5,6},{6,7},{7,4},{8,9},{9,10},{10,1... | collective-permute-start | bytes 3538952 | tf_op jit(solution)/shard_map/ppermute | solution.py:265
  14.1 2.9 %collective-permute-start.5 = (bf16[192,3072]{1,0:T(8,128)(2,1)}, bf16[192,3072]{1,0:T(8,128)(2,1)}, u32[]{:S(2)}, u32[]{:S(2)}) collective-permute-start(bf16[192,3072]{1,0:T(8,128)(2,1)} %get-tuple-element.29), channel_id=1, source_target_pairs={{0,2},{1,3},{2,0},{3,1},{4,6},{5,7},{6,4},{7,5},{8,10},{9,11},{10,... | collective-permute-start | bytes 3538952 | tf_op jit(solution)/shard_map/ppermute | solution.py:265
  17.0 1.3 %collective-permute-start.6 = (bf16[192,3072]{1,0:T(8,128)(2,1)}, bf16[192,3072]{1,0:T(8,128)(2,1)}, u32[]{:S(2)}, u32[]{:S(2)}) collective-permute-start(bf16[192,3072]{1,0:T(8,128)(2,1)} %get-tuple-element.30), channel_id=1, source_target_pairs={{0,3},{1,0},{2,1},{3,2},{4,7},{5,4},{6,5},{7,6},{8,11},{9,8},{10,9... | collective-permute-start | bytes 3538952 | tf_op jit(solution)/shard_map/ppermute | solution.py:265
  18.3 1.0 pad_maximum_fusion
  19.3 0.9 slice.3
  20.7 0.7 broadcast_in_dim.33
  21.4 5.5 %all-to-all-start = ((f32[16,32,128]{2,1,0:T(8,128)}), f32[16,32,128]{2,1,0:T(8,128)S(1)}, u32[]{:S(2)}, u32[]{:S(2)}) async-start(f32[16,32,128]{2,1,0:T(8,128)} %broadcast_in_dim.33), calls=%async_computation | async-start | bytes 524288 | tf_op jit(solution)/shard_map/all_to_all | solution.py:320
  27.0 3.1 %collective-permute-done.4.refs_1_ = bf16[192,3072]{1,0:T(8,128)(2,1)S(1)} collective-permute-done((bf16[192,3072]{1,0:T(8,128)(2,1)}, bf16[192,3072]{1,0:T(8,128)(2,1)S(1)}, u32[]{:S(2)}, u32[]{:S(2)}) %collective-permute-start.4) | collective-permute-done | bytes 1179680 | tf_op jit(solution)/shard_map/ppermute | solution.py:265
  30.0 15.5 %collective-permute-done.5.refs_2_ = bf16[192,3072]{1,0:T(8,128)(2,1)} collective-permute-done((bf16[192,3072]{1,0:T(8,128)(2,1)}, bf16[192,3072]{1,0:T(8,128)(2,1)}, u32[]{:S(2)}, u32[]{:S(2)}) %collective-permute-start.5) | collective-permute-done | bytes 1179680 | tf_op jit(solution)/shard_map/ppermute | solution.py:265
  45.5 3.3 %shard_map.114 = (f32[48,3072]{1,0:T(8,128)S(1)}, bf16[48,3072]{1,0:T(8,128)(2,1)}, bf16[48,3072]{1,0:T(8,128)(2,1)}, bf16[48,3072]{1,0:T(8,128)(2,1)}) custom-call(s32[3]{0:T(128)S(1)} %copy-done.6, bf16[192,3072]{1,0:T(8,128)(2,1)S(1)} %copy-done, bf16[192,3072]{1,0:T(8,128)(2,1)S(1)} %collective-permute-done.4.refs_1_, ...), custom_call_target="tpu_custom_call" | custom-call | flops 1 | bytes 1 | tf_op jit(solution)/shard_map/pallas_call | solution.py:229
  48.8 1.9 %collective-permute-start.7 = (bf16[48,3072]{1,0:T(8,128)(2,1)}, bf16[48,3072]{1,0:T(8,128)(2,1)S(1)}, u32[]{:S(2)}, u32[]{:S(2)}) collective-permute-start(bf16[48,3072]{1,0:T(8,128)(2,1)} %get-tuple-element.32), channel_id=1, source_target_pairs={{0,4},{1,5},{2,6},{3,7},{4,8},{5,9},{6,10},{7,11},{8,12},{9,13},{1... | collective-permute-start | bytes 884744 | tf_op jit(solution)/shard_map/ppermute | solution.py:265
  50.8 3.6 %collective-permute-start.8 = (bf16[48,3072]{1,0:T(8,128)(2,1)}, bf16[48,3072]{1,0:T(8,128)(2,1)S(1)}, u32[]{:S(2)}, u32[]{:S(2)}) collective-permute-start(bf16[48,3072]{1,0:T(8,128)(2,1)} %get-tuple-element.33), channel_id=1, source_target_pairs={{0,8},{1,9},{2,10},{3,11},{4,12},{5,13},{6,14},{7,15},{8,0},{9,1},... | collective-permute-start | bytes 884744 | tf_op jit(solution)/shard_map/ppermute | solution.py:265
  54.3 1.0 collective-permute-start.9
  55.7 2.1 %collective-permute-done.7.a = bf16[48,3072]{1,0:T(8,128)(2,1)S(1)} collective-permute-done((bf16[48,3072]{1,0:T(8,128)(2,1)}, bf16[48,3072]{1,0:T(8,128)(2,1)S(1)}, u32[]{:S(2)}, u32[]{:S(2)}) %collective-permute-start.7) | collective-permute-done | bytes 294944 | tf_op jit(solution)/shard_map/ppermute | solution.py:265
  57.8 4.6 %collective-permute-done.8.b = bf16[48,3072]{1,0:T(8,128)(2,1)S(1)} collective-permute-done((bf16[48,3072]{1,0:T(8,128)(2,1)}, bf16[48,3072]{1,0:T(8,128)(2,1)S(1)}, u32[]{:S(2)}, u32[]{:S(2)}) %collective-permute-start.8) | collective-permute-done | bytes 294944 | tf_op jit(solution)/shard_map/ppermute | solution.py:265
  62.4 1.8 %shard_map.115.refs_0_ = bf16[48,3072]{1,0:T(8,128)(2,1)S(1)} custom-call(s32[3]{0:T(128)S(1)} %copy-done.6, f32[48,3072]{1,0:T(8,128)S(1)} %get-tuple-element.31.keep, bf16[48,3072]{1,0:T(8,128)(2,1)S(1)} %collective-permute-done.7.a, bf16[48,3072]{1,0:T(8,128)(2,1)S(1)} %collective-permute-done.8.b, bf16[48,3072]{1,0:T(8,128)(2,1)S(1)} %collective-permute-done.9.c, ...), custom_call_target="tpu_custom_call" | custom-call | flops 1 | bytes 1 | tf_op jit(solution)/shard_map/pallas_call | solution.py:229
  64.2 2.2 %collective-permute-start.10 = (bf16[48,3072]{1,0:T(8,128)(2,1)S(1)}, bf16[48,3072]{1,0:T(8,128)(2,1)S(1)}, u32[]{:S(2)}, u32[]{:S(2)}) collective-permute-start(bf16[48,3072]{1,0:T(8,128)(2,1)S(1)} %shard_map.115.refs_0_), channel_id=1, source_target_pairs={{0,12},{1,13},{2,14},{3,15},{4,0},{5,1},{6,2},{7,3},{8,4},{9,5},{1... | collective-permute-start | bytes 884744 | tf_op jit(solution)/shard_map/ppermute | solution.py:265
  66.4 1.4 %collective-permute-start.11 = (bf16[48,3072]{1,0:T(8,128)(2,1)S(1)}, bf16[48,3072]{1,0:T(8,128)(2,1)S(1)}, u32[]{:S(2)}, u32[]{:S(2)}) collective-permute-start(bf16[48,3072]{1,0:T(8,128)(2,1)S(1)} %shard_map.115.refs_0_), channel_id=1, source_target_pairs={{0,8},{1,9},{2,10},{3,11},{4,12},{5,13},{6,14},{7,15},{8,0},{9,1},... | collective-permute-start | bytes 884744 | tf_op jit(solution)/shard_map/ppermute | solution.py:265
  68.2 1.1 shard_map.116.normed_t
  69.3 4.5 %collective-permute-done.10.refs_1_ = bf16[48,3072]{1,0:T(8,128)(2,1)S(1)} collective-permute-done((bf16[48,3072]{1,0:T(8,128)(2,1)S(1)}, bf16[48,3072]{1,0:T(8,128)(2,1)S(1)}, u32[]{:S(2)}, u32[]{:S(2)}) %collective-permute-start.10) | collective-permute-done | bytes 294944 | tf_op jit(solution)/shard_map/ppermute | solution.py:265
  73.8 0.9 collective-permute-done.11.refs_2_
  74.7 3.1 %collective-permute-done.12.refs_3_ = bf16[48,3072]{1,0:T(8,128)(2,1)S(1)} collective-permute-done((bf16[48,3072]{1,0:T(8,128)(2,1)S(1)}, bf16[48,3072]{1,0:T(8,128)(2,1)S(1)}, u32[]{:S(2)}, u32[]{:S(2)}) %collective-permute-start.12) | collective-permute-done | bytes 294944 | tf_op jit(solution)/shard_map/ppermute | solution.py:265
  77.8 0.6 shard_map.117
  78.4 2.4 %collective-permute-start.13 = (bf16[128,3072]{1,0:T(8,128)(2,1)S(1)}, bf16[128,3072]{1,0:T(8,128)(2,1)S(1)}, u32[]{:S(2)}, u32[]{:S(2)}) collective-permute-start(bf16[128,3072]{1,0:T(8,128)(2,1)S(1)} %get-tuple-element.39.b0), channel_id=1, source_target_pairs={{0,3},{1,0},{2,1},{3,2},{4,7},{5,4},{6,5},{7,6},{8,11},{9,8},{10,9... | collective-permute-start | bytes 2359304 | tf_op jit(solution)/shard_map/ppermute | solution.py:265
  80.7 1.4 %collective-permute-start.14 = (bf16[128,3072]{1,0:T(8,128)(2,1)S(1)}, bf16[128,3072]{1,0:T(8,128)(2,1)S(1)}, u32[]{:S(2)}, u32[]{:S(2)}) collective-permute-start(bf16[128,3072]{1,0:T(8,128)(2,1)S(1)} %get-tuple-element.39.b0), channel_id=1, source_target_pairs={{0,2},{1,3},{2,0},{3,1},{4,6},{5,7},{6,4},{7,5},{8,10},{9,11},{10,... | collective-permute-start | bytes 2359304 | tf_op jit(solution)/shard_map/ppermute | solution.py:265
  82.2 0.6 collective-permute-start.15
  82.7 1.9 %constant_dynamic-slice_fusion.w_out = bf16[3072,384]{1,0:T(8,128)(2,1)S(1)} fusion(bf16[6144,384]{1,0:T(8,128)(2,1)} %w_out.1, s32[]{:T(128)S(6)} %select_n.68), kind=kLoop, calls=%fused_computation.22 | loop fusion | bytes 4718596 | tf_op jit(solution)/shard_map/dynamic_slice | solution.py:360
  84.6 1.9 %constant_dynamic-slice_fusion.1.w_in = bf16[384,3072]{1,0:T(8,128)(2,1)S(1)} fusion(bf16[384,6144]{1,0:T(8,128)(2,1)} %w_in.1, s32[]{:T(128)S(6)} %select_n.68), kind=kLoop, calls=%fused_computation.23 | loop fusion | bytes 4718596 | tf_op jit(solution)/shard_map/dynamic_slice | solution.py:359
  86.5 12.2 %collective-permute-done.13.b1 = bf16[128,3072]{1,0:T(8,128)(2,1)S(1)} collective-permute-done((bf16[128,3072]{1,0:T(8,128)(2,1)S(1)}, bf16[128,3072]{1,0:T(8,128)(2,1)S(1)}, u32[]{:S(2)}, u32[]{:S(2)}) %collective-permute-start.13) | collective-permute-done | bytes 786464 | tf_op jit(solution)/shard_map/ppermute | solution.py:265
  98.7 3.7 %collective-permute-start.16 = (bf16[64,3072]{1,0:T(8,128)(2,1)S(1)}, bf16[64,3072]{1,0:T(8,128)(2,1)S(1)}, u32[]{:S(2)}, u32[]{:S(2)}) collective-permute-start(bf16[64,3072]{1,0:T(8,128)(2,1)S(1)} %get-tuple-element.48.b0), channel_id=1, source_target_pairs={{0,3},{1,0},{2,1},{3,2},{4,7},{5,4},{6,5},{7,6},{8,11},{9,8},{10,9... | collective-permute-start | bytes 1179656 | tf_op jit(solution)/shard_map/ppermute | solution.py:265
  102.4 0.9 collective-permute-start.18
  103.2 3.6 %shard_map.118 = f32[32,1,3072]{2,1,0:T(1,128)} custom-call(s32[3]{0:T(128)S(1)} %copy-done.6, bf16[128,3072]{1,0:T(8,128)(2,1)S(1)} %get-tuple-element.39.b0, bf16[128,3072]{1,0:T(8,128)(2,1)S(1)} %collective-permute-done.13.b1, bf16[128,3072]{1,0:T(8,128)(2,1)S(1)} %collective-permute-done.14.b2, bf16[128,3072]{1,0:T(8,128)(2,1)S(1)} %collective-permute-done.15.b3, ...), custom_call_target="tpu_custom_call" | custom-call | flops 1 | bytes 1 | tf_op jit(solution)/shard_map/pallas_call | solution.py:229
  106.9 5.3 %all-to-all-start.1 = ((f32[32,1,3072]{2,1,0:T(1,128)}), f32[32,1,3072]{2,1,0:T(1,128)}, u32[]{:S(2)}, u32[]{:S(2)}) async-start(f32[32,1,3072]{2,1,0:T(1,128)} %shard_map.118), calls=%async_computation.1 | async-start | bytes 786432 | tf_op jit(solution)/shard_map/all_to_all | solution.py:374
  112.2 3.4 %collective-permute-done.18.b3 = bf16[64,3072]{1,0:T(8,128)(2,1)} collective-permute-done((bf16[64,3072]{1,0:T(8,128)(2,1)S(1)}, bf16[64,3072]{1,0:T(8,128)(2,1)}, u32[]{:S(2)}, u32[]{:S(2)}) %collective-permute-start.18) | collective-permute-done | bytes 393248 | tf_op jit(solution)/shard_map/ppermute | solution.py:265
  115.7 3.4 %shard_map.119 = (f32[128,384]{1,0:T(8,128)S(1)}, f32[128,384]{1,0:T(8,128)}) custom-call(s32[3]{0:T(128)S(1)} %copy-done.6, bf16[64,3072]{1,0:T(8,128)(2,1)S(1)} %get-tuple-element.48.b0, bf16[64,3072]{1,0:T(8,128)(2,1)S(1)} %collective-permute-done.16.b1, bf16[64,3072]{1,0:T(8,128)(2,1)S(1)} %collective-permute-done.17.b2, ...), custom_call_target="tpu_custom_call" | custom-call | flops 1 | bytes 1 | tf_op jit(solution)/shard_map/pallas_call | solution.py:229
  119.1 0.7 copy-done.4
  119.8 1.6 %collective-permute-done.19 = f32[128,384]{1,0:T(8,128)S(1)} collective-permute-done((f32[128,384]{1,0:T(8,128)}, f32[128,384]{1,0:T(8,128)S(1)}, u32[]{:S(2)}, u32[]{:S(2)}) %collective-permute-start.19) | collective-permute-done | bytes 196640 | tf_op jit(solution)/shard_map/ppermute | solution.py:384
  121.5 0.9 add.88
  122.5 1.6 %collective-permute-start.20 = (f32[4,8,384]{2,1,0:T(8,128)S(1)}, f32[4,8,384]{2,1,0:T(8,128)S(1)}, u32[]{:S(2)}, u32[]{:S(2)}) collective-permute-start(f32[4,8,384]{2,1,0:T(8,128)S(1)} %get-tuple-element.54), channel_id=1, source_target_pairs={{0,16},{16,32},{32,48},{48,0},{1,17},{17,33},{33,49},{49,1},{2,18}... | collective-permute-start | bytes 147464 | tf_op jit(solution)/shard_map/ppermute | solution.py:389
  124.0 2.7 %collective-permute-start.21 = (f32[4,8,384]{2,1,0:T(8,128)S(1)}, f32[4,8,384]{2,1,0:T(8,128)S(1)}, u32[]{:S(2)}, u32[]{:S(2)}) collective-permute-start(f32[4,8,384]{2,1,0:T(8,128)S(1)} %get-tuple-element.52), channel_id=1, source_target_pairs={{0,32},{16,48},{32,0},{48,16},{1,33},{17,49},{33,1},{49,17},{2,34}... | collective-permute-start | bytes 147464 | tf_op jit(solution)/shard_map/ppermute | solution.py:389
  126.8 1.4 %collective-permute-start.22 = (f32[4,8,384]{2,1,0:T(8,128)S(1)}, f32[4,8,384]{2,1,0:T(8,128)S(1)}, u32[]{:S(2)}, u32[]{:S(2)}) collective-permute-start(f32[4,8,384]{2,1,0:T(8,128)S(1)} %get-tuple-element.53), channel_id=1, source_target_pairs={{0,48},{16,0},{32,16},{48,32},{1,49},{17,1},{33,17},{49,33},{2,50}... | collective-permute-start | bytes 147464 | tf_op jit(solution)/shard_map/ppermute | solution.py:389
  128.2 1.1 copy.12
  129.3 0.6 copy.13
  130.0 0.9 collective-permute-done.22
  130.9 0.7 fusion.7
  (62 shorter events, 3.6 us)
Async XLA Ops:
  0.6 2.9 %collective-permute-start = (bf16[128,384]{1,0:T(8,128)(2,1)}, bf16[128,384]{1,0:T(8,128)(2,1)S(1)}, u32[]{:S(2)}, u32[]{:S(2)}) collective-permute-start(bf16[128,384]{1,0:T(8,128)(2,1)} %own.1), channel_id=1, source_target_pairs={{0,64},{64,0},{1,65},{65,1},{2,66},{66,2},{3,67},{67,3},{4,68},{68... | collective-permute-start | bytes 294920 | tf_op jit(solution)/shard_map/ppermute | solution.py:292
  0.7 2.8 %collective-permute-start.2 = (bf16[128,384]{1,0:T(8,128)(2,1)}, bf16[128,384]{1,0:T(8,128)(2,1)S(1)}, u32[]{:S(2)}, u32[]{:S(2)}) collective-permute-start(bf16[128,384]{1,0:T(8,128)(2,1)} %r0.1), channel_id=1, source_target_pairs={{0,64},{64,0},{1,65},{65,1},{2,66},{66,2},{3,67},{67,3},{4,68},{68... | collective-permute-start | bytes 294920 | tf_op jit(solution)/shard_map/ppermute | solution.py:293
  1.2 2.3 %collective-permute-start.3 = (s32[1,128]{1,0:T(1,128)}, s32[1,128]{1,0:T(1,128)S(1)}, u32[]{:S(2)}, u32[]{:S(2)}) collective-permute-start(s32[1,128]{1,0:T(1,128)} %bitcast.45), channel_id=1, source_target_pairs={{0,64},{64,0},{1,65},{65,1},{2,66},{66,2},{3,67},{67,3},{4,68},{68... | collective-permute-start | bytes 1544 | tf_op jit(solution)/shard_map/ppermute | solution.py:295
  1.3 2.3 %collective-permute-start.1 = (bf16[128,384]{1,0:T(8,128)(2,1)}, bf16[128,384]{1,0:T(8,128)(2,1)S(1)}, u32[]{:S(2)}, u32[]{:S(2)}) collective-permute-start(bf16[128,384]{1,0:T(8,128)(2,1)} %g0.1), channel_id=1, source_target_pairs={{0,64},{64,0},{1,65},{65,1},{2,66},{66,2},{3,67},{67,3},{4,68},{68... | collective-permute-start | bytes 294920 | tf_op jit(solution)/shard_map/ppermute | solution.py:294
  3.5 14.8 %copy-start.1 = (bf16[128,384]{1,0:T(8,128)(2,1)S(1)}, bf16[128,384]{1,0:T(8,128)(2,1)}, u32[]{:S(2)}) copy-start(bf16[128,384]{1,0:T(8,128)(2,1)} %own.1) | copy-start | bytes 294916
  3.5 14.8 %copy-start.8 = (bf16[128,384]{1,0:T(8,128)(2,1)S(1)}, bf16[128,384]{1,0:T(8,128)(2,1)}, u32[]{:S(2)}) copy-start(bf16[128,384]{1,0:T(8,128)(2,1)} %r0.1) | copy-start | bytes 294916
  3.5 0.5 copy-start.13
  3.6 0.6 copy-start.2
  3.6 0.7 copy-start.9
  4.2 0.6 copy-start.10
  12.3 33.2 %copy-start = (bf16[192,3072]{1,0:T(8,128)(2,1)S(1)}, bf16[192,3072]{1,0:T(8,128)(2,1)}, u32[]{:S(2)}) copy-start(bf16[192,3072]{1,0:T(8,128)(2,1)} %get-tuple-element.27.refs_0_) | copy-start | bytes 3538948
  12.3 33.2 %copy-start.6 = (s32[3]{0:T(128)S(1)}, s32[3]{0:T(128)}, u32[]{:S(2)}) copy-start(s32[3]{0:T(128)} %pad_add_fusion.where) | copy-start | bytes 40
  12.3 17.7 %collective-permute-start.4 = (bf16[192,3072]{1,0:T(8,128)(2,1)}, bf16[192,3072]{1,0:T(8,128)(2,1)S(1)}, u32[]{:S(2)}, u32[]{:S(2)}) collective-permute-start(bf16[192,3072]{1,0:T(8,128)(2,1)} %get-tuple-element.28), channel_id=1, source_target_pairs={{0,1},{1,2},{2,3},{3,0},{4,5},{5,6},{6,7},{7,4},{8,9},{9,10},{10,1... | collective-permute-start | bytes 3538952 | tf_op jit(solution)/shard_map/ppermute | solution.py:265
  14.1 31.4 %collective-permute-start.5 = (bf16[192,3072]{1,0:T(8,128)(2,1)}, bf16[192,3072]{1,0:T(8,128)(2,1)}, u32[]{:S(2)}, u32[]{:S(2)}) collective-permute-start(bf16[192,3072]{1,0:T(8,128)(2,1)} %get-tuple-element.29), channel_id=1, source_target_pairs={{0,2},{1,3},{2,0},{3,1},{4,6},{5,7},{6,4},{7,5},{8,10},{9,11},{10,... | collective-permute-start | bytes 3538952 | tf_op jit(solution)/shard_map/ppermute | solution.py:265
  17.0 28.5 %collective-permute-start.6 = (bf16[192,3072]{1,0:T(8,128)(2,1)}, bf16[192,3072]{1,0:T(8,128)(2,1)}, u32[]{:S(2)}, u32[]{:S(2)}) collective-permute-start(bf16[192,3072]{1,0:T(8,128)(2,1)} %get-tuple-element.30), channel_id=1, source_target_pairs={{0,3},{1,0},{2,1},{3,2},{4,7},{5,4},{6,5},{7,6},{8,11},{9,8},{10,9... | collective-permute-start | bytes 3538952 | tf_op jit(solution)/shard_map/ppermute | solution.py:265
  21.4 34.2 %all-to-all-start = ((f32[16,32,128]{2,1,0:T(8,128)}), f32[16,32,128]{2,1,0:T(8,128)S(1)}, u32[]{:S(2)}, u32[]{:S(2)}) async-start(f32[16,32,128]{2,1,0:T(8,128)} %broadcast_in_dim.33), calls=%async_computation | async-start | bytes 524288 | tf_op jit(solution)/shard_map/all_to_all | solution.py:320
  27.0 28.4 %copy-start.14 = (s32[128]{0:T(128)S(1)}, s32[128]{0:T(128)}, u32[]{:S(2)}) copy-start(s32[128]{0:T(128)} %param.19) | copy-start | bytes 1540
  27.0 28.6 %copy-start.11 = (f32[6144]{0:T(1024)S(1)}, f32[6144]{0:T(1024)}, u32[]{:S(2)}) copy-start(f32[6144]{0:T(1024)} %param.16) | copy-start | bytes 73732
  48.8 19.3 %copy-start.3 = (bf16[128,384]{1,0:T(8,128)(2,1)S(1)}, bf16[128,384]{1,0:T(8,128)(2,1)}, u32[]{:S(2)}) copy-start(bf16[128,384]{1,0:T(8,128)(2,1)} %copy-done.2) | copy-start | bytes 294916
  48.8 19.3 %copy-start.7 = (f32[1,384]{1,0:T(1,128)S(1)}, f32[1,384]{1,0:T(1,128)}, u32[]{:S(2)}) copy-start(f32[1,384]{1,0:T(1,128)} %broadcast_in_dim.29.gain) | copy-start | bytes 4612
  48.8 8.9 %collective-permute-start.7 = (bf16[48,3072]{1,0:T(8,128)(2,1)}, bf16[48,3072]{1,0:T(8,128)(2,1)S(1)}, u32[]{:S(2)}, u32[]{:S(2)}) collective-permute-start(bf16[48,3072]{1,0:T(8,128)(2,1)} %get-tuple-element.32), channel_id=1, source_target_pairs={{0,4},{1,5},{2,6},{3,7},{4,8},{5,9},{6,10},{7,11},{8,12},{9,13},{1... | collective-permute-start | bytes 884744 | tf_op jit(solution)/shard_map/ppermute | solution.py:265
  50.8 11.6 %collective-permute-start.8 = (bf16[48,3072]{1,0:T(8,128)(2,1)}, bf16[48,3072]{1,0:T(8,128)(2,1)S(1)}, u32[]{:S(2)}, u32[]{:S(2)}) collective-permute-start(bf16[48,3072]{1,0:T(8,128)(2,1)} %get-tuple-element.33), channel_id=1, source_target_pairs={{0,8},{1,9},{2,10},{3,11},{4,12},{5,13},{6,14},{7,15},{8,0},{9,1},... | collective-permute-start | bytes 884744 | tf_op jit(solution)/shard_map/ppermute | solution.py:265
  54.3 8.1 %collective-permute-start.9 = (bf16[48,3072]{1,0:T(8,128)(2,1)}, bf16[48,3072]{1,0:T(8,128)(2,1)S(1)}, u32[]{:S(2)}, u32[]{:S(2)}) collective-permute-start(bf16[48,3072]{1,0:T(8,128)(2,1)} %get-tuple-element.34), channel_id=1, source_target_pairs={{0,12},{1,13},{2,14},{3,15},{4,0},{5,1},{6,2},{7,3},{8,4},{9,5},{1... | collective-permute-start | bytes 884744 | tf_op jit(solution)/shard_map/ppermute | solution.py:265
  64.2 9.7 %collective-permute-start.10 = (bf16[48,3072]{1,0:T(8,128)(2,1)S(1)}, bf16[48,3072]{1,0:T(8,128)(2,1)S(1)}, u32[]{:S(2)}, u32[]{:S(2)}) collective-permute-start(bf16[48,3072]{1,0:T(8,128)(2,1)S(1)} %shard_map.115.refs_0_), channel_id=1, source_target_pairs={{0,12},{1,13},{2,14},{3,15},{4,0},{5,1},{6,2},{7,3},{8,4},{9,5},{1... | collective-permute-start | bytes 884744 | tf_op jit(solution)/shard_map/ppermute | solution.py:265
  66.4 8.3 %collective-permute-start.11 = (bf16[48,3072]{1,0:T(8,128)(2,1)S(1)}, bf16[48,3072]{1,0:T(8,128)(2,1)S(1)}, u32[]{:S(2)}, u32[]{:S(2)}) collective-permute-start(bf16[48,3072]{1,0:T(8,128)(2,1)S(1)} %shard_map.115.refs_0_), channel_id=1, source_target_pairs={{0,8},{1,9},{2,10},{3,11},{4,12},{5,13},{6,14},{7,15},{8,0},{9,1},... | collective-permute-start | bytes 884744 | tf_op jit(solution)/shard_map/ppermute | solution.py:265
  67.8 10.0 %collective-permute-start.12 = (bf16[48,3072]{1,0:T(8,128)(2,1)S(1)}, bf16[48,3072]{1,0:T(8,128)(2,1)S(1)}, u32[]{:S(2)}, u32[]{:S(2)}) collective-permute-start(bf16[48,3072]{1,0:T(8,128)(2,1)S(1)} %shard_map.115.refs_0_), channel_id=1, source_target_pairs={{0,4},{1,5},{2,6},{3,7},{4,8},{5,9},{6,10},{7,11},{8,12},{9,13},{1... | collective-permute-start | bytes 884744 | tf_op jit(solution)/shard_map/ppermute | solution.py:265
  78.4 20.3 %collective-permute-start.13 = (bf16[128,3072]{1,0:T(8,128)(2,1)S(1)}, bf16[128,3072]{1,0:T(8,128)(2,1)S(1)}, u32[]{:S(2)}, u32[]{:S(2)}) collective-permute-start(bf16[128,3072]{1,0:T(8,128)(2,1)S(1)} %get-tuple-element.39.b0), channel_id=1, source_target_pairs={{0,3},{1,0},{2,1},{3,2},{4,7},{5,4},{6,5},{7,6},{8,11},{9,8},{10,9... | collective-permute-start | bytes 2359304 | tf_op jit(solution)/shard_map/ppermute | solution.py:265
  80.7 22.5 %collective-permute-start.14 = (bf16[128,3072]{1,0:T(8,128)(2,1)S(1)}, bf16[128,3072]{1,0:T(8,128)(2,1)S(1)}, u32[]{:S(2)}, u32[]{:S(2)}) collective-permute-start(bf16[128,3072]{1,0:T(8,128)(2,1)S(1)} %get-tuple-element.39.b0), channel_id=1, source_target_pairs={{0,2},{1,3},{2,0},{3,1},{4,6},{5,7},{6,4},{7,5},{8,10},{9,11},{10,... | collective-permute-start | bytes 2359304 | tf_op jit(solution)/shard_map/ppermute | solution.py:265
  82.2 21.1 %collective-permute-start.15 = (bf16[128,3072]{1,0:T(8,128)(2,1)S(1)}, bf16[128,3072]{1,0:T(8,128)(2,1)S(1)}, u32[]{:S(2)}, u32[]{:S(2)}) collective-permute-start(bf16[128,3072]{1,0:T(8,128)(2,1)S(1)} %get-tuple-element.39.b0), channel_id=1, source_target_pairs={{0,1},{1,2},{2,3},{3,0},{4,5},{5,6},{6,7},{7,4},{8,9},{9,10},{10,1... | collective-permute-start | bytes 2359304 | tf_op jit(solution)/shard_map/ppermute | solution.py:265
  84.6 18.6 %copy-start.5 = (bf16[256,384]{1,0:T(8,128)(2,1)S(1)}, bf16[256,384]{1,0:T(8,128)(2,1)}, u32[]{:S(2)}) copy-start(bf16[256,384]{1,0:T(8,128)(2,1)} %get-tuple-element.45.grad_y) | copy-start | bytes 589828
  98.7 13.5 %collective-permute-start.16 = (bf16[64,3072]{1,0:T(8,128)(2,1)S(1)}, bf16[64,3072]{1,0:T(8,128)(2,1)S(1)}, u32[]{:S(2)}, u32[]{:S(2)}) collective-permute-start(bf16[64,3072]{1,0:T(8,128)(2,1)S(1)} %get-tuple-element.48.b0), channel_id=1, source_target_pairs={{0,3},{1,0},{2,1},{3,2},{4,7},{5,4},{6,5},{7,6},{8,11},{9,8},{10,9... | collective-permute-start | bytes 1179656 | tf_op jit(solution)/shard_map/ppermute | solution.py:265
  102.4 9.9 %collective-permute-start.17 = (bf16[64,3072]{1,0:T(8,128)(2,1)S(1)}, bf16[64,3072]{1,0:T(8,128)(2,1)S(1)}, u32[]{:S(2)}, u32[]{:S(2)}) collective-permute-start(bf16[64,3072]{1,0:T(8,128)(2,1)S(1)} %get-tuple-element.48.b0), channel_id=1, source_target_pairs={{0,2},{1,3},{2,0},{3,1},{4,6},{5,7},{6,4},{7,5},{8,10},{9,11},{10,... | collective-permute-start | bytes 1179656 | tf_op jit(solution)/shard_map/ppermute | solution.py:265
  102.4 13.3 %collective-permute-start.18 = (bf16[64,3072]{1,0:T(8,128)(2,1)S(1)}, bf16[64,3072]{1,0:T(8,128)(2,1)}, u32[]{:S(2)}, u32[]{:S(2)}) collective-permute-start(bf16[64,3072]{1,0:T(8,128)(2,1)S(1)} %get-tuple-element.48.b0), channel_id=1, source_target_pairs={{0,1},{1,2},{2,3},{3,0},{4,5},{5,6},{6,7},{7,4},{8,9},{9,10},{10,1... | collective-permute-start | bytes 1179656 | tf_op jit(solution)/shard_map/ppermute | solution.py:265
  106.9 21.3 %all-to-all-start.1 = ((f32[32,1,3072]{2,1,0:T(1,128)}), f32[32,1,3072]{2,1,0:T(1,128)}, u32[]{:S(2)}, u32[]{:S(2)}) async-start(f32[32,1,3072]{2,1,0:T(1,128)} %shard_map.118), calls=%async_computation.1 | async-start | bytes 786432 | tf_op jit(solution)/shard_map/all_to_all | solution.py:374
  119.1 0.7 copy-start.4
  119.8 11.0 %copy-start.12 = (f32[384]{0:T(512)S(1)}, f32[384]{0:T(512)}, u32[]{:S(2)}) copy-start(f32[384]{0:T(512)} %param.18) | copy-start | bytes 4612
  119.8 1.7 %collective-permute-start.19 = (f32[128,384]{1,0:T(8,128)}, f32[128,384]{1,0:T(8,128)S(1)}, u32[]{:S(2)}, u32[]{:S(2)}) collective-permute-start(f32[128,384]{1,0:T(8,128)} %get-tuple-element.50), channel_id=1, source_target_pairs={{0,64},{64,0},{1,65},{65,1},{2,66},{66,2},{3,67},{67,3},{4,68},{68... | collective-permute-start | bytes 589832 | tf_op jit(solution)/shard_map/ppermute | solution.py:384
  122.5 5.7 %collective-permute-start.20 = (f32[4,8,384]{2,1,0:T(8,128)S(1)}, f32[4,8,384]{2,1,0:T(8,128)S(1)}, u32[]{:S(2)}, u32[]{:S(2)}) collective-permute-start(f32[4,8,384]{2,1,0:T(8,128)S(1)} %get-tuple-element.54), channel_id=1, source_target_pairs={{0,16},{16,32},{32,48},{48,0},{1,17},{17,33},{33,49},{49,1},{2,18}... | collective-permute-start | bytes 147464 | tf_op jit(solution)/shard_map/ppermute | solution.py:389
  124.0 5.9 %collective-permute-start.21 = (f32[4,8,384]{2,1,0:T(8,128)S(1)}, f32[4,8,384]{2,1,0:T(8,128)S(1)}, u32[]{:S(2)}, u32[]{:S(2)}) collective-permute-start(f32[4,8,384]{2,1,0:T(8,128)S(1)} %get-tuple-element.52), channel_id=1, source_target_pairs={{0,32},{16,48},{32,0},{48,16},{1,33},{17,49},{33,1},{49,17},{2,34}... | collective-permute-start | bytes 147464 | tf_op jit(solution)/shard_map/ppermute | solution.py:389
  126.8 4.1 %collective-permute-start.22 = (f32[4,8,384]{2,1,0:T(8,128)S(1)}, f32[4,8,384]{2,1,0:T(8,128)S(1)}, u32[]{:S(2)}, u32[]{:S(2)}) collective-permute-start(f32[4,8,384]{2,1,0:T(8,128)S(1)} %get-tuple-element.53), channel_id=1, source_target_pairs={{0,48},{16,0},{32,16},{48,32},{1,49},{17,1},{33,17},{49,33},{2,50}... | collective-permute-start | bytes 147464 | tf_op jit(solution)/shard_map/ppermute | solution.py:389

commit v8 on v7

--- a/solution.py
+++ b/solution.py
@@ -70,14 +70,14 @@
         def centred(own, other):
             x = jnp.concatenate([own[...], other[...]], axis=0).astype(F32)
             mean = jnp.sum(x, axis=1, keepdims=True) / x.shape[1]
-            return ((x - mean) * gain[...]).astype(BF16)
+            return ((x - mean) * gain[...][None, :]).astype(BF16)
 
         lhs[0:256, :] = reorder(sel, centred(f0, f1))
         lhs[256:512, :] = reorder(sel, centred(r0, r1))
         kept = jnp.concatenate([l0[...], l1[...]], axis=1) == 1
         sel = jnp.where(kept, sel.astype(F32), 0.0).astype(BF16)
         rows_g[...] = reorder(sel, jnp.concatenate([g0[...], g1[...]], axis=0))
-        a = jnp.broadcast_to(gain[...], (16, gain.shape[1]))
+        a = jnp.broadcast_to(gain[...][None, :], (16, gain.shape[0]))
         for k in range(3):
             part = a.astype(BF16)
             lhs[512 + k * 16 : 528 + k * 16, :] = part
@@ -159,7 +159,7 @@
         _, mean, scale = merged(width, share[:, k, :], share[:, k + 4, :], 0)
         rows = jnp.concatenate([mean, scale, mean, mean, mean, mean, mean, mean], axis=0)
         cols = jnp.transpose(rows)
-        normed.append((x[...].astype(F32) - cols[:, 0:1]) * cols[:, 1:2] * gain[...])
+        normed.append((x[...].astype(F32) - cols[:, 0:1]) * cols[:, 1:2] * gain[...][None, :])
     x = jnp.concatenate(normed, axis=0).astype(BF16)
     rows = jnp.dot(row_order(where), x, preferred_element_type=F32)
     out[...] = jnp.transpose(rows).astype(BF16)
@@ -286,7 +286,7 @@
     half = w_in.shape[1] // 2
     steps = half // TILE
     where = jnp.stack([core, y, z]).astype(jnp.int32)
-    gain = ln_gain[None, :]
+    gain = ln_gain
 
     labels = forget_labels[None, :]
     other_f = lax.ppermute(forget_tokens, "dp", SWAP)
@@ -358,10 +358,12 @@
     first, last, _ = lax.optimization_barrier((w_in, w_out, forget))
     first = lax.dynamic_slice_in_dim(first, core * half, half, 1)
     last = lax.dynamic_slice_in_dim(last, core * half, half, 0)
-    retain, far[0], first, last = lax.optimization_barrier((retain, far[0], first, last))
+    retain, first = lax.optimization_barrier((retain, first))
+    second, last = lax.optimization_barrier((retain, last))
+    far[0], first, last = lax.optimization_barrier((far[0], first, last))
     w_in_tile = (first, (width, TILE), lambda t, w: (0, t))
     w_out_tile = (last, (TILE, width), lambda t, w: (t, 0))
-    retain_far = permutes([retain] * 3, True, -1)
+    retain_far = permutes([retain, second, second], True, -1)
 
     terms = call(
         saliency_terms,
@@ -371,6 +373,7 @@
         (),
         steps,
     )[0]
+    retain_far[0], _ = lax.optimization_barrier((retain_far[0], terms))
     terms = lax.all_to_all(terms, ("dp", "col"), 0, 0, tiled=True)
 
     mine, theirs = call(
@@ -389,6 +392,7 @@
     from_rows = [lax.ppermute(for_row(row + k), "row", shift_row(k)) for k in (1, 2, 3)]
     terms, _ = lax.optimization_barrier((terms, from_rows[0]))
     saliency = jnp.sum(terms.reshape(2, 16, half), axis=1).reshape(2 * half) / D
+    from_rows[1], saliency = lax.optimization_barrier((from_rows[1], saliency))
     total = for_row(row)
     for part in from_rows:
         total = total + part

time: 132 us -> 127 us (0.962)
  waiting for transfers between devices: 51.9 us -> 49.6 us
  local copies, waits for them, and re-layouts: 10.4 us -> 8.71 us
  starting transfers between devices: 43 us -> 41.5 us
    ppermute x15, waiting for transfers between devices: 49.4 us -> 46.5 us  [permutes(): lax.ppermute(parts[k], ('dp', 'col'), pairs(first, sign * (k + 1)))]
  transfers between devices with their start and end apart: 25 -> 25, of which waited for: 11 -> 14; matrix products, arithmetic and copies ran while one was open for 9% -> 8% of each run, Pallas kernels for 9% -> 9%
where the time goes in v8:
time: 127 us; the launch traced here: 126 us
  waiting for transfers between devices  49.6 us (39%)
  starting transfers between devices  41.5 us (33%)
  Pallas kernels  21.3 us (17%)
  local copies, waits for them, and re-layouts  8.71 us (7%)
  other arithmetic  4.02 us (3%)
    ppermute x15, waiting for transfers between devices, permutes(): lax.ppermute(parts[k], ('dp', 'col'), pairs(first, sign * (k + 1)))  46.5 us
    ppermute x15, starting transfers between devices, permutes(): lax.ppermute(parts[k], ('dp', 'col'), pairs(first, sign * (k + 1)))  24.6 us
    pallas_call x7, Pallas kernels, call(): pl.pallas_call(kernel, grid_spec=pltpu.PrefetchScalarGridSpec(num_scalar_...  21.3 us
    ppermute x3, starting transfers between devices, local(): lax.ppermute(for_row(row + k), 'row', shift_row(k))  5.72 us
    all_to_all x1, starting transfers between devices, local(): share = lax.all_to_all(share, 'col', 0, 0, tiled=True)  5.53 us
    all_to_all x1, starting transfers between devices, local(): terms = lax.all_to_all(terms, ('dp', 'col'), 0, 0, tiled=True)  4.59 us
    unnamed x32, local copies, waits for them, and re-layouts  3.33 us
  transfers between devices with their start and end apart: 25, of which 14 were waited for; matrix products, arithmetic and copies ran while one was open for 8% of the time, Pallas kernels for 9%

profile of v8, /device:TPU:0, one launch (start us, length us, event | category | flops | bytes accessed | tf_op | source)
XLA Modules:
  0.0 126.0 jit_solution(538878368406022266)
XLA Ops:
  1.7 0.6 pad_add_fusion.where
  3.2 0.6 copy-done.10
  3.8 7.4 %shard_map.113 = (bf16[192,3072]{1,0:T(8,128)(2,1)}, bf16[192,3072]{1,0:T(8,128)(2,1)}, bf16[192,3072]{1,0:T(8,128)(2,1)}, bf16[192,3072]{1,0:T(8,128)(2,1)}, bf...) custom-call(s32[3]{0:T(128)} %pad_add_fusion.where, bf16[128,384]{1,0:T(8,128)(2,1)} %own.1, bf16[128,384]{1,0:T(8,128)(2,1)} %copy-done.2, ...), custom_call_target="tpu_custom_call" | custom-call | flops 1 | bytes 1 | tf_op jit(solution)/shard_map/pallas_call | solution.py:229
  11.3 1.7 %collective-permute-start.4 = (bf16[192,3072]{1,0:T(8,128)(2,1)}, bf16[192,3072]{1,0:T(8,128)(2,1)S(1)}, u32[]{:S(2)}, u32[]{:S(2)}) collective-permute-start(bf16[192,3072]{1,0:T(8,128)(2,1)} %get-tuple-element.34), channel_id=1, source_target_pairs={{0,1},{1,2},{2,3},{3,0},{4,5},{5,6},{6,7},{7,4},{8,9},{9,10},{10,1... | collective-permute-start | bytes 3538952 | tf_op jit(solution)/shard_map/ppermute | solution.py:265
  13.0 2.9 %collective-permute-start.5 = (bf16[192,3072]{1,0:T(8,128)(2,1)}, bf16[192,3072]{1,0:T(8,128)(2,1)}, u32[]{:S(2)}, u32[]{:S(2)}) collective-permute-start(bf16[192,3072]{1,0:T(8,128)(2,1)} %get-tuple-element.35), channel_id=1, source_target_pairs={{0,2},{1,3},{2,0},{3,1},{4,6},{5,7},{6,4},{7,5},{8,10},{9,11},{10,... | collective-permute-start | bytes 3538952 | tf_op jit(solution)/shard_map/ppermute | solution.py:265
  15.9 1.3 %collective-permute-start.6 = (bf16[192,3072]{1,0:T(8,128)(2,1)}, bf16[192,3072]{1,0:T(8,128)(2,1)}, u32[]{:S(2)}, u32[]{:S(2)}) collective-permute-start(bf16[192,3072]{1,0:T(8,128)(2,1)} %get-tuple-element.36), channel_id=1, source_target_pairs={{0,3},{1,0},{2,1},{3,2},{4,7},{5,4},{6,5},{7,6},{8,11},{9,8},{10,9... | collective-permute-start | bytes 3538952 | tf_op jit(solution)/shard_map/ppermute | solution.py:265
  17.3 1.0 pad_maximum_fusion
  18.3 0.9 slice.3
  19.6 0.7 broadcast_in_dim.29
  20.3 5.5 %all-to-all-start = ((f32[16,32,128]{2,1,0:T(8,128)}), f32[16,32,128]{2,1,0:T(8,128)S(1)}, u32[]{:S(2)}, u32[]{:S(2)}) async-start(f32[16,32,128]{2,1,0:T(8,128)} %broadcast_in_dim.29), calls=%async_computation | async-start | bytes 524288 | tf_op jit(solution)/shard_map/all_to_all | solution.py:320
  25.9 3.0 %collective-permute-done.4.refs_1_ = bf16[192,3072]{1,0:T(8,128)(2,1)S(1)} collective-permute-done((bf16[192,3072]{1,0:T(8,128)(2,1)}, bf16[192,3072]{1,0:T(8,128)(2,1)S(1)}, u32[]{:S(2)}, u32[]{:S(2)}) %collective-permute-start.4) | collective-permute-done | bytes 1179680 | tf_op jit(solution)/shard_map/ppermute | solution.py:265
  29.0 15.5 %collective-permute-done.5.refs_2_ = bf16[192,3072]{1,0:T(8,128)(2,1)} collective-permute-done((bf16[192,3072]{1,0:T(8,128)(2,1)}, bf16[192,3072]{1,0:T(8,128)(2,1)}, u32[]{:S(2)}, u32[]{:S(2)}) %collective-permute-start.5) | collective-permute-done | bytes 1179680 | tf_op jit(solution)/shard_map/ppermute | solution.py:265
  44.4 3.3 %shard_map.114 = (f32[48,3072]{1,0:T(8,128)S(1)}, bf16[48,3072]{1,0:T(8,128)(2,1)}, bf16[48,3072]{1,0:T(8,128)(2,1)}, bf16[48,3072]{1,0:T(8,128)(2,1)}) custom-call(s32[3]{0:T(128)S(1)} %copy-done.6, bf16[192,3072]{1,0:T(8,128)(2,1)S(1)} %copy-done, bf16[192,3072]{1,0:T(8,128)(2,1)S(1)} %collective-permute-done.4.refs_1_, ...), custom_call_target="tpu_custom_call" | custom-call | flops 1 | bytes 1 | tf_op jit(solution)/shard_map/pallas_call | solution.py:229
  47.8 1.9 %collective-permute-start.7 = (bf16[48,3072]{1,0:T(8,128)(2,1)}, bf16[48,3072]{1,0:T(8,128)(2,1)S(1)}, u32[]{:S(2)}, u32[]{:S(2)}) collective-permute-start(bf16[48,3072]{1,0:T(8,128)(2,1)} %get-tuple-element.38), channel_id=1, source_target_pairs={{0,4},{1,5},{2,6},{3,7},{4,8},{5,9},{6,10},{7,11},{8,12},{9,13},{1... | collective-permute-start | bytes 884744 | tf_op jit(solution)/shard_map/ppermute | solution.py:265
  49.7 3.6 %collective-permute-start.8 = (bf16[48,3072]{1,0:T(8,128)(2,1)}, bf16[48,3072]{1,0:T(8,128)(2,1)S(1)}, u32[]{:S(2)}, u32[]{:S(2)}) collective-permute-start(bf16[48,3072]{1,0:T(8,128)(2,1)} %get-tuple-element.39), channel_id=1, source_target_pairs={{0,8},{1,9},{2,10},{3,11},{4,12},{5,13},{6,14},{7,15},{8,0},{9,1},... | collective-permute-start | bytes 884744 | tf_op jit(solution)/shard_map/ppermute | solution.py:265
  53.3 1.0 collective-permute-start.9
  54.6 2.1 %collective-permute-done.7.a = bf16[48,3072]{1,0:T(8,128)(2,1)S(1)} collective-permute-done((bf16[48,3072]{1,0:T(8,128)(2,1)}, bf16[48,3072]{1,0:T(8,128)(2,1)S(1)}, u32[]{:S(2)}, u32[]{:S(2)}) %collective-permute-start.7) | collective-permute-done | bytes 294944 | tf_op jit(solution)/shard_map/ppermute | solution.py:265
  56.7 4.6 %collective-permute-done.8.b = bf16[48,3072]{1,0:T(8,128)(2,1)S(1)} collective-permute-done((bf16[48,3072]{1,0:T(8,128)(2,1)}, bf16[48,3072]{1,0:T(8,128)(2,1)S(1)}, u32[]{:S(2)}, u32[]{:S(2)}) %collective-permute-start.8) | collective-permute-done | bytes 294944 | tf_op jit(solution)/shard_map/ppermute | solution.py:265
  61.3 1.8 %shard_map.115.refs_0_ = bf16[48,3072]{1,0:T(8,128)(2,1)S(1)} custom-call(s32[3]{0:T(128)S(1)} %copy-done.6, f32[48,3072]{1,0:T(8,128)S(1)} %get-tuple-element.37.keep, bf16[48,3072]{1,0:T(8,128)(2,1)S(1)} %collective-permute-done.7.a, bf16[48,3072]{1,0:T(8,128)(2,1)S(1)} %collective-permute-done.8.b, bf16[48,3072]{1,0:T(8,128)(2,1)S(1)} %collective-permute-done.9.c, ...), custom_call_target="tpu_custom_call" | custom-call | flops 1 | bytes 1 | tf_op jit(solution)/shard_map/pallas_call | solution.py:229
  63.1 2.2 %collective-permute-start.10 = (bf16[48,3072]{1,0:T(8,128)(2,1)S(1)}, bf16[48,3072]{1,0:T(8,128)(2,1)S(1)}, u32[]{:S(2)}, u32[]{:S(2)}) collective-permute-start(bf16[48,3072]{1,0:T(8,128)(2,1)S(1)} %shard_map.115.refs_0_), channel_id=1, source_target_pairs={{0,12},{1,13},{2,14},{3,15},{4,0},{5,1},{6,2},{7,3},{8,4},{9,5},{1... | collective-permute-start | bytes 884744 | tf_op jit(solution)/shard_map/ppermute | solution.py:265
  65.3 1.4 %collective-permute-start.11 = (bf16[48,3072]{1,0:T(8,128)(2,1)S(1)}, bf16[48,3072]{1,0:T(8,128)(2,1)S(1)}, u32[]{:S(2)}, u32[]{:S(2)}) collective-permute-start(bf16[48,3072]{1,0:T(8,128)(2,1)S(1)} %shard_map.115.refs_0_), channel_id=1, source_target_pairs={{0,8},{1,9},{2,10},{3,11},{4,12},{5,13},{6,14},{7,15},{8,0},{9,1},... | collective-permute-start | bytes 884744 | tf_op jit(solution)/shard_map/ppermute | solution.py:265
  67.1 1.1 shard_map.116.normed_t
  68.2 4.5 %collective-permute-done.10.refs_1_ = bf16[48,3072]{1,0:T(8,128)(2,1)S(1)} collective-permute-done((bf16[48,3072]{1,0:T(8,128)(2,1)S(1)}, bf16[48,3072]{1,0:T(8,128)(2,1)S(1)}, u32[]{:S(2)}, u32[]{:S(2)}) %collective-permute-start.10) | collective-permute-done | bytes 294944 | tf_op jit(solution)/shard_map/ppermute | solution.py:265
  72.7 0.9 collective-permute-done.11.refs_2_
  73.6 3.1 %collective-permute-done.12.refs_3_ = bf16[48,3072]{1,0:T(8,128)(2,1)S(1)} collective-permute-done((bf16[48,3072]{1,0:T(8,128)(2,1)S(1)}, bf16[48,3072]{1,0:T(8,128)(2,1)S(1)}, u32[]{:S(2)}, u32[]{:S(2)}) %collective-permute-start.12) | collective-permute-done | bytes 294944 | tf_op jit(solution)/shard_map/ppermute | solution.py:265
  76.7 0.6 shard_map.117
  77.3 2.3 %collective-permute-start.14 = (bf16[128,3072]{1,0:T(8,128)(2,1)S(1)}, bf16[128,3072]{1,0:T(8,128)(2,1)S(1)}, u32[]{:S(2)}, u32[]{:S(2)}) collective-permute-start(bf16[128,3072]{1,0:T(8,128)(2,1)S(1)} %get-tuple-element.46.b0), channel_id=1, source_target_pairs={{0,3},{1,0},{2,1},{3,2},{4,7},{5,4},{6,5},{7,6},{8,11},{9,8},{10,9... | collective-permute-start | bytes 2359304 | tf_op jit(solution)/shard_map/ppermute | solution.py:265
  79.7 1.4 %collective-permute-start.15 = (bf16[128,3072]{1,0:T(8,128)(2,1)S(1)}, bf16[128,3072]{1,0:T(8,128)(2,1)S(1)}, u32[]{:S(2)}, u32[]{:S(2)}) collective-permute-start(bf16[128,3072]{1,0:T(8,128)(2,1)S(1)} %get-tuple-element.46.b0), channel_id=1, source_target_pairs={{0,2},{1,3},{2,0},{3,1},{4,6},{5,7},{6,4},{7,5},{8,10},{9,11},{10,... | collective-permute-start | bytes 2359304 | tf_op jit(solution)/shard_map/ppermute | solution.py:265
  81.1 0.6 collective-permute-start.16
  81.7 1.8 %constant_dynamic-slice_fusion.1.w_in = bf16[384,3072]{1,0:T(8,128)(2,1)S(1)} fusion(bf16[384,6144]{1,0:T(8,128)(2,1)} %w_in.1, s32[]{:T(128)S(6)} %select_n.68), kind=kLoop, calls=%fused_computation.23 | loop fusion | bytes 4718596 | tf_op jit(solution)/shard_map/dynamic_slice | solution.py:359
  83.5 2.7 %collective-permute-start.13 = (bf16[64,3072]{1,0:T(8,128)(2,1)S(1)}, bf16[64,3072]{1,0:T(8,128)(2,1)S(1)}, u32[]{:S(2)}, u32[]{:S(2)}) collective-permute-start(bf16[64,3072]{1,0:T(8,128)(2,1)S(1)} %get-tuple-element.58.b0), channel_id=1, source_target_pairs={{0,3},{1,0},{2,1},{3,2},{4,7},{5,4},{6,5},{7,6},{8,11},{9,8},{10,9... | collective-permute-start | bytes 1179656 | tf_op jit(solution)/shard_map/ppermute | solution.py:265
  86.2 1.9 %constant_dynamic-slice_fusion.w_out = bf16[3072,384]{1,0:T(8,128)(2,1)S(1)} fusion(bf16[6144,384]{1,0:T(8,128)(2,1)} %w_out.1, s32[]{:T(128)S(6)} %select_n.68), kind=kLoop, calls=%fused_computation.22 | loop fusion | bytes 4718596 | tf_op jit(solution)/shard_map/dynamic_slice | solution.py:360
  88.1 1.0 collective-permute-start.17
  89.1 8.5 %collective-permute-done.14.b1 = bf16[128,3072]{1,0:T(8,128)(2,1)S(1)} collective-permute-done((bf16[128,3072]{1,0:T(8,128)(2,1)S(1)}, bf16[128,3072]{1,0:T(8,128)(2,1)S(1)}, u32[]{:S(2)}, u32[]{:S(2)}) %collective-permute-start.14) | collective-permute-done | bytes 786464 | tf_op jit(solution)/shard_map/ppermute | solution.py:265
  97.6 3.9 %collective-permute-done.16.b3 = bf16[128,3072]{1,0:T(8,128)(2,1)S(1)} collective-permute-done((bf16[128,3072]{1,0:T(8,128)(2,1)S(1)}, bf16[128,3072]{1,0:T(8,128)(2,1)S(1)}, u32[]{:S(2)}, u32[]{:S(2)}) %collective-permute-start.16) | collective-permute-done | bytes 786464 | tf_op jit(solution)/shard_map/ppermute | solution.py:265
  101.6 3.6 %shard_map.118 = f32[32,1,3072]{2,1,0:T(1,128)} custom-call(s32[3]{0:T(128)S(1)} %copy-done.6, bf16[128,3072]{1,0:T(8,128)(2,1)S(1)} %get-tuple-element.46.b0, bf16[128,3072]{1,0:T(8,128)(2,1)S(1)} %collective-permute-done.14.b1, bf16[128,3072]{1,0:T(8,128)(2,1)S(1)} %collective-permute-done.15.b2, bf16[128,3072]{1,0:T(8,128)(2,1)S(1)} %collective-permute-done.16.b3, ...), custom_call_target="tpu_custom_call" | custom-call | flops 1 | bytes 1 | tf_op jit(solution)/shard_map/pallas_call | solution.py:229
  105.2 4.6 %all-to-all-start.1 = ((f32[32,1,3072]{2,1,0:T(1,128)}), f32[32,1,3072]{2,1,0:T(1,128)}, u32[]{:S(2)}, u32[]{:S(2)}) async-start(f32[32,1,3072]{2,1,0:T(1,128)} %shard_map.118), calls=%async_computation.1 | async-start | bytes 786432 | tf_op jit(solution)/shard_map/all_to_all | solution.py:377
  110.2 3.5 %shard_map.119 = (f32[128,384]{1,0:T(8,128)S(1)}, f32[128,384]{1,0:T(8,128)}) custom-call(s32[3]{0:T(128)S(1)} %copy-done.6, bf16[64,3072]{1,0:T(8,128)(2,1)S(1)} %get-tuple-element.58.b0, bf16[64,3072]{1,0:T(8,128)(2,1)S(1)} %collective-permute-done.13.b1, bf16[64,3072]{1,0:T(8,128)(2,1)S(1)} %collective-permute-done.17.b2, ...), custom_call_target="tpu_custom_call" | custom-call | flops 1 | bytes 1 | tf_op jit(solution)/shard_map/pallas_call | solution.py:229
  113.6 0.7 copy-done.4
  114.3 1.6 %collective-permute-done.19 = f32[128,384]{1,0:T(8,128)S(1)} collective-permute-done((f32[128,384]{1,0:T(8,128)}, f32[128,384]{1,0:T(8,128)S(1)}, u32[]{:S(2)}, u32[]{:S(2)}) %collective-permute-start.19) | collective-permute-done | bytes 196640 | tf_op jit(solution)/shard_map/ppermute | solution.py:387
  116.0 0.9 add.88
  116.9 1.6 %collective-permute-start.21 = (f32[4,8,384]{2,1,0:T(8,128)S(1)}, f32[4,8,384]{2,1,0:T(8,128)S(1)}, u32[]{:S(2)}, u32[]{:S(2)}) collective-permute-start(f32[4,8,384]{2,1,0:T(8,128)S(1)} %get-tuple-element.65), channel_id=1, source_target_pairs={{0,16},{16,32},{32,48},{48,0},{1,17},{17,33},{33,49},{49,1},{2,18}... | collective-permute-start | bytes 147464 | tf_op jit(solution)/shard_map/ppermute | solution.py:392
  118.5 2.7 %collective-permute-start.20 = (f32[4,8,384]{2,1,0:T(8,128)S(1)}, f32[4,8,384]{2,1,0:T(8,128)S(1)}, u32[]{:S(2)}, u32[]{:S(2)}) collective-permute-start(f32[4,8,384]{2,1,0:T(8,128)S(1)} %get-tuple-element.66), channel_id=1, source_target_pairs={{0,32},{16,48},{32,0},{48,16},{1,33},{17,49},{33,1},{49,17},{2,34}... | collective-permute-start | bytes 147464 | tf_op jit(solution)/shard_map/ppermute | solution.py:392
  121.2 1.4 %collective-permute-start.22 = (f32[4,8,384]{2,1,0:T(8,128)S(1)}, f32[4,8,384]{2,1,0:T(8,128)S(1)}, u32[]{:S(2)}, u32[]{:S(2)}) collective-permute-start(f32[4,8,384]{2,1,0:T(8,128)S(1)} %get-tuple-element.64), channel_id=1, source_target_pairs={{0,48},{16,0},{32,16},{48,32},{1,49},{17,1},{33,17},{49,33},{2,50}... | collective-permute-start | bytes 147464 | tf_op jit(solution)/shard_map/ppermute | solution.py:392
  122.7 1.1 copy.12
  123.8 0.6 copy.13
  124.4 0.9 collective-permute-done.22
  125.3 0.7 fusion.7
  (61 shorter events, 3.5 us)
Async XLA Ops:
  0.6 1.9 %collective-permute-start = (bf16[128,384]{1,0:T(8,128)(2,1)}, bf16[128,384]{1,0:T(8,128)(2,1)S(1)}, u32[]{:S(2)}, u32[]{:S(2)}) collective-permute-start(bf16[128,384]{1,0:T(8,128)(2,1)} %own.1), channel_id=1, source_target_pairs={{0,64},{64,0},{1,65},{65,1},{2,66},{66,2},{3,67},{67,3},{4,68},{68... | collective-permute-start | bytes 294920 | tf_op jit(solution)/shard_map/ppermute | solution.py:292
  0.7 1.8 %collective-permute-start.2 = (bf16[128,384]{1,0:T(8,128)(2,1)}, bf16[128,384]{1,0:T(8,128)(2,1)S(1)}, u32[]{:S(2)}, u32[]{:S(2)}) collective-permute-start(bf16[128,384]{1,0:T(8,128)(2,1)} %r0.1), channel_id=1, source_target_pairs={{0,64},{64,0},{1,65},{65,1},{2,66},{66,2},{3,67},{67,3},{4,68},{68... | collective-permute-start | bytes 294920 | tf_op jit(solution)/shard_map/ppermute | solution.py:293
  1.2 1.3 collective-permute-start.3
  1.3 1.6 %collective-permute-start.1 = (bf16[128,384]{1,0:T(8,128)(2,1)}, bf16[128,384]{1,0:T(8,128)(2,1)S(1)}, u32[]{:S(2)}, u32[]{:S(2)}) collective-permute-start(bf16[128,384]{1,0:T(8,128)(2,1)} %g0.1), channel_id=1, source_target_pairs={{0,64},{64,0},{1,65},{65,1},{2,66},{66,2},{3,67},{67,3},{4,68},{68... | collective-permute-start | bytes 294920 | tf_op jit(solution)/shard_map/ppermute | solution.py:294
  2.3 14.9 %copy-start.1 = (bf16[128,384]{1,0:T(8,128)(2,1)S(1)}, bf16[128,384]{1,0:T(8,128)(2,1)}, u32[]{:S(2)}) copy-start(bf16[128,384]{1,0:T(8,128)(2,1)} %own.1) | copy-start | bytes 294916
  2.3 14.9 %copy-start.8 = (bf16[128,384]{1,0:T(8,128)(2,1)S(1)}, bf16[128,384]{1,0:T(8,128)(2,1)}, u32[]{:S(2)}) copy-start(bf16[128,384]{1,0:T(8,128)(2,1)} %r0.1) | copy-start | bytes 294916
  2.5 0.5 copy-start.13
  2.5 0.6 copy-start.2
  2.5 0.7 copy-start.9
  3.2 0.6 copy-start.10
  11.2 33.2 %copy-start = (bf16[192,3072]{1,0:T(8,128)(2,1)S(1)}, bf16[192,3072]{1,0:T(8,128)(2,1)}, u32[]{:S(2)}) copy-start(bf16[192,3072]{1,0:T(8,128)(2,1)} %get-tuple-element.33.refs_0_) | copy-start | bytes 3538948
  11.3 33.2 %copy-start.6 = (s32[3]{0:T(128)S(1)}, s32[3]{0:T(128)}, u32[]{:S(2)}) copy-start(s32[3]{0:T(128)} %pad_add_fusion.where) | copy-start | bytes 40
  11.3 17.7 %collective-permute-start.4 = (bf16[192,3072]{1,0:T(8,128)(2,1)}, bf16[192,3072]{1,0:T(8,128)(2,1)S(1)}, u32[]{:S(2)}, u32[]{:S(2)}) collective-permute-start(bf16[192,3072]{1,0:T(8,128)(2,1)} %get-tuple-element.34), channel_id=1, source_target_pairs={{0,1},{1,2},{2,3},{3,0},{4,5},{5,6},{6,7},{7,4},{8,9},{9,10},{10,1... | collective-permute-start | bytes 3538952 | tf_op jit(solution)/shard_map/ppermute | solution.py:265
  13.0 31.4 %collective-permute-start.5 = (bf16[192,3072]{1,0:T(8,128)(2,1)}, bf16[192,3072]{1,0:T(8,128)(2,1)}, u32[]{:S(2)}, u32[]{:S(2)}) collective-permute-start(bf16[192,3072]{1,0:T(8,128)(2,1)} %get-tuple-element.35), channel_id=1, source_target_pairs={{0,2},{1,3},{2,0},{3,1},{4,6},{5,7},{6,4},{7,5},{8,10},{9,11},{10,... | collective-permute-start | bytes 3538952 | tf_op jit(solution)/shard_map/ppermute | solution.py:265
  15.9 28.5 %collective-permute-start.6 = (bf16[192,3072]{1,0:T(8,128)(2,1)}, bf16[192,3072]{1,0:T(8,128)(2,1)}, u32[]{:S(2)}, u32[]{:S(2)}) collective-permute-start(bf16[192,3072]{1,0:T(8,128)(2,1)} %get-tuple-element.36), channel_id=1, source_target_pairs={{0,3},{1,0},{2,1},{3,2},{4,7},{5,4},{6,5},{7,6},{8,11},{9,8},{10,9... | collective-permute-start | bytes 3538952 | tf_op jit(solution)/shard_map/ppermute | solution.py:265
  20.3 34.2 %all-to-all-start = ((f32[16,32,128]{2,1,0:T(8,128)}), f32[16,32,128]{2,1,0:T(8,128)S(1)}, u32[]{:S(2)}, u32[]{:S(2)}) async-start(f32[16,32,128]{2,1,0:T(8,128)} %broadcast_in_dim.29), calls=%async_computation | async-start | bytes 524288 | tf_op jit(solution)/shard_map/all_to_all | solution.py:320
  25.9 28.4 %copy-start.14 = (s32[128]{0:T(128)S(1)}, s32[128]{0:T(128)}, u32[]{:S(2)}) copy-start(s32[128]{0:T(128)} %param.19) | copy-start | bytes 1540
  25.9 28.7 %copy-start.11 = (f32[6144]{0:T(1024)S(1)}, f32[6144]{0:T(1024)}, u32[]{:S(2)}) copy-start(f32[6144]{0:T(1024)} %param.16) | copy-start | bytes 73732
  47.7 19.4 %copy-start.3 = (bf16[128,384]{1,0:T(8,128)(2,1)S(1)}, bf16[128,384]{1,0:T(8,128)(2,1)}, u32[]{:S(2)}) copy-start(bf16[128,384]{1,0:T(8,128)(2,1)} %copy-done.2) | copy-start | bytes 294916
  47.7 19.4 %copy-start.7 = (f32[384]{0:T(512)S(1)}, f32[384]{0:T(512)}, u32[]{:S(2)}) copy-start(f32[384]{0:T(512)} %gain.3) | copy-start | bytes 4612
  47.8 9.0 %collective-permute-start.7 = (bf16[48,3072]{1,0:T(8,128)(2,1)}, bf16[48,3072]{1,0:T(8,128)(2,1)S(1)}, u32[]{:S(2)}, u32[]{:S(2)}) collective-permute-start(bf16[48,3072]{1,0:T(8,128)(2,1)} %get-tuple-element.38), channel_id=1, source_target_pairs={{0,4},{1,5},{2,6},{3,7},{4,8},{5,9},{6,10},{7,11},{8,12},{9,13},{1... | collective-permute-start | bytes 884744 | tf_op jit(solution)/shard_map/ppermute | solution.py:265
  49.7 11.7 %collective-permute-start.8 = (bf16[48,3072]{1,0:T(8,128)(2,1)}, bf16[48,3072]{1,0:T(8,128)(2,1)S(1)}, u32[]{:S(2)}, u32[]{:S(2)}) collective-permute-start(bf16[48,3072]{1,0:T(8,128)(2,1)} %get-tuple-element.39), channel_id=1, source_target_pairs={{0,8},{1,9},{2,10},{3,11},{4,12},{5,13},{6,14},{7,15},{8,0},{9,1},... | collective-permute-start | bytes 884744 | tf_op jit(solution)/shard_map/ppermute | solution.py:265
  53.3 8.1 %collective-permute-start.9 = (bf16[48,3072]{1,0:T(8,128)(2,1)}, bf16[48,3072]{1,0:T(8,128)(2,1)S(1)}, u32[]{:S(2)}, u32[]{:S(2)}) collective-permute-start(bf16[48,3072]{1,0:T(8,128)(2,1)} %get-tuple-element.40), channel_id=1, source_target_pairs={{0,12},{1,13},{2,14},{3,15},{4,0},{5,1},{6,2},{7,3},{8,4},{9,5},{1... | collective-permute-start | bytes 884744 | tf_op jit(solution)/shard_map/ppermute | solution.py:265
  63.1 9.7 %collective-permute-start.10 = (bf16[48,3072]{1,0:T(8,128)(2,1)S(1)}, bf16[48,3072]{1,0:T(8,128)(2,1)S(1)}, u32[]{:S(2)}, u32[]{:S(2)}) collective-permute-start(bf16[48,3072]{1,0:T(8,128)(2,1)S(1)} %shard_map.115.refs_0_), channel_id=1, source_target_pairs={{0,12},{1,13},{2,14},{3,15},{4,0},{5,1},{6,2},{7,3},{8,4},{9,5},{1... | collective-permute-start | bytes 884744 | tf_op jit(solution)/shard_map/ppermute | solution.py:265
  65.3 8.3 %collective-permute-start.11 = (bf16[48,3072]{1,0:T(8,128)(2,1)S(1)}, bf16[48,3072]{1,0:T(8,128)(2,1)S(1)}, u32[]{:S(2)}, u32[]{:S(2)}) collective-permute-start(bf16[48,3072]{1,0:T(8,128)(2,1)S(1)} %shard_map.115.refs_0_), channel_id=1, source_target_pairs={{0,8},{1,9},{2,10},{3,11},{4,12},{5,13},{6,14},{7,15},{8,0},{9,1},... | collective-permute-start | bytes 884744 | tf_op jit(solution)/shard_map/ppermute | solution.py:265
  66.7 10.0 %collective-permute-start.12 = (bf16[48,3072]{1,0:T(8,128)(2,1)S(1)}, bf16[48,3072]{1,0:T(8,128)(2,1)S(1)}, u32[]{:S(2)}, u32[]{:S(2)}) collective-permute-start(bf16[48,3072]{1,0:T(8,128)(2,1)S(1)} %shard_map.115.refs_0_), channel_id=1, source_target_pairs={{0,4},{1,5},{2,6},{3,7},{4,8},{5,9},{6,10},{7,11},{8,12},{9,13},{1... | collective-permute-start | bytes 884744 | tf_op jit(solution)/shard_map/ppermute | solution.py:265
  77.3 20.3 %collective-permute-start.14 = (bf16[128,3072]{1,0:T(8,128)(2,1)S(1)}, bf16[128,3072]{1,0:T(8,128)(2,1)S(1)}, u32[]{:S(2)}, u32[]{:S(2)}) collective-permute-start(bf16[128,3072]{1,0:T(8,128)(2,1)S(1)} %get-tuple-element.46.b0), channel_id=1, source_target_pairs={{0,3},{1,0},{2,1},{3,2},{4,7},{5,4},{6,5},{7,6},{8,11},{9,8},{10,9... | collective-permute-start | bytes 2359304 | tf_op jit(solution)/shard_map/ppermute | solution.py:265
  79.7 18.0 %collective-permute-start.15 = (bf16[128,3072]{1,0:T(8,128)(2,1)S(1)}, bf16[128,3072]{1,0:T(8,128)(2,1)S(1)}, u32[]{:S(2)}, u32[]{:S(2)}) collective-permute-start(bf16[128,3072]{1,0:T(8,128)(2,1)S(1)} %get-tuple-element.46.b0), channel_id=1, source_target_pairs={{0,2},{1,3},{2,0},{3,1},{4,6},{5,7},{6,4},{7,5},{8,10},{9,11},{10,... | collective-permute-start | bytes 2359304 | tf_op jit(solution)/shard_map/ppermute | solution.py:265
  81.1 20.5 %collective-permute-start.16 = (bf16[128,3072]{1,0:T(8,128)(2,1)S(1)}, bf16[128,3072]{1,0:T(8,128)(2,1)S(1)}, u32[]{:S(2)}, u32[]{:S(2)}) collective-permute-start(bf16[128,3072]{1,0:T(8,128)(2,1)S(1)} %get-tuple-element.46.b0), channel_id=1, source_target_pairs={{0,1},{1,2},{2,3},{3,0},{4,5},{5,6},{6,7},{7,4},{8,9},{9,10},{10,1... | collective-permute-start | bytes 2359304 | tf_op jit(solution)/shard_map/ppermute | solution.py:265
  83.5 18.1 %copy-start.5 = (bf16[256,384]{1,0:T(8,128)(2,1)S(1)}, bf16[256,384]{1,0:T(8,128)(2,1)}, u32[]{:S(2)}) copy-start(bf16[256,384]{1,0:T(8,128)(2,1)} %get-tuple-element.54.grad_y) | copy-start | bytes 589828
  83.5 26.3 %collective-permute-start.13 = (bf16[64,3072]{1,0:T(8,128)(2,1)S(1)}, bf16[64,3072]{1,0:T(8,128)(2,1)S(1)}, u32[]{:S(2)}, u32[]{:S(2)}) collective-permute-start(bf16[64,3072]{1,0:T(8,128)(2,1)S(1)} %get-tuple-element.58.b0), channel_id=1, source_target_pairs={{0,3},{1,0},{2,1},{3,2},{4,7},{5,4},{6,5},{7,6},{8,11},{9,8},{10,9... | collective-permute-start | bytes 1179656 | tf_op jit(solution)/shard_map/ppermute | solution.py:265
  88.1 21.7 %collective-permute-start.17 = (bf16[64,3072]{1,0:T(8,128)(2,1)S(1)}, bf16[64,3072]{1,0:T(8,128)(2,1)S(1)}, u32[]{:S(2)}, u32[]{:S(2)}) collective-permute-start(bf16[64,3072]{1,0:T(8,128)(2,1)S(1)} %get-tuple-element.58.b0), channel_id=1, source_target_pairs={{0,2},{1,3},{2,0},{3,1},{4,6},{5,7},{6,4},{7,5},{8,10},{9,11},{10,... | collective-permute-start | bytes 1179656 | tf_op jit(solution)/shard_map/ppermute | solution.py:265
  97.6 12.5 %collective-permute-start.18 = (bf16[64,3072]{1,0:T(8,128)(2,1)S(1)}, bf16[64,3072]{1,0:T(8,128)(2,1)}, u32[]{:S(2)}, u32[]{:S(2)}) collective-permute-start(bf16[64,3072]{1,0:T(8,128)(2,1)S(1)} %get-tuple-element.58.b0), channel_id=1, source_target_pairs={{0,1},{1,2},{2,3},{3,0},{4,5},{5,6},{6,7},{7,4},{8,9},{9,10},{10,1... | collective-permute-start | bytes 1179656 | tf_op jit(solution)/shard_map/ppermute | solution.py:265
  105.2 17.4 %all-to-all-start.1 = ((f32[32,1,3072]{2,1,0:T(1,128)}), f32[32,1,3072]{2,1,0:T(1,128)}, u32[]{:S(2)}, u32[]{:S(2)}) async-start(f32[32,1,3072]{2,1,0:T(1,128)} %shard_map.118), calls=%async_computation.1 | async-start | bytes 786432 | tf_op jit(solution)/shard_map/all_to_all | solution.py:377
  113.6 0.7 copy-start.4
  114.3 11.0 %copy-start.12 = (f32[384]{0:T(512)S(1)}, f32[384]{0:T(512)}, u32[]{:S(2)}) copy-start(f32[384]{0:T(512)} %param.18) | copy-start | bytes 4612
  114.3 1.7 %collective-permute-start.19 = (f32[128,384]{1,0:T(8,128)}, f32[128,384]{1,0:T(8,128)S(1)}, u32[]{:S(2)}, u32[]{:S(2)}) collective-permute-start(f32[128,384]{1,0:T(8,128)} %get-tuple-element.60), channel_id=1, source_target_pairs={{0,64},{64,0},{1,65},{65,1},{2,66},{66,2},{3,67},{67,3},{4,68},{68... | collective-permute-start | bytes 589832 | tf_op jit(solution)/shard_map/ppermute | solution.py:387
  116.9 5.7 %collective-permute-start.21 = (f32[4,8,384]{2,1,0:T(8,128)S(1)}, f32[4,8,384]{2,1,0:T(8,128)S(1)}, u32[]{:S(2)}, u32[]{:S(2)}) collective-permute-start(f32[4,8,384]{2,1,0:T(8,128)S(1)} %get-tuple-element.65), channel_id=1, source_target_pairs={{0,16},{16,32},{32,48},{48,0},{1,17},{17,33},{33,49},{49,1},{2,18}... | collective-permute-start | bytes 147464 | tf_op jit(solution)/shard_map/ppermute | solution.py:392
  118.5 6.0 %collective-permute-start.20 = (f32[4,8,384]{2,1,0:T(8,128)S(1)}, f32[4,8,384]{2,1,0:T(8,128)S(1)}, u32[]{:S(2)}, u32[]{:S(2)}) collective-permute-start(f32[4,8,384]{2,1,0:T(8,128)S(1)} %get-tuple-element.66), channel_id=1, source_target_pairs={{0,32},{16,48},{32,0},{48,16},{1,33},{17,49},{33,1},{49,17},{2,34}... | collective-permute-start | bytes 147464 | tf_op jit(solution)/shard_map/ppermute | solution.py:392
  121.2 4.1 %collective-permute-start.22 = (f32[4,8,384]{2,1,0:T(8,128)S(1)}, f32[4,8,384]{2,1,0:T(8,128)S(1)}, u32[]{:S(2)}, u32[]{:S(2)}) collective-permute-start(f32[4,8,384]{2,1,0:T(8,128)S(1)} %get-tuple-element.64), channel_id=1, source_target_pairs={{0,48},{16,0},{32,16},{48,32},{1,49},{17,1},{33,17},{49,33},{2,50}... | collective-permute-start | bytes 147464 | tf_op jit(solution)/shard_map/ppermute | solution.py:392

commit v9 on v8

--- a/solution.py
+++ b/solution.py
@@ -220,7 +220,7 @@
         store(True)
 
 
-def call(kernel, where, args, outs, scratch=(), steps=6, vmem=28 * 2**20):
+def call(kernel, where, args, outs, scratch=(), steps=6, vmem=18 * 2**20):
     def spec(shape, block, index):
         if block is None:
             return pl.BlockSpec(shape, lambda t, w: (0,) * len(shape))

time: 127 us -> 124 us (0.976)
    unnamed x32 -> x30, local copies, waits for them, and re-layouts: 3.33 us -> 2.65 us
where the time goes in v9:
time: 124 us
  waiting for transfers between devices  49.4 us (40%)
  starting transfers between devices  41.6 us (34%)
  Pallas kernels  20.8 us (17%)
  local copies, waits for them, and re-layouts  8.03 us (6%)
  other arithmetic  3.06 us (2%)
    ppermute x15, waiting for transfers between devices, permutes(): lax.ppermute(parts[k], ('dp', 'col'), pairs(first, sign * (k + 1)))  46.5 us
    ppermute x15, starting transfers between devices, permutes(): lax.ppermute(parts[k], ('dp', 'col'), pairs(first, sign * (k + 1)))  24.6 us
    pallas_call x7, Pallas kernels, call(): pl.pallas_call(kernel, grid_spec=pltpu.PrefetchScalarGridSpec(num_scalar_...  20.8 us
    ppermute x3, starting transfers between devices, local(): lax.ppermute(for_row(row + k), 'row', shift_row(k))  5.72 us
    all_to_all x1, starting transfers between devices, local(): share = lax.all_to_all(share, 'col', 0, 0, tiled=True)  5.53 us
    all_to_all x1, starting transfers between devices, local(): terms = lax.all_to_all(terms, ('dp', 'col'), 0, 0, tiled=True)  4.59 us
    unnamed x30, local copies, waits for them, and re-layouts  2.65 us
  transfers between devices with their start and end apart: 25, of which 14 were waited for; matrix products, arithmetic and copies ran while one was open for 8% of the time, Pallas kernels for 9%

profile of v9, /device:TPU:0, one launch (start us, length us, event | category | flops | bytes accessed | tf_op | source)
XLA Modules:
  0.0 123.8 jit_solution(9772559496249786565)
XLA Ops:
  0.7 0.5 collective-permute-start.2
  1.3 0.4 collective-permute-start.1
  1.7 0.6 pad_add_fusion.where
  3.2 0.6 copy-done.9
  3.8 7.5 %shard_map.113 = (bf16[192,3072]{1,0:T(8,128)(2,1)}, bf16[192,3072]{1,0:T(8,128)(2,1)}, bf16[192,3072]{1,0:T(8,128)(2,1)}, bf16[192,3072]{1,0:T(8,128)(2,1)}, bf...) custom-call(s32[3]{0:T(128)} %pad_add_fusion.where, bf16[128,384]{1,0:T(8,128)(2,1)} %own.1, bf16[128,384]{1,0:T(8,128)(2,1)} %copy-done.2, ...), custom_call_target="tpu_custom_call" | custom-call | flops 1 | bytes 1 | tf_op jit(solution)/shard_map/pallas_call | solution.py:229
  11.4 1.7 %collective-permute-start.4 = (bf16[192,3072]{1,0:T(8,128)(2,1)}, bf16[192,3072]{1,0:T(8,128)(2,1)S(1)}, u32[]{:S(2)}, u32[]{:S(2)}) collective-permute-start(bf16[192,3072]{1,0:T(8,128)(2,1)} %get-tuple-element.34), channel_id=1, source_target_pairs={{0,1},{1,2},{2,3},{3,0},{4,5},{5,6},{6,7},{7,4},{8,9},{9,10},{10,1... | collective-permute-start | bytes 3538952 | tf_op jit(solution)/shard_map/ppermute | solution.py:265
  13.1 2.9 %collective-permute-start.5 = (bf16[192,3072]{1,0:T(8,128)(2,1)}, bf16[192,3072]{1,0:T(8,128)(2,1)}, u32[]{:S(2)}, u32[]{:S(2)}) collective-permute-start(bf16[192,3072]{1,0:T(8,128)(2,1)} %get-tuple-element.35), channel_id=1, source_target_pairs={{0,2},{1,3},{2,0},{3,1},{4,6},{5,7},{6,4},{7,5},{8,10},{9,11},{10,... | collective-permute-start | bytes 3538952 | tf_op jit(solution)/shard_map/ppermute | solution.py:265
  16.0 1.3 %collective-permute-start.6 = (bf16[192,3072]{1,0:T(8,128)(2,1)}, bf16[192,3072]{1,0:T(8,128)(2,1)}, u32[]{:S(2)}, u32[]{:S(2)}) collective-permute-start(bf16[192,3072]{1,0:T(8,128)(2,1)} %get-tuple-element.36), channel_id=1, source_target_pairs={{0,3},{1,0},{2,1},{3,2},{4,7},{5,4},{6,5},{7,6},{8,11},{9,8},{10,9... | collective-permute-start | bytes 3538952 | tf_op jit(solution)/shard_map/ppermute | solution.py:265
  17.3 1.0 pad_maximum_fusion
  18.4 0.9 slice.3
  19.7 0.7 broadcast_in_dim.29
  20.4 5.5 %all-to-all-start = ((f32[16,32,128]{2,1,0:T(8,128)}), f32[16,32,128]{2,1,0:T(8,128)S(1)}, u32[]{:S(2)}, u32[]{:S(2)}) async-start(f32[16,32,128]{2,1,0:T(8,128)} %broadcast_in_dim.29), calls=%async_computation | async-start | bytes 524288 | tf_op jit(solution)/shard_map/all_to_all | solution.py:320
  26.0 3.1 %collective-permute-done.4.refs_1_ = bf16[192,3072]{1,0:T(8,128)(2,1)S(1)} collective-permute-done((bf16[192,3072]{1,0:T(8,128)(2,1)}, bf16[192,3072]{1,0:T(8,128)(2,1)S(1)}, u32[]{:S(2)}, u32[]{:S(2)}) %collective-permute-start.4) | collective-permute-done | bytes 1179680 | tf_op jit(solution)/shard_map/ppermute | solution.py:265
  29.0 15.5 %collective-permute-done.5.refs_2_ = bf16[192,3072]{1,0:T(8,128)(2,1)} collective-permute-done((bf16[192,3072]{1,0:T(8,128)(2,1)}, bf16[192,3072]{1,0:T(8,128)(2,1)}, u32[]{:S(2)}, u32[]{:S(2)}) %collective-permute-start.5) | collective-permute-done | bytes 1179680 | tf_op jit(solution)/shard_map/ppermute | solution.py:265
  44.5 3.3 %shard_map.114 = (f32[48,3072]{1,0:T(8,128)S(1)}, bf16[48,3072]{1,0:T(8,128)(2,1)}, bf16[48,3072]{1,0:T(8,128)(2,1)}, bf16[48,3072]{1,0:T(8,128)(2,1)}) custom-call(s32[3]{0:T(128)S(1)} %copy-done.5, bf16[192,3072]{1,0:T(8,128)(2,1)S(1)} %copy-done, bf16[192,3072]{1,0:T(8,128)(2,1)S(1)} %collective-permute-done.4.refs_1_, ...), custom_call_target="tpu_custom_call" | custom-call | flops 1 | bytes 1 | tf_op jit(solution)/shard_map/pallas_call | solution.py:229
  47.9 1.9 %collective-permute-start.7 = (bf16[48,3072]{1,0:T(8,128)(2,1)}, bf16[48,3072]{1,0:T(8,128)(2,1)S(1)}, u32[]{:S(2)}, u32[]{:S(2)}) collective-permute-start(bf16[48,3072]{1,0:T(8,128)(2,1)} %get-tuple-element.38), channel_id=1, source_target_pairs={{0,4},{1,5},{2,6},{3,7},{4,8},{5,9},{6,10},{7,11},{8,12},{9,13},{1... | collective-permute-start | bytes 884744 | tf_op jit(solution)/shard_map/ppermute | solution.py:265
  49.8 3.6 %collective-permute-start.8 = (bf16[48,3072]{1,0:T(8,128)(2,1)}, bf16[48,3072]{1,0:T(8,128)(2,1)S(1)}, u32[]{:S(2)}, u32[]{:S(2)}) collective-permute-start(bf16[48,3072]{1,0:T(8,128)(2,1)} %get-tuple-element.39), channel_id=1, source_target_pairs={{0,8},{1,9},{2,10},{3,11},{4,12},{5,13},{6,14},{7,15},{8,0},{9,1},... | collective-permute-start | bytes 884744 | tf_op jit(solution)/shard_map/ppermute | solution.py:265
  53.4 1.0 collective-permute-start.9
  54.7 2.1 %collective-permute-done.7.a = bf16[48,3072]{1,0:T(8,128)(2,1)S(1)} collective-permute-done((bf16[48,3072]{1,0:T(8,128)(2,1)}, bf16[48,3072]{1,0:T(8,128)(2,1)S(1)}, u32[]{:S(2)}, u32[]{:S(2)}) %collective-permute-start.7) | collective-permute-done | bytes 294944 | tf_op jit(solution)/shard_map/ppermute | solution.py:265
  56.8 4.6 %collective-permute-done.8.b = bf16[48,3072]{1,0:T(8,128)(2,1)S(1)} collective-permute-done((bf16[48,3072]{1,0:T(8,128)(2,1)}, bf16[48,3072]{1,0:T(8,128)(2,1)S(1)}, u32[]{:S(2)}, u32[]{:S(2)}) %collective-permute-start.8) | collective-permute-done | bytes 294944 | tf_op jit(solution)/shard_map/ppermute | solution.py:265
  61.4 1.8 %shard_map.115.refs_0_ = bf16[48,3072]{1,0:T(8,128)(2,1)S(1)} custom-call(s32[3]{0:T(128)S(1)} %copy-done.5, f32[48,3072]{1,0:T(8,128)S(1)} %get-tuple-element.37.keep, bf16[48,3072]{1,0:T(8,128)(2,1)S(1)} %collective-permute-done.7.a, bf16[48,3072]{1,0:T(8,128)(2,1)S(1)} %collective-permute-done.8.b, bf16[48,3072]{1,0:T(8,128)(2,1)S(1)} %collective-permute-done.9.c, ...), custom_call_target="tpu_custom_call" | custom-call | flops 1 | bytes 1 | tf_op jit(solution)/shard_map/pallas_call | solution.py:229
  63.2 2.2 %collective-permute-start.10 = (bf16[48,3072]{1,0:T(8,128)(2,1)S(1)}, bf16[48,3072]{1,0:T(8,128)(2,1)S(1)}, u32[]{:S(2)}, u32[]{:S(2)}) collective-permute-start(bf16[48,3072]{1,0:T(8,128)(2,1)S(1)} %shard_map.115.refs_0_), channel_id=1, source_target_pairs={{0,12},{1,13},{2,14},{3,15},{4,0},{5,1},{6,2},{7,3},{8,4},{9,5},{1... | collective-permute-start | bytes 884744 | tf_op jit(solution)/shard_map/ppermute | solution.py:265
  65.4 1.4 %collective-permute-start.11 = (bf16[48,3072]{1,0:T(8,128)(2,1)S(1)}, bf16[48,3072]{1,0:T(8,128)(2,1)S(1)}, u32[]{:S(2)}, u32[]{:S(2)}) collective-permute-start(bf16[48,3072]{1,0:T(8,128)(2,1)S(1)} %shard_map.115.refs_0_), channel_id=1, source_target_pairs={{0,8},{1,9},{2,10},{3,11},{4,12},{5,13},{6,14},{7,15},{8,0},{9,1},... | collective-permute-start | bytes 884744 | tf_op jit(solution)/shard_map/ppermute | solution.py:265
  67.2 1.1 shard_map.116.normed_t
  68.3 4.5 %collective-permute-done.10.refs_1_ = bf16[48,3072]{1,0:T(8,128)(2,1)S(1)} collective-permute-done((bf16[48,3072]{1,0:T(8,128)(2,1)S(1)}, bf16[48,3072]{1,0:T(8,128)(2,1)S(1)}, u32[]{:S(2)}, u32[]{:S(2)}) %collective-permute-start.10) | collective-permute-done | bytes 294944 | tf_op jit(solution)/shard_map/ppermute | solution.py:265
  72.8 0.9 collective-permute-done.11.refs_2_
  73.7 3.1 %collective-permute-done.12.refs_3_ = bf16[48,3072]{1,0:T(8,128)(2,1)S(1)} collective-permute-done((bf16[48,3072]{1,0:T(8,128)(2,1)S(1)}, bf16[48,3072]{1,0:T(8,128)(2,1)S(1)}, u32[]{:S(2)}, u32[]{:S(2)}) %collective-permute-start.12) | collective-permute-done | bytes 294944 | tf_op jit(solution)/shard_map/ppermute | solution.py:265
  76.8 0.6 shard_map.117
  77.4 2.4 %collective-permute-start.14 = (bf16[128,3072]{1,0:T(8,128)(2,1)S(1)}, bf16[128,3072]{1,0:T(8,128)(2,1)S(1)}, u32[]{:S(2)}, u32[]{:S(2)}) collective-permute-start(bf16[128,3072]{1,0:T(8,128)(2,1)S(1)} %get-tuple-element.46.b0), channel_id=1, source_target_pairs={{0,3},{1,0},{2,1},{3,2},{4,7},{5,4},{6,5},{7,6},{8,11},{9,8},{10,9... | collective-permute-start | bytes 2359304 | tf_op jit(solution)/shard_map/ppermute | solution.py:265
  79.8 1.4 %collective-permute-start.15 = (bf16[128,3072]{1,0:T(8,128)(2,1)S(1)}, bf16[128,3072]{1,0:T(8,128)(2,1)S(1)}, u32[]{:S(2)}, u32[]{:S(2)}) collective-permute-start(bf16[128,3072]{1,0:T(8,128)(2,1)S(1)} %get-tuple-element.46.b0), channel_id=1, source_target_pairs={{0,2},{1,3},{2,0},{3,1},{4,6},{5,7},{6,4},{7,5},{8,10},{9,11},{10,... | collective-permute-start | bytes 2359304 | tf_op jit(solution)/shard_map/ppermute | solution.py:265
  81.2 0.6 collective-permute-start.16
  81.8 1.8 %constant_dynamic-slice_fusion.1.w_in = bf16[384,3072]{1,0:T(8,128)(2,1)S(1)} fusion(bf16[384,6144]{1,0:T(8,128)(2,1)} %w_in.1, s32[]{:T(128)S(6)} %select_n.68), kind=kLoop, calls=%fused_computation.23 | loop fusion | bytes 4718596 | tf_op jit(solution)/shard_map/dynamic_slice | solution.py:359
  83.6 2.7 %collective-permute-start.13 = (bf16[64,3072]{1,0:T(8,128)(2,1)S(1)}, bf16[64,3072]{1,0:T(8,128)(2,1)S(1)}, u32[]{:S(2)}, u32[]{:S(2)}) collective-permute-start(bf16[64,3072]{1,0:T(8,128)(2,1)S(1)} %get-tuple-element.58.b0), channel_id=1, source_target_pairs={{0,3},{1,0},{2,1},{3,2},{4,7},{5,4},{6,5},{7,6},{8,11},{9,8},{10,9... | collective-permute-start | bytes 1179656 | tf_op jit(solution)/shard_map/ppermute | solution.py:265
  86.3 1.9 %constant_dynamic-slice_fusion.w_out = bf16[3072,384]{1,0:T(8,128)(2,1)S(1)} fusion(bf16[6144,384]{1,0:T(8,128)(2,1)} %w_out.1, s32[]{:T(128)S(6)} %select_n.68), kind=kLoop, calls=%fused_computation.22 | loop fusion | bytes 4718596 | tf_op jit(solution)/shard_map/dynamic_slice | solution.py:360
  88.2 1.0 collective-permute-start.17
  89.2 8.5 %collective-permute-done.14.b1 = bf16[128,3072]{1,0:T(8,128)(2,1)S(1)} collective-permute-done((bf16[128,3072]{1,0:T(8,128)(2,1)S(1)}, bf16[128,3072]{1,0:T(8,128)(2,1)S(1)}, u32[]{:S(2)}, u32[]{:S(2)}) %collective-permute-start.14) | collective-permute-done | bytes 786464 | tf_op jit(solution)/shard_map/ppermute | solution.py:265
  97.8 3.9 %collective-permute-done.16.b3 = bf16[128,3072]{1,0:T(8,128)(2,1)S(1)} collective-permute-done((bf16[128,3072]{1,0:T(8,128)(2,1)S(1)}, bf16[128,3072]{1,0:T(8,128)(2,1)S(1)}, u32[]{:S(2)}, u32[]{:S(2)}) %collective-permute-start.16) | collective-permute-done | bytes 786464 | tf_op jit(solution)/shard_map/ppermute | solution.py:265
  101.7 3.6 %shard_map.118 = f32[32,1,3072]{2,1,0:T(1,128)} custom-call(s32[3]{0:T(128)S(1)} %copy-done.5, bf16[128,3072]{1,0:T(8,128)(2,1)S(1)} %get-tuple-element.46.b0, bf16[128,3072]{1,0:T(8,128)(2,1)S(1)} %collective-permute-done.14.b1, bf16[128,3072]{1,0:T(8,128)(2,1)S(1)} %collective-permute-done.15.b2, bf16[128,3072]{1,0:T(8,128)(2,1)S(1)} %collective-permute-done.16.b3, ...), custom_call_target="tpu_custom_call" | custom-call | flops 1 | bytes 1 | tf_op jit(solution)/shard_map/pallas_call | solution.py:229
  105.3 4.6 %all-to-all-start.1 = ((f32[32,1,3072]{2,1,0:T(1,128)}), f32[32,1,3072]{2,1,0:T(1,128)}, u32[]{:S(2)}, u32[]{:S(2)}) async-start(f32[32,1,3072]{2,1,0:T(1,128)} %shard_map.118), calls=%async_computation.1 | async-start | bytes 786432 | tf_op jit(solution)/shard_map/all_to_all | solution.py:377
  110.3 2.9 %shard_map.119 = (f32[128,384]{1,0:T(8,128)S(1)}, f32[128,384]{1,0:T(8,128)S(1)}) custom-call(s32[3]{0:T(128)S(1)} %copy-done.5, bf16[64,3072]{1,0:T(8,128)(2,1)S(1)} %get-tuple-element.58.b0, bf16[64,3072]{1,0:T(8,128)(2,1)S(1)} %collective-permute-done.13.b1, bf16[64,3072]{1,0:T(8,128)(2,1)} %collective-permute-done.17.b2, ...), custom_call_target="tpu_custom_call" | custom-call | flops 1 | bytes 1 | tf_op jit(solution)/shard_map/pallas_call | solution.py:229
  113.3 1.4 %collective-permute-done.19 = f32[128,384]{1,0:T(8,128)S(1)} collective-permute-done((f32[128,384]{1,0:T(8,128)S(1)}, f32[128,384]{1,0:T(8,128)S(1)}, u32[]{:S(2)}, u32[]{:S(2)}) %collective-permute-start.19) | collective-permute-done | bytes 196640 | tf_op jit(solution)/shard_map/ppermute | solution.py:387
  114.8 1.6 %collective-permute-start.21 = (f32[4,8,384]{2,1,0:T(8,128)S(1)}, f32[4,8,384]{2,1,0:T(8,128)S(1)}, u32[]{:S(2)}, u32[]{:S(2)}) collective-permute-start(f32[4,8,384]{2,1,0:T(8,128)S(1)} %get-tuple-element.65), channel_id=1, source_target_pairs={{0,16},{16,32},{32,48},{48,0},{1,17},{17,33},{33,49},{49,1},{2,18}... | collective-permute-start | bytes 147464 | tf_op jit(solution)/shard_map/ppermute | solution.py:392
  116.3 2.7 %collective-permute-start.20 = (f32[4,8,384]{2,1,0:T(8,128)S(1)}, f32[4,8,384]{2,1,0:T(8,128)S(1)}, u32[]{:S(2)}, u32[]{:S(2)}) collective-permute-start(f32[4,8,384]{2,1,0:T(8,128)S(1)} %get-tuple-element.66), channel_id=1, source_target_pairs={{0,32},{16,48},{32,0},{48,16},{1,33},{17,49},{33,1},{49,17},{2,34}... | collective-permute-start | bytes 147464 | tf_op jit(solution)/shard_map/ppermute | solution.py:392
  119.0 1.4 %collective-permute-start.22 = (f32[4,8,384]{2,1,0:T(8,128)S(1)}, f32[4,8,384]{2,1,0:T(8,128)S(1)}, u32[]{:S(2)}, u32[]{:S(2)}) collective-permute-start(f32[4,8,384]{2,1,0:T(8,128)S(1)} %get-tuple-element.64), channel_id=1, source_target_pairs={{0,48},{16,0},{32,16},{48,32},{1,49},{17,1},{33,17},{49,33},{2,50}... | collective-permute-start | bytes 147464 | tf_op jit(solution)/shard_map/ppermute | solution.py:392
  120.5 1.1 copy.12
  121.7 0.6 copy.13
  122.3 0.9 collective-permute-done.22
  123.2 0.7 fusion.7
  (59 shorter events, 2.8 us)
Async XLA Ops:
  0.6 1.9 %collective-permute-start = (bf16[128,384]{1,0:T(8,128)(2,1)}, bf16[128,384]{1,0:T(8,128)(2,1)S(1)}, u32[]{:S(2)}, u32[]{:S(2)}) collective-permute-start(bf16[128,384]{1,0:T(8,128)(2,1)} %own.1), channel_id=1, source_target_pairs={{0,64},{64,0},{1,65},{65,1},{2,66},{66,2},{3,67},{67,3},{4,68},{68... | collective-permute-start | bytes 294920 | tf_op jit(solution)/shard_map/ppermute | solution.py:292
  0.7 1.8 %collective-permute-start.2 = (bf16[128,384]{1,0:T(8,128)(2,1)}, bf16[128,384]{1,0:T(8,128)(2,1)S(1)}, u32[]{:S(2)}, u32[]{:S(2)}) collective-permute-start(bf16[128,384]{1,0:T(8,128)(2,1)} %r0.1), channel_id=1, source_target_pairs={{0,64},{64,0},{1,65},{65,1},{2,66},{66,2},{3,67},{67,3},{4,68},{68... | collective-permute-start | bytes 294920 | tf_op jit(solution)/shard_map/ppermute | solution.py:293
  1.2 1.3 %collective-permute-start.3 = (s32[1,128]{1,0:T(1,128)}, s32[1,128]{1,0:T(1,128)S(1)}, u32[]{:S(2)}, u32[]{:S(2)}) collective-permute-start(s32[1,128]{1,0:T(1,128)} %bitcast.45), channel_id=1, source_target_pairs={{0,64},{64,0},{1,65},{65,1},{2,66},{66,2},{3,67},{67,3},{4,68},{68... | collective-permute-start | bytes 1544 | tf_op jit(solution)/shard_map/ppermute | solution.py:295
  1.3 1.6 %collective-permute-start.1 = (bf16[128,384]{1,0:T(8,128)(2,1)}, bf16[128,384]{1,0:T(8,128)(2,1)S(1)}, u32[]{:S(2)}, u32[]{:S(2)}) collective-permute-start(bf16[128,384]{1,0:T(8,128)(2,1)} %g0.1), channel_id=1, source_target_pairs={{0,64},{64,0},{1,65},{65,1},{2,66},{66,2},{3,67},{67,3},{4,68},{68... | collective-permute-start | bytes 294920 | tf_op jit(solution)/shard_map/ppermute | solution.py:294
  2.3 15.1 %copy-start.1 = (bf16[128,384]{1,0:T(8,128)(2,1)S(1)}, bf16[128,384]{1,0:T(8,128)(2,1)}, u32[]{:S(2)}) copy-start(bf16[128,384]{1,0:T(8,128)(2,1)} %own.1) | copy-start | bytes 294916
  2.3 15.1 %copy-start.7 = (bf16[128,384]{1,0:T(8,128)(2,1)S(1)}, bf16[128,384]{1,0:T(8,128)(2,1)}, u32[]{:S(2)}) copy-start(bf16[128,384]{1,0:T(8,128)(2,1)} %r0.1) | copy-start | bytes 294916
  2.5 0.6 copy-start.12
  2.5 0.6 copy-start.2
  2.5 0.7 copy-start.8
  3.2 0.6 copy-start.9
  11.3 33.2 %copy-start = (bf16[192,3072]{1,0:T(8,128)(2,1)S(1)}, bf16[192,3072]{1,0:T(8,128)(2,1)}, u32[]{:S(2)}) copy-start(bf16[192,3072]{1,0:T(8,128)(2,1)} %get-tuple-element.33.refs_0_) | copy-start | bytes 3538948
  11.3 33.2 %copy-start.5 = (s32[3]{0:T(128)S(1)}, s32[3]{0:T(128)}, u32[]{:S(2)}) copy-start(s32[3]{0:T(128)} %pad_add_fusion.where) | copy-start | bytes 40
  11.4 17.7 %collective-permute-start.4 = (bf16[192,3072]{1,0:T(8,128)(2,1)}, bf16[192,3072]{1,0:T(8,128)(2,1)S(1)}, u32[]{:S(2)}, u32[]{:S(2)}) collective-permute-start(bf16[192,3072]{1,0:T(8,128)(2,1)} %get-tuple-element.34), channel_id=1, source_target_pairs={{0,1},{1,2},{2,3},{3,0},{4,5},{5,6},{6,7},{7,4},{8,9},{9,10},{10,1... | collective-permute-start | bytes 3538952 | tf_op jit(solution)/shard_map/ppermute | solution.py:265
  13.1 31.4 %collective-permute-start.5 = (bf16[192,3072]{1,0:T(8,128)(2,1)}, bf16[192,3072]{1,0:T(8,128)(2,1)}, u32[]{:S(2)}, u32[]{:S(2)}) collective-permute-start(bf16[192,3072]{1,0:T(8,128)(2,1)} %get-tuple-element.35), channel_id=1, source_target_pairs={{0,2},{1,3},{2,0},{3,1},{4,6},{5,7},{6,4},{7,5},{8,10},{9,11},{10,... | collective-permute-start | bytes 3538952 | tf_op jit(solution)/shard_map/ppermute | solution.py:265
  16.0 28.5 %collective-permute-start.6 = (bf16[192,3072]{1,0:T(8,128)(2,1)}, bf16[192,3072]{1,0:T(8,128)(2,1)}, u32[]{:S(2)}, u32[]{:S(2)}) collective-permute-start(bf16[192,3072]{1,0:T(8,128)(2,1)} %get-tuple-element.36), channel_id=1, source_target_pairs={{0,3},{1,0},{2,1},{3,2},{4,7},{5,4},{6,5},{7,6},{8,11},{9,8},{10,9... | collective-permute-start | bytes 3538952 | tf_op jit(solution)/shard_map/ppermute | solution.py:265
  20.4 34.3 %all-to-all-start = ((f32[16,32,128]{2,1,0:T(8,128)}), f32[16,32,128]{2,1,0:T(8,128)S(1)}, u32[]{:S(2)}, u32[]{:S(2)}) async-start(f32[16,32,128]{2,1,0:T(8,128)} %broadcast_in_dim.29), calls=%async_computation | async-start | bytes 524288 | tf_op jit(solution)/shard_map/all_to_all | solution.py:320
  26.0 28.4 %copy-start.13 = (s32[128]{0:T(128)S(1)}, s32[128]{0:T(128)}, u32[]{:S(2)}) copy-start(s32[128]{0:T(128)} %param.19) | copy-start | bytes 1540
  26.0 28.7 %copy-start.10 = (f32[6144]{0:T(1024)S(1)}, f32[6144]{0:T(1024)}, u32[]{:S(2)}) copy-start(f32[6144]{0:T(1024)} %param.16) | copy-start | bytes 73732
  47.9 19.3 %copy-start.3 = (bf16[128,384]{1,0:T(8,128)(2,1)S(1)}, bf16[128,384]{1,0:T(8,128)(2,1)}, u32[]{:S(2)}) copy-start(bf16[128,384]{1,0:T(8,128)(2,1)} %copy-done.2) | copy-start | bytes 294916
  47.9 19.3 %copy-start.6 = (f32[384]{0:T(512)S(1)}, f32[384]{0:T(512)}, u32[]{:S(2)}) copy-start(f32[384]{0:T(512)} %gain.3) | copy-start | bytes 4612
  47.9 8.9 %collective-permute-start.7 = (bf16[48,3072]{1,0:T(8,128)(2,1)}, bf16[48,3072]{1,0:T(8,128)(2,1)S(1)}, u32[]{:S(2)}, u32[]{:S(2)}) collective-permute-start(bf16[48,3072]{1,0:T(8,128)(2,1)} %get-tuple-element.38), channel_id=1, source_target_pairs={{0,4},{1,5},{2,6},{3,7},{4,8},{5,9},{6,10},{7,11},{8,12},{9,13},{1... | collective-permute-start | bytes 884744 | tf_op jit(solution)/shard_map/ppermute | solution.py:265
  49.8 11.7 %collective-permute-start.8 = (bf16[48,3072]{1,0:T(8,128)(2,1)}, bf16[48,3072]{1,0:T(8,128)(2,1)S(1)}, u32[]{:S(2)}, u32[]{:S(2)}) collective-permute-start(bf16[48,3072]{1,0:T(8,128)(2,1)} %get-tuple-element.39), channel_id=1, source_target_pairs={{0,8},{1,9},{2,10},{3,11},{4,12},{5,13},{6,14},{7,15},{8,0},{9,1},... | collective-permute-start | bytes 884744 | tf_op jit(solution)/shard_map/ppermute | solution.py:265
  53.4 8.1 %collective-permute-start.9 = (bf16[48,3072]{1,0:T(8,128)(2,1)}, bf16[48,3072]{1,0:T(8,128)(2,1)S(1)}, u32[]{:S(2)}, u32[]{:S(2)}) collective-permute-start(bf16[48,3072]{1,0:T(8,128)(2,1)} %get-tuple-element.40), channel_id=1, source_target_pairs={{0,12},{1,13},{2,14},{3,15},{4,0},{5,1},{6,2},{7,3},{8,4},{9,5},{1... | collective-permute-start | bytes 884744 | tf_op jit(solution)/shard_map/ppermute | solution.py:265
  63.2 9.7 %collective-permute-start.10 = (bf16[48,3072]{1,0:T(8,128)(2,1)S(1)}, bf16[48,3072]{1,0:T(8,128)(2,1)S(1)}, u32[]{:S(2)}, u32[]{:S(2)}) collective-permute-start(bf16[48,3072]{1,0:T(8,128)(2,1)S(1)} %shard_map.115.refs_0_), channel_id=1, source_target_pairs={{0,12},{1,13},{2,14},{3,15},{4,0},{5,1},{6,2},{7,3},{8,4},{9,5},{1... | collective-permute-start | bytes 884744 | tf_op jit(solution)/shard_map/ppermute | solution.py:265
  65.4 8.3 %collective-permute-start.11 = (bf16[48,3072]{1,0:T(8,128)(2,1)S(1)}, bf16[48,3072]{1,0:T(8,128)(2,1)S(1)}, u32[]{:S(2)}, u32[]{:S(2)}) collective-permute-start(bf16[48,3072]{1,0:T(8,128)(2,1)S(1)} %shard_map.115.refs_0_), channel_id=1, source_target_pairs={{0,8},{1,9},{2,10},{3,11},{4,12},{5,13},{6,14},{7,15},{8,0},{9,1},... | collective-permute-start | bytes 884744 | tf_op jit(solution)/shard_map/ppermute | solution.py:265
  66.8 10.0 %collective-permute-start.12 = (bf16[48,3072]{1,0:T(8,128)(2,1)S(1)}, bf16[48,3072]{1,0:T(8,128)(2,1)S(1)}, u32[]{:S(2)}, u32[]{:S(2)}) collective-permute-start(bf16[48,3072]{1,0:T(8,128)(2,1)S(1)} %shard_map.115.refs_0_), channel_id=1, source_target_pairs={{0,4},{1,5},{2,6},{3,7},{4,8},{5,9},{6,10},{7,11},{8,12},{9,13},{1... | collective-permute-start | bytes 884744 | tf_op jit(solution)/shard_map/ppermute | solution.py:265
  77.4 20.3 %collective-permute-start.14 = (bf16[128,3072]{1,0:T(8,128)(2,1)S(1)}, bf16[128,3072]{1,0:T(8,128)(2,1)S(1)}, u32[]{:S(2)}, u32[]{:S(2)}) collective-permute-start(bf16[128,3072]{1,0:T(8,128)(2,1)S(1)} %get-tuple-element.46.b0), channel_id=1, source_target_pairs={{0,3},{1,0},{2,1},{3,2},{4,7},{5,4},{6,5},{7,6},{8,11},{9,8},{10,9... | collective-permute-start | bytes 2359304 | tf_op jit(solution)/shard_map/ppermute | solution.py:265
  79.8 18.0 %collective-permute-start.15 = (bf16[128,3072]{1,0:T(8,128)(2,1)S(1)}, bf16[128,3072]{1,0:T(8,128)(2,1)S(1)}, u32[]{:S(2)}, u32[]{:S(2)}) collective-permute-start(bf16[128,3072]{1,0:T(8,128)(2,1)S(1)} %get-tuple-element.46.b0), channel_id=1, source_target_pairs={{0,2},{1,3},{2,0},{3,1},{4,6},{5,7},{6,4},{7,5},{8,10},{9,11},{10,... | collective-permute-start | bytes 2359304 | tf_op jit(solution)/shard_map/ppermute | solution.py:265
  81.2 20.5 %collective-permute-start.16 = (bf16[128,3072]{1,0:T(8,128)(2,1)S(1)}, bf16[128,3072]{1,0:T(8,128)(2,1)S(1)}, u32[]{:S(2)}, u32[]{:S(2)}) collective-permute-start(bf16[128,3072]{1,0:T(8,128)(2,1)S(1)} %get-tuple-element.46.b0), channel_id=1, source_target_pairs={{0,1},{1,2},{2,3},{3,0},{4,5},{5,6},{6,7},{7,4},{8,9},{9,10},{10,1... | collective-permute-start | bytes 2359304 | tf_op jit(solution)/shard_map/ppermute | solution.py:265
  83.6 18.1 %copy-start.4 = (bf16[256,384]{1,0:T(8,128)(2,1)S(1)}, bf16[256,384]{1,0:T(8,128)(2,1)}, u32[]{:S(2)}) copy-start(bf16[256,384]{1,0:T(8,128)(2,1)} %get-tuple-element.54.grad_y) | copy-start | bytes 589828
  83.6 26.3 %collective-permute-start.13 = (bf16[64,3072]{1,0:T(8,128)(2,1)S(1)}, bf16[64,3072]{1,0:T(8,128)(2,1)S(1)}, u32[]{:S(2)}, u32[]{:S(2)}) collective-permute-start(bf16[64,3072]{1,0:T(8,128)(2,1)S(1)} %get-tuple-element.58.b0), channel_id=1, source_target_pairs={{0,3},{1,0},{2,1},{3,2},{4,7},{5,4},{6,5},{7,6},{8,11},{9,8},{10,9... | collective-permute-start | bytes 1179656 | tf_op jit(solution)/shard_map/ppermute | solution.py:265
  88.2 21.7 %collective-permute-start.17 = (bf16[64,3072]{1,0:T(8,128)(2,1)S(1)}, bf16[64,3072]{1,0:T(8,128)(2,1)}, u32[]{:S(2)}, u32[]{:S(2)}) collective-permute-start(bf16[64,3072]{1,0:T(8,128)(2,1)S(1)} %get-tuple-element.58.b0), channel_id=1, source_target_pairs={{0,2},{1,3},{2,0},{3,1},{4,6},{5,7},{6,4},{7,5},{8,10},{9,11},{10,... | collective-permute-start | bytes 1179656 | tf_op jit(solution)/shard_map/ppermute | solution.py:265
  97.7 12.5 %collective-permute-start.18 = (bf16[64,3072]{1,0:T(8,128)(2,1)S(1)}, bf16[64,3072]{1,0:T(8,128)(2,1)}, u32[]{:S(2)}, u32[]{:S(2)}) collective-permute-start(bf16[64,3072]{1,0:T(8,128)(2,1)S(1)} %get-tuple-element.58.b0), channel_id=1, source_target_pairs={{0,1},{1,2},{2,3},{3,0},{4,5},{5,6},{6,7},{7,4},{8,9},{9,10},{10,1... | collective-permute-start | bytes 1179656 | tf_op jit(solution)/shard_map/ppermute | solution.py:265
  105.3 15.2 %all-to-all-start.1 = ((f32[32,1,3072]{2,1,0:T(1,128)}), f32[32,1,3072]{2,1,0:T(1,128)}, u32[]{:S(2)}, u32[]{:S(2)}) async-start(f32[32,1,3072]{2,1,0:T(1,128)} %shard_map.118), calls=%async_computation.1 | async-start | bytes 786432 | tf_op jit(solution)/shard_map/all_to_all | solution.py:377
  113.2 10.0 %copy-start.11 = (f32[384]{0:T(512)S(1)}, f32[384]{0:T(512)}, u32[]{:S(2)}) copy-start(f32[384]{0:T(512)} %param.18) | copy-start | bytes 4612
  113.2 1.5 %collective-permute-start.19 = (f32[128,384]{1,0:T(8,128)S(1)}, f32[128,384]{1,0:T(8,128)S(1)}, u32[]{:S(2)}, u32[]{:S(2)}) collective-permute-start(f32[128,384]{1,0:T(8,128)S(1)} %get-tuple-element.60), channel_id=1, source_target_pairs={{0,64},{64,0},{1,65},{65,1},{2,66},{66,2},{3,67},{67,3},{4,68},{68... | collective-permute-start | bytes 589832 | tf_op jit(solution)/shard_map/ppermute | solution.py:387
  114.8 5.7 %collective-permute-start.21 = (f32[4,8,384]{2,1,0:T(8,128)S(1)}, f32[4,8,384]{2,1,0:T(8,128)S(1)}, u32[]{:S(2)}, u32[]{:S(2)}) collective-permute-start(f32[4,8,384]{2,1,0:T(8,128)S(1)} %get-tuple-element.65), channel_id=1, source_target_pairs={{0,16},{16,32},{32,48},{48,0},{1,17},{17,33},{33,49},{49,1},{2,18}... | collective-permute-start | bytes 147464 | tf_op jit(solution)/shard_map/ppermute | solution.py:392
  116.3 6.0 %collective-permute-start.20 = (f32[4,8,384]{2,1,0:T(8,128)S(1)}, f32[4,8,384]{2,1,0:T(8,128)S(1)}, u32[]{:S(2)}, u32[]{:S(2)}) collective-permute-start(f32[4,8,384]{2,1,0:T(8,128)S(1)} %get-tuple-element.66), channel_id=1, source_target_pairs={{0,32},{16,48},{32,0},{48,16},{1,33},{17,49},{33,1},{49,17},{2,34}... | collective-permute-start | bytes 147464 | tf_op jit(solution)/shard_map/ppermute | solution.py:392
  119.0 4.1 %collective-permute-start.22 = (f32[4,8,384]{2,1,0:T(8,128)S(1)}, f32[4,8,384]{2,1,0:T(8,128)S(1)}, u32[]{:S(2)}, u32[]{:S(2)}) collective-permute-start(f32[4,8,384]{2,1,0:T(8,128)S(1)} %get-tuple-element.64), channel_id=1, source_target_pairs={{0,48},{16,0},{32,16},{48,32},{1,49},{17,1},{33,17},{49,33},{2,50}... | collective-permute-start | bytes 147464 | tf_op jit(solution)/shard_map/ppermute | solution.py:392
